TPU v7x, 512 devices: a whole 4x4x16 slice. The times are simulated.
512 devices in a mesh: branch: 4 (over z_lo), row: 16 (over x, y), col: 8 (over z_hi, core).
Axes of the slice: x: 4, y: 4, z: 16 (z_hi: 4, z_lo: 4; z = z_hi * 4 + z_lo), core: 2. Of those that a mesh axis runs over, the one named last changes fastest.
Arguments:
- alignment: bfloat16 [256, 512, 256], P(('branch', 'row'), 'col'), may hold values from -32 to 32
- pair_features: bfloat16 [512, 512, 128], P('col', 'row'), may hold values from -32 to 32
- w_row: bfloat16 [256, 1024], replicated, may hold values from -8 to 8
- row_output_weight: bfloat16 [256, 256], replicated, may hold values from -1.5 to 1.5
- w_bias: bfloat16 [128, 8], replicated, may hold values from -1 to 1
- w_column: bfloat16 [256, 1024], replicated, may hold values from -8 to 8
- column_output_weight: bfloat16 [256, 256], replicated, may hold values from -1.5 to 1.5
- outer_input_weight: bfloat16 [256, 64], replicated, may hold values from -0.375 to 0.375
- w_outer_out: bfloat16 [1024, 128], replicated, may hold values from -1.5 to 1.5
- w_triangle_in: bfloat16 [128, 512], replicated, may hold values from -0.5 to 0.5
- w_triangle_gate: bfloat16 [128, 128], replicated, may hold values from -0.5 to 0.5
- w_triangle_out: bfloat16 [128, 128], replicated, may hold values from -0.5 to 0.5
Outputs:
- alignment_out: bfloat16 [256, 512, 256], P(('branch', 'row'), 'col')
- pair_out: bfloat16 [512, 512, 128], P('col', 'row', 'branch')
All inputs are finite; a program needn't handle non-finite values.
Results may differ from a plain program's by a relative error of at most 0.013.
Values may be sent and summed in bfloat16 or wider, within the bound.
No kernel may reach another device: no remote copies, remote signals or barrier semaphores. Data moves between devices by JAX's collectives and lax.ppermute only.
A program may use at most 64 MiB of HBM per device.

v0:
```python
import functools

import jax
import jax.numpy as jnp
from jax import lax
from jax.experimental import pallas as pl
from jax.experimental.pallas import tpu as pltpu
from jax.sharding import PartitionSpec as P

BF = jnp.bfloat16
F32 = jnp.float32
EPSILON = 1e-05
SCALE = 32**-0.5

NT = (((1,), (1,)), ((), ()))
TN = (((0,), (0,)), ((), ()))
TT = (((0,), (1,)), ((), ()))


def mm(a, b, dims):
    return lax.dot_general(a, b, dims, preferred_element_type=F32)


def layer_norm(inputs):
    inputs = inputs.astype(F32)
    average = jnp.mean(inputs, axis=-1, keepdims=True)
    centered = inputs - average
    variance = jnp.mean(jnp.square(centered), axis=-1, keepdims=True)
    return centered * lax.rsqrt(variance + EPSILON)


def sigmoid(x):
    return 1.0 / (1.0 + jnp.exp(-x))


def softmax_rows(scores):
    top = jnp.max(scores, axis=0, keepdims=True)
    weights = jnp.exp(scores - top)
    total = jnp.sum(weights, axis=0, keepdims=True)
    return (weights * (1.0 / total)).astype(BF)


def row_kernel(place, *refs):
    blocks = refs[:8]
    w_ref, bias_ref, wo_ref, out_ref, rows = refs[8:]
    me = place[0]
    own = None
    for m in range(8):
        normed = layer_norm(blocks[m][0]).astype(BF)
        if m == 0:
            own = normed
        start = pl.multiple_of((me ^ m) * 64, 64)
        rows[pl.ds(start, 64), :] = normed
    x = rows[...]
    key = jnp.dot(x, w_ref[:, 256:512], preferred_element_type=F32).astype(BF)
    value_t = mm(w_ref[:, 512:768], x, TT).astype(BF)
    query_t = (mm(w_ref[:, 0:256], own, TT) * SCALE).astype(BF)
    gate_t = sigmoid(mm(w_ref[:, 768:1024], own, TT))
    twice = jnp.concatenate([query_t, query_t], axis=1)
    head_row = lax.broadcasted_iota(jnp.int32, (256, 128), 0) // 32
    head_lane = lax.broadcasted_iota(jnp.int32, (256, 128), 1) // 64
    upper = lax.broadcasted_iota(jnp.int32, (64, 64), 0) < 32
    parts = []
    for p in range(4):
        diag = jnp.where(head_row == 2 * p + head_lane, twice, jnp.zeros_like(twice))
        scores = jnp.dot(key, diag, preferred_element_type=F32)
        scores = scores + bias_ref[:, p * 128 : (p + 1) * 128].astype(F32)
        weights = softmax_rows(scores)
        mixed = jnp.dot(value_t[p * 64 : (p + 1) * 64], weights, preferred_element_type=F32)
        parts.append(jnp.where(upper, mixed[:, :64], mixed[:, 64:]))
    attended_t = jnp.concatenate(parts, axis=0)
    gated = (gate_t * attended_t).astype(BF)
    update = mm(gated, wo_ref[...], TN)
    out_ref[0] = (blocks[0][0].astype(F32) + update).astype(BF)


def row_attention(place, blocks, w_row, bias, w_out):
    block = pl.BlockSpec((1, 64, 256), lambda s, p: (s, 0, 0))
    full = lambda *shape: pl.BlockSpec(shape, lambda s, p: (0,) * len(shape))
    return pl.pallas_call(
        row_kernel,
        out_shape=jax.ShapeDtypeStruct((4, 64, 256), BF),
        grid_spec=pltpu.PrefetchScalarGridSpec(
            num_scalar_prefetch=1,
            grid=(4,),
            in_specs=[block] * 8 + [full(256, 1024), full(512, 512), full(256, 256)],
            out_specs=block,
            scratch_shapes=[pltpu.VMEM((512, 256), BF)],
        ),
        name="row_attention",
    )(place, *blocks, w_row, bias, w_out)


def column_kernel(x_ref, w_ref, wo_ref, wf_ref, out_ref, factor_ref):
    x = x_ref[...]
    normed = layer_norm(x).astype(BF)
    key = jnp.dot(normed, w_ref[:, 256:512], preferred_element_type=F32).astype(BF)
    value_t = mm(w_ref[:, 512:768], normed, TT).astype(BF)
    query_t = (mm(w_ref[:, 0:256], normed, TT) * SCALE).astype(BF)
    gate_t = sigmoid(mm(w_ref[:, 768:1024], normed, TT))
    head_row = lax.broadcasted_iota(jnp.int32, (256, 256), 0) // 32
    parts = []
    for h in range(8):
        diag = jnp.where(head_row == h, query_t, jnp.zeros_like(query_t))
        weights = softmax_rows(jnp.dot(key, diag, preferred_element_type=F32))
        parts.append(
            jnp.dot(value_t[h * 32 : (h + 1) * 32], weights, preferred_element_type=F32)
        )
    gated = (gate_t * jnp.concatenate(parts, axis=0)).astype(BF)
    result = (x.astype(F32) + mm(gated, wo_ref[...], TN)).astype(BF)
    out_ref[...] = result
    factor_ref[...] = mm(wf_ref[...], layer_norm(result).astype(BF), TT).astype(BF)


def column_attention(x, w_column, w_out, w_factor):
    return pl.pallas_call(
        column_kernel,
        out_shape=(jax.ShapeDtypeStruct((256, 256), BF), jax.ShapeDtypeStruct((64, 256), BF)),
        name="column_attention",
    )(x, w_column, w_out, w_factor)


def pick_kernel(index, source_ref, out_ref):
    for r in range(16):
        out_ref[r] = source_ref[index[r // 2]]


def pick(index, source):
    return pl.pallas_call(
        pick_kernel,
        out_shape=jax.ShapeDtypeStruct((16, 32, 256), BF),
        grid_spec=pltpu.PrefetchScalarGridSpec(
            num_scalar_prefetch=1,
            grid=(1,),
            in_specs=[pl.BlockSpec((8, 32, 256), lambda g, p: (0, 0, 0))],
            out_specs=pl.BlockSpec((16, 32, 256), lambda g, p: (0, 0, 0)),
        ),
        name="pick",
    )(index, source)


def sides_kernel(n_ref, w_ref, out_ref, scratch):
    rows = n_ref[...]
    lane = lax.broadcasted_iota(jnp.int32, (64, 128), 1) < 64
    for side in range(2):
        base = side * 256
        value = mm(w_ref[:, base : base + 128], rows, TT)
        gate = mm(w_ref[:, base + 128 : base + 256], rows, TT)
        both = sigmoid(gate) * value
        for pair in range(4):
            low = both[:64, pair * 128 : (pair + 1) * 128]
            high = both[64:, pair * 128 : (pair + 1) * 128]
            scratch[side, :, 2 * pair, :] = jnp.where(lane, low, pltpu.roll(high, 64, 1))
            scratch[side, :, 2 * pair + 1, :] = jnp.where(lane, pltpu.roll(low, 64, 1), high)
    out_ref[:, 0] = scratch[0].astype(BF)
    out_ref[:, 1] = scratch[1].astype(BF)


def triangle_sides(normed, w_in):
    return pl.pallas_call(
        sides_kernel,
        out_shape=jax.ShapeDtypeStruct((64, 2, 8, 128), BF),
        scratch_shapes=[pltpu.VMEM((2, 64, 8, 128), F32)],
        name="triangle_sides",
    )(normed, w_in)


def triangle_kernel(place, left_ref, *refs):
    rights, out_ref = refs[:8], refs[8]
    me = place[0]
    left = left_ref[...]
    lane = lax.broadcasted_iota(jnp.int32, (64, 128), 1) < 64
    for m in range(8):
        product = mm(rights[m][...], left, TN)
        block = jnp.where(lane, product[:64], product[64:]).astype(BF)
        target = (me ^ m) * 2
        for b in range(4):
            for h in range(2):
                out_ref[b * 16 + target + h] = block[(b * 2 + h) * 8 : (b * 2 + h + 1) * 8]


def triangle_sums(place, left, rights):
    full = lambda *shape: pl.BlockSpec(shape, lambda g, p: (0,) * len(shape))
    return pl.pallas_call(
        triangle_kernel,
        out_shape=jax.ShapeDtypeStruct((64, 8, 128), BF),
        grid_spec=pltpu.PrefetchScalarGridSpec(
            num_scalar_prefetch=1,
            grid=(1,),
            in_specs=[full(512, 128)] * 9,
            out_specs=full(64, 8, 128),
        ),
        name="triangle_sums",
    )(place, left, *rights)


def output_kernel(sum_ref, mid_ref, n_ref, wg_ref, w_ref, out_ref, scratch):
    sums = sum_ref[...].astype(F32)
    fold = lambda v: (v + pltpu.roll(v, 64, 1)) * (1.0 / 128)
    average = fold(jnp.sum(sums, axis=0))
    centered = sums - average[None]
    variance = fold(jnp.sum(jnp.square(centered), axis=0))
    scratch[...] = centered * lax.rsqrt(variance + EPSILON)[None]
    gate = sigmoid(jnp.dot(n_ref[...], wg_ref[...], preferred_element_type=F32))
    for j in range(8):
        product = mm(scratch[:, j, :].astype(BF), w_ref[...], TN)
        mixed = product[:64, :128] + product[64:, 128:]
        part = mid_ref[j].astype(F32) + gate[j * 64 : (j + 1) * 64] * mixed
        out_ref[j] = part.astype(BF)


def pair_output(sums, mid, normed, w_gate, w_out):
    return pl.pallas_call(
        output_kernel,
        out_shape=jax.ShapeDtypeStruct((8, 64, 128), BF),
        scratch_shapes=[pltpu.VMEM((64, 8, 128), F32)],
        name="pair_output",
    )(sums, mid, normed, w_gate, w_out)


def swap(x, mask):
    return lax.ppermute(x, "col", [(c, c ^ mask) for c in range(8)])


def to_targets(x):
    s = x.reshape(4, 2, 4, 8, 2, 128)
    return jnp.transpose(s, (2, 1, 3, 4, 0, 5)).reshape(64, 8, 128)


def local(
    alignment,
    pair_features,
    w_row,
    row_output_weight,
    w_bias,
    w_column,
    column_output_weight,
    outer_input_weight,
    w_outer_out,
    w_triangle_in,
    w_triangle_gate,
    w_triangle_out,
):
    branch = lax.axis_index("branch")
    row = lax.axis_index("row")
    col = lax.axis_index("col")
    place = col.reshape(1).astype(jnp.int32)
    both = ("branch", "row")

    near, far = {0: alignment}, {}
    for mask in (2, 6, 4):
        near[mask] = swap(alignment, mask)
    for mask in (0, 2, 6, 4):
        far[mask ^ 1] = swap(near[mask], 1)
    blocks = [(near | far)[m] for m in range(8)]

    pair_normed = layer_norm(pair_features).astype(BF)
    bias_tile = jnp.einsum(
        "ijc,ch->jhi", pair_normed, w_bias, preferred_element_type=F32
    ).astype(BF)
    bias_tile = bias_tile.reshape(32, 512)
    bias = lax.all_to_all(
        jnp.broadcast_to(bias_tile[None], (16, 32, 512)), "row", 0, 0, tiled=True
    ).reshape(512, 512)

    pair_part = lax.dynamic_slice_in_dim(pair_features, branch * 8, 8, 1)
    pair_part = jnp.transpose(pair_part.reshape(2, 4, 8, 8, 128), (3, 1, 0, 2, 4))
    pair_part = pair_part.reshape(8, 64, 128)

    alignment_row = row_attention(place, blocks, w_row, bias, row_output_weight)
    columns = lax.all_to_all(to_targets(alignment_row), both, 0, 0, tiled=True)
    columns = jnp.transpose(columns.reshape(64, 2, 4, 128), (0, 2, 1, 3)).reshape(256, 256)
    column_new, factors = column_attention(
        columns, w_column, column_output_weight, outer_input_weight
    )

    left = lax.all_to_all(
        jnp.broadcast_to(factors[None, :32], (64, 32, 256)), both, 0, 0, tiled=True
    )
    right = factors[None, 32:]
    right = jnp.concatenate([right, swap(right, 1)])
    right = jnp.concatenate([right, swap(right, 2)])
    right = jnp.concatenate([right, swap(right, 6)])
    relative = jnp.arange(8, dtype=jnp.int32) ^ col.astype(jnp.int32)
    position = jnp.where(relative >= 4, relative ^ 2, relative)
    right = lax.all_to_all(pick(position, right), "row", 0, 0, tiled=True)
    right = lax.dynamic_slice_in_dim(right, (row % 2) * 8, 8, 0)

    outer = jnp.einsum("ncs,jes->jnce", left, right, preferred_element_type=F32) * (1.0 / 256)
    update = jnp.dot(
        outer.reshape(512, 1024).astype(BF), w_outer_out, preferred_element_type=F32
    ).astype(BF)
    pair_mid = (pair_part.reshape(512, 128).astype(F32) + update.astype(F32)).astype(BF)
    tri_normed = layer_norm(pair_mid).astype(BF)
    sides = triangle_sides(tri_normed, w_triangle_in)

    returning = jnp.transpose(column_new.reshape(64, 4, 2, 128), (0, 2, 1, 3))
    message = jnp.concatenate([sides, returning.reshape(64, 1, 8, 128)], axis=1)
    message = lax.all_to_all(message, both, 0, 0, tiled=True)
    back = message[:, 2].reshape(4, 2, 8, 2, 4, 128)
    alignment_out = jnp.transpose(back, (4, 1, 0, 2, 3, 5)).reshape(4, 64, 256)
    tri_left = message[:, 0].reshape(512, 128)
    tri_right = message[:, 1].reshape(512, 128)
    near, far = {0: tri_right}, {}
    for mask in (2, 6, 4):
        near[mask] = swap(tri_right, mask)
    for mask in (0, 2, 6, 4):
        far[mask ^ 1] = swap(near[mask], 1)
    rights = [(near | far)[m] for m in range(8)]
    sums = triangle_sums(place, tri_left, rights)
    sums = lax.all_to_all(sums, both, 0, 0, tiled=True)
    w_out = jnp.concatenate([w_triangle_out[:64], w_triangle_out[64:]], axis=1)
    pair_new = pair_output(sums, pair_mid.reshape(8, 64, 128), tri_normed, w_triangle_gate, w_out)

    parts = jnp.transpose(pair_new.reshape(8, 64, 4, 32), (2, 0, 1, 3))
    parts = lax.all_to_all(parts, "branch", 0, 0, tiled=True)
    parts = parts.reshape(4, 8, 4, 2, 8, 32)
    pair_out = jnp.transpose(parts, (3, 2, 4, 0, 1, 5)).reshape(64, 32, 32)
    return (alignment_out, pair_out)


def solution(mesh):
    in_specs = (P(("branch", "row"), "col", None), P("col", "row", None)) + (P(),) * 10
    out_specs = (P(("branch", "row"), "col", None), P("col", "row", "branch"))
    return jax.shard_map(local, mesh=mesh, in_specs=in_specs, out_specs=out_specs, check_vma=False)
```

profile of v0, /device:TPU:32, one launch (start us, length us, event | category | flops | bytes accessed | tf_op | source)
XLA Modules:
  0.0 285.4 jit_solution(12459294556870669828)
XLA Ops:
  0.7 1.4 convert_reduce_fusion
  2.1 1.7 fusion.7
  3.8 1.9 fusion.6
  6.9 7.2 %all-to-all-start = ((bf16[16,32,512]{2,1,0:T(8,128)(2,1)}), bf16[16,32,512]{2,1,0:T(8,128)(2,1)S(1)}, u32[]{:S(2)}, u32[]{:S(2)}) async-start(bf16[16,32,512]{2,1,0:T(8,128)(2,1)} %broadcast_in_dim.9), calls=%async_computation | async-start | bytes 1048576 | tf_op jit(solution)/shard_map/all_to_all | solution.py:262
  14.0 9.1 %collective-permute-start.1 = (bf16[4,64,256]{2,1,0:T(8,128)(2,1)S(1)}, bf16[4,64,256]{2,1,0:T(8,128)(2,1)S(1)}, u32[]{:S(2)}, u32[]{:S(2)}) collective-permute-start(bf16[4,64,256]{2,1,0:T(8,128)(2,1)S(1)} %copy-done.6), channel_id=1, source_target_pairs={{0,2},{1,3},{2,0},{3,1},{4,6},{5,7},{6,4},{7,5},{8,10},{9,11},{10,... | collective-permute-start | bytes 393224 | tf_op jit(solution)/shard_map/ppermute | solution.py:222
  23.1 10.0 %collective-permute-start.3 = (bf16[4,64,256]{2,1,0:T(8,128)(2,1)S(1)}, bf16[4,64,256]{2,1,0:T(8,128)(2,1)S(1)}, u32[]{:S(2)}, u32[]{:S(2)}) collective-permute-start(bf16[4,64,256]{2,1,0:T(8,128)(2,1)S(1)} %copy-done.6), channel_id=1, source_target_pairs={{0,4},{1,5},{2,6},{3,7},{4,0},{5,1},{6,2},{7,3},{8,12},{9,13},{10,... | collective-permute-start | bytes 393224 | tf_op jit(solution)/shard_map/ppermute | solution.py:222
  33.2 1.9 collective-permute-start.5
  35.1 1.9 collective-permute-start
  37.1 2.4 collective-permute-start.2
  39.5 2.4 collective-permute-done.3.refs_4_
  41.9 1.9 collective-permute-start.4
  43.8 11.7 %collective-permute-done.5.refs_6_ = bf16[4,64,256]{2,1,0:T(8,128)(2,1)S(1)} collective-permute-done((bf16[4,64,256]{2,1,0:T(8,128)(2,1)S(1)}, bf16[4,64,256]{2,1,0:T(8,128)(2,1)S(1)}, u32[]{:S(2)}, u32[]{:S(2)}) %collective-permute-start.5) | collective-permute-done | bytes 131104 | tf_op jit(solution)/shard_map/ppermute | solution.py:222
  55.5 1.9 collective-permute-start.6
  59.6 12.8 %row_attention.1 = bf16[4,64,256]{2,1,0:T(8,128)(2,1)} custom-call(s32[1]{0:T(128)} %bitcast.3.place, bf16[4,64,256]{2,1,0:T(8,128)(2,1)} %refs_0_.1, bf16[4,64,256]{2,1,0:T(8,128)(2,1)} %copy-done.11, bf16[4,64,256]{2,1,0:T(8,128)(2,1)} %copy-done.7, bf16[4,64,256]{2,1,0:T(8,128)(2,1)} %copy-done.14, bf16[4,64,256]{2,1,0:T(8,128)(2,1)} %copy-done.8, ...), custom_call_target="tpu_custom_call" | custom-call | tf_op jit(solution)/shard_map/row_attention/pallas_call | solution.py:80
  74.1 12.0 %all-to-all-start.1 = ((bf16[64,8,128]{2,1,0:T(8,128)(2,1)}), bf16[64,8,128]{2,1,0:T(8,128)(2,1)S(1)}, u32[]{:S(2)}, u32[]{:S(2)}) async-start(bf16[64,8,128]{2,1,0:T(8,128)(2,1)} %copy.45), calls=%async_computation.1 | async-start | bytes 262144 | tf_op jit(solution)/shard_map/all_to_all | solution.py:271
  86.8 8.9 %all-to-all-done.1 = bf16[64,8,128]{2,1,0:T(8,128)(2,1)S(1)} async-done(((bf16[64,8,128]{2,1,0:T(8,128)(2,1)}), bf16[64,8,128]{2,1,0:T(8,128)(2,1)S(1)}, u32[]{:S(2)}, u32[]{:S(2)}) %all-to-all-start.1) | async-done | bytes 131104 | tf_op jit(solution)/shard_map/all_to_all | solution.py:271
  96.6 5.2 %column_attention.1 = (bf16[256,256]{1,0:T(8,128)(2,1)}, bf16[64,256]{1,0:T(8,128)(2,1)}) custom-call(bf16[256,256]{1,0:T(8,128)(2,1)} %bitcast.80, bf16[256,1024]{1,0:T(8,128)(2,1)} %w_ref.2, bf16[256,256]{1,0:T(8,128)(2,1)} %wo_ref.1, bf16[256,64]{1,0:T(8,128)(2,1)} %copy.48.wf_ref), custom_call_target="tpu_custom_call" | custom-call | tf_op jit(solution)/shard_map/column_attention/pallas_call | solution.py:116
  102.5 1.9 collective-permute-start.7
  105.6 5.4 %collective-permute-start.8 = (bf16[2,32,256]{2,1,0:T(8,128)(2,1)S(1)}, bf16[2,32,256]{2,1,0:T(8,128)(2,1)S(1)}, u32[]{:S(2)}, u32[]{:S(2)}) collective-permute-start(bf16[2,32,256]{2,1,0:T(8,128)(2,1)S(1)} %pad_maximum_fusion.3), channel_id=1, source_target_pairs={{0,2},{1,3},{2,0},{3,1},{4,6},{5,7},{6,4},{7,5},{8,10},{9,11},{10,... | collective-permute-start | bytes 98312 | tf_op jit(solution)/shard_map/ppermute | solution.py:222
  111.0 5.3 %collective-permute-done.8 = bf16[2,32,256]{2,1,0:T(8,128)(2,1)S(1)} collective-permute-done((bf16[2,32,256]{2,1,0:T(8,128)(2,1)S(1)}, bf16[2,32,256]{2,1,0:T(8,128)(2,1)S(1)}, u32[]{:S(2)}, u32[]{:S(2)}) %collective-permute-start.8) | collective-permute-done | bytes 32800 | tf_op jit(solution)/shard_map/ppermute | solution.py:222
  116.2 7.5 %collective-permute-start.9 = (bf16[4,32,256]{2,1,0:T(8,128)(2,1)S(1)}, bf16[4,32,256]{2,1,0:T(8,128)(2,1)S(1)}, u32[]{:S(2)}, u32[]{:S(2)}) collective-permute-start(bf16[4,32,256]{2,1,0:T(8,128)(2,1)S(1)} %pad_maximum_fusion.2), channel_id=1, source_target_pairs={{0,6},{1,7},{2,4},{3,5},{4,2},{5,3},{6,0},{7,1},{8,14},{9,15},{10,... | collective-permute-start | bytes 196616 | tf_op jit(solution)/shard_map/ppermute | solution.py:222
  124.2 2.8 collective-permute-done.9
  127.7 2.3 pick.1
  130.0 12.7 %all_to_all.35 = bf16[16,32,256]{2,1,0:T(8,128)(2,1)S(1)} all-to-all(bf16[16,32,256]{2,1,0:T(8,128)(2,1)} %pick.1), channel_id=1, replica_groups=mesh['branch'=4,'row'=16,'col'=8] {'row'}, dimensions={0} | all-to-all | bytes 524288 | tf_op jit(solution)/shard_map/all_to_all | solution.py:286
  143.8 8.4 %all-to-all-start.3 = ((bf16[64,32,256]{2,1,0:T(8,128)(2,1)}), bf16[64,32,256]{2,1,0:T(8,128)(2,1)S(1)}, u32[]{:S(2)}, u32[]{:S(2)}) async-start(bf16[64,32,256]{2,1,0:T(8,128)(2,1)} %broadcast_in_dim.11), calls=%async_computation.3 | async-start | bytes 2097152 | tf_op jit(solution)/shard_map/all_to_all | solution.py:277
  154.7 20.9 %all-to-all-done.3 = bf16[64,32,256]{2,1,0:T(8,128)(2,1)S(1)} async-done(((bf16[64,32,256]{2,1,0:T(8,128)(2,1)}), bf16[64,32,256]{2,1,0:T(8,128)(2,1)S(1)}, u32[]{:S(2)}, u32[]{:S(2)}) %all-to-all-start.3) | async-done | bytes 1048608 | tf_op jit(solution)/shard_map/all_to_all | solution.py:277
  175.6 1.7 fusion
  177.3 2.4 copy.50
  181.1 1.5 convert_reduce_fusion.1
  183.7 2.4 triangle_sides.1
  187.1 20.2 %all_to_all.36 = bf16[64,3,8,128]{3,2,1,0:T(8,128)(2,1)S(1)} all-to-all(bf16[64,3,8,128]{3,2,1,0:T(8,128)(2,1)S(1)} %pad_maximum_fusion), channel_id=1, replica_groups=mesh['branch'=4,'row'=16,'col'=8] {'branch','row'}, dimensions={0} | all-to-all | bytes 786432 | tf_op jit(solution)/shard_map/all_to_all | solution.py:299
  208.0 5.9 %collective-permute-start.11 = (bf16[512,128]{1,0:T(8,128)(2,1)S(1)}, bf16[512,128]{1,0:T(8,128)(2,1)S(1)}, u32[]{:S(2)}, u32[]{:S(2)}) collective-permute-start(bf16[512,128]{1,0:T(8,128)(2,1)S(1)} %get-tuple-element.12.refs_0_), channel_id=1, source_target_pairs={{0,2},{1,3},{2,0},{3,1},{4,6},{5,7},{6,4},{7,5},{8,10},{9,11},{10,... | collective-permute-start | bytes 393224 | tf_op jit(solution)/shard_map/ppermute | solution.py:222
  213.9 10.4 %collective-permute-start.13 = (bf16[512,128]{1,0:T(8,128)(2,1)S(1)}, bf16[512,128]{1,0:T(8,128)(2,1)S(1)}, u32[]{:S(2)}, u32[]{:S(2)}) collective-permute-start(bf16[512,128]{1,0:T(8,128)(2,1)S(1)} %get-tuple-element.12.refs_0_), channel_id=1, source_target_pairs={{0,4},{1,5},{2,6},{3,7},{4,0},{5,1},{6,2},{7,3},{8,12},{9,13},{10,... | collective-permute-start | bytes 393224 | tf_op jit(solution)/shard_map/ppermute | solution.py:222
  224.3 1.9 collective-permute-start.15
  226.2 1.9 collective-permute-start.10
  228.1 1.3 collective-permute-done.11.refs_2_
  229.5 1.9 collective-permute-start.12
  231.4 2.8 collective-permute-done.13.refs_4_
  234.2 1.9 collective-permute-start.14
  236.1 9.7 %collective-permute-done.15.refs_6_ = bf16[512,128]{1,0:T(8,128)(2,1)S(1)} collective-permute-done((bf16[512,128]{1,0:T(8,128)(2,1)S(1)}, bf16[512,128]{1,0:T(8,128)(2,1)S(1)}, u32[]{:S(2)}, u32[]{:S(2)}) %collective-permute-start.15) | collective-permute-done | bytes 131104 | tf_op jit(solution)/shard_map/ppermute | solution.py:222
  245.8 1.9 collective-permute-start.16
  249.7 2.5 triangle_sums.1
  252.2 6.1 %all-to-all-start.5 = ((bf16[64,8,128]{2,1,0:T(8,128)(2,1)}), bf16[64,8,128]{2,1,0:T(8,128)(2,1)S(1)}, u32[]{:S(2)}, u32[]{:S(2)}) async-start(bf16[64,8,128]{2,1,0:T(8,128)(2,1)} %triangle_sums.1), calls=%async_computation.5 | async-start | bytes 262144 | tf_op jit(solution)/shard_map/all_to_all | solution.py:311
  258.8 9.0 %all-to-all-done.5.sum_ref = bf16[64,8,128]{2,1,0:T(8,128)(2,1)S(1)} async-done(((bf16[64,8,128]{2,1,0:T(8,128)(2,1)}), bf16[64,8,128]{2,1,0:T(8,128)(2,1)S(1)}, u32[]{:S(2)}, u32[]{:S(2)}) %all-to-all-start.5) | async-done | bytes 131104 | tf_op jit(solution)/shard_map/all_to_all | solution.py:311
  268.5 2.5 pair_output.1
  273.1 5.1 %all-to-all-start.6 = ((bf16[4,2,8192]{2,1,0:T(2,128)(2,1)}), bf16[4,2,8192]{2,1,0:T(2,128)(2,1)S(1)}, u32[]{:S(2)}, u32[]{:S(2)}) async-start(bf16[4,2,8192]{2,1,0:T(2,128)(2,1)} %reshape.94), calls=%async_computation.6 | async-start | bytes 262144 | tf_op jit(solution)/shard_map/all_to_all | solution.py:316
  278.8 4.5 %all-to-all-done.6 = bf16[4,2,8192]{2,1,0:T(2,128)(2,1)S(1)} async-done(((bf16[4,2,8192]{2,1,0:T(2,128)(2,1)}), bf16[4,2,8192]{2,1,0:T(2,128)(2,1)S(1)}, u32[]{:S(2)}, u32[]{:S(2)}) %all-to-all-start.6) | async-done | bytes 131104 | tf_op jit(solution)/shard_map/all_to_all | solution.py:316
  284.1 1.3 copy.57
  (96 shorter events, 23.8 us)
Async XLA Ops:
  0.6 180.4 %copy-start = (bf16[1024,128]{1,0:T(8,128)(2,1)S(1)}, bf16[1024,128]{1,0:T(8,128)(2,1)}, u32[]{:S(2)}) copy-start(bf16[1024,128]{1,0:T(8,128)(2,1)} %param.20) | copy-start | bytes 786436
  0.6 13.4 %copy-start.6 = (bf16[4,64,256]{2,1,0:T(8,128)(2,1)S(1)}, bf16[4,64,256]{2,1,0:T(8,128)(2,1)}, u32[]{:S(2)}) copy-start(bf16[4,64,256]{2,1,0:T(8,128)(2,1)} %refs_0_.1) | copy-start | bytes 393220
  6.9 79.2 %copy-start.22 = (bf16[256,64]{0,1:T(8,128)(2,1)S(1)}, bf16[256,64]{0,1:T(8,128)(2,1)}, u32[]{:S(2)}) copy-start(bf16[256,64]{0,1:T(8,128)(2,1)} %param.19) | copy-start | bytes 98308
  6.9 51.9 %all-to-all-start = ((bf16[16,32,512]{2,1,0:T(8,128)(2,1)}), bf16[16,32,512]{2,1,0:T(8,128)(2,1)S(1)}, u32[]{:S(2)}, u32[]{:S(2)}) async-start(bf16[16,32,512]{2,1,0:T(8,128)(2,1)} %broadcast_in_dim.9), calls=%async_computation | async-start | bytes 1048576 | tf_op jit(solution)/shard_map/all_to_all | solution.py:262
  14.0 23.0 %collective-permute-start.1 = (bf16[4,64,256]{2,1,0:T(8,128)(2,1)S(1)}, bf16[4,64,256]{2,1,0:T(8,128)(2,1)S(1)}, u32[]{:S(2)}, u32[]{:S(2)}) collective-permute-start(bf16[4,64,256]{2,1,0:T(8,128)(2,1)S(1)} %copy-done.6), channel_id=1, source_target_pairs={{0,2},{1,3},{2,0},{3,1},{4,6},{5,7},{6,4},{7,5},{8,10},{9,11},{10,... | collective-permute-start | bytes 393224 | tf_op jit(solution)/shard_map/ppermute | solution.py:222
  23.1 18.7 %collective-permute-start.3 = (bf16[4,64,256]{2,1,0:T(8,128)(2,1)S(1)}, bf16[4,64,256]{2,1,0:T(8,128)(2,1)S(1)}, u32[]{:S(2)}, u32[]{:S(2)}) collective-permute-start(bf16[4,64,256]{2,1,0:T(8,128)(2,1)S(1)} %copy-done.6), channel_id=1, source_target_pairs={{0,4},{1,5},{2,6},{3,7},{4,0},{5,1},{6,2},{7,3},{8,12},{9,13},{10,... | collective-permute-start | bytes 393224 | tf_op jit(solution)/shard_map/ppermute | solution.py:222
  33.2 22.3 %collective-permute-start.5 = (bf16[4,64,256]{2,1,0:T(8,128)(2,1)S(1)}, bf16[4,64,256]{2,1,0:T(8,128)(2,1)S(1)}, u32[]{:S(2)}, u32[]{:S(2)}) collective-permute-start(bf16[4,64,256]{2,1,0:T(8,128)(2,1)S(1)} %copy-done.6), channel_id=1, source_target_pairs={{0,6},{1,7},{2,4},{3,5},{4,2},{5,3},{6,0},{7,1},{8,14},{9,15},{10,... | collective-permute-start | bytes 393224 | tf_op jit(solution)/shard_map/ppermute | solution.py:222
  35.1 22.3 %collective-permute-start = (bf16[4,64,256]{2,1,0:T(8,128)(2,1)S(1)}, bf16[4,64,256]{2,1,0:T(8,128)(2,1)S(1)}, u32[]{:S(2)}, u32[]{:S(2)}) collective-permute-start(bf16[4,64,256]{2,1,0:T(8,128)(2,1)S(1)} %copy-done.6), channel_id=1, source_target_pairs={{0,1},{1,0},{2,3},{3,2},{4,5},{5,4},{6,7},{7,6},{8,9},{9,8},{10,11... | collective-permute-start | bytes 393224 | tf_op jit(solution)/shard_map/ppermute | solution.py:222
  37.0 21.7 %copy-start.7 = (bf16[4,64,256]{2,1,0:T(8,128)(2,1)}, bf16[4,64,256]{2,1,0:T(8,128)(2,1)S(1)}, u32[]{:S(2)}) copy-start(bf16[4,64,256]{2,1,0:T(8,128)(2,1)S(1)} %collective-permute-done.1.refs_2_) | copy-start | bytes 393220
  37.1 20.4 %collective-permute-start.2 = (bf16[4,64,256]{2,1,0:T(8,128)(2,1)S(1)}, bf16[4,64,256]{2,1,0:T(8,128)(2,1)S(1)}, u32[]{:S(2)}, u32[]{:S(2)}) collective-permute-start(bf16[4,64,256]{2,1,0:T(8,128)(2,1)S(1)} %collective-permute-done.1.refs_2_), channel_id=1, source_target_pairs={{0,1},{1,0},{2,3},{3,2},{4,5},{5,4},{6,7},{7,6},{8,9},{9,8},{10,11... | collective-permute-start | bytes 393224 | tf_op jit(solution)/shard_map/ppermute | solution.py:222
  41.9 16.9 %copy-start.8 = (bf16[4,64,256]{2,1,0:T(8,128)(2,1)}, bf16[4,64,256]{2,1,0:T(8,128)(2,1)S(1)}, u32[]{:S(2)}) copy-start(bf16[4,64,256]{2,1,0:T(8,128)(2,1)S(1)} %collective-permute-done.3.refs_4_) | copy-start | bytes 393220
  41.9 15.6 %collective-permute-start.4 = (bf16[4,64,256]{2,1,0:T(8,128)(2,1)S(1)}, bf16[4,64,256]{2,1,0:T(8,128)(2,1)S(1)}, u32[]{:S(2)}, u32[]{:S(2)}) collective-permute-start(bf16[4,64,256]{2,1,0:T(8,128)(2,1)S(1)} %collective-permute-done.3.refs_4_), channel_id=1, source_target_pairs={{0,1},{1,0},{2,3},{3,2},{4,5},{5,4},{6,7},{7,6},{8,9},{9,8},{10,11... | collective-permute-start | bytes 393224 | tf_op jit(solution)/shard_map/ppermute | solution.py:222
  55.5 3.3 %copy-start.9 = (bf16[4,64,256]{2,1,0:T(8,128)(2,1)}, bf16[4,64,256]{2,1,0:T(8,128)(2,1)S(1)}, u32[]{:S(2)}) copy-start(bf16[4,64,256]{2,1,0:T(8,128)(2,1)S(1)} %collective-permute-done.5.refs_6_) | copy-start | bytes 393220
  55.5 3.2 %collective-permute-start.6 = (bf16[4,64,256]{2,1,0:T(8,128)(2,1)S(1)}, bf16[4,64,256]{2,1,0:T(8,128)(2,1)S(1)}, u32[]{:S(2)}, u32[]{:S(2)}) collective-permute-start(bf16[4,64,256]{2,1,0:T(8,128)(2,1)S(1)} %collective-permute-done.5.refs_6_), channel_id=1, source_target_pairs={{0,1},{1,0},{2,3},{3,2},{4,5},{5,4},{6,7},{7,6},{8,9},{9,8},{10,11... | collective-permute-start | bytes 393224 | tf_op jit(solution)/shard_map/ppermute | solution.py:222
  57.4 1.3 copy-start.11
  57.5 1.3 copy-start.14
  57.5 1.3 copy-start.16
  58.7 0.6 copy-start.18
  58.7 0.9 copy-start.1
  74.1 21.7 %all-to-all-start.1 = ((bf16[64,8,128]{2,1,0:T(8,128)(2,1)}), bf16[64,8,128]{2,1,0:T(8,128)(2,1)S(1)}, u32[]{:S(2)}, u32[]{:S(2)}) async-start(bf16[64,8,128]{2,1,0:T(8,128)(2,1)} %copy.45), calls=%async_computation.1 | async-start | bytes 262144 | tf_op jit(solution)/shard_map/all_to_all | solution.py:271
  102.5 3.1 %collective-permute-start.7 = (bf16[1,32,256]{2,1,0:T(8,128)(2,1)S(1)}, bf16[1,32,256]{2,1,0:T(8,128)(2,1)S(1)}, u32[]{:S(2)}, u32[]{:S(2)}) collective-permute-start(bf16[1,32,256]{2,1,0:T(8,128)(2,1)S(1)} %get-tuple-element.17), channel_id=1, source_target_pairs={{0,1},{1,0},{2,3},{3,2},{4,5},{5,4},{6,7},{7,6},{8,9},{9,8},{10,11... | collective-permute-start | bytes 49160 | tf_op jit(solution)/shard_map/ppermute | solution.py:222
  105.6 10.7 %collective-permute-start.8 = (bf16[2,32,256]{2,1,0:T(8,128)(2,1)S(1)}, bf16[2,32,256]{2,1,0:T(8,128)(2,1)S(1)}, u32[]{:S(2)}, u32[]{:S(2)}) collective-permute-start(bf16[2,32,256]{2,1,0:T(8,128)(2,1)S(1)} %pad_maximum_fusion.3), channel_id=1, source_target_pairs={{0,2},{1,3},{2,0},{3,1},{4,6},{5,7},{6,4},{7,5},{8,10},{9,11},{10,... | collective-permute-start | bytes 98312 | tf_op jit(solution)/shard_map/ppermute | solution.py:222
  116.2 10.8 %collective-permute-start.9 = (bf16[4,32,256]{2,1,0:T(8,128)(2,1)S(1)}, bf16[4,32,256]{2,1,0:T(8,128)(2,1)S(1)}, u32[]{:S(2)}, u32[]{:S(2)}) collective-permute-start(bf16[4,32,256]{2,1,0:T(8,128)(2,1)S(1)} %pad_maximum_fusion.2), channel_id=1, source_target_pairs={{0,6},{1,7},{2,4},{3,5},{4,2},{5,3},{6,0},{7,1},{8,14},{9,15},{10,... | collective-permute-start | bytes 196616 | tf_op jit(solution)/shard_map/ppermute | solution.py:222
  130.0 23.9 %copy-start.21 = (bf16[256,256]{1,0:T(8,128)(2,1)S(1)}, bf16[256,256]{1,0:T(8,128)(2,1)}, u32[]{:S(2)}) copy-start(bf16[256,256]{1,0:T(8,128)(2,1)} %get-tuple-element.5) | copy-start | bytes 393220
  143.8 31.8 %all-to-all-start.3 = ((bf16[64,32,256]{2,1,0:T(8,128)(2,1)}), bf16[64,32,256]{2,1,0:T(8,128)(2,1)S(1)}, u32[]{:S(2)}, u32[]{:S(2)}) async-start(bf16[64,32,256]{2,1,0:T(8,128)(2,1)} %broadcast_in_dim.11), calls=%async_computation.3 | async-start | bytes 2097152 | tf_op jit(solution)/shard_map/all_to_all | solution.py:277
  181.0 5.1 %copy-start.4 = (bf16[64,4,2,128]{3,1,2,0:T(4,128)(2,1)S(1)}, bf16[64,4,2,128]{3,1,2,0:T(4,128)(2,1)}, u32[]{:S(2)}) copy-start(bf16[64,4,2,128]{3,1,2,0:T(4,128)(2,1)} %copy.51) | copy-start | bytes 393220
  182.6 69.6 %copy-start.2 = (bf16[512,128]{1,0:T(8,128)(2,1)}, bf16[512,128]{1,0:T(8,128)(2,1)S(1)}, u32[]{:S(2)}) copy-start(bf16[512,128]{1,0:T(8,128)(2,1)S(1)} %get-tuple-element.20) | copy-start | bytes 393220
  186.1 72.1 %copy-start.23 = (bf16[128,128]{1,0:T(8,128)(2,1)S(1)}, bf16[128,128]{1,0:T(8,128)(2,1)}, u32[]{:S(2)}) copy-start(bf16[128,128]{1,0:T(8,128)(2,1)} %param.23) | copy-start | bytes 98308
  208.0 41.0 %copy-start.3 = (bf16[512,128]{1,0:T(8,128)(2,1)}, bf16[512,128]{1,0:T(8,128)(2,1)S(1)}, u32[]{:S(2)}) copy-start(bf16[512,128]{1,0:T(8,128)(2,1)S(1)} %get-tuple-element.12.refs_0_) | copy-start | bytes 393220
  208.0 21.4 %collective-permute-start.11 = (bf16[512,128]{1,0:T(8,128)(2,1)S(1)}, bf16[512,128]{1,0:T(8,128)(2,1)S(1)}, u32[]{:S(2)}, u32[]{:S(2)}) collective-permute-start(bf16[512,128]{1,0:T(8,128)(2,1)S(1)} %get-tuple-element.12.refs_0_), channel_id=1, source_target_pairs={{0,2},{1,3},{2,0},{3,1},{4,6},{5,7},{6,4},{7,5},{8,10},{9,11},{10,... | collective-permute-start | bytes 393224 | tf_op jit(solution)/shard_map/ppermute | solution.py:222
  213.9 20.3 %collective-permute-start.13 = (bf16[512,128]{1,0:T(8,128)(2,1)S(1)}, bf16[512,128]{1,0:T(8,128)(2,1)S(1)}, u32[]{:S(2)}, u32[]{:S(2)}) collective-permute-start(bf16[512,128]{1,0:T(8,128)(2,1)S(1)} %get-tuple-element.12.refs_0_), channel_id=1, source_target_pairs={{0,4},{1,5},{2,6},{3,7},{4,0},{5,1},{6,2},{7,3},{8,12},{9,13},{10,... | collective-permute-start | bytes 393224 | tf_op jit(solution)/shard_map/ppermute | solution.py:222
  224.3 21.5 %collective-permute-start.15 = (bf16[512,128]{1,0:T(8,128)(2,1)S(1)}, bf16[512,128]{1,0:T(8,128)(2,1)S(1)}, u32[]{:S(2)}, u32[]{:S(2)}) collective-permute-start(bf16[512,128]{1,0:T(8,128)(2,1)S(1)} %get-tuple-element.12.refs_0_), channel_id=1, source_target_pairs={{0,6},{1,7},{2,4},{3,5},{4,2},{5,3},{6,0},{7,1},{8,14},{9,15},{10,... | collective-permute-start | bytes 393224 | tf_op jit(solution)/shard_map/ppermute | solution.py:222
  226.2 21.5 %collective-permute-start.10 = (bf16[512,128]{1,0:T(8,128)(2,1)S(1)}, bf16[512,128]{1,0:T(8,128)(2,1)S(1)}, u32[]{:S(2)}, u32[]{:S(2)}) collective-permute-start(bf16[512,128]{1,0:T(8,128)(2,1)S(1)} %get-tuple-element.12.refs_0_), channel_id=1, source_target_pairs={{0,1},{1,0},{2,3},{3,2},{4,5},{5,4},{6,7},{7,6},{8,9},{9,8},{10,11... | collective-permute-start | bytes 393224 | tf_op jit(solution)/shard_map/ppermute | solution.py:222
  229.4 19.6 %copy-start.10 = (bf16[512,128]{1,0:T(8,128)(2,1)}, bf16[512,128]{1,0:T(8,128)(2,1)S(1)}, u32[]{:S(2)}) copy-start(bf16[512,128]{1,0:T(8,128)(2,1)S(1)} %collective-permute-done.11.refs_2_) | copy-start | bytes 393220
  229.5 18.3 %collective-permute-start.12 = (bf16[512,128]{1,0:T(8,128)(2,1)S(1)}, bf16[512,128]{1,0:T(8,128)(2,1)S(1)}, u32[]{:S(2)}, u32[]{:S(2)}) collective-permute-start(bf16[512,128]{1,0:T(8,128)(2,1)S(1)} %collective-permute-done.11.refs_2_), channel_id=1, source_target_pairs={{0,1},{1,0},{2,3},{3,2},{4,5},{5,4},{6,7},{7,6},{8,9},{9,8},{10,11... | collective-permute-start | bytes 393224 | tf_op jit(solution)/shard_map/ppermute | solution.py:222
  234.2 14.9 %copy-start.12 = (bf16[512,128]{1,0:T(8,128)(2,1)}, bf16[512,128]{1,0:T(8,128)(2,1)S(1)}, u32[]{:S(2)}) copy-start(bf16[512,128]{1,0:T(8,128)(2,1)S(1)} %collective-permute-done.13.refs_4_) | copy-start | bytes 393220
  234.2 13.6 %collective-permute-start.14 = (bf16[512,128]{1,0:T(8,128)(2,1)S(1)}, bf16[512,128]{1,0:T(8,128)(2,1)S(1)}, u32[]{:S(2)}, u32[]{:S(2)}) collective-permute-start(bf16[512,128]{1,0:T(8,128)(2,1)S(1)} %collective-permute-done.13.refs_4_), channel_id=1, source_target_pairs={{0,1},{1,0},{2,3},{3,2},{4,5},{5,4},{6,7},{7,6},{8,9},{9,8},{10,11... | collective-permute-start | bytes 393224 | tf_op jit(solution)/shard_map/ppermute | solution.py:222
  245.8 3.2 %copy-start.13 = (bf16[512,128]{1,0:T(8,128)(2,1)}, bf16[512,128]{1,0:T(8,128)(2,1)S(1)}, u32[]{:S(2)}) copy-start(bf16[512,128]{1,0:T(8,128)(2,1)S(1)} %collective-permute-done.15.refs_6_) | copy-start | bytes 393220
  245.8 3.2 %collective-permute-start.16 = (bf16[512,128]{1,0:T(8,128)(2,1)S(1)}, bf16[512,128]{1,0:T(8,128)(2,1)S(1)}, u32[]{:S(2)}, u32[]{:S(2)}) collective-permute-start(bf16[512,128]{1,0:T(8,128)(2,1)S(1)} %collective-permute-done.15.refs_6_), channel_id=1, source_target_pairs={{0,1},{1,0},{2,3},{3,2},{4,5},{5,4},{6,7},{7,6},{8,9},{9,8},{10,11... | collective-permute-start | bytes 393224 | tf_op jit(solution)/shard_map/ppermute | solution.py:222
  247.7 1.3 copy-start.15
  247.7 1.3 copy-start.17
  247.8 1.3 copy-start.19
  249.0 0.7 copy-start.20
  252.2 15.7 %all-to-all-start.5 = ((bf16[64,8,128]{2,1,0:T(8,128)(2,1)}), bf16[64,8,128]{2,1,0:T(8,128)(2,1)S(1)}, u32[]{:S(2)}, u32[]{:S(2)}) async-start(bf16[64,8,128]{2,1,0:T(8,128)(2,1)} %triangle_sums.1), calls=%async_computation.5 | async-start | bytes 262144 | tf_op jit(solution)/shard_map/all_to_all | solution.py:311
  267.9 0.7 copy-start.5
  273.1 10.2 %all-to-all-start.6 = ((bf16[4,2,8192]{2,1,0:T(2,128)(2,1)}), bf16[4,2,8192]{2,1,0:T(2,128)(2,1)S(1)}, u32[]{:S(2)}, u32[]{:S(2)}) async-start(bf16[4,2,8192]{2,1,0:T(2,128)(2,1)} %reshape.94), calls=%async_computation.6 | async-start | bytes 262144 | tf_op jit(solution)/shard_map/all_to_all | solution.py:316
where the time goes:
time: 287 us; the launch traced here: 285 us
  starting transfers between devices  109 us (38%)
  waiting for transfers between devices  83 us (29%)
  blocking collectives  32.9 us (11%)
  Pallas kernels  27.7 us (10%)
  local copies, waits for them, and re-layouts  19.9 us (7%)
  other arithmetic  7.03 us (2%)
  matrix products  5.17 us (2%)
    ppermute x17, starting transfers between devices, swap(): return lax.ppermute(x, 'col', [(c, c ^ mask) for c in range(8)])  69.8 us
    ppermute x17, waiting for transfers between devices, swap(): return lax.ppermute(x, 'col', [(c, c ^ mask) for c in range(8)])  39.6 us
    all_to_all x1, waiting for transfers between devices, local(): lax.all_to_all(jnp.broadcast_to(factors[None, :32], (64, 32, 256)), both,...  20.9 us
    all_to_all x1, blocking collectives, local(): message = lax.all_to_all(message, both, 0, 0, tiled=True)  20.2 us
    pallas_call x1, Pallas kernels, row_attention(): pl.pallas_call(row_kernel, out_shape=jax.ShapeDtypeStruct((4, 64, 256), B...  12.8 us
    all_to_all x1, blocking collectives, local(): right = lax.all_to_all(pick(position, right), 'row', 0, 0, tiled=True)  12.7 us
    all_to_all x1, starting transfers between devices, local(): columns = lax.all_to_all(to_targets(alignment_row), both, 0, 0, tiled=True)  12 us
    all_to_all x1, waiting for transfers between devices, local(): sums = lax.all_to_all(sums, both, 0, 0, tiled=True)  9.01 us
  transfers between devices with their start and end apart: 22, of which 14 were waited for; matrix products, arithmetic and copies ran while one was open for 2% of the time, Pallas kernels for 0%

commit v1 on v0

v1 whole, which is shorter than its diff:
```python
import jax
import jax.numpy as jnp
from jax import lax
from jax.experimental import pallas as pl
from jax.experimental.pallas import tpu as pltpu
from jax.sharding import PartitionSpec as P


BF = jnp.bfloat16
F32 = jnp.float32
EPSILON = 1e-05
SCALE = 32**-0.5

NT = (((1,), (1,)), ((), ()))
TN = (((0,), (0,)), ((), ()))


def mm(a, b, dims):
    return lax.dot_general(a, b, dims, preferred_element_type=F32)


def layer_norm(inputs):
    inputs = inputs.astype(F32)
    average = jnp.mean(inputs, axis=-1, keepdims=True)
    centered = inputs - average
    variance = jnp.mean(jnp.square(centered), axis=-1, keepdims=True)
    return centered * lax.rsqrt(variance + EPSILON)


def sigmoid(x):
    return 1.0 / (1.0 + jnp.exp(-x))


def exp_rows(scores):
    top = jnp.max(scores, axis=0, keepdims=True)
    weights = jnp.exp(scores - top)
    total = jnp.sum(weights, axis=0, keepdims=True)
    return weights.astype(BF), 1.0 / total


def row_kernel(places, *refs):
    blocks = refs[:8]
    w_ref, bias_ref, wo_ref, out_ref, rows, packed = refs[8:]
    s = pl.program_id(0)
    own = None
    for m in range(8):
        normed = layer_norm(blocks[m][0]).astype(BF)
        if m == 0:
            own = normed
        start = pl.multiple_of(places[m] * 64, 64)
        rows[pl.ds(start, 64), :] = normed
    x = rows[...]
    key = mm(x, w_ref[256:512], NT).astype(BF)
    value_t = mm(w_ref[512:768], x, NT).astype(BF)
    query_t = (mm(w_ref[0:256], own, NT) * SCALE).astype(BF)
    gate_t = sigmoid(mm(w_ref[768:1024], own, NT))
    twice = jnp.concatenate([query_t, query_t], axis=1)
    head_row = lax.broadcasted_iota(jnp.int32, (256, 128), 0) // 32
    head_lane = lax.broadcasted_iota(jnp.int32, (256, 128), 1) // 64
    upper = lax.broadcasted_iota(jnp.int32, (64, 64), 0) < 32
    parts = []
    for p in range(4):
        diag = jnp.where(head_row == 2 * p + head_lane, twice, jnp.zeros_like(twice))
        scores = jnp.dot(key, diag, preferred_element_type=F32)
        scores = scores + bias_ref[:, p * 128 : (p + 1) * 128].astype(F32)
        weights, scale = exp_rows(scores)
        mixed = jnp.dot(value_t[p * 64 : (p + 1) * 64], weights, preferred_element_type=F32)
        mixed = mixed * scale
        parts.append(jnp.where(upper, mixed[:, :64], mixed[:, 64:]))
    attended_t = jnp.concatenate(parts, axis=0)
    gated = (gate_t * attended_t).astype(BF)
    result = blocks[0][0].astype(F32) + mm(gated, wo_ref[...], TN)
    for h in range(2):
        for b in range(4):
            source = (h * 4 + b) * 8
            target = (b * 2 + h) * 8
            for half in range(2):
                packed[half, s, target : target + 8, :] = result[
                    source : source + 8, half * 128 : (half + 1) * 128
                ]

    @pl.when(s == 3)
    def _():
        parts = [packed[half, t][:, None, :] for half in range(2) for t in range(4)]
        out_ref[...] = jnp.concatenate(parts, axis=1).astype(BF)


def row_attention(places, blocks, w_row_t, bias, w_out):
    block = pl.BlockSpec((1, 64, 256), lambda s, p: (s, 0, 0))
    full = lambda *shape: pl.BlockSpec(shape, lambda s, p: (0,) * len(shape))
    return pl.pallas_call(
        row_kernel,
        out_shape=jax.ShapeDtypeStruct((64, 8, 128), BF),
        grid_spec=pltpu.PrefetchScalarGridSpec(
            num_scalar_prefetch=1,
            grid=(4,),
            in_specs=[block] * 8 + [full(1024, 256), full(512, 512), full(256, 256)],
            out_specs=full(64, 8, 128),
            scratch_shapes=[pltpu.VMEM((512, 256), BF), pltpu.VMEM((2, 4, 64, 128), F32)],
        ),
        name="row_attention",
    )(places, *blocks, w_row_t, bias, w_out)


def column_kernel(x_ref, w_ref, wo_ref, wf_ref, out_ref, left_ref, right_ref, scratch):
    scratch[...] = x_ref[...].astype(F32)
    x = jnp.concatenate(
        [
            jnp.concatenate([scratch[:, s, :], scratch[:, 4 + s, :]], axis=1)
            for s in range(4)
        ],
        axis=0,
    )
    normed = layer_norm(x).astype(BF)
    key = mm(normed, w_ref[256:512], NT).astype(BF)
    value_t = mm(w_ref[512:768], normed, NT).astype(BF)
    query_t = (mm(w_ref[0:256], normed, NT) * SCALE).astype(BF)
    gate_t = sigmoid(mm(w_ref[768:1024], normed, NT))
    head_row = lax.broadcasted_iota(jnp.int32, (256, 256), 0) // 32
    parts = []
    for h in range(8):
        diag = jnp.where(head_row == h, query_t, jnp.zeros_like(query_t))
        weights, scale = exp_rows(jnp.dot(key, diag, preferred_element_type=F32))
        mixed = jnp.dot(value_t[h * 32 : (h + 1) * 32], weights, preferred_element_type=F32)
        parts.append(mixed * scale)
    gated = (gate_t * jnp.concatenate(parts, axis=0)).astype(BF)
    result = (x + mm(gated, wo_ref[...], TN)).astype(BF)
    factors = mm(wf_ref[...], layer_norm(result).astype(BF), NT).astype(BF)
    left_ref[...] = factors[:32]
    right_ref[...] = factors[32:]
    wide = result.astype(F32)
    for s in range(4):
        for half in range(2):
            scratch[:, half * 4 + s, :] = wide[
                s * 64 : (s + 1) * 64, half * 128 : (half + 1) * 128
            ]
    out_ref[...] = scratch[...].astype(BF)


def column_attention(x, w_column_t, w_out, w_factor_t):
    factor = jax.ShapeDtypeStruct((32, 256), BF)
    return pl.pallas_call(
        column_kernel,
        out_shape=(jax.ShapeDtypeStruct((64, 8, 128), BF), factor, factor),
        scratch_shapes=[pltpu.VMEM((64, 8, 128), F32)],
        name="column_attention",
    )(x, w_column_t, w_out, w_factor_t)


def spread_kernel(index, left_ref, right_ref, out_ref):
    left = left_ref[...].reshape(128, 256)
    for r in range(16):
        out_ref[r, :128] = left
        out_ref[r, 128:] = right_ref[index[r // 2]]


def spread(index, left, right):
    full = lambda *shape: pl.BlockSpec(shape, lambda g, p: (0,) * len(shape))
    return pl.pallas_call(
        spread_kernel,
        out_shape=jax.ShapeDtypeStruct((16, 160, 256), BF),
        grid_spec=pltpu.PrefetchScalarGridSpec(
            num_scalar_prefetch=1,
            grid=(1,),
            in_specs=[full(4, 32, 256), full(8, 32, 256)],
            out_specs=full(16, 160, 256),
        ),
        name="spread",
    )(index, left, right)


def block_transpose(arrays):
    rows = arrays[0].shape[0]
    lane = lax.broadcasted_iota(jnp.int32, (rows, 128), 1)
    low = lane < 64
    even = (lane // 32) % 2 == 0
    a0, a1, a2, a3 = arrays
    u0 = jnp.where(low, a0, pltpu.roll(a2, 64, 1))
    u2 = jnp.where(low, pltpu.roll(a0, 64, 1), a2)
    u1 = jnp.where(low, a1, pltpu.roll(a3, 64, 1))
    u3 = jnp.where(low, pltpu.roll(a1, 64, 1), a3)
    b0 = jnp.where(even, u0, pltpu.roll(u1, 32, 1))
    b1 = jnp.where(even, pltpu.roll(u0, 96, 1), u1)
    b2 = jnp.where(even, u2, pltpu.roll(u3, 32, 1))
    b3 = jnp.where(even, pltpu.roll(u2, 96, 1), u3)
    return b0, b1, b2, b3


def pair_kernel(half_ref, factor_ref, pair_ref, wo_ref, w_ref, back_ref, mid_ref, out_ref,
                outer, flat, scratch):
    start = half_ref[0] * 8
    right = factor_ref[pl.ds(start, 8), 128:, :].reshape(256, 256)
    for b in range(4):
        left = factor_ref[:, b * 32 : (b + 1) * 32, :].reshape(512, 256)
        product = mm(left, right, NT) * (1.0 / 256)
        outer[b * 16 : (b + 1) * 16] = product.reshape(16, 32, 256)
    for group in range(8):
        chans = [outer[:, group * 4 + k, :] for k in range(4)]
        for tile in range(2):
            moved = block_transpose([c[:, tile * 128 : (tile + 1) * 128] for c in chans])
            for k in range(4):
                j = tile * 4 + k
                flat[j * 64 : (j + 1) * 64, group * 128 : (group + 1) * 128] = moved[k].astype(BF)
    update = jnp.dot(flat[...], wo_ref[...], preferred_element_type=F32).astype(BF)
    mid = (pair_ref[...].astype(F32) + update.astype(F32)).astype(BF)
    mid_ref[...] = mid
    rows = layer_norm(mid).astype(BF)
    lane = lax.broadcasted_iota(jnp.int32, (64, 128), 1) < 64
    for side in range(2):
        base = side * 256
        value = mm(w_ref[base : base + 128], rows, NT)
        gate = mm(w_ref[base + 128 : base + 256], rows, NT)
        both = sigmoid(gate) * value
        for pair in range(4):
            low = both[:64, pair * 128 : (pair + 1) * 128]
            high = both[64:, pair * 128 : (pair + 1) * 128]
            scratch[side, :, 2 * pair, :] = jnp.where(lane, low, pltpu.roll(high, 64, 1))
            scratch[side, :, 2 * pair + 1, :] = jnp.where(lane, pltpu.roll(low, 64, 1), high)
    out_ref[:, 0] = scratch[0].astype(BF)
    out_ref[:, 1] = scratch[1].astype(BF)
    out_ref[:, 2] = back_ref[...]


def pair_update(half, factors, pair_part, w_outer, w_in_t, returning):
    full = lambda *shape: pl.BlockSpec(shape, lambda g, p: (0,) * len(shape))
    return pl.pallas_call(
        pair_kernel,
        out_shape=(
            jax.ShapeDtypeStruct((512, 128), BF),
            jax.ShapeDtypeStruct((64, 3, 8, 128), BF),
        ),
        grid_spec=pltpu.PrefetchScalarGridSpec(
            num_scalar_prefetch=1,
            grid=(1,),
            in_specs=[
                full(16, 160, 256),
                full(512, 128),
                full(1024, 128),
                full(512, 128),
                full(64, 8, 128),
            ],
            out_specs=(full(512, 128), full(64, 3, 8, 128)),
            scratch_shapes=[
                pltpu.VMEM((64, 32, 256), F32),
                pltpu.VMEM((512, 1024), BF),
                pltpu.VMEM((2, 64, 8, 128), F32),
            ],
        ),
        name="pair_update",
    )(half, factors, pair_part, w_outer, w_in_t, returning)


def triangle_kernel(places, left_ref, *refs):
    rights, out_ref = refs[:8], refs[8]
    left = left_ref[...]
    lane = lax.broadcasted_iota(jnp.int32, (64, 128), 1) < 64
    for m in range(8):
        product = mm(rights[m][...], left, TN)
        block = jnp.where(lane, product[:64], product[64:]).astype(BF)
        target = places[m] * 2
        for b in range(4):
            for h in range(2):
                out_ref[b * 16 + target + h] = block[(b * 2 + h) * 8 : (b * 2 + h + 1) * 8]


def triangle_sums(places, left, rights):
    full = lambda *shape: pl.BlockSpec(shape, lambda g, p: (0,) * len(shape))
    return pl.pallas_call(
        triangle_kernel,
        out_shape=jax.ShapeDtypeStruct((64, 8, 128), BF),
        grid_spec=pltpu.PrefetchScalarGridSpec(
            num_scalar_prefetch=1,
            grid=(1,),
            in_specs=[full(512, 128)] * 9,
            out_specs=full(64, 8, 128),
        ),
        name="triangle_sums",
    )(places, left, *rights)


def output_kernel(sum_ref, mid_ref, wg_ref, w_ref, out_ref, scratch):
    sums = sum_ref[...].astype(F32)
    fold = lambda v: (v + pltpu.roll(v, 64, 1)) * (1.0 / 128)
    average = fold(jnp.sum(sums, axis=0))
    centered = sums - average[None]
    variance = fold(jnp.sum(jnp.square(centered), axis=0))
    scratch[...] = centered * lax.rsqrt(variance + EPSILON)[None]
    mid = mid_ref[...]
    rows = layer_norm(mid).astype(BF)
    gate = sigmoid(jnp.dot(rows, wg_ref[...], preferred_element_type=F32))
    for j in range(8):
        product = mm(scratch[:, j, :].astype(BF), w_ref[...], TN)
        mixed = product[:64, :128] + product[64:, 128:]
        part = mid[j * 64 : (j + 1) * 64].astype(F32) + gate[j * 64 : (j + 1) * 64] * mixed
        moved = block_transpose([part[u * 16 : (u + 1) * 16] for u in range(4)])
        for b in range(4):
            out_ref[b, j] = moved[b].astype(BF)


def pair_output(sums, mid, w_gate, w_out):
    return pl.pallas_call(
        output_kernel,
        out_shape=jax.ShapeDtypeStruct((4, 8, 16, 128), BF),
        scratch_shapes=[pltpu.VMEM((64, 8, 128), F32)],
        name="pair_output",
    )(sums, mid, w_gate, w_out)


def shifted(x, step, flip):
    perm = [(c, (c // 2 - step) % 4 * 2 + (c % 2 ^ flip)) for c in range(8)]
    return lax.ppermute(x, "col", perm)


def gather_col(x):
    parts = {(0, 0): x}
    for step in (1, 2, 3):
        parts[step, 0] = shifted(x, step, 0)
    for step in (0, 1, 3, 2):
        parts[step, 1] = shifted(parts[step, 0], 0, 1)
    return [parts[m // 2, m % 2] for m in range(8)]


def local(
    alignment,
    pair_features,
    w_row,
    row_output_weight,
    w_bias,
    w_column,
    column_output_weight,
    outer_input_weight,
    w_outer_out,
    w_triangle_in,
    w_triangle_gate,
    w_triangle_out,
):
    branch = lax.axis_index("branch").astype(jnp.int32)
    row = lax.axis_index("row").astype(jnp.int32)
    col = lax.axis_index("col").astype(jnp.int32)
    both = ("branch", "row")
    order = jnp.arange(8, dtype=jnp.int32)
    places = (col // 2 + order // 2) % 4 * 2 + (col % 2 ^ order % 2)

    blocks = gather_col(alignment)
    w_row_t = w_row.T
    w_column_t = w_column.T
    w_factor_t = outer_input_weight.T
    w_in_t = w_triangle_in.T
    w_out = jnp.concatenate([w_triangle_out[:64], w_triangle_out[64:]], axis=1)
    pair_part = lax.dynamic_slice_in_dim(pair_features, branch * 8, 8, 1)
    pair_part = jnp.transpose(pair_part.reshape(2, 4, 8, 8, 128), (3, 1, 0, 2, 4))
    pair_part = pair_part.reshape(512, 128)
    pair_normed = layer_norm(pair_features).astype(BF)
    bias_tile = jnp.einsum(
        "ijc,ch->jhi", pair_normed, w_bias, preferred_element_type=F32
    ).astype(BF)
    bias_tile = jnp.broadcast_to(bias_tile.reshape(1, 32, 512), (16, 32, 512))
    bias = lax.all_to_all(bias_tile, "row", 0, 0, tiled=True).reshape(512, 512)

    columns = row_attention(places, blocks, w_row_t, bias, row_output_weight)
    columns = lax.all_to_all(columns, both, 0, 0, tiled=True)
    returning, left, right = column_attention(
        columns, w_column_t, column_output_weight, w_factor_t
    )

    right = jnp.stack([right, shifted(right, 0, 1)])
    rights = [right] + [shifted(right, step, 0) for step in (1, 2, 3)]
    left = lax.all_to_all(jnp.broadcast_to(left[None], (4, 32, 256)), "branch", 0, 0, tiled=True)
    rights = jnp.concatenate(rights)
    position = (order // 2 - col // 2) % 4 * 2 + (order % 2 ^ col % 2)
    factors = lax.all_to_all(spread(position, left, rights), "row", 0, 0, tiled=True)

    half = (row % 2).reshape(1)
    mid, message = pair_update(half, factors, pair_part, w_outer_out, w_in_t, returning)
    message = lax.all_to_all(message, both, 0, 0, tiled=True)
    tri_left = message[:, 0].reshape(512, 128)
    rights = gather_col(message[:, 1].reshape(512, 128))
    back = message[:, 2].reshape(4, 2, 8, 2, 4, 128)
    alignment_out = jnp.transpose(back, (4, 1, 0, 2, 3, 5)).reshape(4, 64, 256)
    sums = triangle_sums(places, tri_left, rights)
    sums = lax.all_to_all(sums, both, 0, 0, tiled=True)
    parts = pair_output(sums, mid, w_triangle_gate, w_out)
    parts = lax.all_to_all(parts, "branch", 0, 0, tiled=True)
    parts = parts.reshape(4, 8, 2, 8, 4, 32)
    pair_out = jnp.transpose(parts, (2, 4, 3, 0, 1, 5)).reshape(64, 32, 32)
    return (alignment_out, pair_out)


def solution(mesh):
    in_specs = (P(("branch", "row"), "col", None), P("col", "row", None)) + (P(),) * 10
    out_specs = (P(("branch", "row"), "col", None), P("col", "row", "branch"))
    return jax.shard_map(local, mesh=mesh, in_specs=in_specs, out_specs=out_specs, check_vma=False)
```

time: 287 us -> 267 us (0.930)
  waiting for transfers between devices: 83 us -> 63 us
  starting transfers between devices: 109 us -> 124 us
  blocking collectives: 32.9 us -> 21.5 us
  Pallas kernels: 27.7 us -> 31.9 us
  local copies, waits for them, and re-layouts: 19.9 us -> 16 us
  matrix products: 5.17 us -> 1.96 us
    ppermute x17 -> x18, waiting for transfers between devices: 39.6 us -> 22.9 us  [shifted(): return lax.ppermute(x, 'col', perm)]
    all_to_all x1 -> x0, blocking collectives: 12.7 us -> none  [local(): right = lax.all_to_all(pick(position, right), 'row', 0, 0, tiled=True)]
    ppermute x17 -> x18, starting transfers between devices: 69.8 us -> 80.6 us  [shifted(): return lax.ppermute(x, 'col', perm)]
    convert_element_type x3 -> x0, local copies, waits for them, and re-layouts: 4.42 us -> none  [the longest x2 3.69 us: local(): outer.reshape(512, 1024).astype(BF)]
    unnamed x53 -> x62, local copies, waits for them, and re-layouts: 5.95 us -> 9.99 us
    pallas_call x5, Pallas kernels: 25.2 us -> 28.7 us  [the longest x1 12.6 us: row_attention(): pl.pallas_call(row_kernel, out_shape=jax.ShapeDtypeStruct((64, 8, 128), B...]
    dot_general x2 -> x0, matrix products: 3.27 us -> none  [the longest x1 1.73 us: local(): jnp.einsum('ncs,jes->jnce', left, right, preferred_element_type=F32)]
    all_to_all x3 -> x4, waiting for transfers between devices: 29.9 us -> 26.8 us  [the longest x1 18.8 us: local(): lax.all_to_all(spread(position, left, rights), 'row', 0, 0, tiled=True)]
  transfers between devices with their start and end apart: 22 -> 24, of which waited for: 14 -> 11; matrix products, arithmetic and copies ran while one was open for 2% -> 4% of each run, Pallas kernels for 0% -> 0%
where the time goes in v1:
time: 267 us; the launch traced here: 265 us
  starting transfers between devices  124 us (46%)
  waiting for transfers between devices  63 us (24%)
  Pallas kernels  31.9 us (12%)
  blocking collectives  21.5 us (8%)
  local copies, waits for them, and re-layouts  16 us (6%)
  other arithmetic  5.51 us (2%)
    ppermute x18, starting transfers between devices, shifted(): return lax.ppermute(x, 'col', perm)  80.6 us
    ppermute x18, waiting for transfers between devices, shifted(): return lax.ppermute(x, 'col', perm)  22.9 us
    all_to_all x1, blocking collectives, local(): message = lax.all_to_all(message, both, 0, 0, tiled=True)  21.5 us
    all_to_all x1, waiting for transfers between devices, local(): lax.all_to_all(spread(position, left, rights), 'row', 0, 0, tiled=True)  18.8 us
    all_to_all x1, starting transfers between devices, local(): columns = lax.all_to_all(columns, both, 0, 0, tiled=True)  13.9 us
    pallas_call x1, Pallas kernels, row_attention(): pl.pallas_call(row_kernel, out_shape=jax.ShapeDtypeStruct((64, 8, 128), B...  12.6 us
    unnamed x62, local copies, waits for them, and re-layouts  9.99 us
    all_to_all x1, waiting for transfers between devices, local(): sums = lax.all_to_all(sums, both, 0, 0, tiled=True)  8.87 us
  transfers between devices with their start and end apart: 24, of which 11 were waited for; matrix products, arithmetic and copies ran while one was open for 4% of the time, Pallas kernels for 0%

profile of v1, /device:TPU:32, one launch (start us, length us, event | category | flops | bytes accessed | tf_op | source)
XLA Modules:
  0.0 264.9 jit_solution(12537548122840215628)
XLA Ops:
  0.6 1.4 convert_reduce_fusion
  2.1 1.7 fusion.3
  3.8 2.0 fusion.2
  6.9 7.0 %all-to-all-start = ((bf16[16,32,512]{2,1,0:T(8,128)(2,1)}), bf16[16,32,512]{2,1,0:T(8,128)(2,1)S(1)}, u32[]{:S(2)}, u32[]{:S(2)}) async-start(bf16[16,32,512]{2,1,0:T(8,128)(2,1)} %broadcast_in_dim.7), calls=%async_computation | async-start | bytes 1048576 | tf_op jit(solution)/shard_map/all_to_all | solution.py:358
  13.9 11.8 %collective-permute-start.1 = (bf16[4,64,256]{2,1,0:T(8,128)(2,1)S(1)}, bf16[4,64,256]{2,1,0:T(8,128)(2,1)S(1)}, u32[]{:S(2)}, u32[]{:S(2)}) collective-permute-start(bf16[4,64,256]{2,1,0:T(8,128)(2,1)S(1)} %copy-done.10), channel_id=1, source_target_pairs={{0,6},{1,7},{2,0},{3,1},{4,2},{5,3},{6,4},{7,5},{8,14},{9,15},{10,... | collective-permute-start | bytes 393224 | tf_op jit(solution)/shard_map/ppermute | solution.py:311
  25.8 4.9 %collective-permute-start.3 = (bf16[4,64,256]{2,1,0:T(8,128)(2,1)S(1)}, bf16[4,64,256]{2,1,0:T(8,128)(2,1)S(1)}, u32[]{:S(2)}, u32[]{:S(2)}) collective-permute-start(bf16[4,64,256]{2,1,0:T(8,128)(2,1)S(1)} %copy-done.10), channel_id=1, source_target_pairs={{0,4},{1,5},{2,6},{3,7},{4,0},{5,1},{6,2},{7,3},{8,12},{9,13},{10,... | collective-permute-start | bytes 393224 | tf_op jit(solution)/shard_map/ppermute | solution.py:311
  30.7 7.8 %collective-permute-start.5 = (bf16[4,64,256]{2,1,0:T(8,128)(2,1)S(1)}, bf16[4,64,256]{2,1,0:T(8,128)(2,1)S(1)}, u32[]{:S(2)}, u32[]{:S(2)}) collective-permute-start(bf16[4,64,256]{2,1,0:T(8,128)(2,1)S(1)} %copy-done.10), channel_id=1, source_target_pairs={{0,2},{1,3},{2,4},{3,5},{4,6},{5,7},{6,0},{7,1},{8,10},{9,11},{10,... | collective-permute-start | bytes 393224 | tf_op jit(solution)/shard_map/ppermute | solution.py:311
  38.5 1.9 collective-permute-start
  40.5 2.4 collective-permute-start.2
  43.6 1.9 collective-permute-start.4
  45.5 6.6 %collective-permute-done.5.refs_6_ = bf16[4,64,256]{2,1,0:T(8,128)(2,1)S(1)} collective-permute-done((bf16[4,64,256]{2,1,0:T(8,128)(2,1)S(1)}, bf16[4,64,256]{2,1,0:T(8,128)(2,1)S(1)}, u32[]{:S(2)}, u32[]{:S(2)}) %collective-permute-start.5) | collective-permute-done | bytes 131104 | tf_op jit(solution)/shard_map/ppermute | solution.py:311
  52.2 1.9 collective-permute-start.6
  54.1 1.0 copy.19
  56.7 12.6 %row_attention.1 = bf16[64,8,128]{2,1,0:T(8,128)(2,1)} custom-call(s32[8]{0:T(128)} %fusion.13.places, bf16[4,64,256]{2,1,0:T(8,128)(2,1)} %refs_0_.1, bf16[4,64,256]{2,1,0:T(8,128)(2,1)} %copy-done.14, bf16[4,64,256]{2,1,0:T(8,128)(2,1)} %copy-done.11, bf16[4,64,256]{2,1,0:T(8,128)(2,1)} %copy-done.15, bf16[4,64,256]{2,1,0:T(8,128)(2,1)} %copy-done.12, ...), custom_call_target="tpu_custom_call" | custom-call | tf_op jit(solution)/shard_map/row_attention/pallas_call | solution.py:91
  69.3 13.9 %all-to-all-start.1 = ((bf16[64,8,128]{2,1,0:T(8,128)(2,1)}), bf16[64,8,128]{2,1,0:T(8,128)(2,1)S(1)}, u32[]{:S(2)}, u32[]{:S(2)}) async-start(bf16[64,8,128]{2,1,0:T(8,128)(2,1)} %row_attention.1), calls=%async_computation.1 | async-start | bytes 262144 | tf_op jit(solution)/shard_map/all_to_all | solution.py:361
  83.2 1.0 copy.21
  84.7 8.0 %all-to-all-done.1.x_ref = bf16[64,8,128]{2,1,0:T(8,128)(2,1)S(1)} async-done(((bf16[64,8,128]{2,1,0:T(8,128)(2,1)}), bf16[64,8,128]{2,1,0:T(8,128)(2,1)S(1)}, u32[]{:S(2)}, u32[]{:S(2)}) %all-to-all-start.1) | async-done | bytes 131104 | tf_op jit(solution)/shard_map/all_to_all | solution.py:361
  93.3 5.2 %column_attention.1 = (bf16[64,8,128]{2,1,0:T(8,128)(2,1)}, bf16[32,256]{1,0:T(8,128)(2,1)}, bf16[32,256]{1,0:T(8,128)(2,1)}) custom-call(bf16[64,8,128]{2,1,0:T(8,128)(2,1)} %copy-done.4, bf16[1024,256]{1,0:T(8,128)(2,1)} %bitcast.34, bf16[256,256]{1,0:T(8,128)(2,1)} %wo_ref.2, bf16[64,256]{1,0:T(8,128)(2,1)} %bitcast.43), custom_call_target="tpu_custom_call" | custom-call | tf_op jit(solution)/shard_map/column_attention/pallas_call | solution.py:142
  98.6 1.9 collective-permute-start.7
  101.2 1.3 broadcast_in_dim.8
  102.6 5.0 %all-to-all-start.2 = ((bf16[4,32,256]{2,1,0:T(8,128)(2,1)}), bf16[4,32,256]{2,1,0:T(8,128)(2,1)S(1)}, u32[]{:S(2)}, u32[]{:S(2)}) async-start(bf16[4,32,256]{2,1,0:T(8,128)(2,1)} %broadcast_in_dim.8), calls=%async_computation.2 | async-start | bytes 131072 | tf_op jit(solution)/shard_map/all_to_all | solution.py:368
  108.3 7.7 %collective-permute-start.8 = (bf16[2,32,256]{2,1,0:T(8,128)(2,1)S(1)}, bf16[2,32,256]{2,1,0:T(8,128)(2,1)S(1)}, u32[]{:S(2)}, u32[]{:S(2)}) collective-permute-start(bf16[2,32,256]{2,1,0:T(8,128)(2,1)S(1)} %pad_maximum_fusion), channel_id=1, source_target_pairs={{0,6},{1,7},{2,0},{3,1},{4,2},{5,3},{6,4},{7,5},{8,14},{9,15},{10,... | collective-permute-start | bytes 98312 | tf_op jit(solution)/shard_map/ppermute | solution.py:311
  116.0 5.4 %collective-permute-start.9 = (bf16[2,32,256]{2,1,0:T(8,128)(2,1)S(1)}, bf16[2,32,256]{2,1,0:T(8,128)(2,1)S(1)}, u32[]{:S(2)}, u32[]{:S(2)}) collective-permute-start(bf16[2,32,256]{2,1,0:T(8,128)(2,1)S(1)} %pad_maximum_fusion), channel_id=1, source_target_pairs={{0,4},{1,5},{2,6},{3,7},{4,0},{5,1},{6,2},{7,3},{8,12},{9,13},{10,... | collective-permute-start | bytes 98312 | tf_op jit(solution)/shard_map/ppermute | solution.py:311
  121.4 7.0 %collective-permute-start.10 = (bf16[2,32,256]{2,1,0:T(8,128)(2,1)S(1)}, bf16[2,32,256]{2,1,0:T(8,128)(2,1)S(1)}, u32[]{:S(2)}, u32[]{:S(2)}) collective-permute-start(bf16[2,32,256]{2,1,0:T(8,128)(2,1)S(1)} %pad_maximum_fusion), channel_id=1, source_target_pairs={{0,2},{1,3},{2,4},{3,5},{4,6},{5,7},{6,0},{7,1},{8,10},{9,11},{10,... | collective-permute-start | bytes 98312 | tf_op jit(solution)/shard_map/ppermute | solution.py:311
  128.4 2.1 collective-permute-done.9
  130.5 1.4 collective-permute-done.10
  133.2 2.8 %spread.1 = bf16[16,160,256]{2,1,0:T(8,128)(2,1)} custom-call(s32[8]{0:T(128)} %fusion.11.index, bf16[4,32,256]{2,1,0:T(8,128)(2,1)} %copy-done.8, bf16[8,32,256]{2,1,0:T(8,128)(2,1)} %copy-done.9), custom_call_target="tpu_custom_call" | custom-call | tf_op jit(solution)/shard_map/spread/pallas_call | solution.py:159
  136.0 3.8 %all-to-all-start.3 = ((bf16[16,160,256]{2,1,0:T(8,128)(2,1)}), bf16[16,160,256]{2,1,0:T(8,128)(2,1)S(1)}, u32[]{:S(2)}, u32[]{:S(2)}) async-start(bf16[16,160,256]{2,1,0:T(8,128)(2,1)} %spread.1), calls=%async_computation.3 | async-start | bytes 2621440 | tf_op jit(solution)/shard_map/all_to_all | solution.py:371
  142.2 18.8 %all-to-all-done.3.factor_ref = bf16[16,160,256]{2,1,0:T(8,128)(2,1)S(1)} async-done(((bf16[16,160,256]{2,1,0:T(8,128)(2,1)}), bf16[16,160,256]{2,1,0:T(8,128)(2,1)S(1)}, u32[]{:S(2)}, u32[]{:S(2)}) %all-to-all-start.3) | async-done | bytes 1310752 | tf_op jit(solution)/shard_map/all_to_all | solution.py:371
  161.0 1.1 copy-done.1
  162.1 5.3 %pair_update.1 = (bf16[512,128]{1,0:T(8,128)(2,1)}, bf16[64,3,8,128]{3,2,1,0:T(8,128)(2,1)}) custom-call(s32[1]{0:T(128)} %bitcast.half_ref, bf16[16,160,256]{2,1,0:T(8,128)(2,1)} %copy-done.1, bf16[512,128]{1,0:T(8,128)(2,1)} %bitcast.36, bf16[1024,128]{1,0:T(8,128)(2,1)} %wo_ref.3, bf16[512,128]{1,0:T(8,128)(2,1)} %bitcast.37, ...), custom_call_target="tpu_custom_call" | custom-call | tf_op jit(solution)/shard_map/pair_update/pallas_call | solution.py:226
  167.5 21.5 %all_to_all.35 = bf16[64,3,8,128]{3,2,1,0:T(8,128)(2,1)S(1)} all-to-all(bf16[64,3,8,128]{3,2,1,0:T(8,128)(2,1)} %get-tuple-element.10), channel_id=1, replica_groups=mesh['branch'=4,'row'=16,'col'=8] {'branch','row'}, dimensions={0} | all-to-all | bytes 786432 | tf_op jit(solution)/shard_map/all_to_all | solution.py:375
  189.7 4.4 %collective-permute-start.12 = (bf16[512,128]{1,0:T(8,128)(2,1)S(1)}, bf16[512,128]{1,0:T(8,128)(2,1)S(1)}, u32[]{:S(2)}, u32[]{:S(2)}) collective-permute-start(bf16[512,128]{1,0:T(8,128)(2,1)S(1)} %get-tuple-element.14.refs_0_), channel_id=1, source_target_pairs={{0,6},{1,7},{2,0},{3,1},{4,2},{5,3},{6,4},{7,5},{8,14},{9,15},{10,... | collective-permute-start | bytes 393224 | tf_op jit(solution)/shard_map/ppermute | solution.py:311
  194.1 8.6 %collective-permute-start.14 = (bf16[512,128]{1,0:T(8,128)(2,1)S(1)}, bf16[512,128]{1,0:T(8,128)(2,1)S(1)}, u32[]{:S(2)}, u32[]{:S(2)}) collective-permute-start(bf16[512,128]{1,0:T(8,128)(2,1)S(1)} %get-tuple-element.14.refs_0_), channel_id=1, source_target_pairs={{0,4},{1,5},{2,6},{3,7},{4,0},{5,1},{6,2},{7,3},{8,12},{9,13},{10,... | collective-permute-start | bytes 393224 | tf_op jit(solution)/shard_map/ppermute | solution.py:311
  202.7 4.8 %collective-permute-start.16 = (bf16[512,128]{1,0:T(8,128)(2,1)S(1)}, bf16[512,128]{1,0:T(8,128)(2,1)S(1)}, u32[]{:S(2)}, u32[]{:S(2)}) collective-permute-start(bf16[512,128]{1,0:T(8,128)(2,1)S(1)} %get-tuple-element.14.refs_0_), channel_id=1, source_target_pairs={{0,2},{1,3},{2,4},{3,5},{4,6},{5,7},{6,0},{7,1},{8,10},{9,11},{10,... | collective-permute-start | bytes 393224 | tf_op jit(solution)/shard_map/ppermute | solution.py:311
  207.5 1.9 collective-permute-start.11
  209.4 3.8 %collective-permute-done.12.refs_2_ = bf16[512,128]{1,0:T(8,128)(2,1)S(1)} collective-permute-done((bf16[512,128]{1,0:T(8,128)(2,1)S(1)}, bf16[512,128]{1,0:T(8,128)(2,1)S(1)}, u32[]{:S(2)}, u32[]{:S(2)}) %collective-permute-start.12) | collective-permute-done | bytes 131104 | tf_op jit(solution)/shard_map/ppermute | solution.py:311
  213.2 1.9 collective-permute-start.13
  215.1 7.4 %collective-permute-done.14.refs_4_ = bf16[512,128]{1,0:T(8,128)(2,1)S(1)} collective-permute-done((bf16[512,128]{1,0:T(8,128)(2,1)S(1)}, bf16[512,128]{1,0:T(8,128)(2,1)S(1)}, u32[]{:S(2)}, u32[]{:S(2)}) %collective-permute-start.14) | collective-permute-done | bytes 131104 | tf_op jit(solution)/shard_map/ppermute | solution.py:311
  222.5 1.9 collective-permute-start.15
  224.4 2.4 collective-permute-start.17
  228.4 3.1 %triangle_sums.1 = bf16[64,8,128]{2,1,0:T(8,128)(2,1)} custom-call(s32[8]{0:T(128)} %fusion.13.places, bf16[512,128]{1,0:T(8,128)(2,1)} %get-tuple-element.15.left_ref, bf16[512,128]{1,0:T(8,128)(2,1)} %copy-done.7, bf16[512,128]{1,0:T(8,128)(2,1)} %copy-done.21, bf16[512,128]{1,0:T(8,128)(2,1)} %copy-done.18, bf16[512,128]{1,0:T(8,128)(2,1)} %copy-done.22, ...), custom_call_target="tpu_custom_call" | custom-call | tf_op jit(solution)/shard_map/triangle_sums/pallas_call | solution.py:268
  231.5 8.4 %all-to-all-start.5 = ((bf16[64,8,128]{2,1,0:T(8,128)(2,1)}), bf16[64,8,128]{2,1,0:T(8,128)(2,1)S(1)}, u32[]{:S(2)}, u32[]{:S(2)}) async-start(bf16[64,8,128]{2,1,0:T(8,128)(2,1)} %triangle_sums.1), calls=%async_computation.5 | async-start | bytes 262144 | tf_op jit(solution)/shard_map/all_to_all | solution.py:381
  240.6 8.9 %all-to-all-done.5.sum_ref = bf16[64,8,128]{2,1,0:T(8,128)(2,1)S(1)} async-done(((bf16[64,8,128]{2,1,0:T(8,128)(2,1)}), bf16[64,8,128]{2,1,0:T(8,128)(2,1)S(1)}, u32[]{:S(2)}, u32[]{:S(2)}) %all-to-all-start.5) | async-done | bytes 131104 | tf_op jit(solution)/shard_map/all_to_all | solution.py:381
  250.1 2.7 %pair_output.1 = bf16[4,8,16,128]{3,2,1,0:T(8,128)(2,1)} custom-call(bf16[64,8,128]{2,1,0:T(8,128)(2,1)} %copy-done.3, bf16[512,128]{1,0:T(8,128)(2,1)} %get-tuple-element.11.mid_ref, bf16[128,128]{1,0:T(8,128)(2,1)} %wg_ref.1, bf16[64,256]{1,0:T(8,128)(2,1)} %pad_maximum_fusion.1.w_ref), custom_call_target="tpu_custom_call" | custom-call | tf_op jit(solution)/shard_map/pair_output/pallas_call | solution.py:301
  252.8 5.1 %all-to-all-start.6 = ((bf16[4,8,16,128]{3,2,1,0:T(8,128)(2,1)}), bf16[4,8,16,128]{3,2,1,0:T(8,128)(2,1)S(1)}, u32[]{:S(2)}, u32[]{:S(2)}) async-start(bf16[4,8,16,128]{3,2,1,0:T(8,128)(2,1)} %pair_output.1), calls=%async_computation.6 | async-start | bytes 262144 | tf_op jit(solution)/shard_map/all_to_all | solution.py:383
  258.5 4.5 %all-to-all-done.6 = bf16[4,8,16,128]{3,2,1,0:T(8,128)(2,1)S(1)} async-done(((bf16[4,8,16,128]{3,2,1,0:T(8,128)(2,1)}), bf16[4,8,16,128]{3,2,1,0:T(8,128)(2,1)S(1)}, u32[]{:S(2)}, u32[]{:S(2)}) %all-to-all-start.6) | async-done | bytes 131104 | tf_op jit(solution)/shard_map/all_to_all | solution.py:383
  263.6 1.3 copy.26
  (90 shorter events, 14.4 us)
Async XLA Ops:
  0.6 3.1 %copy-start = (bf16[128,8]{0,1:T(8,128)(2,1)S(1)}, bf16[128,8]{0,1:T(8,128)(2,1)}, u32[]{:S(2)}) copy-start(bf16[128,8]{0,1:T(8,128)(2,1)} %param.16) | copy-start | bytes 6148
  3.8 10.2 %copy-start.10 = (bf16[4,64,256]{2,1,0:T(8,128)(2,1)S(1)}, bf16[4,64,256]{2,1,0:T(8,128)(2,1)}, u32[]{:S(2)}) copy-start(bf16[4,64,256]{2,1,0:T(8,128)(2,1)} %refs_0_.1) | copy-start | bytes 393220
  3.8 50.3 %copy-start.5 = (bf16[256,1024]{1,0:T(8,128)(2,1)S(1)}, bf16[256,1024]{1,0:T(8,128)(2,1)}, u32[]{:S(2)}) copy-start(bf16[256,1024]{1,0:T(8,128)(2,1)} %param.14) | copy-start | bytes 1572868
  6.9 48.9 %all-to-all-start = ((bf16[16,32,512]{2,1,0:T(8,128)(2,1)}), bf16[16,32,512]{2,1,0:T(8,128)(2,1)S(1)}, u32[]{:S(2)}, u32[]{:S(2)}) async-start(bf16[16,32,512]{2,1,0:T(8,128)(2,1)} %broadcast_in_dim.7), calls=%async_computation | async-start | bytes 1048576 | tf_op jit(solution)/shard_map/all_to_all | solution.py:358
  13.9 26.5 %collective-permute-start.1 = (bf16[4,64,256]{2,1,0:T(8,128)(2,1)S(1)}, bf16[4,64,256]{2,1,0:T(8,128)(2,1)S(1)}, u32[]{:S(2)}, u32[]{:S(2)}) collective-permute-start(bf16[4,64,256]{2,1,0:T(8,128)(2,1)S(1)} %copy-done.10), channel_id=1, source_target_pairs={{0,6},{1,7},{2,0},{3,1},{4,2},{5,3},{6,4},{7,5},{8,14},{9,15},{10,... | collective-permute-start | bytes 393224 | tf_op jit(solution)/shard_map/ppermute | solution.py:311
  25.8 17.8 %collective-permute-start.3 = (bf16[4,64,256]{2,1,0:T(8,128)(2,1)S(1)}, bf16[4,64,256]{2,1,0:T(8,128)(2,1)S(1)}, u32[]{:S(2)}, u32[]{:S(2)}) collective-permute-start(bf16[4,64,256]{2,1,0:T(8,128)(2,1)S(1)} %copy-done.10), channel_id=1, source_target_pairs={{0,4},{1,5},{2,6},{3,7},{4,0},{5,1},{6,2},{7,3},{8,12},{9,13},{10,... | collective-permute-start | bytes 393224 | tf_op jit(solution)/shard_map/ppermute | solution.py:311
  30.7 21.5 %collective-permute-start.5 = (bf16[4,64,256]{2,1,0:T(8,128)(2,1)S(1)}, bf16[4,64,256]{2,1,0:T(8,128)(2,1)S(1)}, u32[]{:S(2)}, u32[]{:S(2)}) collective-permute-start(bf16[4,64,256]{2,1,0:T(8,128)(2,1)S(1)} %copy-done.10), channel_id=1, source_target_pairs={{0,2},{1,3},{2,4},{3,5},{4,6},{5,7},{6,0},{7,1},{8,10},{9,11},{10,... | collective-permute-start | bytes 393224 | tf_op jit(solution)/shard_map/ppermute | solution.py:311
  38.5 17.2 %collective-permute-start = (bf16[4,64,256]{2,1,0:T(8,128)(2,1)S(1)}, bf16[4,64,256]{2,1,0:T(8,128)(2,1)S(1)}, u32[]{:S(2)}, u32[]{:S(2)}) collective-permute-start(bf16[4,64,256]{2,1,0:T(8,128)(2,1)S(1)} %copy-done.10), channel_id=1, source_target_pairs={{0,1},{1,0},{2,3},{3,2},{4,5},{5,4},{6,7},{7,6},{8,9},{9,8},{10,11... | collective-permute-start | bytes 393224 | tf_op jit(solution)/shard_map/ppermute | solution.py:311
  40.5 15.3 %copy-start.11 = (bf16[4,64,256]{2,1,0:T(8,128)(2,1)}, bf16[4,64,256]{2,1,0:T(8,128)(2,1)S(1)}, u32[]{:S(2)}) copy-start(bf16[4,64,256]{2,1,0:T(8,128)(2,1)S(1)} %collective-permute-done.1.refs_2_) | copy-start | bytes 393220
  40.5 15.2 %collective-permute-start.2 = (bf16[4,64,256]{2,1,0:T(8,128)(2,1)S(1)}, bf16[4,64,256]{2,1,0:T(8,128)(2,1)S(1)}, u32[]{:S(2)}, u32[]{:S(2)}) collective-permute-start(bf16[4,64,256]{2,1,0:T(8,128)(2,1)S(1)} %collective-permute-done.1.refs_2_), channel_id=1, source_target_pairs={{0,1},{1,0},{2,3},{3,2},{4,5},{5,4},{6,7},{7,6},{8,9},{9,8},{10,11... | collective-permute-start | bytes 393224 | tf_op jit(solution)/shard_map/ppermute | solution.py:311
  43.6 12.2 %copy-start.12 = (bf16[4,64,256]{2,1,0:T(8,128)(2,1)}, bf16[4,64,256]{2,1,0:T(8,128)(2,1)S(1)}, u32[]{:S(2)}) copy-start(bf16[4,64,256]{2,1,0:T(8,128)(2,1)S(1)} %collective-permute-done.3.refs_4_) | copy-start | bytes 393220
  43.6 12.1 %collective-permute-start.4 = (bf16[4,64,256]{2,1,0:T(8,128)(2,1)S(1)}, bf16[4,64,256]{2,1,0:T(8,128)(2,1)S(1)}, u32[]{:S(2)}, u32[]{:S(2)}) collective-permute-start(bf16[4,64,256]{2,1,0:T(8,128)(2,1)S(1)} %collective-permute-done.3.refs_4_), channel_id=1, source_target_pairs={{0,1},{1,0},{2,3},{3,2},{4,5},{5,4},{6,7},{7,6},{8,9},{9,8},{10,11... | collective-permute-start | bytes 393224 | tf_op jit(solution)/shard_map/ppermute | solution.py:311
  52.2 3.6 %copy-start.13 = (bf16[4,64,256]{2,1,0:T(8,128)(2,1)}, bf16[4,64,256]{2,1,0:T(8,128)(2,1)S(1)}, u32[]{:S(2)}) copy-start(bf16[4,64,256]{2,1,0:T(8,128)(2,1)S(1)} %collective-permute-done.5.refs_6_) | copy-start | bytes 393220
  52.2 3.6 %collective-permute-start.6 = (bf16[4,64,256]{2,1,0:T(8,128)(2,1)S(1)}, bf16[4,64,256]{2,1,0:T(8,128)(2,1)S(1)}, u32[]{:S(2)}, u32[]{:S(2)}) collective-permute-start(bf16[4,64,256]{2,1,0:T(8,128)(2,1)S(1)} %collective-permute-done.5.refs_6_), channel_id=1, source_target_pairs={{0,1},{1,0},{2,3},{3,2},{4,5},{5,4},{6,7},{7,6},{8,9},{9,8},{10,11... | collective-permute-start | bytes 393224 | tf_op jit(solution)/shard_map/ppermute | solution.py:311
  55.7 0.7 copy-start.14
  55.7 0.7 copy-start.15
  55.7 0.7 copy-start.16
  55.8 0.7 copy-start.17
  55.8 0.9 copy-start.2
  56.7 26.5 %copy-start.6 = (bf16[256,1024]{1,0:T(8,128)(2,1)S(1)}, bf16[256,1024]{1,0:T(8,128)(2,1)}, u32[]{:S(2)}) copy-start(bf16[256,1024]{1,0:T(8,128)(2,1)} %param.17) | copy-start | bytes 1572868
  69.3 23.4 %all-to-all-start.1 = ((bf16[64,8,128]{2,1,0:T(8,128)(2,1)}), bf16[64,8,128]{2,1,0:T(8,128)(2,1)S(1)}, u32[]{:S(2)}, u32[]{:S(2)}) async-start(bf16[64,8,128]{2,1,0:T(8,128)(2,1)} %row_attention.1), calls=%async_computation.1 | async-start | bytes 262144 | tf_op jit(solution)/shard_map/all_to_all | solution.py:361
  92.7 0.7 copy-start.4
  98.6 9.0 %collective-permute-start.7 = (bf16[32,256]{1,0:T(8,128)(2,1)}, bf16[32,256]{1,0:T(8,128)(2,1)S(1)}, u32[]{:S(2)}, u32[]{:S(2)}) collective-permute-start(bf16[32,256]{1,0:T(8,128)(2,1)} %get-tuple-element.8), channel_id=1, source_target_pairs={{0,1},{1,0},{2,3},{3,2},{4,5},{5,4},{6,7},{7,6},{8,9},{9,8},{10,11... | collective-permute-start | bytes 49160 | tf_op jit(solution)/shard_map/ppermute | solution.py:311
  102.6 29.3 %all-to-all-start.2 = ((bf16[4,32,256]{2,1,0:T(8,128)(2,1)}), bf16[4,32,256]{2,1,0:T(8,128)(2,1)S(1)}, u32[]{:S(2)}, u32[]{:S(2)}) async-start(bf16[4,32,256]{2,1,0:T(8,128)(2,1)} %broadcast_in_dim.8), calls=%async_computation.2 | async-start | bytes 131072 | tf_op jit(solution)/shard_map/all_to_all | solution.py:368
  108.3 20.1 %collective-permute-start.8 = (bf16[2,32,256]{2,1,0:T(8,128)(2,1)S(1)}, bf16[2,32,256]{2,1,0:T(8,128)(2,1)S(1)}, u32[]{:S(2)}, u32[]{:S(2)}) collective-permute-start(bf16[2,32,256]{2,1,0:T(8,128)(2,1)S(1)} %pad_maximum_fusion), channel_id=1, source_target_pairs={{0,6},{1,7},{2,0},{3,1},{4,2},{5,3},{6,4},{7,5},{8,14},{9,15},{10,... | collective-permute-start | bytes 98312 | tf_op jit(solution)/shard_map/ppermute | solution.py:311
  116.0 14.5 %collective-permute-start.9 = (bf16[2,32,256]{2,1,0:T(8,128)(2,1)S(1)}, bf16[2,32,256]{2,1,0:T(8,128)(2,1)S(1)}, u32[]{:S(2)}, u32[]{:S(2)}) collective-permute-start(bf16[2,32,256]{2,1,0:T(8,128)(2,1)S(1)} %pad_maximum_fusion), channel_id=1, source_target_pairs={{0,4},{1,5},{2,6},{3,7},{4,0},{5,1},{6,2},{7,3},{8,12},{9,13},{10,... | collective-permute-start | bytes 98312 | tf_op jit(solution)/shard_map/ppermute | solution.py:311
  121.4 10.5 %collective-permute-start.10 = (bf16[2,32,256]{2,1,0:T(8,128)(2,1)S(1)}, bf16[2,32,256]{2,1,0:T(8,128)(2,1)S(1)}, u32[]{:S(2)}, u32[]{:S(2)}) collective-permute-start(bf16[2,32,256]{2,1,0:T(8,128)(2,1)S(1)} %pad_maximum_fusion), channel_id=1, source_target_pairs={{0,2},{1,3},{2,4},{3,5},{4,6},{5,7},{6,0},{7,1},{8,10},{9,11},{10,... | collective-permute-start | bytes 98312 | tf_op jit(solution)/shard_map/ppermute | solution.py:311
  131.9 0.7 copy-start.9
  136.0 5.5 %copy-start.25 = (bf16[128,512]{1,0:T(8,128)(2,1)S(1)}, bf16[128,512]{1,0:T(8,128)(2,1)}, u32[]{:S(2)}) copy-start(bf16[128,512]{1,0:T(8,128)(2,1)} %param.21) | copy-start | bytes 393220
  136.0 25.0 %all-to-all-start.3 = ((bf16[16,160,256]{2,1,0:T(8,128)(2,1)}), bf16[16,160,256]{2,1,0:T(8,128)(2,1)S(1)}, u32[]{:S(2)}, u32[]{:S(2)}) async-start(bf16[16,160,256]{2,1,0:T(8,128)(2,1)} %spread.1), calls=%async_computation.3 | async-start | bytes 2621440 | tf_op jit(solution)/shard_map/all_to_all | solution.py:371
  161.0 1.1 copy-start.1
  189.0 51.0 %copy-start.26 = (bf16[128,128]{1,0:T(8,128)(2,1)S(1)}, bf16[128,128]{1,0:T(8,128)(2,1)}, u32[]{:S(2)}) copy-start(bf16[128,128]{1,0:T(8,128)(2,1)} %param.23) | copy-start | bytes 98308
  189.7 38.1 %copy-start.7 = (bf16[512,128]{1,0:T(8,128)(2,1)}, bf16[512,128]{1,0:T(8,128)(2,1)S(1)}, u32[]{:S(2)}) copy-start(bf16[512,128]{1,0:T(8,128)(2,1)S(1)} %get-tuple-element.14.refs_0_) | copy-start | bytes 393220
  189.7 23.5 %collective-permute-start.12 = (bf16[512,128]{1,0:T(8,128)(2,1)S(1)}, bf16[512,128]{1,0:T(8,128)(2,1)S(1)}, u32[]{:S(2)}, u32[]{:S(2)}) collective-permute-start(bf16[512,128]{1,0:T(8,128)(2,1)S(1)} %get-tuple-element.14.refs_0_), channel_id=1, source_target_pairs={{0,6},{1,7},{2,0},{3,1},{4,2},{5,3},{6,4},{7,5},{8,14},{9,15},{10,... | collective-permute-start | bytes 393224 | tf_op jit(solution)/shard_map/ppermute | solution.py:311
  194.1 28.4 %collective-permute-start.14 = (bf16[512,128]{1,0:T(8,128)(2,1)S(1)}, bf16[512,128]{1,0:T(8,128)(2,1)S(1)}, u32[]{:S(2)}, u32[]{:S(2)}) collective-permute-start(bf16[512,128]{1,0:T(8,128)(2,1)S(1)} %get-tuple-element.14.refs_0_), channel_id=1, source_target_pairs={{0,4},{1,5},{2,6},{3,7},{4,0},{5,1},{6,2},{7,3},{8,12},{9,13},{10,... | collective-permute-start | bytes 393224 | tf_op jit(solution)/shard_map/ppermute | solution.py:311
  202.7 21.7 %collective-permute-start.16 = (bf16[512,128]{1,0:T(8,128)(2,1)S(1)}, bf16[512,128]{1,0:T(8,128)(2,1)S(1)}, u32[]{:S(2)}, u32[]{:S(2)}) collective-permute-start(bf16[512,128]{1,0:T(8,128)(2,1)S(1)} %get-tuple-element.14.refs_0_), channel_id=1, source_target_pairs={{0,2},{1,3},{2,4},{3,5},{4,6},{5,7},{6,0},{7,1},{8,10},{9,11},{10,... | collective-permute-start | bytes 393224 | tf_op jit(solution)/shard_map/ppermute | solution.py:311
  207.5 19.3 %collective-permute-start.11 = (bf16[512,128]{1,0:T(8,128)(2,1)S(1)}, bf16[512,128]{1,0:T(8,128)(2,1)S(1)}, u32[]{:S(2)}, u32[]{:S(2)}) collective-permute-start(bf16[512,128]{1,0:T(8,128)(2,1)S(1)} %get-tuple-element.14.refs_0_), channel_id=1, source_target_pairs={{0,1},{1,0},{2,3},{3,2},{4,5},{5,4},{6,7},{7,6},{8,9},{9,8},{10,11... | collective-permute-start | bytes 393224 | tf_op jit(solution)/shard_map/ppermute | solution.py:311
  213.2 14.6 %copy-start.18 = (bf16[512,128]{1,0:T(8,128)(2,1)}, bf16[512,128]{1,0:T(8,128)(2,1)S(1)}, u32[]{:S(2)}) copy-start(bf16[512,128]{1,0:T(8,128)(2,1)S(1)} %collective-permute-done.12.refs_2_) | copy-start | bytes 393220
  213.2 13.7 %collective-permute-start.13 = (bf16[512,128]{1,0:T(8,128)(2,1)S(1)}, bf16[512,128]{1,0:T(8,128)(2,1)S(1)}, u32[]{:S(2)}, u32[]{:S(2)}) collective-permute-start(bf16[512,128]{1,0:T(8,128)(2,1)S(1)} %collective-permute-done.12.refs_2_), channel_id=1, source_target_pairs={{0,1},{1,0},{2,3},{3,2},{4,5},{5,4},{6,7},{7,6},{8,9},{9,8},{10,11... | collective-permute-start | bytes 393224 | tf_op jit(solution)/shard_map/ppermute | solution.py:311
  222.5 5.3 %copy-start.19 = (bf16[512,128]{1,0:T(8,128)(2,1)}, bf16[512,128]{1,0:T(8,128)(2,1)S(1)}, u32[]{:S(2)}) copy-start(bf16[512,128]{1,0:T(8,128)(2,1)S(1)} %collective-permute-done.14.refs_4_) | copy-start | bytes 393220
  222.5 4.4 %collective-permute-start.15 = (bf16[512,128]{1,0:T(8,128)(2,1)S(1)}, bf16[512,128]{1,0:T(8,128)(2,1)S(1)}, u32[]{:S(2)}, u32[]{:S(2)}) collective-permute-start(bf16[512,128]{1,0:T(8,128)(2,1)S(1)} %collective-permute-done.14.refs_4_), channel_id=1, source_target_pairs={{0,1},{1,0},{2,3},{3,2},{4,5},{5,4},{6,7},{7,6},{8,9},{9,8},{10,11... | collective-permute-start | bytes 393224 | tf_op jit(solution)/shard_map/ppermute | solution.py:311
  224.4 3.4 %copy-start.20 = (bf16[512,128]{1,0:T(8,128)(2,1)}, bf16[512,128]{1,0:T(8,128)(2,1)S(1)}, u32[]{:S(2)}) copy-start(bf16[512,128]{1,0:T(8,128)(2,1)S(1)} %collective-permute-done.16.refs_6_) | copy-start | bytes 393220
  224.4 3.4 %collective-permute-start.17 = (bf16[512,128]{1,0:T(8,128)(2,1)S(1)}, bf16[512,128]{1,0:T(8,128)(2,1)S(1)}, u32[]{:S(2)}, u32[]{:S(2)}) collective-permute-start(bf16[512,128]{1,0:T(8,128)(2,1)S(1)} %collective-permute-done.16.refs_6_), channel_id=1, source_target_pairs={{0,1},{1,0},{2,3},{3,2},{4,5},{5,4},{6,7},{7,6},{8,9},{9,8},{10,11... | collective-permute-start | bytes 393224 | tf_op jit(solution)/shard_map/ppermute | solution.py:311
  226.8 1.0 copy-start.21
  226.8 1.0 copy-start.22
  226.9 1.0 copy-start.23
  231.5 17.9 %all-to-all-start.5 = ((bf16[64,8,128]{2,1,0:T(8,128)(2,1)}), bf16[64,8,128]{2,1,0:T(8,128)(2,1)S(1)}, u32[]{:S(2)}, u32[]{:S(2)}) async-start(bf16[64,8,128]{2,1,0:T(8,128)(2,1)} %triangle_sums.1), calls=%async_computation.5 | async-start | bytes 262144 | tf_op jit(solution)/shard_map/all_to_all | solution.py:381
  252.8 10.2 %all-to-all-start.6 = ((bf16[4,8,16,128]{3,2,1,0:T(8,128)(2,1)}), bf16[4,8,16,128]{3,2,1,0:T(8,128)(2,1)S(1)}, u32[]{:S(2)}, u32[]{:S(2)}) async-start(bf16[4,8,16,128]{3,2,1,0:T(8,128)(2,1)} %pair_output.1), calls=%async_computation.6 | async-start | bytes 262144 | tf_op jit(solution)/shard_map/all_to_all | solution.py:383
  (3 other events, 1.9 us)

commit v2 on v1

v2 whole, which is shorter than its diff:
```python
import jax
import jax.numpy as jnp
from jax import lax
from jax.experimental import pallas as pl
from jax.experimental.pallas import tpu as pltpu
from jax.sharding import PartitionSpec as P


BF = jnp.bfloat16
F32 = jnp.float32
EPSILON = 1e-05
SCALE = 32**-0.5

NT = (((1,), (1,)), ((), ()))
TN = (((0,), (0,)), ((), ()))
TT = (((0,), (1,)), ((), ()))


def mm(a, b, dims):
    return lax.dot_general(a, b, dims, preferred_element_type=F32)


def layer_norm(inputs):
    inputs = inputs.astype(F32)
    average = jnp.mean(inputs, axis=-1, keepdims=True)
    centered = inputs - average
    variance = jnp.mean(jnp.square(centered), axis=-1, keepdims=True)
    return centered * lax.rsqrt(variance + EPSILON)


def sigmoid(x):
    return 1.0 / (1.0 + jnp.exp(-x))


def exp_rows(scores):
    top = jnp.max(scores, axis=0, keepdims=True)
    weights = jnp.exp(scores - top)
    total = jnp.sum(weights, axis=0, keepdims=True)
    return weights.astype(BF), 1.0 / total


VM = pl.BlockSpec(memory_space=pltpu.VMEM)
SM = pl.BlockSpec(memory_space=pltpu.SMEM)


def in_vmem(kernel, outs, scratch, place, *args):
    args = [pltpu.with_memory_space_constraint(a, pltpu.VMEM) for a in args]
    outs = tuple(pltpu.VMEM(shape, BF) for shape in outs)
    results = pl.pallas_call(
        kernel,
        out_shape=outs,
        in_specs=[SM] + [VM] * len(args),
        out_specs=(VM,) * len(outs),
        scratch_shapes=scratch,
    )(place, *args)
    return results if len(outs) > 1 else results[0]


def source_of(col, m):
    return (((col >> 1) + (m >> 1)) & 3) * 2 + ((col & 1) ^ (m & 1))


def bias_kernel(place, pair_ref, w_ref, out_ref, rows, heads):
    del place
    normed = layer_norm(pair_ref[...].reshape(2048, 128)).astype(BF).astype(F32)
    rows[...] = normed.reshape(64, 32, 128)
    weight = w_ref[...]
    for j in range(16):
        pairs = jnp.concatenate([rows[:, j, :], rows[:, j + 16, :]], axis=0).astype(BF)
        heads[j] = mm(weight, pairs, TT)
    lane = lax.broadcasted_iota(jnp.int32, (16, 128), 1) < 64
    tiles = []
    for p in range(4):
        a = heads[:, 2 * p, :]
        b = heads[:, 2 * p + 1, :]
        first = jnp.where(lane, a, pltpu.roll(b, 64, 1))
        second = jnp.where(lane, pltpu.roll(a, 64, 1), b)
        tiles.append(jnp.concatenate([first, second], axis=0))
    tile = jnp.concatenate(tiles, axis=1).astype(BF)
    for r in range(16):
        out_ref[r] = tile


def row_kernel(place, *refs):
    blocks = refs[:8]
    w_ref, bias_ref, wo_ref, out_ref, rows, keys, values, packed = refs[8:]
    for m in range(8):
        start = pl.multiple_of(source_of(place[0], m) * 64, 64)
        normed = layer_norm(blocks[m][...].reshape(256, 256)).astype(BF)
        if m == 0:
            own = normed
        for s in range(4):
            rows[s, pl.ds(start, 64), :] = normed[s * 64 : (s + 1) * 64]
    x = rows[...].reshape(2048, 256)
    keys[...] = jnp.dot(x, w_ref[:, 256:512], preferred_element_type=F32).astype(BF)
    values[...] = mm(w_ref[:, 512:768], x, TT).astype(BF)
    query_t = (mm(w_ref[:, 0:256], own, TT) * SCALE).astype(BF)
    gate_t = sigmoid(mm(w_ref[:, 768:1024], own, TT))
    head_row = lax.broadcasted_iota(jnp.int32, (256, 128), 0) // 32
    head_lane = lax.broadcasted_iota(jnp.int32, (256, 128), 1) // 64
    upper = lax.broadcasted_iota(jnp.int32, (64, 64), 0) < 32
    for s in range(4):
        mine = query_t[:, s * 64 : (s + 1) * 64]
        twice = jnp.concatenate([mine, mine], axis=1)
        key = keys[s * 512 : (s + 1) * 512]
        parts = []
        for p in range(4):
            diag = jnp.where(head_row == 2 * p + head_lane, twice, jnp.zeros_like(twice))
            scores = jnp.dot(key, diag, preferred_element_type=F32)
            scores = scores + bias_ref[:, p * 128 : (p + 1) * 128].astype(F32)
            weights, scale = exp_rows(scores)
            mixed = jnp.dot(
                values[p * 64 : (p + 1) * 64, s * 512 : (s + 1) * 512],
                weights,
                preferred_element_type=F32,
            )
            mixed = mixed * scale
            parts.append(jnp.where(upper, mixed[:, :64], mixed[:, 64:]))
        attended_t = jnp.concatenate(parts, axis=0)
        gated = (gate_t[:, s * 64 : (s + 1) * 64] * attended_t).astype(BF)
        result = blocks[0][s].astype(F32) + mm(gated, wo_ref[...], TN)
        for h in range(2):
            for b in range(4):
                source = (h * 4 + b) * 8
                target = (b * 2 + h) * 8
                for half in range(2):
                    packed[target : target + 8, half * 4 + s, :] = result[
                        source : source + 8, half * 128 : (half + 1) * 128
                    ]
    out_ref[...] = packed[...].astype(BF)


def column_kernel(place, x_ref, w_ref, wo_ref, wf_ref, out_ref, left_ref, right_ref, scratch):
    del place
    scratch[...] = x_ref[...].astype(F32)
    x = jnp.concatenate(
        [
            jnp.concatenate([scratch[:, s, :], scratch[:, 4 + s, :]], axis=1)
            for s in range(4)
        ],
        axis=0,
    )
    normed = layer_norm(x).astype(BF)
    key = jnp.dot(normed, w_ref[:, 256:512], preferred_element_type=F32).astype(BF)
    value_t = mm(w_ref[:, 512:768], normed, TT).astype(BF)
    query_t = (mm(w_ref[:, 0:256], normed, TT) * SCALE).astype(BF)
    gate_t = sigmoid(mm(w_ref[:, 768:1024], normed, TT))
    head_row = lax.broadcasted_iota(jnp.int32, (256, 256), 0) // 32
    parts = []
    for h in range(8):
        diag = jnp.where(head_row == h, query_t, jnp.zeros_like(query_t))
        weights, scale = exp_rows(jnp.dot(key, diag, preferred_element_type=F32))
        mixed = jnp.dot(value_t[h * 32 : (h + 1) * 32], weights, preferred_element_type=F32)
        parts.append(mixed * scale)
    gated = (gate_t * jnp.concatenate(parts, axis=0)).astype(BF)
    result = (x + mm(gated, wo_ref[...], TN)).astype(BF)
    factors = mm(wf_ref[...], layer_norm(result).astype(BF), TT).astype(BF)
    for b in range(4):
        left_ref[b] = factors[:32]
    right_ref[...] = factors[32:]
    wide = result.astype(F32)
    for s in range(4):
        for half in range(2):
            scratch[:, half * 4 + s, :] = wide[
                s * 64 : (s + 1) * 64, half * 128 : (half + 1) * 128
            ]
    out_ref[...] = scratch[...].astype(BF)


def spread_kernel(place, left_ref, *refs):
    rights, out_ref = refs[:4], refs[4]
    left = left_ref[...].reshape(128, 256)
    for r in range(16):
        out_ref[r, :128] = left
    for m in range(8):
        target = source_of(place[0], m) * 2
        block = rights[m // 2][m % 2]
        out_ref[target, 128:] = block
        out_ref[target + 1, 128:] = block


def block_transpose(arrays):
    rows = arrays[0].shape[0]
    lane = lax.broadcasted_iota(jnp.int32, (rows, 128), 1)
    low = lane < 64
    even = (lane // 32) % 2 == 0
    a0, a1, a2, a3 = arrays
    u0 = jnp.where(low, a0, pltpu.roll(a2, 64, 1))
    u2 = jnp.where(low, pltpu.roll(a0, 64, 1), a2)
    u1 = jnp.where(low, a1, pltpu.roll(a3, 64, 1))
    u3 = jnp.where(low, pltpu.roll(a1, 64, 1), a3)
    b0 = jnp.where(even, u0, pltpu.roll(u1, 32, 1))
    b1 = jnp.where(even, pltpu.roll(u0, 96, 1), u1)
    b2 = jnp.where(even, u2, pltpu.roll(u3, 32, 1))
    b3 = jnp.where(even, pltpu.roll(u2, 96, 1), u3)
    return b0, b1, b2, b3


def by_target(rows):
    order = [(h * 4 + b) * 8 for b in range(4) for h in range(2)]
    count = rows.shape[0] // 64
    return jnp.concatenate(
        [rows[j * 64 + s : j * 64 + s + 8] for j in range(count) for s in order], axis=0
    )


def pair_kernel(place, factor_ref, pair_ref, wo_ref, w_ref, mid_ref, out_ref,
                outer, flat, scratch, tile_rows):
    right = factor_ref[pl.ds(place[1] * 8, 8), 128:, :].reshape(256, 256)
    for b in range(4):
        left = factor_ref[:, b * 32 : (b + 1) * 32, :].reshape(512, 256)
        product = (mm(left, right, NT) * (1.0 / 256)).reshape(16, 32, 256)
        for h in range(2):
            start = (h * 4 + b) * 8
            outer[start : start + 8] = product[h * 8 : (h + 1) * 8]
    for group in range(8):
        chans = [outer[:, group * 4 + k, :] for k in range(4)]
        for tile in range(2):
            moved = block_transpose([c[:, tile * 128 : (tile + 1) * 128] for c in chans])
            for k in range(4):
                j = tile * 4 + k
                flat[j * 64 : (j + 1) * 64, group * 128 : (group + 1) * 128] = moved[k].astype(BF)
    update = jnp.dot(flat[...], wo_ref[...], preferred_element_type=F32).astype(BF)
    first = pl.multiple_of(place[2] * 8, 8)
    tile_rows[...] = pair_ref[:, pl.ds(first, 8), :].astype(F32)
    pair = jnp.concatenate([tile_rows[:, j, :] for j in range(8)], axis=0)
    mid = (pair + update.astype(F32)).astype(BF)
    mid_ref[...] = mid
    normed = layer_norm(mid)
    lane = lax.broadcasted_iota(jnp.int32, (64, 128), 1) < 64
    for side in range(2):
        rows = (by_target(normed) if side else normed).astype(BF)
        base = side * 256
        value = mm(w_ref[:, base : base + 128], rows, TT)
        gate = mm(w_ref[:, base + 128 : base + 256], rows, TT)
        both = sigmoid(gate) * value
        for pair in range(4):
            low = both[:64, pair * 128 : (pair + 1) * 128]
            high = both[64:, pair * 128 : (pair + 1) * 128]
            scratch[side, :, 2 * pair, :] = jnp.where(lane, low, pltpu.roll(high, 64, 1))
            scratch[side, :, 2 * pair + 1, :] = jnp.where(lane, pltpu.roll(low, 64, 1), high)
    out_ref[:, 0] = scratch[0].astype(BF)
    out_ref[:, 1] = scratch[1].astype(BF)


def triangle_kernel(place, left_ref, back_ref, *refs):
    rights, out_ref = refs[:8], refs[8]
    left = left_ref[...]
    lane = lax.broadcasted_iota(jnp.int32, (64, 128), 1) < 64
    for m in range(8):
        product = mm(rights[m][...], left, TN)
        block = jnp.where(lane, product[:64], product[64:]).astype(BF)
        target = source_of(place[0], m) * 2
        for b in range(4):
            for h in range(2):
                out_ref[b * 16 + target + h, 0] = block[(b * 2 + h) * 8 : (b * 2 + h + 1) * 8]
    out_ref[:, 1] = back_ref[...]


def output_kernel(place, sum_ref, mid_ref, wg_ref, w_ref, out_ref, scratch):
    del place
    sums = sum_ref[:, 0].astype(F32)
    fold = lambda v: (v + pltpu.roll(v, 64, 1)) * (1.0 / 128)
    average = fold(jnp.sum(sums, axis=0))
    centered = sums - average[None]
    variance = fold(jnp.sum(jnp.square(centered), axis=0))
    scratch[...] = centered * lax.rsqrt(variance + EPSILON)[None]
    mid = mid_ref[...].astype(F32)
    gate_t = sigmoid(mm(wg_ref[...], layer_norm(mid).astype(BF), TT))
    weight = jnp.concatenate([w_ref[:64], w_ref[64:]], axis=1)
    lane = lax.broadcasted_iota(jnp.int32, (128, 128), 1) < 64

    def mixed_of(j):
        product = mm(weight, scratch[:, j, :].astype(BF), TN)
        return product[:128, :64] + product[128:, 64:]

    for j in range(4):
        mixed = jnp.concatenate([mixed_of(j), mixed_of(j + 4)], axis=1)
        ends = (slice(j * 64, (j + 1) * 64), slice((j + 4) * 64, (j + 5) * 64))
        residual = jnp.concatenate([mid[e] for e in ends], axis=0).T
        gate = jnp.concatenate([gate_t[:, e] for e in ends], axis=1)
        part = (residual + gate * mixed).astype(BF)
        for b in range(4):
            out_ref[b, j] = part[b * 32 : (b + 1) * 32]


def unpack_kernel(x_ref, out_ref):
    for b in range(4):
        for j in range(4):
            block = x_ref[b, j]
            out_ref[b * 8 + j] = block[:, :64]
            out_ref[b * 8 + 4 + j] = block[:, 64:]


def shifted(x, step, flip):
    perm = [(c, (c // 2 - step) % 4 * 2 + (c % 2 ^ flip)) for c in range(8)]
    return lax.ppermute(x, "col", perm)


def gather_col(x):
    parts = {(0, 0): x}
    for step in (1, 3, 2):
        parts[step, 0] = shifted(x, step, 0)
    for step in (0, 1, 3, 2):
        parts[step, 1] = shifted(parts[step, 0], 0, 1)
    return [parts[m // 2, m % 2] for m in range(8)]


def local(
    alignment,
    pair_features,
    w_row,
    row_output_weight,
    w_bias,
    w_column,
    column_output_weight,
    outer_input_weight,
    w_outer_out,
    w_triangle_in,
    w_triangle_gate,
    w_triangle_out,
):
    both = ("branch", "row")
    place = jnp.stack(
        [lax.axis_index("col"), lax.axis_index("row") & 1, lax.axis_index("branch")]
    ).astype(jnp.int32)
    exchange = lambda x, axis: lax.all_to_all(x, axis, 0, 0, tiled=True)

    blocks = gather_col(alignment)
    bias = in_vmem(
        bias_kernel,
        [(16, 32, 512)],
        [pltpu.VMEM((64, 32, 128), F32), pltpu.VMEM((16, 8, 128), F32)],
        place,
        pair_features,
        w_bias,
    )
    bias = exchange(bias, "row").reshape(512, 512)

    columns = in_vmem(
        row_kernel,
        [(64, 8, 128)],
        [
            pltpu.VMEM((4, 512, 256), BF),
            pltpu.VMEM((2048, 256), BF),
            pltpu.VMEM((256, 2048), BF),
            pltpu.VMEM((64, 8, 128), F32),
        ],
        place,
        *blocks,
        w_row,
        bias,
        row_output_weight,
    )
    columns = exchange(columns, both)
    returning, left, right = in_vmem(
        column_kernel,
        [(64, 8, 128), (4, 32, 256), (32, 256)],
        [pltpu.VMEM((64, 8, 128), F32)],
        place,
        columns,
        w_column,
        column_output_weight,
        outer_input_weight,
    )

    right = jnp.stack([right, shifted(right, 0, 1)])
    rights = [right]
    for step in (1, 2, 3):
        rights.append(shifted(right, step, 0))
    left = exchange(left, "branch")
    factors = in_vmem(spread_kernel, [(16, 160, 256)], [], place, left, *rights)
    factors = exchange(factors, "row")

    mid, message = in_vmem(
        pair_kernel,
        [(512, 128), (64, 2, 8, 128)],
        [
            pltpu.VMEM((64, 32, 256), F32),
            pltpu.VMEM((512, 1024), BF),
            pltpu.VMEM((2, 64, 8, 128), F32),
            pltpu.VMEM((64, 8, 128), F32),
        ],
        place,
        factors,
        pair_features,
        w_outer_out,
        w_triangle_in,
    )
    message = exchange(message, both)
    tri_left = message[:, 0].reshape(512, 128)
    rights = gather_col(message[:, 1].reshape(512, 128))
    sums = in_vmem(triangle_kernel, [(64, 2, 8, 128)], [], place, tri_left, returning, *rights)
    sums = exchange(sums, both)
    parts = in_vmem(
        output_kernel,
        [(4, 4, 32, 128)],
        [pltpu.VMEM((64, 8, 128), F32)],
        place,
        sums,
        mid,
        w_triangle_gate,
        w_triangle_out,
    )
    parts = exchange(parts, "branch")
    pair_out = pl.pallas_call(
        unpack_kernel, out_shape=jax.ShapeDtypeStruct((32, 32, 64), BF), name="unpack"
    )(parts)
    back = sums[:, 1].reshape(4, 2, 8, 2, 4, 128)
    alignment_out = jnp.transpose(back, (4, 1, 0, 2, 3, 5)).reshape(4, 64, 256)
    return (alignment_out, jnp.transpose(pair_out, (2, 0, 1)))


def solution(mesh):
    in_specs = (P(("branch", "row"), "col", None), P("col", "row", None)) + (P(),) * 10
    out_specs = (P(("branch", "row"), "col", None), P("col", "row", "branch"))
    return jax.shard_map(local, mesh=mesh, in_specs=in_specs, out_specs=out_specs, check_vma=False)
```

time: 267 us -> 239 us (0.90)
  blocking collectives: 21.5 us -> 58.2 us
  waiting for transfers between devices: 63 us -> 39 us
  starting transfers between devices: 124 us -> 107 us
  local copies, waits for them, and re-layouts: 16 us -> 4.66 us
  Pallas kernels: 31.9 us -> 26.8 us
  other arithmetic: 5.51 us -> 0.66 us
    all_to_all x1 -> x3, blocking collectives: 21.5 us -> 58.2 us  [local(): exchange = lambda x, axis: lax.all_to_all(x, axis, 0, 0, tiled=True)]
    all_to_all x6 -> x4, waiting for transfers between devices: 40.1 us -> 14 us  [local(): exchange = lambda x, axis: lax.all_to_all(x, axis, 0, 0, tiled=True)]
    all_to_all x6 -> x4, starting transfers between devices: 43.2 us -> 30.7 us  [local(): exchange = lambda x, axis: lax.all_to_all(x, axis, 0, 0, tiled=True)]
    unnamed x62 -> x30, local copies, waits for them, and re-layouts: 9.99 us -> 3.96 us
    pallas_call x6 -> x8, Pallas kernels: 31.9 us -> 26.8 us  [the longest x7 25.1 us: in_vmem(): pl.pallas_call(kernel, out_shape=outs, in_specs=[SM] + [VM] * len(args),...]
    ppermute x18, starting transfers between devices: 80.6 us -> 76.6 us  [shifted(): return lax.ppermute(x, 'col', perm)]
    reduce_sum x2 -> x0, other arithmetic: 3.06 us -> none  [the longest x1 1.67 us: layer_norm(): variance = jnp.mean(jnp.square(centered), axis=-1, keepdims=True)]
  transfers between devices with their start and end apart: 24 -> 22, of which waited for: 11 -> 11; matrix products, arithmetic and copies ran while one was open for 4% -> 0% of each run, Pallas kernels for 0% -> 0%
where the time goes in v2:
time: 239 us; the launch traced here: 238 us
  starting transfers between devices  107 us (45%)
  blocking collectives  58.2 us (24%)
  waiting for transfers between devices  39 us (16%)
  Pallas kernels  26.8 us (11%)
  local copies, waits for them, and re-layouts  4.66 us (2%)
    ppermute x18, starting transfers between devices, shifted(): return lax.ppermute(x, 'col', perm)  76.6 us
    all_to_all x3, blocking collectives, local(): exchange = lambda x, axis: lax.all_to_all(x, axis, 0, 0, tiled=True)  58.2 us
    all_to_all x4, starting transfers between devices, local(): exchange = lambda x, axis: lax.all_to_all(x, axis, 0, 0, tiled=True)  30.7 us
    pallas_call x7, Pallas kernels, in_vmem(): pl.pallas_call(kernel, out_shape=outs, in_specs=[SM] + [VM] * len(args),...  25.1 us
    ppermute x18, waiting for transfers between devices, shifted(): return lax.ppermute(x, 'col', perm)  25 us
    all_to_all x4, waiting for transfers between devices, local(): exchange = lambda x, axis: lax.all_to_all(x, axis, 0, 0, tiled=True)  14 us
  transfers between devices with their start and end apart: 22, of which 11 were waited for; matrix products, arithmetic and copies ran while one was open for 0% of the time, Pallas kernels for 0%

profile of v2, /device:TPU:32, one launch (start us, length us, event | category | flops | bytes accessed | tf_op | source)
XLA Modules:
  0.0 237.7 jit_solution(13672354961855944784)
XLA Ops:
  0.6 0.8 copy.14.w_ref
  1.4 0.7 pad_add_fusion.place
  2.1 1.0 copy-done.1
  3.1 3.0 %shard_map.131 = bf16[16,32,512]{2,1,0:T(8,128)(2,1)} custom-call(s32[3]{0:T(128)} %pad_add_fusion.place, bf16[64,32,128]{2,1,0:T(8,128)(2,1)S(1)} %copy-done.1, bf16[128,8]{1,0:T(8,128)(2,1)S(1)} %copy.14.w_ref), custom_call_target="tpu_custom_call" | custom-call | tf_op jit(solution)/shard_map/pallas_call | solution.py:49
  6.2 7.0 %all-to-all-start = ((bf16[16,32,512]{2,1,0:T(8,128)(2,1)}), bf16[16,32,512]{2,1,0:T(8,128)(2,1)S(1)}, u32[]{:S(2)}, u32[]{:S(2)}) async-start(bf16[16,32,512]{2,1,0:T(8,128)(2,1)} %shard_map.131), calls=%async_computation | async-start | bytes 1048576 | tf_op jit(solution)/shard_map/all_to_all | solution.py:327
  13.2 14.8 %collective-permute-start.3 = (bf16[4,64,256]{2,1,0:T(8,128)(2,1)S(1)}, bf16[4,64,256]{2,1,0:T(8,128)(2,1)S(1)}, u32[]{:S(2)}, u32[]{:S(2)}) collective-permute-start(bf16[4,64,256]{2,1,0:T(8,128)(2,1)S(1)} %copy-done.6), channel_id=1, source_target_pairs={{0,4},{1,5},{2,6},{3,7},{4,0},{5,1},{6,2},{7,3},{8,12},{9,13},{10,... | collective-permute-start | bytes 393224 | tf_op jit(solution)/shard_map/ppermute | solution.py:297
  28.1 1.9 collective-permute-start.1
  30.0 7.8 %collective-permute-start.5 = (bf16[4,64,256]{2,1,0:T(8,128)(2,1)S(1)}, bf16[4,64,256]{2,1,0:T(8,128)(2,1)S(1)}, u32[]{:S(2)}, u32[]{:S(2)}) collective-permute-start(bf16[4,64,256]{2,1,0:T(8,128)(2,1)S(1)} %copy-done.6), channel_id=1, source_target_pairs={{0,2},{1,3},{2,4},{3,5},{4,6},{5,7},{6,0},{7,1},{8,10},{9,11},{10,... | collective-permute-start | bytes 393224 | tf_op jit(solution)/shard_map/ppermute | solution.py:297
  37.8 1.9 collective-permute-start
  39.7 4.0 %collective-permute-done.3.refs_4_ = bf16[4,64,256]{2,1,0:T(8,128)(2,1)S(1)} collective-permute-done((bf16[4,64,256]{2,1,0:T(8,128)(2,1)S(1)}, bf16[4,64,256]{2,1,0:T(8,128)(2,1)S(1)}, u32[]{:S(2)}, u32[]{:S(2)}) %collective-permute-start.3) | collective-permute-done | bytes 131104 | tf_op jit(solution)/shard_map/ppermute | solution.py:297
  43.8 1.9 collective-permute-start.4
  45.7 2.4 %collective-permute-start.2 = (bf16[4,64,256]{2,1,0:T(8,128)(2,1)S(1)}, bf16[4,64,256]{2,1,0:T(8,128)(2,1)S(1)}, u32[]{:S(2)}, u32[]{:S(2)}) collective-permute-start(bf16[4,64,256]{2,1,0:T(8,128)(2,1)S(1)} %collective-permute-done.1.refs_2_), channel_id=1, source_target_pairs={{0,1},{1,0},{2,3},{3,2},{4,5},{5,4},{6,7},{7,6},{8,9},{9,8},{10,11... | collective-permute-start | bytes 393224 | tf_op jit(solution)/shard_map/ppermute | solution.py:297
  48.4 1.9 collective-permute-start.6
  50.4 1.3 collective-permute-done.6.refs_7_
  51.7 9.4 %shard_map.132 = bf16[64,8,128]{2,1,0:T(8,128)(2,1)} custom-call(s32[3]{0:T(128)} %pad_add_fusion.place, bf16[4,64,256]{2,1,0:T(8,128)(2,1)S(1)} %copy-done.6, bf16[4,64,256]{2,1,0:T(8,128)(2,1)S(1)} %collective-permute-done.refs_1_, bf16[4,64,256]{2,1,0:T(8,128)(2,1)S(1)} %collective-permute-done.1.refs_2_, ...), custom_call_target="tpu_custom_call" | custom-call | tf_op jit(solution)/shard_map/pallas_call | solution.py:49
  61.1 13.5 %all-to-all-start.1 = ((bf16[64,8,128]{2,1,0:T(8,128)(2,1)}), bf16[64,8,128]{2,1,0:T(8,128)(2,1)S(1)}, u32[]{:S(2)}, u32[]{:S(2)}) async-start(bf16[64,8,128]{2,1,0:T(8,128)(2,1)} %shard_map.132), calls=%async_computation.1 | async-start | bytes 262144 | tf_op jit(solution)/shard_map/all_to_all | solution.py:327
  74.7 9.5 %all-to-all-done.1.x_ref = bf16[64,8,128]{2,1,0:T(8,128)(2,1)S(1)} async-done(((bf16[64,8,128]{2,1,0:T(8,128)(2,1)}), bf16[64,8,128]{2,1,0:T(8,128)(2,1)S(1)}, u32[]{:S(2)}, u32[]{:S(2)}) %all-to-all-start.1) | async-done | bytes 131104 | tf_op jit(solution)/shard_map/all_to_all | solution.py:327
  84.2 4.6 %shard_map.133 = (bf16[64,8,128]{2,1,0:T(8,128)(2,1)S(1)}, bf16[4,32,256]{2,1,0:T(8,128)(2,1)}, bf16[32,256]{1,0:T(8,128)(2,1)S(1)}) custom-call(s32[3]{0:T(128)} %pad_add_fusion.place, bf16[64,8,128]{2,1,0:T(8,128)(2,1)S(1)} %all-to-all-done.1.x_ref, bf16[256,1024]{1,0:T(8,128)(2,1)S(1)} %copy-done.4, bf16[256,256]{1,0:T(8,128)(2,1)S(1)} %copy-done.9, ...), custom_call_target="tpu_custom_call" | custom-call | tf_op jit(solution)/shard_map/pallas_call | solution.py:49
  88.8 5.0 %all-to-all-start.2 = ((bf16[4,32,256]{2,1,0:T(8,128)(2,1)}), bf16[4,32,256]{2,1,0:T(8,128)(2,1)S(1)}, u32[]{:S(2)}, u32[]{:S(2)}) async-start(bf16[4,32,256]{2,1,0:T(8,128)(2,1)} %get-tuple-element.7), calls=%async_computation.2 | async-start | bytes 131072 | tf_op jit(solution)/shard_map/all_to_all | solution.py:327
  93.9 1.9 collective-permute-start.7
  95.8 1.1 collective-permute-done.7
  96.9 5.7 %collective-permute-start.10 = (bf16[2,32,256]{2,1,0:T(8,128)(2,1)S(1)}, bf16[2,32,256]{2,1,0:T(8,128)(2,1)S(1)}, u32[]{:S(2)}, u32[]{:S(2)}) collective-permute-start(bf16[2,32,256]{2,1,0:T(8,128)(2,1)S(1)} %pad_maximum_fusion.refs_0_), channel_id=1, source_target_pairs={{0,2},{1,3},{2,4},{3,5},{4,6},{5,7},{6,0},{7,1},{8,10},{9,11},{10,... | collective-permute-start | bytes 98312 | tf_op jit(solution)/shard_map/ppermute | solution.py:297
  102.7 9.2 %collective-permute-start.9 = (bf16[2,32,256]{2,1,0:T(8,128)(2,1)S(1)}, bf16[2,32,256]{2,1,0:T(8,128)(2,1)S(1)}, u32[]{:S(2)}, u32[]{:S(2)}) collective-permute-start(bf16[2,32,256]{2,1,0:T(8,128)(2,1)S(1)} %pad_maximum_fusion.refs_0_), channel_id=1, source_target_pairs={{0,4},{1,5},{2,6},{3,7},{4,0},{5,1},{6,2},{7,3},{8,12},{9,13},{10,... | collective-permute-start | bytes 98312 | tf_op jit(solution)/shard_map/ppermute | solution.py:297
  111.9 3.2 %collective-permute-start.8 = (bf16[2,32,256]{2,1,0:T(8,128)(2,1)S(1)}, bf16[2,32,256]{2,1,0:T(8,128)(2,1)S(1)}, u32[]{:S(2)}, u32[]{:S(2)}) collective-permute-start(bf16[2,32,256]{2,1,0:T(8,128)(2,1)S(1)} %pad_maximum_fusion.refs_0_), channel_id=1, source_target_pairs={{0,6},{1,7},{2,0},{3,1},{4,2},{5,3},{6,4},{7,5},{8,14},{9,15},{10,... | collective-permute-start | bytes 98312 | tf_op jit(solution)/shard_map/ppermute | solution.py:297
  115.2 2.2 collective-permute-done.9.refs_2_
  117.3 5.3 %collective-permute-done.8.refs_1_ = bf16[2,32,256]{2,1,0:T(8,128)(2,1)S(1)} collective-permute-done((bf16[2,32,256]{2,1,0:T(8,128)(2,1)S(1)}, bf16[2,32,256]{2,1,0:T(8,128)(2,1)S(1)}, u32[]{:S(2)}, u32[]{:S(2)}) %collective-permute-start.8) | collective-permute-done | bytes 32800 | tf_op jit(solution)/shard_map/ppermute | solution.py:297
  122.6 0.8 shard_map.134
  123.4 21.3 %all_to_all.35.factor_ref = bf16[16,160,256]{2,1,0:T(8,128)(2,1)} all-to-all(bf16[16,160,256]{2,1,0:T(8,128)(2,1)S(1)} %shard_map.134), channel_id=1, replica_groups=mesh['branch'=4,'row'=16,'col'=8] {'row'}, dimensions={0} | all-to-all | bytes 2621440 | tf_op jit(solution)/shard_map/all_to_all | solution.py:327
  144.8 1.3 copy-done
  146.1 3.7 %shard_map.135 = (bf16[512,128]{1,0:T(8,128)(2,1)S(1)}, bf16[64,2,8,128]{3,2,1,0:T(8,128)(2,1)S(1)}) custom-call(s32[3]{0:T(128)} %pad_add_fusion.place, bf16[16,160,256]{2,1,0:T(8,128)(2,1)S(1)} %copy-done, bf16[64,32,128]{2,1,0:T(8,128)(2,1)S(1)} %copy-done.2, bf16[1024,128]{1,0:T(8,128)(2,1)S(1)} %copy-done.5, bf16[128,512]{1,0:T(8,128)(2,1)S(1)} %copy-done.8), custom_call_target="tpu_custom_call" | custom-call | tf_op jit(solution)/shard_map/pallas_call | solution.py:49
  149.8 17.7 %all_to_all.36 = bf16[64,2,8,128]{3,2,1,0:T(8,128)(2,1)S(1)} all-to-all(bf16[64,2,8,128]{3,2,1,0:T(8,128)(2,1)S(1)} %get-tuple-element.9), channel_id=1, replica_groups=mesh['branch'=4,'row'=16,'col'=8] {'branch','row'}, dimensions={0} | all-to-all | bytes 524288 | tf_op jit(solution)/shard_map/all_to_all | solution.py:327
  167.6 2.7 %collective-permute-start.16 = (bf16[512,128]{1,0:T(8,128)(2,1)S(1)}, bf16[512,128]{1,0:T(8,128)(2,1)S(1)}, u32[]{:S(2)}, u32[]{:S(2)}) collective-permute-start(bf16[512,128]{1,0:T(8,128)(2,1)S(1)} %get-tuple-element.12.refs_0_), channel_id=1, source_target_pairs={{0,2},{1,3},{2,4},{3,5},{4,6},{5,7},{6,0},{7,1},{8,10},{9,11},{10,... | collective-permute-start | bytes 393224 | tf_op jit(solution)/shard_map/ppermute | solution.py:297
  170.3 7.6 %collective-permute-start.14 = (bf16[512,128]{1,0:T(8,128)(2,1)S(1)}, bf16[512,128]{1,0:T(8,128)(2,1)S(1)}, u32[]{:S(2)}, u32[]{:S(2)}) collective-permute-start(bf16[512,128]{1,0:T(8,128)(2,1)S(1)} %get-tuple-element.12.refs_0_), channel_id=1, source_target_pairs={{0,4},{1,5},{2,6},{3,7},{4,0},{5,1},{6,2},{7,3},{8,12},{9,13},{10,... | collective-permute-start | bytes 393224 | tf_op jit(solution)/shard_map/ppermute | solution.py:297
  177.9 5.4 %collective-permute-start.12 = (bf16[512,128]{1,0:T(8,128)(2,1)S(1)}, bf16[512,128]{1,0:T(8,128)(2,1)S(1)}, u32[]{:S(2)}, u32[]{:S(2)}) collective-permute-start(bf16[512,128]{1,0:T(8,128)(2,1)S(1)} %get-tuple-element.12.refs_0_), channel_id=1, source_target_pairs={{0,6},{1,7},{2,0},{3,1},{4,2},{5,3},{6,4},{7,5},{8,14},{9,15},{10,... | collective-permute-start | bytes 393224 | tf_op jit(solution)/shard_map/ppermute | solution.py:297
  183.3 1.9 collective-permute-start.11
  185.2 2.4 %collective-permute-start.17 = (bf16[512,128]{1,0:T(8,128)(2,1)S(1)}, bf16[512,128]{1,0:T(8,128)(2,1)S(1)}, u32[]{:S(2)}, u32[]{:S(2)}) collective-permute-start(bf16[512,128]{1,0:T(8,128)(2,1)S(1)} %collective-permute-done.16.refs_6_), channel_id=1, source_target_pairs={{0,1},{1,0},{2,3},{3,2},{4,5},{5,4},{6,7},{7,6},{8,9},{9,8},{10,11... | collective-permute-start | bytes 393224 | tf_op jit(solution)/shard_map/ppermute | solution.py:297
  187.6 6.8 %collective-permute-done.14.refs_4_ = bf16[512,128]{1,0:T(8,128)(2,1)S(1)} collective-permute-done((bf16[512,128]{1,0:T(8,128)(2,1)S(1)}, bf16[512,128]{1,0:T(8,128)(2,1)S(1)}, u32[]{:S(2)}, u32[]{:S(2)}) %collective-permute-start.14) | collective-permute-done | bytes 131104 | tf_op jit(solution)/shard_map/ppermute | solution.py:297
  194.4 1.9 collective-permute-start.15
  196.3 2.6 %collective-permute-done.12.refs_2_ = bf16[512,128]{1,0:T(8,128)(2,1)S(1)} collective-permute-done((bf16[512,128]{1,0:T(8,128)(2,1)S(1)}, bf16[512,128]{1,0:T(8,128)(2,1)S(1)}, u32[]{:S(2)}, u32[]{:S(2)}) %collective-permute-start.12) | collective-permute-done | bytes 131104 | tf_op jit(solution)/shard_map/ppermute | solution.py:297
  199.0 1.9 collective-permute-start.13
  200.9 1.3 collective-permute-done.13.refs_3_
  202.2 1.2 shard_map.136
  203.4 19.1 %all_to_all.37.sum_ref = bf16[64,2,8,128]{3,2,1,0:T(8,128)(2,1)S(1)} all-to-all(bf16[64,2,8,128]{3,2,1,0:T(8,128)(2,1)S(1)} %shard_map.136), channel_id=1, replica_groups=mesh['branch'=4,'row'=16,'col'=8] {'branch','row'}, dimensions={0} | all-to-all | bytes 524288 | tf_op jit(solution)/shard_map/all_to_all | solution.py:327
  222.5 2.4 %shard_map.137 = bf16[4,4,32,128]{3,2,1,0:T(8,128)(2,1)} custom-call(s32[3]{0:T(128)} %pad_add_fusion.place, bf16[64,2,8,128]{3,2,1,0:T(8,128)(2,1)S(1)} %all_to_all.37.sum_ref, bf16[512,128]{1,0:T(8,128)(2,1)S(1)} %get-tuple-element.11.mid_ref, bf16[128,128]{1,0:T(8,128)(2,1)S(1)} %copy-done.10, bf16[128,128]{1,0:T(8,128)(2,1)S(1)} %copy-done.11), custom_call_target="tpu_custom_call" | custom-call | tf_op jit(solution)/shard_map/pallas_call | solution.py:49
  224.9 5.2 %all-to-all-start.6 = ((bf16[4,4,32,128]{3,2,1,0:T(8,128)(2,1)}), bf16[4,4,32,128]{3,2,1,0:T(8,128)(2,1)S(1)}, u32[]{:S(2)}, u32[]{:S(2)}) async-start(bf16[4,4,32,128]{3,2,1,0:T(8,128)(2,1)} %shard_map.137), calls=%async_computation.6 | async-start | bytes 262144 | tf_op jit(solution)/shard_map/all_to_all | solution.py:327
  230.1 0.7 copy.16
  230.8 4.5 %all-to-all-done.6.x_ref = bf16[4,4,32,128]{3,2,1,0:T(8,128)(2,1)S(1)} async-done(((bf16[4,4,32,128]{3,2,1,0:T(8,128)(2,1)}), bf16[4,4,32,128]{3,2,1,0:T(8,128)(2,1)S(1)}, u32[]{:S(2)}, u32[]{:S(2)}) %all-to-all-start.6) | async-done | bytes 131104 | tf_op jit(solution)/shard_map/all_to_all | solution.py:327
  235.9 1.7 unpack.1
  (42 shorter events, 1.2 us)
Async XLA Ops:
  2.1 1.0 copy-start.1
  3.1 10.1 %copy-start.6 = (bf16[4,64,256]{2,1,0:T(8,128)(2,1)S(1)}, bf16[4,64,256]{2,1,0:T(8,128)(2,1)}, u32[]{:S(2)}) copy-start(bf16[4,64,256]{2,1,0:T(8,128)(2,1)} %refs_0_.1) | copy-start | bytes 393220
  3.1 48.5 %copy-start.3 = (bf16[256,1024]{1,0:T(8,128)(2,1)S(1)}, bf16[256,1024]{1,0:T(8,128)(2,1)}, u32[]{:S(2)}) copy-start(bf16[256,1024]{1,0:T(8,128)(2,1)} %refs_8_.1) | copy-start | bytes 1572868
  3.1 48.5 %copy-start.7 = (bf16[256,256]{1,0:T(8,128)(2,1)S(1)}, bf16[256,256]{1,0:T(8,128)(2,1)}, u32[]{:S(2)}) copy-start(bf16[256,256]{1,0:T(8,128)(2,1)} %refs_10_.1) | copy-start | bytes 393220
  6.2 45.5 %all-to-all-start = ((bf16[16,32,512]{2,1,0:T(8,128)(2,1)}), bf16[16,32,512]{2,1,0:T(8,128)(2,1)S(1)}, u32[]{:S(2)}, u32[]{:S(2)}) async-start(bf16[16,32,512]{2,1,0:T(8,128)(2,1)} %shard_map.131), calls=%async_computation | async-start | bytes 1048576 | tf_op jit(solution)/shard_map/all_to_all | solution.py:327
  13.2 30.6 %collective-permute-start.3 = (bf16[4,64,256]{2,1,0:T(8,128)(2,1)S(1)}, bf16[4,64,256]{2,1,0:T(8,128)(2,1)S(1)}, u32[]{:S(2)}, u32[]{:S(2)}) collective-permute-start(bf16[4,64,256]{2,1,0:T(8,128)(2,1)S(1)} %copy-done.6), channel_id=1, source_target_pairs={{0,4},{1,5},{2,6},{3,7},{4,0},{5,1},{6,2},{7,3},{8,12},{9,13},{10,... | collective-permute-start | bytes 393224 | tf_op jit(solution)/shard_map/ppermute | solution.py:297
  28.1 17.7 %collective-permute-start.1 = (bf16[4,64,256]{2,1,0:T(8,128)(2,1)S(1)}, bf16[4,64,256]{2,1,0:T(8,128)(2,1)S(1)}, u32[]{:S(2)}, u32[]{:S(2)}) collective-permute-start(bf16[4,64,256]{2,1,0:T(8,128)(2,1)S(1)} %copy-done.6), channel_id=1, source_target_pairs={{0,6},{1,7},{2,0},{3,1},{4,2},{5,3},{6,4},{7,5},{8,14},{9,15},{10,... | collective-permute-start | bytes 393224 | tf_op jit(solution)/shard_map/ppermute | solution.py:297
  30.0 18.4 %collective-permute-start.5 = (bf16[4,64,256]{2,1,0:T(8,128)(2,1)S(1)}, bf16[4,64,256]{2,1,0:T(8,128)(2,1)S(1)}, u32[]{:S(2)}, u32[]{:S(2)}) collective-permute-start(bf16[4,64,256]{2,1,0:T(8,128)(2,1)S(1)} %copy-done.6), channel_id=1, source_target_pairs={{0,2},{1,3},{2,4},{3,5},{4,6},{5,7},{6,0},{7,1},{8,10},{9,11},{10,... | collective-permute-start | bytes 393224 | tf_op jit(solution)/shard_map/ppermute | solution.py:297
  37.8 12.5 %collective-permute-start = (bf16[4,64,256]{2,1,0:T(8,128)(2,1)S(1)}, bf16[4,64,256]{2,1,0:T(8,128)(2,1)S(1)}, u32[]{:S(2)}, u32[]{:S(2)}) collective-permute-start(bf16[4,64,256]{2,1,0:T(8,128)(2,1)S(1)} %copy-done.6), channel_id=1, source_target_pairs={{0,1},{1,0},{2,3},{3,2},{4,5},{5,4},{6,7},{7,6},{8,9},{9,8},{10,11... | collective-permute-start | bytes 393224 | tf_op jit(solution)/shard_map/ppermute | solution.py:297
  43.8 6.5 %collective-permute-start.4 = (bf16[4,64,256]{2,1,0:T(8,128)(2,1)S(1)}, bf16[4,64,256]{2,1,0:T(8,128)(2,1)S(1)}, u32[]{:S(2)}, u32[]{:S(2)}) collective-permute-start(bf16[4,64,256]{2,1,0:T(8,128)(2,1)S(1)} %collective-permute-done.3.refs_4_), channel_id=1, source_target_pairs={{0,1},{1,0},{2,3},{3,2},{4,5},{5,4},{6,7},{7,6},{8,9},{9,8},{10,11... | collective-permute-start | bytes 393224 | tf_op jit(solution)/shard_map/ppermute | solution.py:297
  45.7 4.6 %collective-permute-start.2 = (bf16[4,64,256]{2,1,0:T(8,128)(2,1)S(1)}, bf16[4,64,256]{2,1,0:T(8,128)(2,1)S(1)}, u32[]{:S(2)}, u32[]{:S(2)}) collective-permute-start(bf16[4,64,256]{2,1,0:T(8,128)(2,1)S(1)} %collective-permute-done.1.refs_2_), channel_id=1, source_target_pairs={{0,1},{1,0},{2,3},{3,2},{4,5},{5,4},{6,7},{7,6},{8,9},{9,8},{10,11... | collective-permute-start | bytes 393224 | tf_op jit(solution)/shard_map/ppermute | solution.py:297
  48.4 3.2 %collective-permute-start.6 = (bf16[4,64,256]{2,1,0:T(8,128)(2,1)S(1)}, bf16[4,64,256]{2,1,0:T(8,128)(2,1)S(1)}, u32[]{:S(2)}, u32[]{:S(2)}) collective-permute-start(bf16[4,64,256]{2,1,0:T(8,128)(2,1)S(1)} %collective-permute-done.5.refs_6_), channel_id=1, source_target_pairs={{0,1},{1,0},{2,3},{3,2},{4,5},{5,4},{6,7},{7,6},{8,9},{9,8},{10,11... | collective-permute-start | bytes 393224 | tf_op jit(solution)/shard_map/ppermute | solution.py:297
  51.7 22.9 %copy-start.13 = (bf16[256,64]{0,1:T(8,128)(2,1)S(1)}, bf16[256,64]{0,1:T(8,128)(2,1)}, u32[]{:S(2)}) copy-start(bf16[256,64]{0,1:T(8,128)(2,1)} %param.19) | copy-start | bytes 98308
  51.7 32.5 %copy-start.4 = (bf16[256,1024]{1,0:T(8,128)(2,1)S(1)}, bf16[256,1024]{1,0:T(8,128)(2,1)}, u32[]{:S(2)}) copy-start(bf16[256,1024]{1,0:T(8,128)(2,1)} %w_ref.4) | copy-start | bytes 1572868
  51.7 32.5 %copy-start.9 = (bf16[256,256]{1,0:T(8,128)(2,1)S(1)}, bf16[256,256]{1,0:T(8,128)(2,1)}, u32[]{:S(2)}) copy-start(bf16[256,256]{1,0:T(8,128)(2,1)} %wo_ref.2) | copy-start | bytes 393220
  61.1 23.1 %all-to-all-start.1 = ((bf16[64,8,128]{2,1,0:T(8,128)(2,1)}), bf16[64,8,128]{2,1,0:T(8,128)(2,1)S(1)}, u32[]{:S(2)}, u32[]{:S(2)}) async-start(bf16[64,8,128]{2,1,0:T(8,128)(2,1)} %shard_map.132), calls=%async_computation.1 | async-start | bytes 262144 | tf_op jit(solution)/shard_map/all_to_all | solution.py:327
  88.8 33.8 %all-to-all-start.2 = ((bf16[4,32,256]{2,1,0:T(8,128)(2,1)}), bf16[4,32,256]{2,1,0:T(8,128)(2,1)S(1)}, u32[]{:S(2)}, u32[]{:S(2)}) async-start(bf16[4,32,256]{2,1,0:T(8,128)(2,1)} %get-tuple-element.7), calls=%async_computation.2 | async-start | bytes 131072 | tf_op jit(solution)/shard_map/all_to_all | solution.py:327
  93.9 3.1 %collective-permute-start.7 = (bf16[32,256]{1,0:T(8,128)(2,1)S(1)}, bf16[32,256]{1,0:T(8,128)(2,1)S(1)}, u32[]{:S(2)}, u32[]{:S(2)}) collective-permute-start(bf16[32,256]{1,0:T(8,128)(2,1)S(1)} %get-tuple-element.8), channel_id=1, source_target_pairs={{0,1},{1,0},{2,3},{3,2},{4,5},{5,4},{6,7},{7,6},{8,9},{9,8},{10,11... | collective-permute-start | bytes 49160 | tf_op jit(solution)/shard_map/ppermute | solution.py:297
  96.9 18.2 %collective-permute-start.10 = (bf16[2,32,256]{2,1,0:T(8,128)(2,1)S(1)}, bf16[2,32,256]{2,1,0:T(8,128)(2,1)S(1)}, u32[]{:S(2)}, u32[]{:S(2)}) collective-permute-start(bf16[2,32,256]{2,1,0:T(8,128)(2,1)S(1)} %pad_maximum_fusion.refs_0_), channel_id=1, source_target_pairs={{0,2},{1,3},{2,4},{3,5},{4,6},{5,7},{6,0},{7,1},{8,10},{9,11},{10,... | collective-permute-start | bytes 98312 | tf_op jit(solution)/shard_map/ppermute | solution.py:297
  102.7 14.6 %collective-permute-start.9 = (bf16[2,32,256]{2,1,0:T(8,128)(2,1)S(1)}, bf16[2,32,256]{2,1,0:T(8,128)(2,1)S(1)}, u32[]{:S(2)}, u32[]{:S(2)}) collective-permute-start(bf16[2,32,256]{2,1,0:T(8,128)(2,1)S(1)} %pad_maximum_fusion.refs_0_), channel_id=1, source_target_pairs={{0,4},{1,5},{2,6},{3,7},{4,0},{5,1},{6,2},{7,3},{8,12},{9,13},{10,... | collective-permute-start | bytes 98312 | tf_op jit(solution)/shard_map/ppermute | solution.py:297
  111.9 10.7 %collective-permute-start.8 = (bf16[2,32,256]{2,1,0:T(8,128)(2,1)S(1)}, bf16[2,32,256]{2,1,0:T(8,128)(2,1)S(1)}, u32[]{:S(2)}, u32[]{:S(2)}) collective-permute-start(bf16[2,32,256]{2,1,0:T(8,128)(2,1)S(1)} %pad_maximum_fusion.refs_0_), channel_id=1, source_target_pairs={{0,6},{1,7},{2,0},{3,1},{4,2},{5,3},{6,4},{7,5},{8,14},{9,15},{10,... | collective-permute-start | bytes 98312 | tf_op jit(solution)/shard_map/ppermute | solution.py:297
  123.4 21.4 %copy-start.2 = (bf16[64,32,128]{2,1,0:T(8,128)(2,1)S(1)}, bf16[64,32,128]{2,1,0:T(8,128)(2,1)}, u32[]{:S(2)}) copy-start(bf16[64,32,128]{2,1,0:T(8,128)(2,1)} %pair_ref.3) | copy-start | bytes 1572868
  123.4 21.4 %copy-start.5 = (bf16[1024,128]{1,0:T(8,128)(2,1)S(1)}, bf16[1024,128]{1,0:T(8,128)(2,1)}, u32[]{:S(2)}) copy-start(bf16[1024,128]{1,0:T(8,128)(2,1)} %wo_ref.3) | copy-start | bytes 786436
  123.4 21.3 %copy-start.8 = (bf16[128,512]{1,0:T(8,128)(2,1)S(1)}, bf16[128,512]{1,0:T(8,128)(2,1)}, u32[]{:S(2)}) copy-start(bf16[128,512]{1,0:T(8,128)(2,1)} %w_ref.5) | copy-start | bytes 393220
  144.8 1.3 copy-start
  167.5 55.0 %copy-start.10 = (bf16[128,128]{1,0:T(8,128)(2,1)S(1)}, bf16[128,128]{1,0:T(8,128)(2,1)}, u32[]{:S(2)}) copy-start(bf16[128,128]{1,0:T(8,128)(2,1)} %wg_ref.1) | copy-start | bytes 98308
  167.5 55.0 %copy-start.11 = (bf16[128,128]{1,0:T(8,128)(2,1)S(1)}, bf16[128,128]{1,0:T(8,128)(2,1)}, u32[]{:S(2)}) copy-start(bf16[128,128]{1,0:T(8,128)(2,1)} %w_ref.6) | copy-start | bytes 98308
  167.6 17.6 %collective-permute-start.16 = (bf16[512,128]{1,0:T(8,128)(2,1)S(1)}, bf16[512,128]{1,0:T(8,128)(2,1)S(1)}, u32[]{:S(2)}, u32[]{:S(2)}) collective-permute-start(bf16[512,128]{1,0:T(8,128)(2,1)S(1)} %get-tuple-element.12.refs_0_), channel_id=1, source_target_pairs={{0,2},{1,3},{2,4},{3,5},{4,6},{5,7},{6,0},{7,1},{8,10},{9,11},{10,... | collective-permute-start | bytes 393224 | tf_op jit(solution)/shard_map/ppermute | solution.py:297
  170.3 24.2 %collective-permute-start.14 = (bf16[512,128]{1,0:T(8,128)(2,1)S(1)}, bf16[512,128]{1,0:T(8,128)(2,1)S(1)}, u32[]{:S(2)}, u32[]{:S(2)}) collective-permute-start(bf16[512,128]{1,0:T(8,128)(2,1)S(1)} %get-tuple-element.12.refs_0_), channel_id=1, source_target_pairs={{0,4},{1,5},{2,6},{3,7},{4,0},{5,1},{6,2},{7,3},{8,12},{9,13},{10,... | collective-permute-start | bytes 393224 | tf_op jit(solution)/shard_map/ppermute | solution.py:297
  177.9 21.1 %collective-permute-start.12 = (bf16[512,128]{1,0:T(8,128)(2,1)S(1)}, bf16[512,128]{1,0:T(8,128)(2,1)S(1)}, u32[]{:S(2)}, u32[]{:S(2)}) collective-permute-start(bf16[512,128]{1,0:T(8,128)(2,1)S(1)} %get-tuple-element.12.refs_0_), channel_id=1, source_target_pairs={{0,6},{1,7},{2,0},{3,1},{4,2},{5,3},{6,4},{7,5},{8,14},{9,15},{10,... | collective-permute-start | bytes 393224 | tf_op jit(solution)/shard_map/ppermute | solution.py:297
  183.3 17.6 %collective-permute-start.11 = (bf16[512,128]{1,0:T(8,128)(2,1)S(1)}, bf16[512,128]{1,0:T(8,128)(2,1)S(1)}, u32[]{:S(2)}, u32[]{:S(2)}) collective-permute-start(bf16[512,128]{1,0:T(8,128)(2,1)S(1)} %get-tuple-element.12.refs_0_), channel_id=1, source_target_pairs={{0,1},{1,0},{2,3},{3,2},{4,5},{5,4},{6,7},{7,6},{8,9},{9,8},{10,11... | collective-permute-start | bytes 393224 | tf_op jit(solution)/shard_map/ppermute | solution.py:297
  185.2 15.7 %collective-permute-start.17 = (bf16[512,128]{1,0:T(8,128)(2,1)S(1)}, bf16[512,128]{1,0:T(8,128)(2,1)S(1)}, u32[]{:S(2)}, u32[]{:S(2)}) collective-permute-start(bf16[512,128]{1,0:T(8,128)(2,1)S(1)} %collective-permute-done.16.refs_6_), channel_id=1, source_target_pairs={{0,1},{1,0},{2,3},{3,2},{4,5},{5,4},{6,7},{7,6},{8,9},{9,8},{10,11... | collective-permute-start | bytes 393224 | tf_op jit(solution)/shard_map/ppermute | solution.py:297
  194.4 6.5 %collective-permute-start.15 = (bf16[512,128]{1,0:T(8,128)(2,1)S(1)}, bf16[512,128]{1,0:T(8,128)(2,1)S(1)}, u32[]{:S(2)}, u32[]{:S(2)}) collective-permute-start(bf16[512,128]{1,0:T(8,128)(2,1)S(1)} %collective-permute-done.14.refs_4_), channel_id=1, source_target_pairs={{0,1},{1,0},{2,3},{3,2},{4,5},{5,4},{6,7},{7,6},{8,9},{9,8},{10,11... | collective-permute-start | bytes 393224 | tf_op jit(solution)/shard_map/ppermute | solution.py:297
  199.0 3.2 %collective-permute-start.13 = (bf16[512,128]{1,0:T(8,128)(2,1)S(1)}, bf16[512,128]{1,0:T(8,128)(2,1)S(1)}, u32[]{:S(2)}, u32[]{:S(2)}) collective-permute-start(bf16[512,128]{1,0:T(8,128)(2,1)S(1)} %collective-permute-done.12.refs_2_), channel_id=1, source_target_pairs={{0,1},{1,0},{2,3},{3,2},{4,5},{5,4},{6,7},{7,6},{8,9},{9,8},{10,11... | collective-permute-start | bytes 393224 | tf_op jit(solution)/shard_map/ppermute | solution.py:297
  224.9 10.4 %all-to-all-start.6 = ((bf16[4,4,32,128]{3,2,1,0:T(8,128)(2,1)}), bf16[4,4,32,128]{3,2,1,0:T(8,128)(2,1)S(1)}, u32[]{:S(2)}, u32[]{:S(2)}) async-start(bf16[4,4,32,128]{3,2,1,0:T(8,128)(2,1)} %shard_map.137), calls=%async_computation.6 | async-start | bytes 262144 | tf_op jit(solution)/shard_map/all_to_all | solution.py:327
  235.3 0.6 copy-start.12

commit v3 on v2

--- a/solution.py
+++ b/solution.py
@@ -56,6 +56,18 @@
     return results if len(outs) > 1 else results[0]
 
 
+def col_of(place):
+    return place[0] & 7
+
+
+def half_of(place):
+    return (place[0] >> 3) & 1
+
+
+def branch_of(place):
+    return place[0] >> 7
+
+
 def source_of(col, m):
     return (((col >> 1) + (m >> 1)) & 3) * 2 + ((col & 1) ^ (m & 1))
 
@@ -67,7 +79,7 @@
     weight = w_ref[...]
     for j in range(16):
         pairs = jnp.concatenate([rows[:, j, :], rows[:, j + 16, :]], axis=0).astype(BF)
-        heads[j] = mm(weight, pairs, TT)
+        heads[j] = mm(weight, pairs, NT)
     lane = lax.broadcasted_iota(jnp.int32, (16, 128), 1) < 64
     tiles = []
     for p in range(4):
@@ -82,11 +94,20 @@
 
 
 def row_kernel(place, *refs):
-    blocks = refs[:8]
-    w_ref, bias_ref, wo_ref, out_ref, rows, keys, values, packed = refs[8:]
-    for m in range(8):
-        start = pl.multiple_of(source_of(place[0], m) * 64, 64)
-        normed = layer_norm(blocks[m][...].reshape(256, 256)).astype(BF)
+    own_ref, z1_ref, z3_ref, z2_ref, swap_ref, last_ref = refs[:6]
+    w_ref, bias_ref, wo_ref, out_ref, rows, keys, values, packed = refs[6:]
+    for m, block in (
+        (0, own_ref[...]),
+        (2, z1_ref[...]),
+        (6, z3_ref[...]),
+        (1, swap_ref[0]),
+        (3, swap_ref[1]),
+        (7, swap_ref[2]),
+        (4, z2_ref[...]),
+        (5, last_ref[...]),
+    ):
+        start = pl.multiple_of(source_of(col_of(place), m) * 64, 64)
+        normed = layer_norm(block.reshape(256, 256)).astype(BF)
         if m == 0:
             own = normed
         for s in range(4):
@@ -118,7 +139,7 @@
             parts.append(jnp.where(upper, mixed[:, :64], mixed[:, 64:]))
         attended_t = jnp.concatenate(parts, axis=0)
         gated = (gate_t[:, s * 64 : (s + 1) * 64] * attended_t).astype(BF)
-        result = blocks[0][s].astype(F32) + mm(gated, wo_ref[...], TN)
+        result = own_ref[s].astype(F32) + mm(gated, wo_ref[...], TN)
         for h in range(2):
             for b in range(4):
                 source = (h * 4 + b) * 8
@@ -154,10 +175,10 @@
         parts.append(mixed * scale)
     gated = (gate_t * jnp.concatenate(parts, axis=0)).astype(BF)
     result = (x + mm(gated, wo_ref[...], TN)).astype(BF)
-    factors = mm(wf_ref[...], layer_norm(result).astype(BF), TT).astype(BF)
-    for b in range(4):
-        left_ref[b] = factors[:32]
-    right_ref[...] = factors[32:]
+    factors = mm(wf_ref[...], layer_norm(result).astype(BF), NT).astype(BF)
+    left_ref[...] = factors[:32]
+    for c in range(8):
+        right_ref[c] = factors[32:]
     wide = result.astype(F32)
     for s in range(4):
         for half in range(2):
@@ -167,16 +188,15 @@
     out_ref[...] = scratch[...].astype(BF)
 
 
-def spread_kernel(place, left_ref, *refs):
-    rights, out_ref = refs[:4], refs[4]
-    left = left_ref[...].reshape(128, 256)
+def spread_kernel(place, right_ref, *refs):
+    lefts, out_ref = refs[:4], refs[4]
+    blocks = [left[...] for left in lefts]
+    for mask in range(4):
+        start = pl.multiple_of((branch_of(place) ^ mask) * 32, 32)
+        for r in range(16):
+            out_ref[r, pl.ds(start, 32), :] = blocks[mask]
     for r in range(16):
-        out_ref[r, :128] = left
-    for m in range(8):
-        target = source_of(place[0], m) * 2
-        block = rights[m // 2][m % 2]
-        out_ref[target, 128:] = block
-        out_ref[target + 1, 128:] = block
+        out_ref[r, 128:] = right_ref[r // 2]
 
 
 def block_transpose(arrays):
@@ -206,7 +226,7 @@
 
 def pair_kernel(place, factor_ref, pair_ref, wo_ref, w_ref, mid_ref, out_ref,
                 outer, flat, scratch, tile_rows):
-    right = factor_ref[pl.ds(place[1] * 8, 8), 128:, :].reshape(256, 256)
+    right = factor_ref[pl.ds(half_of(place) * 8, 8), 128:, :].reshape(256, 256)
     for b in range(4):
         left = factor_ref[:, b * 32 : (b + 1) * 32, :].reshape(512, 256)
         product = (mm(left, right, NT) * (1.0 / 256)).reshape(16, 32, 256)
@@ -221,7 +241,7 @@
                 j = tile * 4 + k
                 flat[j * 64 : (j + 1) * 64, group * 128 : (group + 1) * 128] = moved[k].astype(BF)
     update = jnp.dot(flat[...], wo_ref[...], preferred_element_type=F32).astype(BF)
-    first = pl.multiple_of(place[2] * 8, 8)
+    first = pl.multiple_of(branch_of(place) * 8, 8)
     tile_rows[...] = pair_ref[:, pl.ds(first, 8), :].astype(F32)
     pair = jnp.concatenate([tile_rows[:, j, :] for j in range(8)], axis=0)
     mid = (pair + update.astype(F32)).astype(BF)
@@ -250,7 +270,7 @@
     for m in range(8):
         product = mm(rights[m][...], left, TN)
         block = jnp.where(lane, product[:64], product[64:]).astype(BF)
-        target = source_of(place[0], m) * 2
+        target = source_of(col_of(place), m) * 2
         for b in range(4):
             for h in range(2):
                 out_ref[b * 16 + target + h, 0] = block[(b * 2 + h) * 8 : (b * 2 + h + 1) * 8]
@@ -321,19 +341,21 @@
     w_triangle_out,
 ):
     both = ("branch", "row")
-    place = jnp.stack(
-        [lax.axis_index("col"), lax.axis_index("row") & 1, lax.axis_index("branch")]
-    ).astype(jnp.int32)
+    place = lax.axis_index(("branch", "row", "col")).astype(jnp.int32).reshape(1)
     exchange = lambda x, axis: lax.all_to_all(x, axis, 0, 0, tiled=True)
 
-    blocks = gather_col(alignment)
+    blocks = [alignment]
+    for step in (1, 3, 2):
+        blocks.append(shifted(alignment, step, 0))
+    blocks.append(shifted(jnp.stack(blocks[:3]), 0, 1))
+    blocks.append(shifted(blocks[3], 0, 1))
     bias = in_vmem(
         bias_kernel,
         [(16, 32, 512)],
         [pltpu.VMEM((64, 32, 128), F32), pltpu.VMEM((16, 8, 128), F32)],
         place,
         pair_features,
-        w_bias,
+        w_bias.T,
     )
     bias = exchange(bias, "row").reshape(512, 512)
 
@@ -355,21 +377,20 @@
     columns = exchange(columns, both)
     returning, left, right = in_vmem(
         column_kernel,
-        [(64, 8, 128), (4, 32, 256), (32, 256)],
+        [(64, 8, 128), (32, 256), (8, 32, 256)],
         [pltpu.VMEM((64, 8, 128), F32)],
         place,
         columns,
         w_column,
         column_output_weight,
-        outer_input_weight,
-    )
-
-    right = jnp.stack([right, shifted(right, 0, 1)])
-    rights = [right]
-    for step in (1, 2, 3):
-        rights.append(shifted(right, step, 0))
-    left = exchange(left, "branch")
-    factors = in_vmem(spread_kernel, [(16, 160, 256)], [], place, left, *rights)
+        outer_input_weight.T,
+    )
+
+    right = exchange(right, "col")
+    lefts = [left]
+    for mask in (1, 2, 3):
+        lefts.append(lax.ppermute(left, "branch", [(b, b ^ mask) for b in range(4)]))
+    factors = in_vmem(spread_kernel, [(16, 160, 256)], [], place, right, *lefts)
     factors = exchange(factors, "row")
 
     mid, message = in_vmem(
@@ -404,8 +425,11 @@
     )
     parts = exchange(parts, "branch")
     pair_out = pl.pallas_call(
-        unpack_kernel, out_shape=jax.ShapeDtypeStruct((32, 32, 64), BF), name="unpack"
-    )(parts)
+        unpack_kernel,
+        out_shape=jax.ShapeDtypeStruct((32, 32, 64), BF),
+        in_specs=[VM],
+        name="unpack",
+    )(pltpu.with_memory_space_constraint(parts, pltpu.VMEM))
     back = sums[:, 1].reshape(4, 2, 8, 2, 4, 128)
     alignment_out = jnp.transpose(back, (4, 1, 0, 2, 3, 5)).reshape(4, 64, 256)
     return (alignment_out, jnp.transpose(pair_out, (2, 0, 1)))

time: 239 us -> 227 us (0.950)
  blocking collectives: 58.2 us -> 86.6 us
  starting transfers between devices: 107 us -> 82.7 us
  waiting for transfers between devices: 39 us -> 31.4 us
  Pallas kernels: 26.8 us -> 20.5 us
    all_to_all x3 -> x4, blocking collectives: 58.2 us -> 86.6 us  [local(): exchange = lambda x, axis: lax.all_to_all(x, axis, 0, 0, tiled=True)]
    ppermute x18 -> x12, starting transfers between devices: 76.6 us -> 53 us  [shifted(): return lax.ppermute(x, 'col', perm)]
    all_to_all x4 -> x3, starting transfers between devices: 30.7 us -> 19.8 us  [local(): exchange = lambda x, axis: lax.all_to_all(x, axis, 0, 0, tiled=True)]
    ppermute x0 -> x3, starting transfers between devices: none -> 9.86 us  [local(): lax.ppermute(left, 'branch', [(b, b ^ mask) for b in range(4)])]
    all_to_all x4 -> x3, waiting for transfers between devices: 14 us -> 6.4 us  [local(): exchange = lambda x, axis: lax.all_to_all(x, axis, 0, 0, tiled=True)]
    pallas_call x7, Pallas kernels: 25.1 us -> 19.6 us  [in_vmem(): pl.pallas_call(kernel, out_shape=outs, in_specs=[SM] + [VM] * len(args),...]
    ppermute x0 -> x3, waiting for transfers between devices: none -> 3.7 us  [local(): lax.ppermute(left, 'branch', [(b, b ^ mask) for b in range(4)])]
    ppermute x18 -> x12, waiting for transfers between devices: 25 us -> 21.3 us  [shifted(): return lax.ppermute(x, 'col', perm)]
  transfers between devices with their start and end apart: 22 -> 18, of which waited for: 11 -> 10; matrix products, arithmetic and copies ran while one was open for 0% -> 0% of each run, Pallas kernels for 0% -> 1%
where the time goes in v3:
time: 227 us; the launch traced here: 226 us
  blocking collectives  86.6 us (38%)
  starting transfers between devices  82.7 us (36%)
  waiting for transfers between devices  31.4 us (14%)
  Pallas kernels  20.5 us (9%)
  local copies, waits for them, and re-layouts  3.79 us (2%)
    all_to_all x4, blocking collectives, local(): exchange = lambda x, axis: lax.all_to_all(x, axis, 0, 0, tiled=True)  86.6 us
    ppermute x12, starting transfers between devices, shifted(): return lax.ppermute(x, 'col', perm)  53 us
    ppermute x12, waiting for transfers between devices, shifted(): return lax.ppermute(x, 'col', perm)  21.3 us
    all_to_all x3, starting transfers between devices, local(): exchange = lambda x, axis: lax.all_to_all(x, axis, 0, 0, tiled=True)  19.8 us
    pallas_call x7, Pallas kernels, in_vmem(): pl.pallas_call(kernel, out_shape=outs, in_specs=[SM] + [VM] * len(args),...  19.6 us
    ppermute x3, starting transfers between devices, local(): lax.ppermute(left, 'branch', [(b, b ^ mask) for b in range(4)])  9.86 us
    all_to_all x3, waiting for transfers between devices, local(): exchange = lambda x, axis: lax.all_to_all(x, axis, 0, 0, tiled=True)  6.4 us
  transfers between devices with their start and end apart: 18, of which 10 were waited for; matrix products, arithmetic and copies ran while one was open for 0% of the time, Pallas kernels for 1%

profile of v3, /device:TPU:32, one launch (start us, length us, event | category | flops | bytes accessed | tf_op | source)
XLA Modules:
  0.0 225.9 jit_solution(11562236410369497868)
XLA Ops:
  0.6 9.1 %collective-permute-start.1 = (bf16[4,64,256]{2,1,0:T(8,128)(2,1)}, bf16[4,64,256]{2,1,0:T(8,128)(2,1)S(1)}, u32[]{:S(2)}, u32[]{:S(2)}) collective-permute-start(bf16[4,64,256]{2,1,0:T(8,128)(2,1)} %refs_0_.1), channel_id=1, source_target_pairs={{0,2},{1,3},{2,4},{3,5},{4,6},{5,7},{6,0},{7,1},{8,10},{9,11},{10,... | collective-permute-start | bytes 393224 | tf_op jit(solution)/shard_map/ppermute | solution.py:317
  9.7 4.7 %collective-permute-start = (bf16[4,64,256]{2,1,0:T(8,128)(2,1)}, bf16[4,64,256]{2,1,0:T(8,128)(2,1)S(1)}, u32[]{:S(2)}, u32[]{:S(2)}) collective-permute-start(bf16[4,64,256]{2,1,0:T(8,128)(2,1)} %refs_0_.1), channel_id=1, source_target_pairs={{0,6},{1,7},{2,0},{3,1},{4,2},{5,3},{6,4},{7,5},{8,14},{9,15},{10,... | collective-permute-start | bytes 393224 | tf_op jit(solution)/shard_map/ppermute | solution.py:317
  14.4 0.0 copy-start.1
  14.4 1.0 copy-done.1
  15.5 0.7 copy-done.13
  16.1 2.2 shard_map.131
  18.4 7.0 %all-to-all-start = ((bf16[16,32,512]{2,1,0:T(8,128)(2,1)}), bf16[16,32,512]{2,1,0:T(8,128)(2,1)S(1)}, u32[]{:S(2)}, u32[]{:S(2)}) async-start(bf16[16,32,512]{2,1,0:T(8,128)(2,1)} %shard_map.131), calls=%async_computation | async-start | bytes 1048576 | tf_op jit(solution)/shard_map/all_to_all | solution.py:345
  25.4 2.7 %collective-permute-done.refs_1_ = bf16[4,64,256]{2,1,0:T(8,128)(2,1)S(1)} collective-permute-done((bf16[4,64,256]{2,1,0:T(8,128)(2,1)}, bf16[4,64,256]{2,1,0:T(8,128)(2,1)S(1)}, u32[]{:S(2)}, u32[]{:S(2)}) %collective-permute-start) | collective-permute-done | bytes 131104 | tf_op jit(solution)/shard_map/ppermute | solution.py:317
  28.2 1.9 collective-permute-start.3
  30.1 9.2 %collective-permute-start.2 = (bf16[4,64,256]{2,1,0:T(8,128)(2,1)S(1)}, bf16[4,64,256]{2,1,0:T(8,128)(2,1)S(1)}, u32[]{:S(2)}, u32[]{:S(2)}) collective-permute-start(bf16[4,64,256]{2,1,0:T(8,128)(2,1)S(1)} %copy-done.5), channel_id=1, source_target_pairs={{0,4},{1,5},{2,6},{3,7},{4,0},{5,1},{6,2},{7,3},{8,12},{9,13},{10,... | collective-permute-start | bytes 393224 | tf_op jit(solution)/shard_map/ppermute | solution.py:317
  39.3 8.5 %collective-permute-done.2.refs_3_ = bf16[4,64,256]{2,1,0:T(8,128)(2,1)S(1)} collective-permute-done((bf16[4,64,256]{2,1,0:T(8,128)(2,1)S(1)}, bf16[4,64,256]{2,1,0:T(8,128)(2,1)S(1)}, u32[]{:S(2)}, u32[]{:S(2)}) %collective-permute-start.2) | collective-permute-done | bytes 131104 | tf_op jit(solution)/shard_map/ppermute | solution.py:317
  47.9 1.9 collective-permute-start.4
  49.8 1.3 collective-permute-done.4.refs_5_
  51.1 0.0 copy-start.10
  51.2 7.9 %shard_map.132 = bf16[64,8,128]{2,1,0:T(8,128)(2,1)S(1)} custom-call(s32[1]{0:T(128)} %bitcast.place, bf16[4,64,256]{2,1,0:T(8,128)(2,1)S(1)} %copy-done.5, bf16[4,64,256]{2,1,0:T(8,128)(2,1)S(1)} %collective-permute-done.refs_1_, bf16[4,64,256]{2,1,0:T(8,128)(2,1)S(1)} %collective-permute-done.1.refs_2_, ...), custom_call_target="tpu_custom_call" | custom-call | tf_op jit(solution)/shard_map/pallas_call | solution.py:49
  59.1 26.7 %all_to_all.35.x_ref = bf16[64,8,128]{2,1,0:T(8,128)(2,1)S(1)} all-to-all(bf16[64,8,128]{2,1,0:T(8,128)(2,1)S(1)} %shard_map.132), channel_id=1, replica_groups=mesh['branch'=4,'row'=16,'col'=8] {'branch','row'}, dimensions={0} | all-to-all | bytes 262144 | tf_op jit(solution)/shard_map/all_to_all | solution.py:345
  85.8 4.0 %shard_map.133 = (bf16[64,8,128]{2,1,0:T(8,128)(2,1)S(1)}, bf16[32,256]{1,0:T(8,128)(2,1)S(1)}, bf16[8,32,256]{2,1,0:T(8,128)(2,1)}) custom-call(s32[1]{0:T(128)} %bitcast.place, bf16[64,8,128]{2,1,0:T(8,128)(2,1)S(1)} %all_to_all.35.x_ref, bf16[256,1024]{1,0:T(8,128)(2,1)S(1)} %copy-done.4, bf16[256,256]{1,0:T(8,128)(2,1)S(1)} %copy-done.9, ...), custom_call_target="tpu_custom_call" | custom-call | tf_op jit(solution)/shard_map/pallas_call | solution.py:49
  89.8 7.6 %all-to-all-start.2 = ((bf16[8,32,256]{2,1,0:T(8,128)(2,1)}), bf16[8,32,256]{2,1,0:T(8,128)(2,1)S(1)}, u32[]{:S(2)}, u32[]{:S(2)}) async-start(bf16[8,32,256]{2,1,0:T(8,128)(2,1)} %get-tuple-element.7), calls=%async_computation.2 | async-start | bytes 262144 | tf_op jit(solution)/shard_map/all_to_all | solution.py:345
  97.4 2.3 %collective-permute-start.7 = (bf16[32,256]{1,0:T(8,128)(2,1)S(1)}, bf16[32,256]{1,0:T(8,128)(2,1)S(1)}, u32[]{:S(2)}, u32[]{:S(2)}) collective-permute-start(bf16[32,256]{1,0:T(8,128)(2,1)S(1)} %get-tuple-element.8.refs_0_), channel_id=1, source_target_pairs={{0,384},{128,256},{256,128},{384,0},{1,385},{129,257},{257,129},{3... | collective-permute-start | bytes 49160 | tf_op jit(solution)/shard_map/ppermute | solution.py:392
  99.7 5.6 %collective-permute-start.6 = (bf16[32,256]{1,0:T(8,128)(2,1)S(1)}, bf16[32,256]{1,0:T(8,128)(2,1)S(1)}, u32[]{:S(2)}, u32[]{:S(2)}) collective-permute-start(bf16[32,256]{1,0:T(8,128)(2,1)S(1)} %get-tuple-element.8.refs_0_), channel_id=1, source_target_pairs={{0,256},{128,384},{256,0},{384,128},{1,257},{129,385},{257,1},{385... | collective-permute-start | bytes 49160 | tf_op jit(solution)/shard_map/ppermute | solution.py:392
  105.4 1.9 collective-permute-start.5
  107.3 1.7 collective-permute-done.6.refs_2_
  109.0 2.0 collective-permute-done.5.refs_1_
  111.0 1.9 all-to-all-done.2.right_ref
  112.9 0.1 shard_map.134
  113.0 0.0 copy-start.6
  113.1 0.0 copy-start.8
  113.1 23.5 %all_to_all.36.factor_ref = bf16[16,160,256]{2,1,0:T(8,128)(2,1)} all-to-all(bf16[16,160,256]{2,1,0:T(8,128)(2,1)S(1)} %shard_map.134), channel_id=1, replica_groups=mesh['branch'=4,'row'=16,'col'=8] {'row'}, dimensions={0} | all-to-all | bytes 2621440 | tf_op jit(solution)/shard_map/all_to_all | solution.py:345
  136.6 1.3 copy-done
  137.9 3.1 %shard_map.135 = (bf16[512,128]{1,0:T(8,128)(2,1)S(1)}, bf16[64,2,8,128]{3,2,1,0:T(8,128)(2,1)S(1)}) custom-call(s32[1]{0:T(128)} %bitcast.place, bf16[16,160,256]{2,1,0:T(8,128)(2,1)S(1)} %copy-done, bf16[64,32,128]{2,1,0:T(8,128)(2,1)S(1)} %copy-done.2, bf16[1024,128]{1,0:T(8,128)(2,1)S(1)} %copy-done.6, bf16[128,512]{1,0:T(8,128)(2,1)S(1)} %copy-done.8), custom_call_target="tpu_custom_call" | custom-call | tf_op jit(solution)/shard_map/pallas_call | solution.py:49
  141.0 16.8 %all_to_all.37 = bf16[64,2,8,128]{3,2,1,0:T(8,128)(2,1)S(1)} all-to-all(bf16[64,2,8,128]{3,2,1,0:T(8,128)(2,1)S(1)} %get-tuple-element.9), channel_id=1, replica_groups=mesh['branch'=4,'row'=16,'col'=8] {'branch','row'}, dimensions={0} | all-to-all | bytes 524288 | tf_op jit(solution)/shard_map/all_to_all | solution.py:345
  157.8 3.8 %collective-permute-start.13 = (bf16[512,128]{1,0:T(8,128)(2,1)S(1)}, bf16[512,128]{1,0:T(8,128)(2,1)S(1)}, u32[]{:S(2)}, u32[]{:S(2)}) collective-permute-start(bf16[512,128]{1,0:T(8,128)(2,1)S(1)} %get-tuple-element.12.refs_0_), channel_id=1, source_target_pairs={{0,2},{1,3},{2,4},{3,5},{4,6},{5,7},{6,0},{7,1},{8,10},{9,11},{10,... | collective-permute-start | bytes 393224 | tf_op jit(solution)/shard_map/ppermute | solution.py:317
  161.5 7.6 %collective-permute-start.11 = (bf16[512,128]{1,0:T(8,128)(2,1)S(1)}, bf16[512,128]{1,0:T(8,128)(2,1)S(1)}, u32[]{:S(2)}, u32[]{:S(2)}) collective-permute-start(bf16[512,128]{1,0:T(8,128)(2,1)S(1)} %get-tuple-element.12.refs_0_), channel_id=1, source_target_pairs={{0,4},{1,5},{2,6},{3,7},{4,0},{5,1},{6,2},{7,3},{8,12},{9,13},{10,... | collective-permute-start | bytes 393224 | tf_op jit(solution)/shard_map/ppermute | solution.py:317
  169.1 6.8 %collective-permute-start.9 = (bf16[512,128]{1,0:T(8,128)(2,1)S(1)}, bf16[512,128]{1,0:T(8,128)(2,1)S(1)}, u32[]{:S(2)}, u32[]{:S(2)}) collective-permute-start(bf16[512,128]{1,0:T(8,128)(2,1)S(1)} %get-tuple-element.12.refs_0_), channel_id=1, source_target_pairs={{0,6},{1,7},{2,0},{3,1},{4,2},{5,3},{6,4},{7,5},{8,14},{9,15},{10,... | collective-permute-start | bytes 393224 | tf_op jit(solution)/shard_map/ppermute | solution.py:317
  175.8 1.9 collective-permute-start.8
  177.8 2.4 %collective-permute-start.14 = (bf16[512,128]{1,0:T(8,128)(2,1)S(1)}, bf16[512,128]{1,0:T(8,128)(2,1)S(1)}, u32[]{:S(2)}, u32[]{:S(2)}) collective-permute-start(bf16[512,128]{1,0:T(8,128)(2,1)S(1)} %collective-permute-done.13.refs_6_), channel_id=1, source_target_pairs={{0,1},{1,0},{2,3},{3,2},{4,5},{5,4},{6,7},{7,6},{8,9},{9,8},{10,11... | collective-permute-start | bytes 393224 | tf_op jit(solution)/shard_map/ppermute | solution.py:317
  180.2 6.1 %collective-permute-done.11.refs_4_ = bf16[512,128]{1,0:T(8,128)(2,1)S(1)} collective-permute-done((bf16[512,128]{1,0:T(8,128)(2,1)S(1)}, bf16[512,128]{1,0:T(8,128)(2,1)S(1)}, u32[]{:S(2)}, u32[]{:S(2)}) %collective-permute-start.11) | collective-permute-done | bytes 131104 | tf_op jit(solution)/shard_map/ppermute | solution.py:317
  186.3 1.9 collective-permute-start.12
  188.2 1.4 collective-permute-done.9.refs_2_
  189.6 1.9 collective-permute-start.10
  191.5 1.3 collective-permute-done.10.refs_3_
  192.8 0.5 shard_map.136
  193.3 19.6 %all_to_all.38.sum_ref = bf16[64,2,8,128]{3,2,1,0:T(8,128)(2,1)S(1)} all-to-all(bf16[64,2,8,128]{3,2,1,0:T(8,128)(2,1)S(1)} %shard_map.136), channel_id=1, replica_groups=mesh['branch'=4,'row'=16,'col'=8] {'branch','row'}, dimensions={0} | all-to-all | bytes 524288 | tf_op jit(solution)/shard_map/all_to_all | solution.py:345
  212.9 1.7 shard_map.137
  214.7 5.2 %all-to-all-start.6 = ((bf16[4,4,32,128]{3,2,1,0:T(8,128)(2,1)}), bf16[4,4,32,128]{3,2,1,0:T(8,128)(2,1)S(1)}, u32[]{:S(2)}, u32[]{:S(2)}) async-start(bf16[4,4,32,128]{3,2,1,0:T(8,128)(2,1)} %shard_map.137), calls=%async_computation.6 | async-start | bytes 262144 | tf_op jit(solution)/shard_map/all_to_all | solution.py:345
  219.9 0.7 copy.14
  220.5 4.5 %all-to-all-done.6.x_ref = bf16[4,4,32,128]{3,2,1,0:T(8,128)(2,1)S(1)} async-done(((bf16[4,4,32,128]{3,2,1,0:T(8,128)(2,1)}), bf16[4,4,32,128]{3,2,1,0:T(8,128)(2,1)S(1)}, u32[]{:S(2)}, u32[]{:S(2)}) %all-to-all-start.6) | async-done | bytes 131104 | tf_op jit(solution)/shard_map/all_to_all | solution.py:345
  225.0 0.8 unpack.1
  (32 shorter events, 0.1 us)
Async XLA Ops:
  0.6 24.8 %collective-permute-start.1 = (bf16[4,64,256]{2,1,0:T(8,128)(2,1)}, bf16[4,64,256]{2,1,0:T(8,128)(2,1)S(1)}, u32[]{:S(2)}, u32[]{:S(2)}) collective-permute-start(bf16[4,64,256]{2,1,0:T(8,128)(2,1)} %refs_0_.1), channel_id=1, source_target_pairs={{0,2},{1,3},{2,4},{3,5},{4,6},{5,7},{6,0},{7,1},{8,10},{9,11},{10,... | collective-permute-start | bytes 393224 | tf_op jit(solution)/shard_map/ppermute | solution.py:317
  9.7 18.4 %collective-permute-start = (bf16[4,64,256]{2,1,0:T(8,128)(2,1)}, bf16[4,64,256]{2,1,0:T(8,128)(2,1)S(1)}, u32[]{:S(2)}, u32[]{:S(2)}) collective-permute-start(bf16[4,64,256]{2,1,0:T(8,128)(2,1)} %refs_0_.1), channel_id=1, source_target_pairs={{0,6},{1,7},{2,0},{3,1},{4,2},{5,3},{6,4},{7,5},{8,14},{9,15},{10,... | collective-permute-start | bytes 393224 | tf_op jit(solution)/shard_map/ppermute | solution.py:317
  14.4 1.0 copy-start.1
  15.5 0.7 copy-start.13
  16.1 12.0 %copy-start.5 = (bf16[4,64,256]{2,1,0:T(8,128)(2,1)S(1)}, bf16[4,64,256]{2,1,0:T(8,128)(2,1)}, u32[]{:S(2)}) copy-start(bf16[4,64,256]{2,1,0:T(8,128)(2,1)} %refs_0_.1) | copy-start | bytes 393220
  16.1 35.0 %copy-start.3 = (bf16[256,1024]{1,0:T(8,128)(2,1)S(1)}, bf16[256,1024]{1,0:T(8,128)(2,1)}, u32[]{:S(2)}) copy-start(bf16[256,1024]{1,0:T(8,128)(2,1)} %refs_6_.1) | copy-start | bytes 1572868
  16.1 35.0 %copy-start.7 = (bf16[256,256]{1,0:T(8,128)(2,1)S(1)}, bf16[256,256]{1,0:T(8,128)(2,1)}, u32[]{:S(2)}) copy-start(bf16[256,256]{1,0:T(8,128)(2,1)} %refs_8_.1) | copy-start | bytes 393220
  18.4 32.7 %all-to-all-start = ((bf16[16,32,512]{2,1,0:T(8,128)(2,1)}), bf16[16,32,512]{2,1,0:T(8,128)(2,1)S(1)}, u32[]{:S(2)}, u32[]{:S(2)}) async-start(bf16[16,32,512]{2,1,0:T(8,128)(2,1)} %shard_map.131), calls=%async_computation | async-start | bytes 1048576 | tf_op jit(solution)/shard_map/all_to_all | solution.py:345
  28.2 22.9 %collective-permute-start.3 = (bf16[3,4,64,256]{3,2,1,0:T(8,128)(2,1)S(1)}, bf16[3,4,64,256]{3,2,1,0:T(8,128)(2,1)S(1)}, u32[]{:S(2)}, u32[]{:S(2)}) collective-permute-start(bf16[3,4,64,256]{3,2,1,0:T(8,128)(2,1)S(1)} %pad_maximum_fusion), channel_id=1, source_target_pairs={{0,1},{1,0},{2,3},{3,2},{4,5},{5,4},{6,7},{7,6},{8,9},{9,8},{10,11... | collective-permute-start | bytes 1179656 | tf_op jit(solution)/shard_map/ppermute | solution.py:317
  30.1 17.8 %collective-permute-start.2 = (bf16[4,64,256]{2,1,0:T(8,128)(2,1)S(1)}, bf16[4,64,256]{2,1,0:T(8,128)(2,1)S(1)}, u32[]{:S(2)}, u32[]{:S(2)}) collective-permute-start(bf16[4,64,256]{2,1,0:T(8,128)(2,1)S(1)} %copy-done.5), channel_id=1, source_target_pairs={{0,4},{1,5},{2,6},{3,7},{4,0},{5,1},{6,2},{7,3},{8,12},{9,13},{10,... | collective-permute-start | bytes 393224 | tf_op jit(solution)/shard_map/ppermute | solution.py:317
  47.9 3.2 %collective-permute-start.4 = (bf16[4,64,256]{2,1,0:T(8,128)(2,1)S(1)}, bf16[4,64,256]{2,1,0:T(8,128)(2,1)S(1)}, u32[]{:S(2)}, u32[]{:S(2)}) collective-permute-start(bf16[4,64,256]{2,1,0:T(8,128)(2,1)S(1)} %collective-permute-done.2.refs_3_), channel_id=1, source_target_pairs={{0,1},{1,0},{2,3},{3,2},{4,5},{5,4},{6,7},{7,6},{8,9},{9,8},{10,11... | collective-permute-start | bytes 393224 | tf_op jit(solution)/shard_map/ppermute | solution.py:317
  51.1 34.7 %copy-start.4 = (bf16[256,1024]{1,0:T(8,128)(2,1)S(1)}, bf16[256,1024]{1,0:T(8,128)(2,1)}, u32[]{:S(2)}) copy-start(bf16[256,1024]{1,0:T(8,128)(2,1)} %w_ref.3) | copy-start | bytes 1572868
  51.1 34.7 %copy-start.9 = (bf16[256,256]{1,0:T(8,128)(2,1)S(1)}, bf16[256,256]{1,0:T(8,128)(2,1)}, u32[]{:S(2)}) copy-start(bf16[256,256]{1,0:T(8,128)(2,1)} %wo_ref.2) | copy-start | bytes 393220
  51.1 34.7 %copy-start.10 = (bf16[256,64]{0,1:T(8,128)(2,1)S(1)}, bf16[256,64]{0,1:T(8,128)(2,1)}, u32[]{:S(2)}) copy-start(bf16[256,64]{0,1:T(8,128)(2,1)} %param.19) | copy-start | bytes 98308
  89.8 23.1 %all-to-all-start.2 = ((bf16[8,32,256]{2,1,0:T(8,128)(2,1)}), bf16[8,32,256]{2,1,0:T(8,128)(2,1)S(1)}, u32[]{:S(2)}, u32[]{:S(2)}) async-start(bf16[8,32,256]{2,1,0:T(8,128)(2,1)} %get-tuple-element.7), calls=%async_computation.2 | async-start | bytes 262144 | tf_op jit(solution)/shard_map/all_to_all | solution.py:345
  97.4 9.9 %collective-permute-start.7 = (bf16[32,256]{1,0:T(8,128)(2,1)S(1)}, bf16[32,256]{1,0:T(8,128)(2,1)S(1)}, u32[]{:S(2)}, u32[]{:S(2)}) collective-permute-start(bf16[32,256]{1,0:T(8,128)(2,1)S(1)} %get-tuple-element.8.refs_0_), channel_id=1, source_target_pairs={{0,384},{128,256},{256,128},{384,0},{1,385},{129,257},{257,129},{3... | collective-permute-start | bytes 49160 | tf_op jit(solution)/shard_map/ppermute | solution.py:392
  99.7 9.2 %collective-permute-start.6 = (bf16[32,256]{1,0:T(8,128)(2,1)S(1)}, bf16[32,256]{1,0:T(8,128)(2,1)S(1)}, u32[]{:S(2)}, u32[]{:S(2)}) collective-permute-start(bf16[32,256]{1,0:T(8,128)(2,1)S(1)} %get-tuple-element.8.refs_0_), channel_id=1, source_target_pairs={{0,256},{128,384},{256,0},{384,128},{1,257},{129,385},{257,1},{385... | collective-permute-start | bytes 49160 | tf_op jit(solution)/shard_map/ppermute | solution.py:392
  105.4 5.6 %collective-permute-start.5 = (bf16[32,256]{1,0:T(8,128)(2,1)S(1)}, bf16[32,256]{1,0:T(8,128)(2,1)S(1)}, u32[]{:S(2)}, u32[]{:S(2)}) collective-permute-start(bf16[32,256]{1,0:T(8,128)(2,1)S(1)} %get-tuple-element.8.refs_0_), channel_id=1, source_target_pairs={{0,128},{128,0},{256,384},{384,256},{1,129},{129,1},{257,385},{385... | collective-permute-start | bytes 49160 | tf_op jit(solution)/shard_map/ppermute | solution.py:392
  113.0 23.6 %copy-start.2 = (bf16[64,32,128]{2,1,0:T(8,128)(2,1)S(1)}, bf16[64,32,128]{2,1,0:T(8,128)(2,1)}, u32[]{:S(2)}) copy-start(bf16[64,32,128]{2,1,0:T(8,128)(2,1)} %pair_ref.3) | copy-start | bytes 1572868
  113.0 23.5 %copy-start.6 = (bf16[1024,128]{1,0:T(8,128)(2,1)S(1)}, bf16[1024,128]{1,0:T(8,128)(2,1)}, u32[]{:S(2)}) copy-start(bf16[1024,128]{1,0:T(8,128)(2,1)} %wo_ref.3) | copy-start | bytes 786436
  113.1 23.5 %copy-start.8 = (bf16[128,512]{1,0:T(8,128)(2,1)S(1)}, bf16[128,512]{1,0:T(8,128)(2,1)}, u32[]{:S(2)}) copy-start(bf16[128,512]{1,0:T(8,128)(2,1)} %w_ref.4) | copy-start | bytes 393220
  136.6 1.3 copy-start
  157.7 55.2 %copy-start.11 = (bf16[128,128]{1,0:T(8,128)(2,1)S(1)}, bf16[128,128]{1,0:T(8,128)(2,1)}, u32[]{:S(2)}) copy-start(bf16[128,128]{1,0:T(8,128)(2,1)} %wg_ref.1) | copy-start | bytes 98308
  157.7 55.2 %copy-start.12 = (bf16[128,128]{1,0:T(8,128)(2,1)S(1)}, bf16[128,128]{1,0:T(8,128)(2,1)}, u32[]{:S(2)}) copy-start(bf16[128,128]{1,0:T(8,128)(2,1)} %w_ref.5) | copy-start | bytes 98308
  157.8 20.0 %collective-permute-start.13 = (bf16[512,128]{1,0:T(8,128)(2,1)S(1)}, bf16[512,128]{1,0:T(8,128)(2,1)S(1)}, u32[]{:S(2)}, u32[]{:S(2)}) collective-permute-start(bf16[512,128]{1,0:T(8,128)(2,1)S(1)} %get-tuple-element.12.refs_0_), channel_id=1, source_target_pairs={{0,2},{1,3},{2,4},{3,5},{4,6},{5,7},{6,0},{7,1},{8,10},{9,11},{10,... | collective-permute-start | bytes 393224 | tf_op jit(solution)/shard_map/ppermute | solution.py:317
  161.5 24.7 %collective-permute-start.11 = (bf16[512,128]{1,0:T(8,128)(2,1)S(1)}, bf16[512,128]{1,0:T(8,128)(2,1)S(1)}, u32[]{:S(2)}, u32[]{:S(2)}) collective-permute-start(bf16[512,128]{1,0:T(8,128)(2,1)S(1)} %get-tuple-element.12.refs_0_), channel_id=1, source_target_pairs={{0,4},{1,5},{2,6},{3,7},{4,0},{5,1},{6,2},{7,3},{8,12},{9,13},{10,... | collective-permute-start | bytes 393224 | tf_op jit(solution)/shard_map/ppermute | solution.py:317
  169.1 20.5 %collective-permute-start.9 = (bf16[512,128]{1,0:T(8,128)(2,1)S(1)}, bf16[512,128]{1,0:T(8,128)(2,1)S(1)}, u32[]{:S(2)}, u32[]{:S(2)}) collective-permute-start(bf16[512,128]{1,0:T(8,128)(2,1)S(1)} %get-tuple-element.12.refs_0_), channel_id=1, source_target_pairs={{0,6},{1,7},{2,0},{3,1},{4,2},{5,3},{6,4},{7,5},{8,14},{9,15},{10,... | collective-permute-start | bytes 393224 | tf_op jit(solution)/shard_map/ppermute | solution.py:317
  175.8 15.7 %collective-permute-start.8 = (bf16[512,128]{1,0:T(8,128)(2,1)S(1)}, bf16[512,128]{1,0:T(8,128)(2,1)S(1)}, u32[]{:S(2)}, u32[]{:S(2)}) collective-permute-start(bf16[512,128]{1,0:T(8,128)(2,1)S(1)} %get-tuple-element.12.refs_0_), channel_id=1, source_target_pairs={{0,1},{1,0},{2,3},{3,2},{4,5},{5,4},{6,7},{7,6},{8,9},{9,8},{10,11... | collective-permute-start | bytes 393224 | tf_op jit(solution)/shard_map/ppermute | solution.py:317
  177.8 13.7 %collective-permute-start.14 = (bf16[512,128]{1,0:T(8,128)(2,1)S(1)}, bf16[512,128]{1,0:T(8,128)(2,1)S(1)}, u32[]{:S(2)}, u32[]{:S(2)}) collective-permute-start(bf16[512,128]{1,0:T(8,128)(2,1)S(1)} %collective-permute-done.13.refs_6_), channel_id=1, source_target_pairs={{0,1},{1,0},{2,3},{3,2},{4,5},{5,4},{6,7},{7,6},{8,9},{9,8},{10,11... | collective-permute-start | bytes 393224 | tf_op jit(solution)/shard_map/ppermute | solution.py:317
  186.3 5.3 %collective-permute-start.12 = (bf16[512,128]{1,0:T(8,128)(2,1)S(1)}, bf16[512,128]{1,0:T(8,128)(2,1)S(1)}, u32[]{:S(2)}, u32[]{:S(2)}) collective-permute-start(bf16[512,128]{1,0:T(8,128)(2,1)S(1)} %collective-permute-done.11.refs_4_), channel_id=1, source_target_pairs={{0,1},{1,0},{2,3},{3,2},{4,5},{5,4},{6,7},{7,6},{8,9},{9,8},{10,11... | collective-permute-start | bytes 393224 | tf_op jit(solution)/shard_map/ppermute | solution.py:317
  189.6 3.2 %collective-permute-start.10 = (bf16[512,128]{1,0:T(8,128)(2,1)S(1)}, bf16[512,128]{1,0:T(8,128)(2,1)S(1)}, u32[]{:S(2)}, u32[]{:S(2)}) collective-permute-start(bf16[512,128]{1,0:T(8,128)(2,1)S(1)} %collective-permute-done.9.refs_2_), channel_id=1, source_target_pairs={{0,1},{1,0},{2,3},{3,2},{4,5},{5,4},{6,7},{7,6},{8,9},{9,8},{10,11... | collective-permute-start | bytes 393224 | tf_op jit(solution)/shard_map/ppermute | solution.py:317
  214.7 10.4 %all-to-all-start.6 = ((bf16[4,4,32,128]{3,2,1,0:T(8,128)(2,1)}), bf16[4,4,32,128]{3,2,1,0:T(8,128)(2,1)S(1)}, u32[]{:S(2)}, u32[]{:S(2)}) async-start(bf16[4,4,32,128]{3,2,1,0:T(8,128)(2,1)} %shard_map.137), calls=%async_computation.6 | async-start | bytes 262144 | tf_op jit(solution)/shard_map/all_to_all | solution.py:345

commit v4 on v3

--- a/solution.py
+++ b/solution.py
@@ -41,18 +41,21 @@
 
 VM = pl.BlockSpec(memory_space=pltpu.VMEM)
 SM = pl.BlockSpec(memory_space=pltpu.SMEM)
-
-
-def in_vmem(kernel, outs, scratch, place, *args):
-    args = [pltpu.with_memory_space_constraint(a, pltpu.VMEM) for a in args]
+HB = pl.BlockSpec(memory_space=pltpu.HBM)
+
+
+def in_vmem(kernel, outs, scratch, place, *args, loose=0):
+    loosely = [pltpu.with_memory_space_constraint(a, pltpu.HBM) for a in args[:loose]]
+    fixed = [pltpu.with_memory_space_constraint(a, pltpu.VMEM) for a in args[loose:]]
     outs = tuple(pltpu.VMEM(shape, BF) for shape in outs)
     results = pl.pallas_call(
         kernel,
         out_shape=outs,
-        in_specs=[SM] + [VM] * len(args),
+        in_specs=[SM] + [HB] * loose + [VM] * len(fixed),
         out_specs=(VM,) * len(outs),
         scratch_shapes=scratch,
-    )(place, *args)
+        compiler_params=pltpu.CompilerParams(vmem_limit_bytes=24 << 20),
+    )(place, *loosely, *fixed)
     return results if len(outs) > 1 else results[0]
 
 
@@ -72,14 +75,22 @@
     return (((col >> 1) + (m >> 1)) & 3) * 2 + ((col & 1) ^ (m & 1))
 
 
-def bias_kernel(place, pair_ref, w_ref, out_ref, rows, heads):
+def bias_kernel(place, pair_ref, w_ref, out_ref, pair, weight, rows, heads, sems):
     del place
-    normed = layer_norm(pair_ref[...].reshape(2048, 128)).astype(BF).astype(F32)
-    rows[...] = normed.reshape(64, 32, 128)
-    weight = w_ref[...]
+    copies = [pltpu.make_async_copy(w_ref, weight, sems.at[4])]
+    for q in range(4):
+        part = pl.ds(q * 16, 16)
+        copies.append(pltpu.make_async_copy(pair_ref.at[part], pair.at[part], sems.at[q]))
+    for copy in copies:
+        copy.start()
+    for q in range(4):
+        copies[q + 1].wait()
+        block = pair[q * 16 : (q + 1) * 16].reshape(512, 128)
+        rows[q * 16 : (q + 1) * 16] = layer_norm(block).astype(BF).astype(F32).reshape(16, 32, 128)
+    copies[0].wait()
     for j in range(16):
         pairs = jnp.concatenate([rows[:, j, :], rows[:, j + 16, :]], axis=0).astype(BF)
-        heads[j] = mm(weight, pairs, NT)
+        heads[j] = mm(weight[...], pairs, NT)
     lane = lax.broadcasted_iota(jnp.int32, (16, 128), 1) < 64
     tiles = []
     for p in range(4):
@@ -93,47 +104,52 @@
         out_ref[r] = tile
 
 
-def row_kernel(place, *refs):
-    own_ref, z1_ref, z3_ref, z2_ref, swap_ref, last_ref = refs[:6]
-    w_ref, bias_ref, wo_ref, out_ref, rows, keys, values, packed = refs[6:]
-    for m, block in (
-        (0, own_ref[...]),
-        (2, z1_ref[...]),
-        (6, z3_ref[...]),
-        (1, swap_ref[0]),
-        (3, swap_ref[1]),
-        (7, swap_ref[2]),
-        (4, z2_ref[...]),
-        (5, last_ref[...]),
-    ):
-        start = pl.multiple_of(source_of(col_of(place), m) * 64, 64)
-        normed = layer_norm(block.reshape(256, 256)).astype(BF)
-        if m == 0:
-            own = normed
-        for s in range(4):
-            rows[s, pl.ds(start, 64), :] = normed[s * 64 : (s + 1) * 64]
-    x = rows[...].reshape(2048, 256)
-    keys[...] = jnp.dot(x, w_ref[:, 256:512], preferred_element_type=F32).astype(BF)
-    values[...] = mm(w_ref[:, 512:768], x, TT).astype(BF)
+EARLY = (0, 1, 2, 3, 6, 7)
+LATE = (4, 5)
+
+
+def project_kernel(place, own_ref, z1_ref, z3_ref, swap_ref, w_ref, key_ref, value_ref):
+    del place
+    blocks = (own_ref[...], swap_ref[0], z1_ref[...], swap_ref[1], z3_ref[...], swap_ref[2])
+    normed = [layer_norm(block.reshape(256, 256)).astype(BF) for block in blocks]
+    w_key = w_ref[:, 256:512]
+    w_value = w_ref[:, 512:768]
+    for s in range(4):
+        x = jnp.concatenate([n[s * 64 : (s + 1) * 64] for n in normed], axis=0)
+        key_ref[s] = jnp.dot(x, w_key, preferred_element_type=F32).astype(BF)
+        value_ref[s] = mm(w_value, x, TT).astype(BF)
+
+
+def row_kernel(place, z2_ref, last_ref, own_ref, key_ref, value_ref, w_ref, bias_ref, wo_ref,
+               out_ref, bias_rows, packed):
+    own = layer_norm(own_ref[...].reshape(256, 256)).astype(BF)
     query_t = (mm(w_ref[:, 0:256], own, TT) * SCALE).astype(BF)
     gate_t = sigmoid(mm(w_ref[:, 768:1024], own, TT))
+    for k, m in enumerate(EARLY + LATE):
+        start = pl.multiple_of(source_of(col_of(place), m) * 64, 64)
+        bias_rows[k * 64 : (k + 1) * 64] = bias_ref[pl.ds(start, 64), :].astype(F32)
+    late = [layer_norm(r[...].reshape(256, 256)).astype(BF) for r in (z2_ref, last_ref)]
+    w_key = w_ref[:, 256:512]
+    w_value = w_ref[:, 512:768]
     head_row = lax.broadcasted_iota(jnp.int32, (256, 128), 0) // 32
     head_lane = lax.broadcasted_iota(jnp.int32, (256, 128), 1) // 64
     upper = lax.broadcasted_iota(jnp.int32, (64, 64), 0) < 32
     for s in range(4):
+        x = jnp.concatenate([n[s * 64 : (s + 1) * 64] for n in late], axis=0)
+        key = jnp.concatenate(
+            [key_ref[s], jnp.dot(x, w_key, preferred_element_type=F32).astype(BF)], axis=0
+        )
+        value_t = jnp.concatenate([value_ref[s], mm(w_value, x, TT).astype(BF)], axis=1)
         mine = query_t[:, s * 64 : (s + 1) * 64]
         twice = jnp.concatenate([mine, mine], axis=1)
-        key = keys[s * 512 : (s + 1) * 512]
         parts = []
         for p in range(4):
             diag = jnp.where(head_row == 2 * p + head_lane, twice, jnp.zeros_like(twice))
             scores = jnp.dot(key, diag, preferred_element_type=F32)
-            scores = scores + bias_ref[:, p * 128 : (p + 1) * 128].astype(F32)
+            scores = scores + bias_rows[:, p * 128 : (p + 1) * 128]
             weights, scale = exp_rows(scores)
             mixed = jnp.dot(
-                values[p * 64 : (p + 1) * 64, s * 512 : (s + 1) * 512],
-                weights,
-                preferred_element_type=F32,
+                value_t[p * 64 : (p + 1) * 64], weights, preferred_element_type=F32
             )
             mixed = mixed * scale
             parts.append(jnp.where(upper, mixed[:, :64], mixed[:, 64:]))
@@ -263,17 +279,18 @@
     out_ref[:, 1] = scratch[1].astype(BF)
 
 
-def triangle_kernel(place, left_ref, back_ref, *refs):
-    rights, out_ref = refs[:8], refs[8]
+def triangle_kernel(place, left_ref, back_ref, same_ref, other_ref, out_ref):
     left = left_ref[...]
     lane = lax.broadcasted_iota(jnp.int32, (64, 128), 1) < 64
-    for m in range(8):
-        product = mm(rights[m][...], left, TN)
-        block = jnp.where(lane, product[:64], product[64:]).astype(BF)
-        target = source_of(col_of(place), m) * 2
-        for b in range(4):
-            for h in range(2):
-                out_ref[b * 16 + target + h, 0] = block[(b * 2 + h) * 8 : (b * 2 + h + 1) * 8]
+    core = col_of(place) & 1
+    for chip in range(4):
+        for right_ref, source in ((same_ref, core), (other_ref, core ^ 1)):
+            product = mm(right_ref[chip], left, TN)
+            block = jnp.where(lane, product[:64], product[64:]).astype(BF)
+            target = (chip * 2 + source) * 2
+            for b in range(4):
+                for h in range(2):
+                    out_ref[b * 16 + target + h, 0] = block[(b * 2 + h) * 8 : (b * 2 + h + 1) * 8]
     out_ref[:, 1] = back_ref[...]
 
 
@@ -315,15 +332,6 @@
 def shifted(x, step, flip):
     perm = [(c, (c // 2 - step) % 4 * 2 + (c % 2 ^ flip)) for c in range(8)]
     return lax.ppermute(x, "col", perm)
-
-
-def gather_col(x):
-    parts = {(0, 0): x}
-    for step in (1, 3, 2):
-        parts[step, 0] = shifted(x, step, 0)
-    for step in (0, 1, 3, 2):
-        parts[step, 1] = shifted(parts[step, 0], 0, 1)
-    return [parts[m // 2, m % 2] for m in range(8)]
 
 
 def local(
@@ -347,29 +355,37 @@
     blocks = [alignment]
     for step in (1, 3, 2):
         blocks.append(shifted(alignment, step, 0))
-    blocks.append(shifted(jnp.stack(blocks[:3]), 0, 1))
-    blocks.append(shifted(blocks[3], 0, 1))
+    swapped = shifted(jnp.stack(blocks[:3]), 0, 1)
+    last = shifted(blocks[3], 0, 1)
     bias = in_vmem(
         bias_kernel,
         [(16, 32, 512)],
-        [pltpu.VMEM((64, 32, 128), F32), pltpu.VMEM((16, 8, 128), F32)],
+        [
+            pltpu.VMEM((64, 32, 128), BF),
+            pltpu.VMEM((8, 128), BF),
+            pltpu.VMEM((64, 32, 128), F32),
+            pltpu.VMEM((16, 8, 128), F32),
+            pltpu.SemaphoreType.DMA((5,)),
+        ],
         place,
         pair_features,
         w_bias.T,
+        loose=2,
     )
     bias = exchange(bias, "row").reshape(512, 512)
 
+    projected = in_vmem(
+        project_kernel, [(4, 384, 256), (4, 256, 384)], [], place, *blocks[:3], swapped, w_row
+    )
     columns = in_vmem(
         row_kernel,
         [(64, 8, 128)],
-        [
-            pltpu.VMEM((4, 512, 256), BF),
-            pltpu.VMEM((2048, 256), BF),
-            pltpu.VMEM((256, 2048), BF),
-            pltpu.VMEM((64, 8, 128), F32),
-        ],
-        place,
-        *blocks,
+        [pltpu.VMEM((512, 512), F32), pltpu.VMEM((64, 8, 128), F32)],
+        place,
+        blocks[3],
+        last,
+        alignment,
+        *projected,
         w_row,
         bias,
         row_output_weight,
@@ -410,8 +426,20 @@
     )
     message = exchange(message, both)
     tri_left = message[:, 0].reshape(512, 128)
-    rights = gather_col(message[:, 1].reshape(512, 128))
-    sums = in_vmem(triangle_kernel, [(64, 2, 8, 128)], [], place, tri_left, returning, *rights)
+    same = lax.all_to_all(
+        jnp.broadcast_to(message[None, :, 1], (4, 64, 8, 128)).reshape(4, 512, 128),
+        "col", 0, 0, tiled=True, axis_index_groups=[[0, 2, 4, 6], [1, 3, 5, 7]],
+    )
+    sums = in_vmem(
+        triangle_kernel,
+        [(64, 2, 8, 128)],
+        [],
+        place,
+        tri_left,
+        returning,
+        same,
+        shifted(same, 0, 1),
+    )
     sums = exchange(sums, both)
     parts = in_vmem(
         output_kernel,

time: 227 us -> 230 us (1.013)
  blocking collectives: 86.6 us -> 116 us
  starting transfers between devices: 82.7 us -> 57.4 us
  local copies, waits for them, and re-layouts: 3.79 us -> 0.83 us
    all_to_all x0 -> x1, blocking collectives: none -> 37 us  [local(): lax.all_to_all(jnp.broadcast_to(message[None, :, 1], (4, 64, 8, 128)).res...]
    ppermute x12 -> x6, starting transfers between devices: 53 us -> 27.2 us  [shifted(): return lax.ppermute(x, 'col', perm)]
    all_to_all x4, blocking collectives: 86.6 us -> 79.3 us  [local(): exchange = lambda x, axis: lax.all_to_all(x, axis, 0, 0, tiled=True)]
    all_to_all x3, waiting for transfers between devices: 6.4 us -> 9.75 us  [local(): exchange = lambda x, axis: lax.all_to_all(x, axis, 0, 0, tiled=True)]
    unnamed x28 -> x22, local copies, waits for them, and re-layouts: 3.08 us -> 0.06 us
    ppermute x12 -> x6, waiting for transfers between devices: 21.3 us -> 18.6 us  [shifted(): return lax.ppermute(x, 'col', perm)]
    pallas_call x7 -> x8, Pallas kernels: 19.6 us -> 21.8 us  [in_vmem(): pl.pallas_call(kernel, out_shape=outs, in_specs=[SM] + [HB] * loose + [VM...]
  transfers between devices with their start and end apart: 18 -> 12, of which waited for: 10 -> 8; matrix products, arithmetic and copies ran while one was open for 0% -> 0% of each run, Pallas kernels for 1% -> 2%
where the time goes in v4:
time: 230 us; the launch traced here: 229 us
  blocking collectives  116 us (50%)
  starting transfers between devices  57.4 us (25%)
  waiting for transfers between devices  31.1 us (14%)
  Pallas kernels  22.7 us (10%)
    all_to_all x4, blocking collectives, local(): exchange = lambda x, axis: lax.all_to_all(x, axis, 0, 0, tiled=True)  79.3 us
    all_to_all x1, blocking collectives, local(): lax.all_to_all(jnp.broadcast_to(message[None, :, 1], (4, 64, 8, 128)).res...  37 us
    ppermute x6, starting transfers between devices, shifted(): return lax.ppermute(x, 'col', perm)  27.2 us
    pallas_call x8, Pallas kernels, in_vmem(): pl.pallas_call(kernel, out_shape=outs, in_specs=[SM] + [HB] * loose + [VM...  21.8 us
    all_to_all x3, starting transfers between devices, local(): exchange = lambda x, axis: lax.all_to_all(x, axis, 0, 0, tiled=True)  20.9 us
    ppermute x6, waiting for transfers between devices, shifted(): return lax.ppermute(x, 'col', perm)  18.6 us
    all_to_all x3, waiting for transfers between devices, local(): exchange = lambda x, axis: lax.all_to_all(x, axis, 0, 0, tiled=True)  9.75 us
    ppermute x3, starting transfers between devices, local(): lax.ppermute(left, 'branch', [(b, b ^ mask) for b in range(4)])  9.38 us
  transfers between devices with their start and end apart: 12, of which 8 were waited for; matrix products, arithmetic and copies ran while one was open for 0% of the time, Pallas kernels for 2%

profile of v4, /device:TPU:32, one launch (start us, length us, event | category | flops | bytes accessed | tf_op | source)
XLA Modules:
  0.0 229.3 jit_solution(4258510960504048705)
XLA Ops:
  0.6 12.0 %collective-permute-start.2 = (bf16[4,64,256]{2,1,0:T(8,128)(2,1)}, bf16[4,64,256]{2,1,0:T(8,128)(2,1)S(1)}, u32[]{:S(2)}, u32[]{:S(2)}) collective-permute-start(bf16[4,64,256]{2,1,0:T(8,128)(2,1)} %own_ref.3), channel_id=1, source_target_pairs={{0,6},{1,7},{2,0},{3,1},{4,2},{5,3},{6,4},{7,5},{8,14},{9,15},{10,... | collective-permute-start | bytes 393224 | tf_op jit(solution)/shard_map/ppermute | solution.py:334
  12.6 1.9 collective-permute-start.3
  14.6 3.6 %shard_map.132 = bf16[16,32,512]{2,1,0:T(8,128)(2,1)} custom-call(s32[1]{0:T(128)} %bitcast.place, bf16[64,32,128]{2,1,0:T(8,128)(2,1)} %pair_ref.3, bf16[8,128]{1,0:T(8,128)(2,1)} %bitcast.24), custom_call_target="tpu_custom_call" | custom-call | tf_op jit(solution)/shard_map/pallas_call | solution.py:51
  18.1 7.0 %all-to-all-start = ((bf16[16,32,512]{2,1,0:T(8,128)(2,1)}), bf16[16,32,512]{2,1,0:T(8,128)(2,1)S(1)}, u32[]{:S(2)}, u32[]{:S(2)}) async-start(bf16[16,32,512]{2,1,0:T(8,128)(2,1)} %shard_map.132), calls=%async_computation | async-start | bytes 1048576 | tf_op jit(solution)/shard_map/all_to_all | solution.py:353
  25.2 0.0 copy-start.5
  25.2 0.0 collective-permute-done.2.z1_ref
  25.2 3.4 %collective-permute-done.3.z3_ref = bf16[4,64,256]{2,1,0:T(8,128)(2,1)S(1)} collective-permute-done((bf16[4,64,256]{2,1,0:T(8,128)(2,1)}, bf16[4,64,256]{2,1,0:T(8,128)(2,1)S(1)}, u32[]{:S(2)}, u32[]{:S(2)}) %collective-permute-start.3) | collective-permute-done | bytes 131104 | tf_op jit(solution)/shard_map/ppermute | solution.py:334
  28.7 1.9 collective-permute-start.4
  30.6 7.4 %collective-permute-start = (bf16[4,64,256]{2,1,0:T(8,128)(2,1)S(1)}, bf16[4,64,256]{2,1,0:T(8,128)(2,1)S(1)}, u32[]{:S(2)}, u32[]{:S(2)}) collective-permute-start(bf16[4,64,256]{2,1,0:T(8,128)(2,1)S(1)} %copy-done.2), channel_id=1, source_target_pairs={{0,4},{1,5},{2,6},{3,7},{4,0},{5,1},{6,2},{7,3},{8,12},{9,13},{10,... | collective-permute-start | bytes 393224 | tf_op jit(solution)/shard_map/ppermute | solution.py:334
  38.0 13.1 %collective-permute-done.z2_ref = bf16[4,64,256]{2,1,0:T(8,128)(2,1)S(1)} collective-permute-done((bf16[4,64,256]{2,1,0:T(8,128)(2,1)S(1)}, bf16[4,64,256]{2,1,0:T(8,128)(2,1)S(1)}, u32[]{:S(2)}, u32[]{:S(2)}) %collective-permute-start) | collective-permute-done | bytes 131104 | tf_op jit(solution)/shard_map/ppermute | solution.py:334
  51.1 1.9 collective-permute-start.1
  53.0 0.0 collective-permute-done.4.swap_ref
  53.0 1.1 shard_map.131
  54.2 0.1 collective-permute-done.1.last_ref
  54.3 0.0 all-to-all-done
  54.3 0.0 copy-done.5
  54.4 0.0 copy-start.7
  54.4 0.0 copy-start.8
  54.4 7.7 %shard_map.133 = bf16[64,8,128]{2,1,0:T(8,128)(2,1)S(1)} custom-call(s32[1]{0:T(128)} %bitcast.place, bf16[4,64,256]{2,1,0:T(8,128)(2,1)S(1)} %collective-permute-done.z2_ref, bf16[4,64,256]{2,1,0:T(8,128)(2,1)S(1)} %collective-permute-done.1.last_ref, bf16[4,64,256]{2,1,0:T(8,128)(2,1)S(1)} %copy-done.2, bf16[4,384,256]{2,1,0:T(8,128)(2,1)S(1)} %get-tuple-element.9.key_ref, ...), custom_call_target="tpu_custom_call" | custom-call | tf_op jit(solution)/shard_map/pallas_call | solution.py:51
  62.1 23.5 %all_to_all.40.x_ref = bf16[64,8,128]{2,1,0:T(8,128)(2,1)S(1)} all-to-all(bf16[64,8,128]{2,1,0:T(8,128)(2,1)S(1)} %shard_map.133), channel_id=1, replica_groups=mesh['branch'=4,'row'=16,'col'=8] {'branch','row'}, dimensions={0} | all-to-all | bytes 262144 | tf_op jit(solution)/shard_map/all_to_all | solution.py:353
  85.6 0.0 copy-done.7
  85.6 4.0 %shard_map.134 = (bf16[64,8,128]{2,1,0:T(8,128)(2,1)S(1)}, bf16[32,256]{1,0:T(8,128)(2,1)S(1)}, bf16[8,32,256]{2,1,0:T(8,128)(2,1)}) custom-call(s32[1]{0:T(128)} %bitcast.place, bf16[64,8,128]{2,1,0:T(8,128)(2,1)S(1)} %all_to_all.40.x_ref, bf16[256,1024]{1,0:T(8,128)(2,1)S(1)} %copy-done.3, bf16[256,256]{1,0:T(8,128)(2,1)S(1)} %copy-done.7, ...), custom_call_target="tpu_custom_call" | custom-call | tf_op jit(solution)/shard_map/pallas_call | solution.py:51
  89.6 8.7 %all-to-all-start.2 = ((bf16[8,32,256]{2,1,0:T(8,128)(2,1)}), bf16[8,32,256]{2,1,0:T(8,128)(2,1)S(1)}, u32[]{:S(2)}, u32[]{:S(2)}) async-start(bf16[8,32,256]{2,1,0:T(8,128)(2,1)} %get-tuple-element.11), calls=%async_computation.2 | async-start | bytes 262144 | tf_op jit(solution)/shard_map/all_to_all | solution.py:353
  98.3 3.7 %collective-permute-start.5 = (bf16[32,256]{1,0:T(8,128)(2,1)S(1)}, bf16[32,256]{1,0:T(8,128)(2,1)S(1)}, u32[]{:S(2)}, u32[]{:S(2)}) collective-permute-start(bf16[32,256]{1,0:T(8,128)(2,1)S(1)} %get-tuple-element.12.refs_0_), channel_id=1, source_target_pairs={{0,128},{128,0},{256,384},{384,256},{1,129},{129,1},{257,385},{385... | collective-permute-start | bytes 49160 | tf_op jit(solution)/shard_map/ppermute | solution.py:408
  102.0 2.1 collective-permute-start.6
  104.0 3.6 %collective-permute-start.7 = (bf16[32,256]{1,0:T(8,128)(2,1)S(1)}, bf16[32,256]{1,0:T(8,128)(2,1)S(1)}, u32[]{:S(2)}, u32[]{:S(2)}) collective-permute-start(bf16[32,256]{1,0:T(8,128)(2,1)S(1)} %get-tuple-element.12.refs_0_), channel_id=1, source_target_pairs={{0,384},{128,256},{256,128},{384,0},{1,385},{129,257},{257,129},{3... | collective-permute-start | bytes 49160 | tf_op jit(solution)/shard_map/ppermute | solution.py:408
  107.7 0.0 collective-permute-done.5.refs_1_
  107.7 2.2 collective-permute-done.6.refs_2_
  109.9 0.6 collective-permute-done.7.refs_3_
  110.5 5.3 %all-to-all-done.2.right_ref = bf16[8,32,256]{2,1,0:T(8,128)(2,1)S(1)} async-done(((bf16[8,32,256]{2,1,0:T(8,128)(2,1)}), bf16[8,32,256]{2,1,0:T(8,128)(2,1)S(1)}, u32[]{:S(2)}, u32[]{:S(2)}) %all-to-all-start.2) | async-done | bytes 131104 | tf_op jit(solution)/shard_map/all_to_all | solution.py:353
  115.8 0.1 shard_map.135
  115.9 0.0 copy-start
  115.9 0.0 copy-start.4
  115.9 0.0 copy-start.6
  115.9 21.7 %all_to_all.41.factor_ref = bf16[16,160,256]{2,1,0:T(8,128)(2,1)S(1)} all-to-all(bf16[16,160,256]{2,1,0:T(8,128)(2,1)S(1)} %shard_map.135), channel_id=1, replica_groups=mesh['branch'=4,'row'=16,'col'=8] {'row'}, dimensions={0} | all-to-all | bytes 2621440 | tf_op jit(solution)/shard_map/all_to_all | solution.py:353
  137.6 3.1 %shard_map.136 = (bf16[512,128]{1,0:T(8,128)(2,1)S(1)}, bf16[64,2,8,128]{3,2,1,0:T(8,128)(2,1)S(1)}) custom-call(s32[1]{0:T(128)} %bitcast.place, bf16[16,160,256]{2,1,0:T(8,128)(2,1)S(1)} %all_to_all.41.factor_ref, bf16[64,32,128]{2,1,0:T(8,128)(2,1)S(1)} %copy-done, bf16[1024,128]{1,0:T(8,128)(2,1)S(1)} %copy-done.4, bf16[128,512]{1,0:T(8,128)(2,1)S(1)} %copy-done.6), custom_call_target="tpu_custom_call" | custom-call | tf_op jit(solution)/shard_map/pallas_call | solution.py:51
  140.7 17.0 %all_to_all.42 = bf16[64,2,8,128]{3,2,1,0:T(8,128)(2,1)S(1)} all-to-all(bf16[64,2,8,128]{3,2,1,0:T(8,128)(2,1)S(1)} %get-tuple-element.13), channel_id=1, replica_groups=mesh['branch'=4,'row'=16,'col'=8] {'branch','row'}, dimensions={0} | all-to-all | bytes 524288 | tf_op jit(solution)/shard_map/all_to_all | solution.py:353
  157.7 0.1 broadcast_in_dim.8
  157.8 37.0 %all_to_all.43.same_ref = bf16[4,512,128]{2,1,0:T(8,128)(2,1)S(1)} all-to-all(bf16[4,512,128]{2,1,0:T(8,128)(2,1)S(1)} %broadcast_in_dim.8), channel_id=1, replica_groups={{0,2,4,6},{1,3,5,7},{8,10,12,14},{9,11,13,15},{16,18,20,22},{17,19,21,2..., dimensions={0} | all-to-all | bytes 1048576 | tf_op jit(solution)/shard_map/all_to_all | solution.py:429
  194.8 2.0 collective-permute-start.8
  196.8 1.9 collective-permute-done.8.other_ref
  198.7 0.5 shard_map.137
  199.2 17.1 %all_to_all.44.sum_ref = bf16[64,2,8,128]{3,2,1,0:T(8,128)(2,1)S(1)} all-to-all(bf16[64,2,8,128]{3,2,1,0:T(8,128)(2,1)S(1)} %shard_map.137), channel_id=1, replica_groups=mesh['branch'=4,'row'=16,'col'=8] {'branch','row'}, dimensions={0} | all-to-all | bytes 524288 | tf_op jit(solution)/shard_map/all_to_all | solution.py:353
  216.3 1.7 shard_map.138
  218.1 5.2 %all-to-all-start.7 = ((bf16[4,4,32,128]{3,2,1,0:T(8,128)(2,1)}), bf16[4,4,32,128]{3,2,1,0:T(8,128)(2,1)S(1)}, u32[]{:S(2)}, u32[]{:S(2)}) async-start(bf16[4,4,32,128]{3,2,1,0:T(8,128)(2,1)} %shard_map.138), calls=%async_computation.7 | async-start | bytes 262144 | tf_op jit(solution)/shard_map/all_to_all | solution.py:353
  223.3 0.7 copy.14
  224.0 4.5 %all-to-all-done.7.x_ref = bf16[4,4,32,128]{3,2,1,0:T(8,128)(2,1)S(1)} async-done(((bf16[4,4,32,128]{3,2,1,0:T(8,128)(2,1)}), bf16[4,4,32,128]{3,2,1,0:T(8,128)(2,1)S(1)}, u32[]{:S(2)}, u32[]{:S(2)}) %all-to-all-start.7) | async-done | bytes 131104 | tf_op jit(solution)/shard_map/all_to_all | solution.py:353
  228.4 0.8 unpack.1
  (17 shorter events, 0.1 us)
Async XLA Ops:
  0.6 28.0 %copy-start.2 = (bf16[4,64,256]{2,1,0:T(8,128)(2,1)S(1)}, bf16[4,64,256]{2,1,0:T(8,128)(2,1)}, u32[]{:S(2)}) copy-start(bf16[4,64,256]{2,1,0:T(8,128)(2,1)} %own_ref.3) | copy-start | bytes 393220
  0.6 24.6 %collective-permute-start.2 = (bf16[4,64,256]{2,1,0:T(8,128)(2,1)}, bf16[4,64,256]{2,1,0:T(8,128)(2,1)S(1)}, u32[]{:S(2)}, u32[]{:S(2)}) collective-permute-start(bf16[4,64,256]{2,1,0:T(8,128)(2,1)} %own_ref.3), channel_id=1, source_target_pairs={{0,6},{1,7},{2,0},{3,1},{4,2},{5,3},{6,4},{7,5},{8,14},{9,15},{10,... | collective-permute-start | bytes 393224 | tf_op jit(solution)/shard_map/ppermute | solution.py:334
  12.6 16.0 %collective-permute-start.3 = (bf16[4,64,256]{2,1,0:T(8,128)(2,1)}, bf16[4,64,256]{2,1,0:T(8,128)(2,1)S(1)}, u32[]{:S(2)}, u32[]{:S(2)}) collective-permute-start(bf16[4,64,256]{2,1,0:T(8,128)(2,1)} %own_ref.3), channel_id=1, source_target_pairs={{0,2},{1,3},{2,4},{3,5},{4,6},{5,7},{6,0},{7,1},{8,10},{9,11},{10,... | collective-permute-start | bytes 393224 | tf_op jit(solution)/shard_map/ppermute | solution.py:334
  14.6 38.5 %copy-start.1 = (bf16[256,1024]{1,0:T(8,128)(2,1)S(1)}, bf16[256,1024]{1,0:T(8,128)(2,1)}, u32[]{:S(2)}) copy-start(bf16[256,1024]{1,0:T(8,128)(2,1)} %w_ref.6) | copy-start | bytes 1572868
  18.1 36.2 %all-to-all-start = ((bf16[16,32,512]{2,1,0:T(8,128)(2,1)}), bf16[16,32,512]{2,1,0:T(8,128)(2,1)S(1)}, u32[]{:S(2)}, u32[]{:S(2)}) async-start(bf16[16,32,512]{2,1,0:T(8,128)(2,1)} %shard_map.132), calls=%async_computation | async-start | bytes 1048576 | tf_op jit(solution)/shard_map/all_to_all | solution.py:353
  25.2 29.2 %copy-start.5 = (bf16[256,256]{1,0:T(8,128)(2,1)S(1)}, bf16[256,256]{1,0:T(8,128)(2,1)}, u32[]{:S(2)}) copy-start(bf16[256,256]{1,0:T(8,128)(2,1)} %wo_ref.3) | copy-start | bytes 393220
  28.7 24.3 %collective-permute-start.4 = (bf16[3,4,64,256]{3,2,1,0:T(8,128)(2,1)S(1)}, bf16[3,4,64,256]{3,2,1,0:T(8,128)(2,1)S(1)}, u32[]{:S(2)}, u32[]{:S(2)}) collective-permute-start(bf16[3,4,64,256]{3,2,1,0:T(8,128)(2,1)S(1)} %pad_maximum_fusion), channel_id=1, source_target_pairs={{0,1},{1,0},{2,3},{3,2},{4,5},{5,4},{6,7},{7,6},{8,9},{9,8},{10,11... | collective-permute-start | bytes 1179656 | tf_op jit(solution)/shard_map/ppermute | solution.py:334
  30.6 20.5 %collective-permute-start = (bf16[4,64,256]{2,1,0:T(8,128)(2,1)S(1)}, bf16[4,64,256]{2,1,0:T(8,128)(2,1)S(1)}, u32[]{:S(2)}, u32[]{:S(2)}) collective-permute-start(bf16[4,64,256]{2,1,0:T(8,128)(2,1)S(1)} %copy-done.2), channel_id=1, source_target_pairs={{0,4},{1,5},{2,6},{3,7},{4,0},{5,1},{6,2},{7,3},{8,12},{9,13},{10,... | collective-permute-start | bytes 393224 | tf_op jit(solution)/shard_map/ppermute | solution.py:334
  51.1 3.2 %collective-permute-start.1 = (bf16[4,64,256]{2,1,0:T(8,128)(2,1)S(1)}, bf16[4,64,256]{2,1,0:T(8,128)(2,1)S(1)}, u32[]{:S(2)}, u32[]{:S(2)}) collective-permute-start(bf16[4,64,256]{2,1,0:T(8,128)(2,1)S(1)} %collective-permute-done.z2_ref), channel_id=1, source_target_pairs={{0,1},{1,0},{2,3},{3,2},{4,5},{5,4},{6,7},{7,6},{8,9},{9,8},{10,11... | collective-permute-start | bytes 393224 | tf_op jit(solution)/shard_map/ppermute | solution.py:334
  54.3 31.3 %copy-start.3 = (bf16[256,1024]{1,0:T(8,128)(2,1)S(1)}, bf16[256,1024]{1,0:T(8,128)(2,1)}, u32[]{:S(2)}) copy-start(bf16[256,1024]{1,0:T(8,128)(2,1)} %w_ref.7) | copy-start | bytes 1572868
  54.4 31.2 %copy-start.7 = (bf16[256,256]{1,0:T(8,128)(2,1)S(1)}, bf16[256,256]{1,0:T(8,128)(2,1)}, u32[]{:S(2)}) copy-start(bf16[256,256]{1,0:T(8,128)(2,1)} %wo_ref.4) | copy-start | bytes 393220
  54.4 31.2 %copy-start.8 = (bf16[256,64]{0,1:T(8,128)(2,1)S(1)}, bf16[256,64]{0,1:T(8,128)(2,1)}, u32[]{:S(2)}) copy-start(bf16[256,64]{0,1:T(8,128)(2,1)} %param.19) | copy-start | bytes 98308
  89.6 26.1 %all-to-all-start.2 = ((bf16[8,32,256]{2,1,0:T(8,128)(2,1)}), bf16[8,32,256]{2,1,0:T(8,128)(2,1)S(1)}, u32[]{:S(2)}, u32[]{:S(2)}) async-start(bf16[8,32,256]{2,1,0:T(8,128)(2,1)} %get-tuple-element.11), calls=%async_computation.2 | async-start | bytes 262144 | tf_op jit(solution)/shard_map/all_to_all | solution.py:353
  98.3 9.4 %collective-permute-start.5 = (bf16[32,256]{1,0:T(8,128)(2,1)S(1)}, bf16[32,256]{1,0:T(8,128)(2,1)S(1)}, u32[]{:S(2)}, u32[]{:S(2)}) collective-permute-start(bf16[32,256]{1,0:T(8,128)(2,1)S(1)} %get-tuple-element.12.refs_0_), channel_id=1, source_target_pairs={{0,128},{128,0},{256,384},{384,256},{1,129},{129,1},{257,385},{385... | collective-permute-start | bytes 49160 | tf_op jit(solution)/shard_map/ppermute | solution.py:408
  102.0 7.9 %collective-permute-start.6 = (bf16[32,256]{1,0:T(8,128)(2,1)S(1)}, bf16[32,256]{1,0:T(8,128)(2,1)S(1)}, u32[]{:S(2)}, u32[]{:S(2)}) collective-permute-start(bf16[32,256]{1,0:T(8,128)(2,1)S(1)} %get-tuple-element.12.refs_0_), channel_id=1, source_target_pairs={{0,256},{128,384},{256,0},{384,128},{1,257},{129,385},{257,1},{385... | collective-permute-start | bytes 49160 | tf_op jit(solution)/shard_map/ppermute | solution.py:408
  104.0 6.4 %collective-permute-start.7 = (bf16[32,256]{1,0:T(8,128)(2,1)S(1)}, bf16[32,256]{1,0:T(8,128)(2,1)S(1)}, u32[]{:S(2)}, u32[]{:S(2)}) collective-permute-start(bf16[32,256]{1,0:T(8,128)(2,1)S(1)} %get-tuple-element.12.refs_0_), channel_id=1, source_target_pairs={{0,384},{128,256},{256,128},{384,0},{1,385},{129,257},{257,129},{3... | collective-permute-start | bytes 49160 | tf_op jit(solution)/shard_map/ppermute | solution.py:408
  115.9 21.7 %copy-start = (bf16[64,32,128]{2,1,0:T(8,128)(2,1)S(1)}, bf16[64,32,128]{2,1,0:T(8,128)(2,1)}, u32[]{:S(2)}) copy-start(bf16[64,32,128]{2,1,0:T(8,128)(2,1)} %pair_ref.3) | copy-start | bytes 1572868
  115.9 21.7 %copy-start.4 = (bf16[1024,128]{1,0:T(8,128)(2,1)S(1)}, bf16[1024,128]{1,0:T(8,128)(2,1)}, u32[]{:S(2)}) copy-start(bf16[1024,128]{1,0:T(8,128)(2,1)} %wo_ref.5) | copy-start | bytes 786436
  115.9 21.7 %copy-start.6 = (bf16[128,512]{1,0:T(8,128)(2,1)S(1)}, bf16[128,512]{1,0:T(8,128)(2,1)}, u32[]{:S(2)}) copy-start(bf16[128,512]{1,0:T(8,128)(2,1)} %w_ref.8) | copy-start | bytes 393220
  194.8 21.6 %copy-start.9 = (bf16[128,128]{1,0:T(8,128)(2,1)S(1)}, bf16[128,128]{1,0:T(8,128)(2,1)}, u32[]{:S(2)}) copy-start(bf16[128,128]{1,0:T(8,128)(2,1)} %wg_ref.1) | copy-start | bytes 98308
  194.8 21.6 %copy-start.10 = (bf16[128,128]{1,0:T(8,128)(2,1)S(1)}, bf16[128,128]{1,0:T(8,128)(2,1)}, u32[]{:S(2)}) copy-start(bf16[128,128]{1,0:T(8,128)(2,1)} %w_ref.9) | copy-start | bytes 98308
  194.8 3.9 %collective-permute-start.8 = (bf16[4,512,128]{2,1,0:T(8,128)(2,1)S(1)}, bf16[4,512,128]{2,1,0:T(8,128)(2,1)S(1)}, u32[]{:S(2)}, u32[]{:S(2)}) collective-permute-start(bf16[4,512,128]{2,1,0:T(8,128)(2,1)S(1)} %all_to_all.43.same_ref), channel_id=1, source_target_pairs={{0,1},{1,0},{2,3},{3,2},{4,5},{5,4},{6,7},{7,6},{8,9},{9,8},{10,11... | collective-permute-start | bytes 1572872 | tf_op jit(solution)/shard_map/ppermute | solution.py:334
  218.1 10.4 %all-to-all-start.7 = ((bf16[4,4,32,128]{3,2,1,0:T(8,128)(2,1)}), bf16[4,4,32,128]{3,2,1,0:T(8,128)(2,1)S(1)}, u32[]{:S(2)}, u32[]{:S(2)}) async-start(bf16[4,4,32,128]{3,2,1,0:T(8,128)(2,1)} %shard_map.138), calls=%async_computation.7 | async-start | bytes 262144 | tf_op jit(solution)/shard_map/all_to_all | solution.py:353

commit v5 on v3

--- a/solution.py
+++ b/solution.py
@@ -41,18 +41,21 @@
 
 VM = pl.BlockSpec(memory_space=pltpu.VMEM)
 SM = pl.BlockSpec(memory_space=pltpu.SMEM)
-
-
-def in_vmem(kernel, outs, scratch, place, *args):
-    args = [pltpu.with_memory_space_constraint(a, pltpu.VMEM) for a in args]
+HB = pl.BlockSpec(memory_space=pltpu.HBM)
+
+
+def in_vmem(kernel, outs, scratch, place, *args, loose=0):
+    loosely = [pltpu.with_memory_space_constraint(a, pltpu.HBM) for a in args[:loose]]
+    fixed = [pltpu.with_memory_space_constraint(a, pltpu.VMEM) for a in args[loose:]]
     outs = tuple(pltpu.VMEM(shape, BF) for shape in outs)
     results = pl.pallas_call(
         kernel,
         out_shape=outs,
-        in_specs=[SM] + [VM] * len(args),
+        in_specs=[SM] + [HB] * loose + [VM] * len(fixed),
         out_specs=(VM,) * len(outs),
         scratch_shapes=scratch,
-    )(place, *args)
+        compiler_params=pltpu.CompilerParams(vmem_limit_bytes=24 << 20),
+    )(place, *loosely, *fixed)
     return results if len(outs) > 1 else results[0]
 
 
@@ -72,14 +75,22 @@
     return (((col >> 1) + (m >> 1)) & 3) * 2 + ((col & 1) ^ (m & 1))
 
 
-def bias_kernel(place, pair_ref, w_ref, out_ref, rows, heads):
+def bias_kernel(place, pair_ref, w_ref, out_ref, pair, weight, rows, heads, sems):
     del place
-    normed = layer_norm(pair_ref[...].reshape(2048, 128)).astype(BF).astype(F32)
-    rows[...] = normed.reshape(64, 32, 128)
-    weight = w_ref[...]
+    copies = [pltpu.make_async_copy(w_ref, weight, sems.at[4])]
+    for q in range(4):
+        part = pl.ds(q * 16, 16)
+        copies.append(pltpu.make_async_copy(pair_ref.at[part], pair.at[part], sems.at[q]))
+    for copy in copies:
+        copy.start()
+    for q in range(4):
+        copies[q + 1].wait()
+        block = pair[q * 16 : (q + 1) * 16].reshape(512, 128)
+        rows[q * 16 : (q + 1) * 16] = layer_norm(block).astype(BF).astype(F32).reshape(16, 32, 128)
+    copies[0].wait()
     for j in range(16):
         pairs = jnp.concatenate([rows[:, j, :], rows[:, j + 16, :]], axis=0).astype(BF)
-        heads[j] = mm(weight, pairs, NT)
+        heads[j] = mm(weight[...], pairs, NT)
     lane = lax.broadcasted_iota(jnp.int32, (16, 128), 1) < 64
     tiles = []
     for p in range(4):
@@ -117,25 +128,31 @@
     values[...] = mm(w_ref[:, 512:768], x, TT).astype(BF)
     query_t = (mm(w_ref[:, 0:256], own, TT) * SCALE).astype(BF)
     gate_t = sigmoid(mm(w_ref[:, 768:1024], own, TT))
-    head_row = lax.broadcasted_iota(jnp.int32, (256, 128), 0) // 32
-    head_lane = lax.broadcasted_iota(jnp.int32, (256, 128), 1) // 64
+    head_row = lax.broadcasted_iota(jnp.int32, (256, 512), 0) // 32
+    head_lane = lax.broadcasted_iota(jnp.int32, (256, 512), 1) // 64
     upper = lax.broadcasted_iota(jnp.int32, (64, 64), 0) < 32
+
+    def scores_of(s):
+        wide = jnp.concatenate([query_t[:, s * 64 : (s + 1) * 64]] * 8, axis=1)
+        diag = jnp.where(head_row == head_lane, wide, jnp.zeros_like(wide))
+        scores = jnp.dot(keys[s * 512 : (s + 1) * 512], diag, preferred_element_type=F32)
+        return scores + bias_ref[...].astype(F32)
+
+    ahead = scores_of(0)
     for s in range(4):
-        mine = query_t[:, s * 64 : (s + 1) * 64]
-        twice = jnp.concatenate([mine, mine], axis=1)
-        key = keys[s * 512 : (s + 1) * 512]
+        scores = ahead
+        if s < 3:
+            ahead = scores_of(s + 1)
+        weights, scale = exp_rows(scores)
         parts = []
         for p in range(4):
-            diag = jnp.where(head_row == 2 * p + head_lane, twice, jnp.zeros_like(twice))
-            scores = jnp.dot(key, diag, preferred_element_type=F32)
-            scores = scores + bias_ref[:, p * 128 : (p + 1) * 128].astype(F32)
-            weights, scale = exp_rows(scores)
+            lanes = slice(p * 128, (p + 1) * 128)
             mixed = jnp.dot(
                 values[p * 64 : (p + 1) * 64, s * 512 : (s + 1) * 512],
-                weights,
+                weights[:, lanes],
                 preferred_element_type=F32,
             )
-            mixed = mixed * scale
+            mixed = mixed * scale[:, lanes]
             parts.append(jnp.where(upper, mixed[:, :64], mixed[:, 64:]))
         attended_t = jnp.concatenate(parts, axis=0)
         gated = (gate_t[:, s * 64 : (s + 1) * 64] * attended_t).astype(BF)
@@ -166,13 +183,28 @@
     value_t = mm(w_ref[:, 512:768], normed, TT).astype(BF)
     query_t = (mm(w_ref[:, 0:256], normed, TT) * SCALE).astype(BF)
     gate_t = sigmoid(mm(w_ref[:, 768:1024], normed, TT))
-    head_row = lax.broadcasted_iota(jnp.int32, (256, 256), 0) // 32
+    head_row = lax.broadcasted_iota(jnp.int32, (256, 1024), 0) // 32
+    head_lane = lax.broadcasted_iota(jnp.int32, (256, 1024), 1) // 256
+    wide = jnp.concatenate([query_t] * 4, axis=1)
+
+    def scores_of(group):
+        diag = jnp.where(head_row == head_lane + group * 4, wide, jnp.zeros_like(wide))
+        return jnp.dot(key, diag, preferred_element_type=F32)
+
     parts = []
-    for h in range(8):
-        diag = jnp.where(head_row == h, query_t, jnp.zeros_like(query_t))
-        weights, scale = exp_rows(jnp.dot(key, diag, preferred_element_type=F32))
-        mixed = jnp.dot(value_t[h * 32 : (h + 1) * 32], weights, preferred_element_type=F32)
-        parts.append(mixed * scale)
+    ahead = scores_of(0)
+    for group in range(2):
+        scores = ahead
+        if group == 0:
+            ahead = scores_of(1)
+        weights, scale = exp_rows(scores)
+        for k in range(4):
+            h = group * 4 + k
+            lanes = slice(k * 256, (k + 1) * 256)
+            mixed = jnp.dot(
+                value_t[h * 32 : (h + 1) * 32], weights[:, lanes], preferred_element_type=F32
+            )
+            parts.append(mixed * scale[:, lanes])
     gated = (gate_t * jnp.concatenate(parts, axis=0)).astype(BF)
     result = (x + mm(gated, wo_ref[...], TN)).astype(BF)
     factors = mm(wf_ref[...], layer_norm(result).astype(BF), NT).astype(BF)
@@ -264,11 +296,13 @@
 
 
 def triangle_kernel(place, left_ref, back_ref, *refs):
-    rights, out_ref = refs[:8], refs[8]
+    same, other, out_ref = refs[:4], refs[4:6], refs[6]
     left = left_ref[...]
     lane = lax.broadcasted_iota(jnp.int32, (64, 128), 1) < 64
     for m in range(8):
-        product = mm(rights[m][...], left, TN)
+        step = m // 2
+        right = other[step % 2][step // 2] if m % 2 else same[step][...]
+        product = mm(right, left, TN)
         block = jnp.where(lane, product[:64], product[64:]).astype(BF)
         target = source_of(col_of(place), m) * 2
         for b in range(4):
@@ -318,12 +352,12 @@
 
 
 def gather_col(x):
-    parts = {(0, 0): x}
-    for step in (1, 3, 2):
-        parts[step, 0] = shifted(x, step, 0)
-    for step in (0, 1, 3, 2):
-        parts[step, 1] = shifted(parts[step, 0], 0, 1)
-    return [parts[m // 2, m % 2] for m in range(8)]
+    same, other = {0: x}, {}
+    for step in (2, 1, 3):
+        same[step] = shifted(x, step, 0)
+    for pair in ((0, 2), (1, 3)):
+        other[pair[0]] = shifted(jnp.stack([same[k] for k in pair]), 0, 1)
+    return [same[k] for k in range(4)], [other[0], other[1]]
 
 
 def local(
@@ -352,10 +386,17 @@
     bias = in_vmem(
         bias_kernel,
         [(16, 32, 512)],
-        [pltpu.VMEM((64, 32, 128), F32), pltpu.VMEM((16, 8, 128), F32)],
+        [
+            pltpu.VMEM((64, 32, 128), BF),
+            pltpu.VMEM((8, 128), BF),
+            pltpu.VMEM((64, 32, 128), F32),
+            pltpu.VMEM((16, 8, 128), F32),
+            pltpu.SemaphoreType.DMA((5,)),
+        ],
         place,
         pair_features,
         w_bias.T,
+        loose=2,
     )
     bias = exchange(bias, "row").reshape(512, 512)
 
@@ -410,8 +451,10 @@
     )
     message = exchange(message, both)
     tri_left = message[:, 0].reshape(512, 128)
-    rights = gather_col(message[:, 1].reshape(512, 128))
-    sums = in_vmem(triangle_kernel, [(64, 2, 8, 128)], [], place, tri_left, returning, *rights)
+    same, other = gather_col(message[:, 1].reshape(512, 128))
+    sums = in_vmem(
+        triangle_kernel, [(64, 2, 8, 128)], [], place, tri_left, returning, *same, *other
+    )
     sums = exchange(sums, both)
     parts = in_vmem(
         output_kernel,

time: 227 us -> 221 us (0.974)
  waiting for transfers between devices: 31.4 us -> 38.5 us
  starting transfers between devices: 82.7 us -> 78.4 us
  Pallas kernels: 20.5 us -> 16.9 us
  local copies, waits for them, and re-layouts: 3.79 us -> 0.8 us
    ppermute x12 -> x10, waiting for transfers between devices: 21.3 us -> 28.4 us  [shifted(): return lax.ppermute(x, 'col', perm)]
    ppermute x12 -> x10, starting transfers between devices: 53 us -> 48.6 us  [shifted(): return lax.ppermute(x, 'col', perm)]
    pallas_call x7, Pallas kernels: 19.6 us -> 16 us  [in_vmem(): pl.pallas_call(kernel, out_shape=outs, in_specs=[SM] + [HB] * loose + [VM...]
    unnamed x28 -> x22, local copies, waits for them, and re-layouts: 3.08 us -> 0.06 us
  transfers between devices with their start and end apart: 18 -> 16, of which waited for: 10 -> 10; matrix products, arithmetic and copies ran while one was open for 0% -> 0% of each run, Pallas kernels for 1% -> 2%
where the time goes in v5:
time: 221 us; the launch traced here: 220 us
  blocking collectives  84.5 us (38%)
  starting transfers between devices  78.4 us (35%)
  waiting for transfers between devices  38.5 us (17%)
  Pallas kernels  16.9 us (8%)
    all_to_all x4, blocking collectives, local(): exchange = lambda x, axis: lax.all_to_all(x, axis, 0, 0, tiled=True)  84.5 us
    ppermute x10, starting transfers between devices, shifted(): return lax.ppermute(x, 'col', perm)  48.6 us
    ppermute x10, waiting for transfers between devices, shifted(): return lax.ppermute(x, 'col', perm)  28.4 us
    all_to_all x3, starting transfers between devices, local(): exchange = lambda x, axis: lax.all_to_all(x, axis, 0, 0, tiled=True)  19.9 us
    pallas_call x7, Pallas kernels, in_vmem(): pl.pallas_call(kernel, out_shape=outs, in_specs=[SM] + [HB] * loose + [VM...  16 us
    ppermute x3, starting transfers between devices, local(): lax.ppermute(left, 'branch', [(b, b ^ mask) for b in range(4)])  9.86 us
    all_to_all x3, waiting for transfers between devices, local(): exchange = lambda x, axis: lax.all_to_all(x, axis, 0, 0, tiled=True)  6.41 us
  transfers between devices with their start and end apart: 16, of which 10 were waited for; matrix products, arithmetic and copies ran while one was open for 0% of the time, Pallas kernels for 2%

profile of v5, /device:TPU:32, one launch (start us, length us, event | category | flops | bytes accessed | tf_op | source)
XLA Modules:
  0.0 220.1 jit_solution(9016126186872393411)
XLA Ops:
  0.6 9.2 %collective-permute-start.1 = (bf16[4,64,256]{2,1,0:T(8,128)(2,1)}, bf16[4,64,256]{2,1,0:T(8,128)(2,1)S(1)}, u32[]{:S(2)}, u32[]{:S(2)}) collective-permute-start(bf16[4,64,256]{2,1,0:T(8,128)(2,1)} %refs_0_.1), channel_id=1, source_target_pairs={{0,2},{1,3},{2,4},{3,5},{4,6},{5,7},{6,0},{7,1},{8,10},{9,11},{10,... | collective-permute-start | bytes 393224 | tf_op jit(solution)/shard_map/ppermute | solution.py:351
  9.9 4.7 %collective-permute-start = (bf16[4,64,256]{2,1,0:T(8,128)(2,1)}, bf16[4,64,256]{2,1,0:T(8,128)(2,1)S(1)}, u32[]{:S(2)}, u32[]{:S(2)}) collective-permute-start(bf16[4,64,256]{2,1,0:T(8,128)(2,1)} %refs_0_.1), channel_id=1, source_target_pairs={{0,6},{1,7},{2,0},{3,1},{4,2},{5,3},{6,4},{7,5},{8,14},{9,15},{10,... | collective-permute-start | bytes 393224 | tf_op jit(solution)/shard_map/ppermute | solution.py:351
  14.6 3.6 %shard_map.131 = bf16[16,32,512]{2,1,0:T(8,128)(2,1)} custom-call(s32[1]{0:T(128)} %bitcast.place, bf16[64,32,128]{2,1,0:T(8,128)(2,1)} %pair_ref.3, bf16[8,128]{1,0:T(8,128)(2,1)} %bitcast.32), custom_call_target="tpu_custom_call" | custom-call | tf_op jit(solution)/shard_map/pallas_call | solution.py:51
  18.1 7.0 %all-to-all-start = ((bf16[16,32,512]{2,1,0:T(8,128)(2,1)}), bf16[16,32,512]{2,1,0:T(8,128)(2,1)S(1)}, u32[]{:S(2)}, u32[]{:S(2)}) async-start(bf16[16,32,512]{2,1,0:T(8,128)(2,1)} %shard_map.131), calls=%async_computation | async-start | bytes 1048576 | tf_op jit(solution)/shard_map/all_to_all | solution.py:379
  25.2 0.0 collective-permute-done.1.refs_2_
  25.2 3.0 %collective-permute-done.refs_1_ = bf16[4,64,256]{2,1,0:T(8,128)(2,1)S(1)} collective-permute-done((bf16[4,64,256]{2,1,0:T(8,128)(2,1)}, bf16[4,64,256]{2,1,0:T(8,128)(2,1)S(1)}, u32[]{:S(2)}, u32[]{:S(2)}) %collective-permute-start) | collective-permute-done | bytes 131104 | tf_op jit(solution)/shard_map/ppermute | solution.py:351
  28.3 1.9 collective-permute-start.3
  30.2 9.2 %collective-permute-start.2 = (bf16[4,64,256]{2,1,0:T(8,128)(2,1)S(1)}, bf16[4,64,256]{2,1,0:T(8,128)(2,1)S(1)}, u32[]{:S(2)}, u32[]{:S(2)}) collective-permute-start(bf16[4,64,256]{2,1,0:T(8,128)(2,1)S(1)} %copy-done.3), channel_id=1, source_target_pairs={{0,4},{1,5},{2,6},{3,7},{4,0},{5,1},{6,2},{7,3},{8,12},{9,13},{10,... | collective-permute-start | bytes 393224 | tf_op jit(solution)/shard_map/ppermute | solution.py:351
  39.5 8.2 %collective-permute-done.2.refs_3_ = bf16[4,64,256]{2,1,0:T(8,128)(2,1)S(1)} collective-permute-done((bf16[4,64,256]{2,1,0:T(8,128)(2,1)S(1)}, bf16[4,64,256]{2,1,0:T(8,128)(2,1)S(1)}, u32[]{:S(2)}, u32[]{:S(2)}) %collective-permute-start.2) | collective-permute-done | bytes 131104 | tf_op jit(solution)/shard_map/ppermute | solution.py:351
  47.6 1.9 collective-permute-start.4
  49.6 1.3 collective-permute-done.4.refs_5_
  50.9 0.0 all-to-all-done
  50.9 0.0 copy-start.2
  50.9 0.0 copy-start.7
  50.9 0.0 copy-start.8
  50.9 4.4 %shard_map.132 = bf16[64,8,128]{2,1,0:T(8,128)(2,1)S(1)} custom-call(s32[1]{0:T(128)} %bitcast.place, bf16[4,64,256]{2,1,0:T(8,128)(2,1)S(1)} %copy-done.3, bf16[4,64,256]{2,1,0:T(8,128)(2,1)S(1)} %collective-permute-done.refs_1_, bf16[4,64,256]{2,1,0:T(8,128)(2,1)S(1)} %collective-permute-done.1.refs_2_, ...), custom_call_target="tpu_custom_call" | custom-call | tf_op jit(solution)/shard_map/pallas_call | solution.py:51
  55.3 27.0 %all_to_all.35.x_ref = bf16[64,8,128]{2,1,0:T(8,128)(2,1)S(1)} all-to-all(bf16[64,8,128]{2,1,0:T(8,128)(2,1)S(1)} %shard_map.132), channel_id=1, replica_groups=mesh['branch'=4,'row'=16,'col'=8] {'branch','row'}, dimensions={0} | all-to-all | bytes 262144 | tf_op jit(solution)/shard_map/all_to_all | solution.py:379
  82.3 2.7 %shard_map.133 = (bf16[64,8,128]{2,1,0:T(8,128)(2,1)S(1)}, bf16[32,256]{1,0:T(8,128)(2,1)S(1)}, bf16[8,32,256]{2,1,0:T(8,128)(2,1)}) custom-call(s32[1]{0:T(128)} %bitcast.place, bf16[64,8,128]{2,1,0:T(8,128)(2,1)S(1)} %all_to_all.35.x_ref, bf16[256,1024]{1,0:T(8,128)(2,1)S(1)} %copy-done.2, bf16[256,256]{1,0:T(8,128)(2,1)S(1)} %copy-done.7, ...), custom_call_target="tpu_custom_call" | custom-call | tf_op jit(solution)/shard_map/pallas_call | solution.py:51
  84.9 7.7 %all-to-all-start.2 = ((bf16[8,32,256]{2,1,0:T(8,128)(2,1)}), bf16[8,32,256]{2,1,0:T(8,128)(2,1)S(1)}, u32[]{:S(2)}, u32[]{:S(2)}) async-start(bf16[8,32,256]{2,1,0:T(8,128)(2,1)} %get-tuple-element.7), calls=%async_computation.2 | async-start | bytes 262144 | tf_op jit(solution)/shard_map/all_to_all | solution.py:379
  92.6 2.3 %collective-permute-start.7 = (bf16[32,256]{1,0:T(8,128)(2,1)S(1)}, bf16[32,256]{1,0:T(8,128)(2,1)S(1)}, u32[]{:S(2)}, u32[]{:S(2)}) collective-permute-start(bf16[32,256]{1,0:T(8,128)(2,1)S(1)} %get-tuple-element.8.refs_0_), channel_id=1, source_target_pairs={{0,384},{128,256},{256,128},{384,0},{1,385},{129,257},{257,129},{3... | collective-permute-start | bytes 49160 | tf_op jit(solution)/shard_map/ppermute | solution.py:433
  94.9 5.6 %collective-permute-start.6 = (bf16[32,256]{1,0:T(8,128)(2,1)S(1)}, bf16[32,256]{1,0:T(8,128)(2,1)S(1)}, u32[]{:S(2)}, u32[]{:S(2)}) collective-permute-start(bf16[32,256]{1,0:T(8,128)(2,1)S(1)} %get-tuple-element.8.refs_0_), channel_id=1, source_target_pairs={{0,256},{128,384},{256,0},{384,128},{1,257},{129,385},{257,1},{385... | collective-permute-start | bytes 49160 | tf_op jit(solution)/shard_map/ppermute | solution.py:433
  100.6 1.9 collective-permute-start.5
  102.5 1.7 collective-permute-done.6.refs_2_
  104.2 2.0 collective-permute-done.5.refs_1_
  106.2 1.9 all-to-all-done.2.right_ref
  108.1 0.1 shard_map.134
  108.2 0.0 copy-start
  108.3 0.0 copy-start.4
  108.3 0.0 copy-start.6
  108.3 22.9 %all_to_all.36.factor_ref = bf16[16,160,256]{2,1,0:T(8,128)(2,1)S(1)} all-to-all(bf16[16,160,256]{2,1,0:T(8,128)(2,1)S(1)} %shard_map.134), channel_id=1, replica_groups=mesh['branch'=4,'row'=16,'col'=8] {'row'}, dimensions={0} | all-to-all | bytes 2621440 | tf_op jit(solution)/shard_map/all_to_all | solution.py:379
  131.2 3.1 %shard_map.135 = (bf16[512,128]{1,0:T(8,128)(2,1)S(1)}, bf16[64,2,8,128]{3,2,1,0:T(8,128)(2,1)S(1)}) custom-call(s32[1]{0:T(128)} %bitcast.place, bf16[16,160,256]{2,1,0:T(8,128)(2,1)S(1)} %all_to_all.36.factor_ref, bf16[64,32,128]{2,1,0:T(8,128)(2,1)S(1)} %copy-done, bf16[1024,128]{1,0:T(8,128)(2,1)S(1)} %copy-done.4, bf16[128,512]{1,0:T(8,128)(2,1)S(1)} %copy-done.6), custom_call_target="tpu_custom_call" | custom-call | tf_op jit(solution)/shard_map/pallas_call | solution.py:51
  134.3 16.8 %all_to_all.37 = bf16[64,2,8,128]{3,2,1,0:T(8,128)(2,1)S(1)} all-to-all(bf16[64,2,8,128]{3,2,1,0:T(8,128)(2,1)S(1)} %get-tuple-element.9), channel_id=1, replica_groups=mesh['branch'=4,'row'=16,'col'=8] {'branch','row'}, dimensions={0} | all-to-all | bytes 524288 | tf_op jit(solution)/shard_map/all_to_all | solution.py:379
  151.2 0.1 slice_bitcast_fusion.1
  151.2 3.6 %collective-permute-start.10 = (bf16[512,128]{1,0:T(8,128)(2,1)S(1)}, bf16[512,128]{1,0:T(8,128)(2,1)S(1)}, u32[]{:S(2)}, u32[]{:S(2)}) collective-permute-start(bf16[512,128]{1,0:T(8,128)(2,1)S(1)} %get-tuple-element.13.refs_0_), channel_id=1, source_target_pairs={{0,2},{1,3},{2,4},{3,5},{4,6},{5,7},{6,0},{7,1},{8,10},{9,11},{10,... | collective-permute-start | bytes 393224 | tf_op jit(solution)/shard_map/ppermute | solution.py:351
  154.9 6.1 %collective-permute-start.8 = (bf16[512,128]{1,0:T(8,128)(2,1)S(1)}, bf16[512,128]{1,0:T(8,128)(2,1)S(1)}, u32[]{:S(2)}, u32[]{:S(2)}) collective-permute-start(bf16[512,128]{1,0:T(8,128)(2,1)S(1)} %get-tuple-element.13.refs_0_), channel_id=1, source_target_pairs={{0,6},{1,7},{2,0},{3,1},{4,2},{5,3},{6,4},{7,5},{8,14},{9,15},{10,... | collective-permute-start | bytes 393224 | tf_op jit(solution)/shard_map/ppermute | solution.py:351
  161.0 8.1 %collective-permute-start.9 = (bf16[512,128]{1,0:T(8,128)(2,1)S(1)}, bf16[512,128]{1,0:T(8,128)(2,1)S(1)}, u32[]{:S(2)}, u32[]{:S(2)}) collective-permute-start(bf16[512,128]{1,0:T(8,128)(2,1)S(1)} %get-tuple-element.13.refs_0_), channel_id=1, source_target_pairs={{0,4},{1,5},{2,6},{3,7},{4,0},{5,1},{6,2},{7,3},{8,12},{9,13},{10,... | collective-permute-start | bytes 393224 | tf_op jit(solution)/shard_map/ppermute | solution.py:351
  169.1 0.9 collective-permute-done.8.refs_1_
  170.1 1.9 collective-permute-start.12
  172.0 13.4 %collective-permute-done.9.refs_2_ = bf16[512,128]{1,0:T(8,128)(2,1)S(1)} collective-permute-done((bf16[512,128]{1,0:T(8,128)(2,1)S(1)}, bf16[512,128]{1,0:T(8,128)(2,1)S(1)}, u32[]{:S(2)}, u32[]{:S(2)}) %collective-permute-start.9) | collective-permute-done | bytes 131104 | tf_op jit(solution)/shard_map/ppermute | solution.py:351
  185.5 1.9 collective-permute-start.11
  187.4 1.5 collective-permute-done.11.refs_4_
  188.9 0.5 shard_map.136
  189.4 17.7 %all_to_all.38.sum_ref = bf16[64,2,8,128]{3,2,1,0:T(8,128)(2,1)S(1)} all-to-all(bf16[64,2,8,128]{3,2,1,0:T(8,128)(2,1)S(1)} %shard_map.136), channel_id=1, replica_groups=mesh['branch'=4,'row'=16,'col'=8] {'branch','row'}, dimensions={0} | all-to-all | bytes 524288 | tf_op jit(solution)/shard_map/all_to_all | solution.py:379
  207.1 1.7 shard_map.137
  208.9 5.2 %all-to-all-start.6 = ((bf16[4,4,32,128]{3,2,1,0:T(8,128)(2,1)}), bf16[4,4,32,128]{3,2,1,0:T(8,128)(2,1)S(1)}, u32[]{:S(2)}, u32[]{:S(2)}) async-start(bf16[4,4,32,128]{3,2,1,0:T(8,128)(2,1)} %shard_map.137), calls=%async_computation.6 | async-start | bytes 262144 | tf_op jit(solution)/shard_map/all_to_all | solution.py:379
  214.1 0.7 copy.14
  214.8 4.5 %all-to-all-done.6.x_ref = bf16[4,4,32,128]{3,2,1,0:T(8,128)(2,1)S(1)} async-done(((bf16[4,4,32,128]{3,2,1,0:T(8,128)(2,1)}), bf16[4,4,32,128]{3,2,1,0:T(8,128)(2,1)S(1)}, u32[]{:S(2)}, u32[]{:S(2)}) %all-to-all-start.6) | async-done | bytes 131104 | tf_op jit(solution)/shard_map/all_to_all | solution.py:379
  219.3 0.8 unpack.1
  (24 shorter events, 0.1 us)
Async XLA Ops:
  0.6 27.6 %copy-start.3 = (bf16[4,64,256]{2,1,0:T(8,128)(2,1)S(1)}, bf16[4,64,256]{2,1,0:T(8,128)(2,1)}, u32[]{:S(2)}) copy-start(bf16[4,64,256]{2,1,0:T(8,128)(2,1)} %refs_0_.1) | copy-start | bytes 393220
  0.6 24.6 %collective-permute-start.1 = (bf16[4,64,256]{2,1,0:T(8,128)(2,1)}, bf16[4,64,256]{2,1,0:T(8,128)(2,1)S(1)}, u32[]{:S(2)}, u32[]{:S(2)}) collective-permute-start(bf16[4,64,256]{2,1,0:T(8,128)(2,1)} %refs_0_.1), channel_id=1, source_target_pairs={{0,2},{1,3},{2,4},{3,5},{4,6},{5,7},{6,0},{7,1},{8,10},{9,11},{10,... | collective-permute-start | bytes 393224 | tf_op jit(solution)/shard_map/ppermute | solution.py:351
  9.9 18.4 %collective-permute-start = (bf16[4,64,256]{2,1,0:T(8,128)(2,1)}, bf16[4,64,256]{2,1,0:T(8,128)(2,1)S(1)}, u32[]{:S(2)}, u32[]{:S(2)}) collective-permute-start(bf16[4,64,256]{2,1,0:T(8,128)(2,1)} %refs_0_.1), channel_id=1, source_target_pairs={{0,6},{1,7},{2,0},{3,1},{4,2},{5,3},{6,4},{7,5},{8,14},{9,15},{10,... | collective-permute-start | bytes 393224 | tf_op jit(solution)/shard_map/ppermute | solution.py:351
  14.6 36.3 %copy-start.1 = (bf16[256,1024]{1,0:T(8,128)(2,1)S(1)}, bf16[256,1024]{1,0:T(8,128)(2,1)}, u32[]{:S(2)}) copy-start(bf16[256,1024]{1,0:T(8,128)(2,1)} %refs_6_.1) | copy-start | bytes 1572868
  14.6 36.3 %copy-start.5 = (bf16[256,256]{1,0:T(8,128)(2,1)S(1)}, bf16[256,256]{1,0:T(8,128)(2,1)}, u32[]{:S(2)}) copy-start(bf16[256,256]{1,0:T(8,128)(2,1)} %refs_8_.1) | copy-start | bytes 393220
  18.1 32.7 %all-to-all-start = ((bf16[16,32,512]{2,1,0:T(8,128)(2,1)}), bf16[16,32,512]{2,1,0:T(8,128)(2,1)S(1)}, u32[]{:S(2)}, u32[]{:S(2)}) async-start(bf16[16,32,512]{2,1,0:T(8,128)(2,1)} %shard_map.131), calls=%async_computation | async-start | bytes 1048576 | tf_op jit(solution)/shard_map/all_to_all | solution.py:379
  28.3 22.6 %collective-permute-start.3 = (bf16[3,4,64,256]{3,2,1,0:T(8,128)(2,1)S(1)}, bf16[3,4,64,256]{3,2,1,0:T(8,128)(2,1)S(1)}, u32[]{:S(2)}, u32[]{:S(2)}) collective-permute-start(bf16[3,4,64,256]{3,2,1,0:T(8,128)(2,1)S(1)} %pad_maximum_fusion), channel_id=1, source_target_pairs={{0,1},{1,0},{2,3},{3,2},{4,5},{5,4},{6,7},{7,6},{8,9},{9,8},{10,11... | collective-permute-start | bytes 1179656 | tf_op jit(solution)/shard_map/ppermute | solution.py:351
  30.2 17.4 %collective-permute-start.2 = (bf16[4,64,256]{2,1,0:T(8,128)(2,1)S(1)}, bf16[4,64,256]{2,1,0:T(8,128)(2,1)S(1)}, u32[]{:S(2)}, u32[]{:S(2)}) collective-permute-start(bf16[4,64,256]{2,1,0:T(8,128)(2,1)S(1)} %copy-done.3), channel_id=1, source_target_pairs={{0,4},{1,5},{2,6},{3,7},{4,0},{5,1},{6,2},{7,3},{8,12},{9,13},{10,... | collective-permute-start | bytes 393224 | tf_op jit(solution)/shard_map/ppermute | solution.py:351
  47.6 3.2 %collective-permute-start.4 = (bf16[4,64,256]{2,1,0:T(8,128)(2,1)S(1)}, bf16[4,64,256]{2,1,0:T(8,128)(2,1)S(1)}, u32[]{:S(2)}, u32[]{:S(2)}) collective-permute-start(bf16[4,64,256]{2,1,0:T(8,128)(2,1)S(1)} %collective-permute-done.2.refs_3_), channel_id=1, source_target_pairs={{0,1},{1,0},{2,3},{3,2},{4,5},{5,4},{6,7},{7,6},{8,9},{9,8},{10,11... | collective-permute-start | bytes 393224 | tf_op jit(solution)/shard_map/ppermute | solution.py:351
  50.9 31.4 %copy-start.2 = (bf16[256,1024]{1,0:T(8,128)(2,1)S(1)}, bf16[256,1024]{1,0:T(8,128)(2,1)}, u32[]{:S(2)}) copy-start(bf16[256,1024]{1,0:T(8,128)(2,1)} %w_ref.3) | copy-start | bytes 1572868
  50.9 31.4 %copy-start.7 = (bf16[256,256]{1,0:T(8,128)(2,1)S(1)}, bf16[256,256]{1,0:T(8,128)(2,1)}, u32[]{:S(2)}) copy-start(bf16[256,256]{1,0:T(8,128)(2,1)} %wo_ref.2) | copy-start | bytes 393220
  50.9 31.3 %copy-start.8 = (bf16[256,64]{0,1:T(8,128)(2,1)S(1)}, bf16[256,64]{0,1:T(8,128)(2,1)}, u32[]{:S(2)}) copy-start(bf16[256,64]{0,1:T(8,128)(2,1)} %param.19) | copy-start | bytes 98308
  84.9 23.2 %all-to-all-start.2 = ((bf16[8,32,256]{2,1,0:T(8,128)(2,1)}), bf16[8,32,256]{2,1,0:T(8,128)(2,1)S(1)}, u32[]{:S(2)}, u32[]{:S(2)}) async-start(bf16[8,32,256]{2,1,0:T(8,128)(2,1)} %get-tuple-element.7), calls=%async_computation.2 | async-start | bytes 262144 | tf_op jit(solution)/shard_map/all_to_all | solution.py:379
  92.6 9.9 %collective-permute-start.7 = (bf16[32,256]{1,0:T(8,128)(2,1)S(1)}, bf16[32,256]{1,0:T(8,128)(2,1)S(1)}, u32[]{:S(2)}, u32[]{:S(2)}) collective-permute-start(bf16[32,256]{1,0:T(8,128)(2,1)S(1)} %get-tuple-element.8.refs_0_), channel_id=1, source_target_pairs={{0,384},{128,256},{256,128},{384,0},{1,385},{129,257},{257,129},{3... | collective-permute-start | bytes 49160 | tf_op jit(solution)/shard_map/ppermute | solution.py:433
  94.9 9.2 %collective-permute-start.6 = (bf16[32,256]{1,0:T(8,128)(2,1)S(1)}, bf16[32,256]{1,0:T(8,128)(2,1)S(1)}, u32[]{:S(2)}, u32[]{:S(2)}) collective-permute-start(bf16[32,256]{1,0:T(8,128)(2,1)S(1)} %get-tuple-element.8.refs_0_), channel_id=1, source_target_pairs={{0,256},{128,384},{256,0},{384,128},{1,257},{129,385},{257,1},{385... | collective-permute-start | bytes 49160 | tf_op jit(solution)/shard_map/ppermute | solution.py:433
  100.6 5.6 %collective-permute-start.5 = (bf16[32,256]{1,0:T(8,128)(2,1)S(1)}, bf16[32,256]{1,0:T(8,128)(2,1)S(1)}, u32[]{:S(2)}, u32[]{:S(2)}) collective-permute-start(bf16[32,256]{1,0:T(8,128)(2,1)S(1)} %get-tuple-element.8.refs_0_), channel_id=1, source_target_pairs={{0,128},{128,0},{256,384},{384,256},{1,129},{129,1},{257,385},{385... | collective-permute-start | bytes 49160 | tf_op jit(solution)/shard_map/ppermute | solution.py:433
  108.2 23.0 %copy-start = (bf16[64,32,128]{2,1,0:T(8,128)(2,1)S(1)}, bf16[64,32,128]{2,1,0:T(8,128)(2,1)}, u32[]{:S(2)}) copy-start(bf16[64,32,128]{2,1,0:T(8,128)(2,1)} %pair_ref.3) | copy-start | bytes 1572868
  108.3 23.0 %copy-start.4 = (bf16[1024,128]{1,0:T(8,128)(2,1)S(1)}, bf16[1024,128]{1,0:T(8,128)(2,1)}, u32[]{:S(2)}) copy-start(bf16[1024,128]{1,0:T(8,128)(2,1)} %wo_ref.3) | copy-start | bytes 786436
  108.3 23.0 %copy-start.6 = (bf16[128,512]{1,0:T(8,128)(2,1)S(1)}, bf16[128,512]{1,0:T(8,128)(2,1)}, u32[]{:S(2)}) copy-start(bf16[128,512]{1,0:T(8,128)(2,1)} %w_ref.4) | copy-start | bytes 393220
  151.2 17.9 %collective-permute-start.10 = (bf16[512,128]{1,0:T(8,128)(2,1)S(1)}, bf16[512,128]{1,0:T(8,128)(2,1)S(1)}, u32[]{:S(2)}, u32[]{:S(2)}) collective-permute-start(bf16[512,128]{1,0:T(8,128)(2,1)S(1)} %get-tuple-element.13.refs_0_), channel_id=1, source_target_pairs={{0,2},{1,3},{2,4},{3,5},{4,6},{5,7},{6,0},{7,1},{8,10},{9,11},{10,... | collective-permute-start | bytes 393224 | tf_op jit(solution)/shard_map/ppermute | solution.py:351
  154.9 15.2 %collective-permute-start.8 = (bf16[512,128]{1,0:T(8,128)(2,1)S(1)}, bf16[512,128]{1,0:T(8,128)(2,1)S(1)}, u32[]{:S(2)}, u32[]{:S(2)}) collective-permute-start(bf16[512,128]{1,0:T(8,128)(2,1)S(1)} %get-tuple-element.13.refs_0_), channel_id=1, source_target_pairs={{0,6},{1,7},{2,0},{3,1},{4,2},{5,3},{6,4},{7,5},{8,14},{9,15},{10,... | collective-permute-start | bytes 393224 | tf_op jit(solution)/shard_map/ppermute | solution.py:351
  161.0 24.4 %collective-permute-start.9 = (bf16[512,128]{1,0:T(8,128)(2,1)S(1)}, bf16[512,128]{1,0:T(8,128)(2,1)S(1)}, u32[]{:S(2)}, u32[]{:S(2)}) collective-permute-start(bf16[512,128]{1,0:T(8,128)(2,1)S(1)} %get-tuple-element.13.refs_0_), channel_id=1, source_target_pairs={{0,4},{1,5},{2,6},{3,7},{4,0},{5,1},{6,2},{7,3},{8,12},{9,13},{10,... | collective-permute-start | bytes 393224 | tf_op jit(solution)/shard_map/ppermute | solution.py:351
  170.1 17.3 %collective-permute-start.12 = (bf16[2,512,128]{2,1,0:T(8,128)(2,1)S(1)}, bf16[2,512,128]{2,1,0:T(8,128)(2,1)S(1)}, u32[]{:S(2)}, u32[]{:S(2)}) collective-permute-start(bf16[2,512,128]{2,1,0:T(8,128)(2,1)S(1)} %pad_maximum_fusion.2), channel_id=1, source_target_pairs={{0,1},{1,0},{2,3},{3,2},{4,5},{5,4},{6,7},{7,6},{8,9},{9,8},{10,11... | collective-permute-start | bytes 786440 | tf_op jit(solution)/shard_map/ppermute | solution.py:351
  185.4 21.7 %copy-start.9 = (bf16[128,128]{1,0:T(8,128)(2,1)S(1)}, bf16[128,128]{1,0:T(8,128)(2,1)}, u32[]{:S(2)}) copy-start(bf16[128,128]{1,0:T(8,128)(2,1)} %wg_ref.1) | copy-start | bytes 98308
  185.4 21.7 %copy-start.10 = (bf16[128,128]{1,0:T(8,128)(2,1)S(1)}, bf16[128,128]{1,0:T(8,128)(2,1)}, u32[]{:S(2)}) copy-start(bf16[128,128]{1,0:T(8,128)(2,1)} %w_ref.5) | copy-start | bytes 98308
  185.5 3.4 %collective-permute-start.11 = (bf16[2,512,128]{2,1,0:T(8,128)(2,1)S(1)}, bf16[2,512,128]{2,1,0:T(8,128)(2,1)S(1)}, u32[]{:S(2)}, u32[]{:S(2)}) collective-permute-start(bf16[2,512,128]{2,1,0:T(8,128)(2,1)S(1)} %pad_maximum_fusion.1), channel_id=1, source_target_pairs={{0,1},{1,0},{2,3},{3,2},{4,5},{5,4},{6,7},{7,6},{8,9},{9,8},{10,11... | collective-permute-start | bytes 786440 | tf_op jit(solution)/shard_map/ppermute | solution.py:351
  208.9 10.4 %all-to-all-start.6 = ((bf16[4,4,32,128]{3,2,1,0:T(8,128)(2,1)}), bf16[4,4,32,128]{3,2,1,0:T(8,128)(2,1)S(1)}, u32[]{:S(2)}, u32[]{:S(2)}) async-start(bf16[4,4,32,128]{3,2,1,0:T(8,128)(2,1)} %shard_map.137), calls=%async_computation.6 | async-start | bytes 262144 | tf_op jit(solution)/shard_map/all_to_all | solution.py:379

commit v6 on v5

--- a/solution.py
+++ b/solution.py
@@ -44,19 +44,21 @@
 HB = pl.BlockSpec(memory_space=pltpu.HBM)
 
 
-def in_vmem(kernel, outs, scratch, place, *args, loose=0):
+def in_vmem(kernel, outs, scratch, place, *args, loose=0, results=0):
     loosely = [pltpu.with_memory_space_constraint(a, pltpu.HBM) for a in args[:loose]]
     fixed = [pltpu.with_memory_space_constraint(a, pltpu.VMEM) for a in args[loose:]]
-    outs = tuple(pltpu.VMEM(shape, BF) for shape in outs)
-    results = pl.pallas_call(
+    inner = len(outs) - results
+    shapes = [pltpu.VMEM(shape, BF) for shape in outs[:inner]]
+    shapes += [jax.ShapeDtypeStruct(shape, BF) for shape in outs[inner:]]
+    outputs = pl.pallas_call(
         kernel,
-        out_shape=outs,
+        out_shape=tuple(shapes),
         in_specs=[SM] + [HB] * loose + [VM] * len(fixed),
-        out_specs=(VM,) * len(outs),
+        out_specs=(VM,) * inner + (pl.BlockSpec(),) * results,
         scratch_shapes=scratch,
         compiler_params=pltpu.CompilerParams(vmem_limit_bytes=24 << 20),
     )(place, *loosely, *fixed)
-    return results if len(outs) > 1 else results[0]
+    return outputs if len(outs) > 1 else outputs[0]
 
 
 def col_of(place):
@@ -296,22 +298,26 @@
 
 
 def triangle_kernel(place, left_ref, back_ref, *refs):
-    same, other, out_ref = refs[:4], refs[4:6], refs[6]
+    same, near, far, out_ref = refs[:4], refs[4], refs[5], refs[6]
     left = left_ref[...]
     lane = lax.broadcasted_iota(jnp.int32, (64, 128), 1) < 64
+    steps = (0, 1, 3, 2)
     for m in range(8):
-        step = m // 2
-        right = other[step % 2][step // 2] if m % 2 else same[step][...]
+        step = steps[m // 2]
+        if m % 2 == 0:
+            right = same[m // 2][...]
+        else:
+            right = far[...] if step == 2 else near[m // 2]
         product = mm(right, left, TN)
         block = jnp.where(lane, product[:64], product[64:]).astype(BF)
-        target = source_of(col_of(place), m) * 2
+        target = source_of(col_of(place), step * 2 + m % 2) * 2
         for b in range(4):
             for h in range(2):
                 out_ref[b * 16 + target + h, 0] = block[(b * 2 + h) * 8 : (b * 2 + h + 1) * 8]
     out_ref[:, 1] = back_ref[...]
 
 
-def output_kernel(place, sum_ref, mid_ref, wg_ref, w_ref, out_ref, scratch):
+def output_kernel(place, sum_ref, mid_ref, wg_ref, w_ref, out_ref, back_ref, scratch, rows):
     del place
     sums = sum_ref[:, 0].astype(F32)
     fold = lambda v: (v + pltpu.roll(v, 64, 1)) * (1.0 / 128)
@@ -336,6 +342,13 @@
         part = (residual + gate * mixed).astype(BF)
         for b in range(4):
             out_ref[b, j] = part[b * 32 : (b + 1) * 32]
+    rows[...] = sum_ref[:, 1].astype(F32)
+    order = [(b * 2 + h) * 8 for h in range(2) for b in range(4)]
+    for s in range(4):
+        for half in range(2):
+            block = rows[:, half * 4 + s, :]
+            block = jnp.concatenate([block[k : k + 8] for k in order], axis=0)
+            back_ref[s, :, half * 128 : (half + 1) * 128] = block.astype(BF)
 
 
 def unpack_kernel(x_ref, out_ref):
@@ -352,12 +365,12 @@
 
 
 def gather_col(x):
-    same, other = {0: x}, {}
-    for step in (2, 1, 3):
-        same[step] = shifted(x, step, 0)
-    for pair in ((0, 2), (1, 3)):
-        other[pair[0]] = shifted(jnp.stack([same[k] for k in pair]), 0, 1)
-    return [same[k] for k in range(4)], [other[0], other[1]]
+    same = [x]
+    for step in (1, 3, 2):
+        same.append(shifted(x, step, 0))
+    near = shifted(jnp.stack(same[:3]), 0, 1)
+    far = shifted(same[3], 0, 1)
+    return same + [near, far]
 
 
 def local(
@@ -378,11 +391,7 @@
     place = lax.axis_index(("branch", "row", "col")).astype(jnp.int32).reshape(1)
     exchange = lambda x, axis: lax.all_to_all(x, axis, 0, 0, tiled=True)
 
-    blocks = [alignment]
-    for step in (1, 3, 2):
-        blocks.append(shifted(alignment, step, 0))
-    blocks.append(shifted(jnp.stack(blocks[:3]), 0, 1))
-    blocks.append(shifted(blocks[3], 0, 1))
+    blocks = gather_col(alignment)
     bias = in_vmem(
         bias_kernel,
         [(16, 32, 512)],
@@ -451,20 +460,19 @@
     )
     message = exchange(message, both)
     tri_left = message[:, 0].reshape(512, 128)
-    same, other = gather_col(message[:, 1].reshape(512, 128))
-    sums = in_vmem(
-        triangle_kernel, [(64, 2, 8, 128)], [], place, tri_left, returning, *same, *other
-    )
+    rights = gather_col(message[:, 1].reshape(512, 128))
+    sums = in_vmem(triangle_kernel, [(64, 2, 8, 128)], [], place, tri_left, returning, *rights)
     sums = exchange(sums, both)
-    parts = in_vmem(
+    parts, alignment_out = in_vmem(
         output_kernel,
-        [(4, 4, 32, 128)],
-        [pltpu.VMEM((64, 8, 128), F32)],
+        [(4, 4, 32, 128), (4, 64, 256)],
+        [pltpu.VMEM((64, 8, 128), F32), pltpu.VMEM((64, 8, 128), F32)],
         place,
         sums,
         mid,
         w_triangle_gate,
         w_triangle_out,
+        results=1,
     )
     parts = exchange(parts, "branch")
     pair_out = pl.pallas_call(
@@ -473,8 +481,6 @@
         in_specs=[VM],
         name="unpack",
     )(pltpu.with_memory_space_constraint(parts, pltpu.VMEM))
-    back = sums[:, 1].reshape(4, 2, 8, 2, 4, 128)
-    alignment_out = jnp.transpose(back, (4, 1, 0, 2, 3, 5)).reshape(4, 64, 256)
     return (alignment_out, jnp.transpose(pair_out, (2, 0, 1)))
 
 

time: 221 us -> 231 us (1.045)
  blocking collectives: 84.5 us -> 100 us
  starting transfers between devices: 78.4 us -> 72.1 us
    all_to_all x4 -> x5, blocking collectives: 84.5 us -> 100 us  [local(): exchange = lambda x, axis: lax.all_to_all(x, axis, 0, 0, tiled=True)]
    ppermute x10, waiting for transfers between devices: 28.4 us -> 34 us  [shifted(): return lax.ppermute(x, 'col', perm)]
    all_to_all x3 -> x2, starting transfers between devices: 19.9 us -> 14.7 us  [local(): exchange = lambda x, axis: lax.all_to_all(x, axis, 0, 0, tiled=True)]
    all_to_all x3 -> x2, waiting for transfers between devices: 6.41 us -> 1.93 us  [local(): exchange = lambda x, axis: lax.all_to_all(x, axis, 0, 0, tiled=True)]
  transfers between devices with their start and end apart: 16 -> 15, of which waited for: 10 -> 10; matrix products, arithmetic and copies ran while one was open for 0% -> 0% of each run, Pallas kernels for 2% -> 2%
where the time goes in v6:
time: 231 us; the launch traced here: 230 us
  blocking collectives  100 us (43%)
  starting transfers between devices  72.1 us (31%)
  waiting for transfers between devices  39.7 us (17%)
  Pallas kernels  17 us (7%)
    all_to_all x5, blocking collectives, local(): exchange = lambda x, axis: lax.all_to_all(x, axis, 0, 0, tiled=True)  100 us
    ppermute x10, starting transfers between devices, shifted(): return lax.ppermute(x, 'col', perm)  47.5 us
    ppermute x10, waiting for transfers between devices, shifted(): return lax.ppermute(x, 'col', perm)  34 us
    pallas_call x7, Pallas kernels, in_vmem(): pl.pallas_call(kernel, out_shape=tuple(shapes), in_specs=[SM] + [HB] * lo...  16.1 us
    all_to_all x2, starting transfers between devices, local(): exchange = lambda x, axis: lax.all_to_all(x, axis, 0, 0, tiled=True)  14.7 us
    ppermute x3, starting transfers between devices, local(): lax.ppermute(left, 'branch', [(b, b ^ mask) for b in range(4)])  9.86 us
  transfers between devices with their start and end apart: 15, of which 10 were waited for; matrix products, arithmetic and copies ran while one was open for 0% of the time, Pallas kernels for 2%

profile of v6, /device:TPU:32, one launch (start us, length us, event | category | flops | bytes accessed | tf_op | source)
XLA Modules:
  0.0 230.0 jit_solution(7264235432564555398)
XLA Ops:
  0.6 9.2 %collective-permute-start.1 = (bf16[4,64,256]{2,1,0:T(8,128)(2,1)}, bf16[4,64,256]{2,1,0:T(8,128)(2,1)S(1)}, u32[]{:S(2)}, u32[]{:S(2)}) collective-permute-start(bf16[4,64,256]{2,1,0:T(8,128)(2,1)} %refs_0_.1), channel_id=1, source_target_pairs={{0,2},{1,3},{2,4},{3,5},{4,6},{5,7},{6,0},{7,1},{8,10},{9,11},{10,... | collective-permute-start | bytes 393224 | tf_op jit(solution)/shard_map/ppermute | solution.py:364
  9.9 4.7 %collective-permute-start = (bf16[4,64,256]{2,1,0:T(8,128)(2,1)}, bf16[4,64,256]{2,1,0:T(8,128)(2,1)S(1)}, u32[]{:S(2)}, u32[]{:S(2)}) collective-permute-start(bf16[4,64,256]{2,1,0:T(8,128)(2,1)} %refs_0_.1), channel_id=1, source_target_pairs={{0,6},{1,7},{2,0},{3,1},{4,2},{5,3},{6,4},{7,5},{8,14},{9,15},{10,... | collective-permute-start | bytes 393224 | tf_op jit(solution)/shard_map/ppermute | solution.py:364
  14.6 3.6 %shard_map.131 = bf16[16,32,512]{2,1,0:T(8,128)(2,1)} custom-call(s32[1]{0:T(128)} %bitcast.place, bf16[64,32,128]{2,1,0:T(8,128)(2,1)} %pair_ref.3, bf16[8,128]{1,0:T(8,128)(2,1)} %bitcast.24), custom_call_target="tpu_custom_call" | custom-call | tf_op jit(solution)/shard_map/pallas_call | solution.py:53
  18.1 7.0 %all-to-all-start = ((bf16[16,32,512]{2,1,0:T(8,128)(2,1)}), bf16[16,32,512]{2,1,0:T(8,128)(2,1)S(1)}, u32[]{:S(2)}, u32[]{:S(2)}) async-start(bf16[16,32,512]{2,1,0:T(8,128)(2,1)} %shard_map.131), calls=%async_computation | async-start | bytes 1048576 | tf_op jit(solution)/shard_map/all_to_all | solution.py:392
  25.2 0.0 collective-permute-done.1.refs_2_
  25.2 3.0 %collective-permute-done.refs_1_ = bf16[4,64,256]{2,1,0:T(8,128)(2,1)S(1)} collective-permute-done((bf16[4,64,256]{2,1,0:T(8,128)(2,1)}, bf16[4,64,256]{2,1,0:T(8,128)(2,1)S(1)}, u32[]{:S(2)}, u32[]{:S(2)}) %collective-permute-start) | collective-permute-done | bytes 131104 | tf_op jit(solution)/shard_map/ppermute | solution.py:364
  28.3 1.9 collective-permute-start.3
  30.2 9.2 %collective-permute-start.2 = (bf16[4,64,256]{2,1,0:T(8,128)(2,1)S(1)}, bf16[4,64,256]{2,1,0:T(8,128)(2,1)S(1)}, u32[]{:S(2)}, u32[]{:S(2)}) collective-permute-start(bf16[4,64,256]{2,1,0:T(8,128)(2,1)S(1)} %copy-done.3), channel_id=1, source_target_pairs={{0,4},{1,5},{2,6},{3,7},{4,0},{5,1},{6,2},{7,3},{8,12},{9,13},{10,... | collective-permute-start | bytes 393224 | tf_op jit(solution)/shard_map/ppermute | solution.py:364
  39.5 8.2 %collective-permute-done.2.refs_3_ = bf16[4,64,256]{2,1,0:T(8,128)(2,1)S(1)} collective-permute-done((bf16[4,64,256]{2,1,0:T(8,128)(2,1)S(1)}, bf16[4,64,256]{2,1,0:T(8,128)(2,1)S(1)}, u32[]{:S(2)}, u32[]{:S(2)}) %collective-permute-start.2) | collective-permute-done | bytes 131104 | tf_op jit(solution)/shard_map/ppermute | solution.py:364
  47.6 1.9 collective-permute-start.4
  49.6 1.3 collective-permute-done.4.refs_5_
  50.9 0.0 all-to-all-done
  50.9 0.0 copy-start.2
  50.9 0.0 copy-start.7
  50.9 0.0 copy-start.8
  50.9 4.4 %shard_map.132 = bf16[64,8,128]{2,1,0:T(8,128)(2,1)S(1)} custom-call(s32[1]{0:T(128)} %bitcast.place, bf16[4,64,256]{2,1,0:T(8,128)(2,1)S(1)} %copy-done.3, bf16[4,64,256]{2,1,0:T(8,128)(2,1)S(1)} %collective-permute-done.refs_1_, bf16[4,64,256]{2,1,0:T(8,128)(2,1)S(1)} %collective-permute-done.1.refs_2_, ...), custom_call_target="tpu_custom_call" | custom-call | tf_op jit(solution)/shard_map/pallas_call | solution.py:53
  55.3 27.0 %all_to_all.35.x_ref = bf16[64,8,128]{2,1,0:T(8,128)(2,1)S(1)} all-to-all(bf16[64,8,128]{2,1,0:T(8,128)(2,1)S(1)} %shard_map.132), channel_id=1, replica_groups=mesh['branch'=4,'row'=16,'col'=8] {'branch','row'}, dimensions={0} | all-to-all | bytes 262144 | tf_op jit(solution)/shard_map/all_to_all | solution.py:392
  82.3 2.7 %shard_map.133 = (bf16[64,8,128]{2,1,0:T(8,128)(2,1)S(1)}, bf16[32,256]{1,0:T(8,128)(2,1)S(1)}, bf16[8,32,256]{2,1,0:T(8,128)(2,1)}) custom-call(s32[1]{0:T(128)} %bitcast.place, bf16[64,8,128]{2,1,0:T(8,128)(2,1)S(1)} %all_to_all.35.x_ref, bf16[256,1024]{1,0:T(8,128)(2,1)S(1)} %copy-done.2, bf16[256,256]{1,0:T(8,128)(2,1)S(1)} %copy-done.7, ...), custom_call_target="tpu_custom_call" | custom-call | tf_op jit(solution)/shard_map/pallas_call | solution.py:53
  84.9 7.7 %all-to-all-start.2 = ((bf16[8,32,256]{2,1,0:T(8,128)(2,1)}), bf16[8,32,256]{2,1,0:T(8,128)(2,1)S(1)}, u32[]{:S(2)}, u32[]{:S(2)}) async-start(bf16[8,32,256]{2,1,0:T(8,128)(2,1)} %get-tuple-element.9), calls=%async_computation.2 | async-start | bytes 262144 | tf_op jit(solution)/shard_map/all_to_all | solution.py:392
  92.6 2.3 %collective-permute-start.7 = (bf16[32,256]{1,0:T(8,128)(2,1)S(1)}, bf16[32,256]{1,0:T(8,128)(2,1)S(1)}, u32[]{:S(2)}, u32[]{:S(2)}) collective-permute-start(bf16[32,256]{1,0:T(8,128)(2,1)S(1)} %get-tuple-element.10.refs_0_), channel_id=1, source_target_pairs={{0,384},{128,256},{256,128},{384,0},{1,385},{129,257},{257,129},{3... | collective-permute-start | bytes 49160 | tf_op jit(solution)/shard_map/ppermute | solution.py:442
  94.9 5.6 %collective-permute-start.6 = (bf16[32,256]{1,0:T(8,128)(2,1)S(1)}, bf16[32,256]{1,0:T(8,128)(2,1)S(1)}, u32[]{:S(2)}, u32[]{:S(2)}) collective-permute-start(bf16[32,256]{1,0:T(8,128)(2,1)S(1)} %get-tuple-element.10.refs_0_), channel_id=1, source_target_pairs={{0,256},{128,384},{256,0},{384,128},{1,257},{129,385},{257,1},{385... | collective-permute-start | bytes 49160 | tf_op jit(solution)/shard_map/ppermute | solution.py:442
  100.6 1.9 collective-permute-start.5
  102.5 0.0 collective-permute-done.7.refs_3_
  102.5 1.7 collective-permute-done.6.refs_2_
  104.2 2.0 collective-permute-done.5.refs_1_
  106.2 1.9 all-to-all-done.2.right_ref
  108.1 0.1 shard_map.134
  108.2 0.0 copy-start
  108.3 0.0 copy-start.4
  108.3 0.0 copy-start.6
  108.3 22.9 %all_to_all.36.factor_ref = bf16[16,160,256]{2,1,0:T(8,128)(2,1)S(1)} all-to-all(bf16[16,160,256]{2,1,0:T(8,128)(2,1)S(1)} %shard_map.134), channel_id=1, replica_groups=mesh['branch'=4,'row'=16,'col'=8] {'row'}, dimensions={0} | all-to-all | bytes 2621440 | tf_op jit(solution)/shard_map/all_to_all | solution.py:392
  131.2 3.1 %shard_map.135 = (bf16[512,128]{1,0:T(8,128)(2,1)S(1)}, bf16[64,2,8,128]{3,2,1,0:T(8,128)(2,1)S(1)}) custom-call(s32[1]{0:T(128)} %bitcast.place, bf16[16,160,256]{2,1,0:T(8,128)(2,1)S(1)} %all_to_all.36.factor_ref, bf16[64,32,128]{2,1,0:T(8,128)(2,1)S(1)} %copy-done, bf16[1024,128]{1,0:T(8,128)(2,1)S(1)} %copy-done.4, bf16[128,512]{1,0:T(8,128)(2,1)S(1)} %copy-done.6), custom_call_target="tpu_custom_call" | custom-call | tf_op jit(solution)/shard_map/pallas_call | solution.py:53
  134.3 16.8 %all_to_all.37 = bf16[64,2,8,128]{3,2,1,0:T(8,128)(2,1)S(1)} all-to-all(bf16[64,2,8,128]{3,2,1,0:T(8,128)(2,1)S(1)} %get-tuple-element.11), channel_id=1, replica_groups=mesh['branch'=4,'row'=16,'col'=8] {'branch','row'}, dimensions={0} | all-to-all | bytes 524288 | tf_op jit(solution)/shard_map/all_to_all | solution.py:392
  151.2 0.1 slice_bitcast_fusion.1
  151.2 3.6 %collective-permute-start.9 = (bf16[512,128]{1,0:T(8,128)(2,1)S(1)}, bf16[512,128]{1,0:T(8,128)(2,1)S(1)}, u32[]{:S(2)}, u32[]{:S(2)}) collective-permute-start(bf16[512,128]{1,0:T(8,128)(2,1)S(1)} %get-tuple-element.17.refs_0_), channel_id=1, source_target_pairs={{0,2},{1,3},{2,4},{3,5},{4,6},{5,7},{6,0},{7,1},{8,10},{9,11},{10,... | collective-permute-start | bytes 393224 | tf_op jit(solution)/shard_map/ppermute | solution.py:364
  154.9 6.1 %collective-permute-start.8 = (bf16[512,128]{1,0:T(8,128)(2,1)S(1)}, bf16[512,128]{1,0:T(8,128)(2,1)S(1)}, u32[]{:S(2)}, u32[]{:S(2)}) collective-permute-start(bf16[512,128]{1,0:T(8,128)(2,1)S(1)} %get-tuple-element.17.refs_0_), channel_id=1, source_target_pairs={{0,6},{1,7},{2,0},{3,1},{4,2},{5,3},{6,4},{7,5},{8,14},{9,15},{10,... | collective-permute-start | bytes 393224 | tf_op jit(solution)/shard_map/ppermute | solution.py:364
  161.0 6.1 %collective-permute-done.9.refs_2_ = bf16[512,128]{1,0:T(8,128)(2,1)S(1)} collective-permute-done((bf16[512,128]{1,0:T(8,128)(2,1)S(1)}, bf16[512,128]{1,0:T(8,128)(2,1)S(1)}, u32[]{:S(2)}, u32[]{:S(2)}) %collective-permute-start.9) | collective-permute-done | bytes 131104 | tf_op jit(solution)/shard_map/ppermute | solution.py:364
  167.1 1.4 collective-permute-done.8.refs_1_
  168.6 1.9 collective-permute-start.11
  170.5 7.0 %collective-permute-start.10 = (bf16[512,128]{1,0:T(8,128)(2,1)S(1)}, bf16[512,128]{1,0:T(8,128)(2,1)S(1)}, u32[]{:S(2)}, u32[]{:S(2)}) collective-permute-start(bf16[512,128]{1,0:T(8,128)(2,1)S(1)} %get-tuple-element.17.refs_0_), channel_id=1, source_target_pairs={{0,4},{1,5},{2,6},{3,7},{4,0},{5,1},{6,2},{7,3},{8,12},{9,13},{10,... | collective-permute-start | bytes 393224 | tf_op jit(solution)/shard_map/ppermute | solution.py:364
  177.5 12.7 %collective-permute-done.10.refs_3_ = bf16[512,128]{1,0:T(8,128)(2,1)S(1)} collective-permute-done((bf16[512,128]{1,0:T(8,128)(2,1)S(1)}, bf16[512,128]{1,0:T(8,128)(2,1)S(1)}, u32[]{:S(2)}, u32[]{:S(2)}) %collective-permute-start.10) | collective-permute-done | bytes 131104 | tf_op jit(solution)/shard_map/ppermute | solution.py:364
  190.1 1.9 collective-permute-start.12
  192.1 1.3 collective-permute-done.12.refs_5_
  193.4 0.5 shard_map.136
  193.9 24.0 %all_to_all.38.sum_ref = bf16[64,2,8,128]{3,2,1,0:T(8,128)(2,1)S(1)} all-to-all(bf16[64,2,8,128]{3,2,1,0:T(8,128)(2,1)S(1)} %shard_map.136), channel_id=1, replica_groups=mesh['branch'=4,'row'=16,'col'=8] {'branch','row'}, dimensions={0} | all-to-all | bytes 524288 | tf_op jit(solution)/shard_map/all_to_all | solution.py:392
  217.9 1.8 shard_map.137
  219.8 9.4 %all_to_all.39.x_ref = bf16[4,4,32,128]{3,2,1,0:T(8,128)(2,1)S(1)} all-to-all(bf16[4,4,32,128]{3,2,1,0:T(8,128)(2,1)S(1)} %get-tuple-element.15), channel_id=1, replica_groups=mesh['branch'=4,'row'=16,'col'=8] {'branch'}, dimensions={0} | all-to-all | bytes 262144 | tf_op jit(solution)/shard_map/all_to_all | solution.py:392
  229.2 0.8 unpack.1
  (20 shorter events, 0.1 us)
Async XLA Ops:
  0.6 27.6 %copy-start.3 = (bf16[4,64,256]{2,1,0:T(8,128)(2,1)S(1)}, bf16[4,64,256]{2,1,0:T(8,128)(2,1)}, u32[]{:S(2)}) copy-start(bf16[4,64,256]{2,1,0:T(8,128)(2,1)} %refs_0_.1) | copy-start | bytes 393220
  0.6 24.6 %collective-permute-start.1 = (bf16[4,64,256]{2,1,0:T(8,128)(2,1)}, bf16[4,64,256]{2,1,0:T(8,128)(2,1)S(1)}, u32[]{:S(2)}, u32[]{:S(2)}) collective-permute-start(bf16[4,64,256]{2,1,0:T(8,128)(2,1)} %refs_0_.1), channel_id=1, source_target_pairs={{0,2},{1,3},{2,4},{3,5},{4,6},{5,7},{6,0},{7,1},{8,10},{9,11},{10,... | collective-permute-start | bytes 393224 | tf_op jit(solution)/shard_map/ppermute | solution.py:364
  9.9 18.4 %collective-permute-start = (bf16[4,64,256]{2,1,0:T(8,128)(2,1)}, bf16[4,64,256]{2,1,0:T(8,128)(2,1)S(1)}, u32[]{:S(2)}, u32[]{:S(2)}) collective-permute-start(bf16[4,64,256]{2,1,0:T(8,128)(2,1)} %refs_0_.1), channel_id=1, source_target_pairs={{0,6},{1,7},{2,0},{3,1},{4,2},{5,3},{6,4},{7,5},{8,14},{9,15},{10,... | collective-permute-start | bytes 393224 | tf_op jit(solution)/shard_map/ppermute | solution.py:364
  14.6 36.3 %copy-start.1 = (bf16[256,1024]{1,0:T(8,128)(2,1)S(1)}, bf16[256,1024]{1,0:T(8,128)(2,1)}, u32[]{:S(2)}) copy-start(bf16[256,1024]{1,0:T(8,128)(2,1)} %refs_6_.1) | copy-start | bytes 1572868
  14.6 36.3 %copy-start.5 = (bf16[256,256]{1,0:T(8,128)(2,1)S(1)}, bf16[256,256]{1,0:T(8,128)(2,1)}, u32[]{:S(2)}) copy-start(bf16[256,256]{1,0:T(8,128)(2,1)} %refs_8_.1) | copy-start | bytes 393220
  18.1 32.7 %all-to-all-start = ((bf16[16,32,512]{2,1,0:T(8,128)(2,1)}), bf16[16,32,512]{2,1,0:T(8,128)(2,1)S(1)}, u32[]{:S(2)}, u32[]{:S(2)}) async-start(bf16[16,32,512]{2,1,0:T(8,128)(2,1)} %shard_map.131), calls=%async_computation | async-start | bytes 1048576 | tf_op jit(solution)/shard_map/all_to_all | solution.py:392
  28.3 22.6 %collective-permute-start.3 = (bf16[3,4,64,256]{3,2,1,0:T(8,128)(2,1)S(1)}, bf16[3,4,64,256]{3,2,1,0:T(8,128)(2,1)S(1)}, u32[]{:S(2)}, u32[]{:S(2)}) collective-permute-start(bf16[3,4,64,256]{3,2,1,0:T(8,128)(2,1)S(1)} %pad_maximum_fusion), channel_id=1, source_target_pairs={{0,1},{1,0},{2,3},{3,2},{4,5},{5,4},{6,7},{7,6},{8,9},{9,8},{10,11... | collective-permute-start | bytes 1179656 | tf_op jit(solution)/shard_map/ppermute | solution.py:364
  30.2 17.4 %collective-permute-start.2 = (bf16[4,64,256]{2,1,0:T(8,128)(2,1)S(1)}, bf16[4,64,256]{2,1,0:T(8,128)(2,1)S(1)}, u32[]{:S(2)}, u32[]{:S(2)}) collective-permute-start(bf16[4,64,256]{2,1,0:T(8,128)(2,1)S(1)} %copy-done.3), channel_id=1, source_target_pairs={{0,4},{1,5},{2,6},{3,7},{4,0},{5,1},{6,2},{7,3},{8,12},{9,13},{10,... | collective-permute-start | bytes 393224 | tf_op jit(solution)/shard_map/ppermute | solution.py:364
  47.6 3.2 %collective-permute-start.4 = (bf16[4,64,256]{2,1,0:T(8,128)(2,1)S(1)}, bf16[4,64,256]{2,1,0:T(8,128)(2,1)S(1)}, u32[]{:S(2)}, u32[]{:S(2)}) collective-permute-start(bf16[4,64,256]{2,1,0:T(8,128)(2,1)S(1)} %collective-permute-done.2.refs_3_), channel_id=1, source_target_pairs={{0,1},{1,0},{2,3},{3,2},{4,5},{5,4},{6,7},{7,6},{8,9},{9,8},{10,11... | collective-permute-start | bytes 393224 | tf_op jit(solution)/shard_map/ppermute | solution.py:364
  50.9 31.4 %copy-start.2 = (bf16[256,1024]{1,0:T(8,128)(2,1)S(1)}, bf16[256,1024]{1,0:T(8,128)(2,1)}, u32[]{:S(2)}) copy-start(bf16[256,1024]{1,0:T(8,128)(2,1)} %w_ref.3) | copy-start | bytes 1572868
  50.9 31.3 %copy-start.7 = (bf16[256,256]{1,0:T(8,128)(2,1)S(1)}, bf16[256,256]{1,0:T(8,128)(2,1)}, u32[]{:S(2)}) copy-start(bf16[256,256]{1,0:T(8,128)(2,1)} %wo_ref.2) | copy-start | bytes 393220
  50.9 31.3 %copy-start.8 = (bf16[256,64]{0,1:T(8,128)(2,1)S(1)}, bf16[256,64]{0,1:T(8,128)(2,1)}, u32[]{:S(2)}) copy-start(bf16[256,64]{0,1:T(8,128)(2,1)} %param.19) | copy-start | bytes 98308
  84.9 23.2 %all-to-all-start.2 = ((bf16[8,32,256]{2,1,0:T(8,128)(2,1)}), bf16[8,32,256]{2,1,0:T(8,128)(2,1)S(1)}, u32[]{:S(2)}, u32[]{:S(2)}) async-start(bf16[8,32,256]{2,1,0:T(8,128)(2,1)} %get-tuple-element.9), calls=%async_computation.2 | async-start | bytes 262144 | tf_op jit(solution)/shard_map/all_to_all | solution.py:392
  92.6 9.9 %collective-permute-start.7 = (bf16[32,256]{1,0:T(8,128)(2,1)S(1)}, bf16[32,256]{1,0:T(8,128)(2,1)S(1)}, u32[]{:S(2)}, u32[]{:S(2)}) collective-permute-start(bf16[32,256]{1,0:T(8,128)(2,1)S(1)} %get-tuple-element.10.refs_0_), channel_id=1, source_target_pairs={{0,384},{128,256},{256,128},{384,0},{1,385},{129,257},{257,129},{3... | collective-permute-start | bytes 49160 | tf_op jit(solution)/shard_map/ppermute | solution.py:442
  94.9 9.2 %collective-permute-start.6 = (bf16[32,256]{1,0:T(8,128)(2,1)S(1)}, bf16[32,256]{1,0:T(8,128)(2,1)S(1)}, u32[]{:S(2)}, u32[]{:S(2)}) collective-permute-start(bf16[32,256]{1,0:T(8,128)(2,1)S(1)} %get-tuple-element.10.refs_0_), channel_id=1, source_target_pairs={{0,256},{128,384},{256,0},{384,128},{1,257},{129,385},{257,1},{385... | collective-permute-start | bytes 49160 | tf_op jit(solution)/shard_map/ppermute | solution.py:442
  100.6 5.6 %collective-permute-start.5 = (bf16[32,256]{1,0:T(8,128)(2,1)S(1)}, bf16[32,256]{1,0:T(8,128)(2,1)S(1)}, u32[]{:S(2)}, u32[]{:S(2)}) collective-permute-start(bf16[32,256]{1,0:T(8,128)(2,1)S(1)} %get-tuple-element.10.refs_0_), channel_id=1, source_target_pairs={{0,128},{128,0},{256,384},{384,256},{1,129},{129,1},{257,385},{385... | collective-permute-start | bytes 49160 | tf_op jit(solution)/shard_map/ppermute | solution.py:442
  108.2 23.0 %copy-start = (bf16[64,32,128]{2,1,0:T(8,128)(2,1)S(1)}, bf16[64,32,128]{2,1,0:T(8,128)(2,1)}, u32[]{:S(2)}) copy-start(bf16[64,32,128]{2,1,0:T(8,128)(2,1)} %pair_ref.3) | copy-start | bytes 1572868
  108.3 23.0 %copy-start.4 = (bf16[1024,128]{1,0:T(8,128)(2,1)S(1)}, bf16[1024,128]{1,0:T(8,128)(2,1)}, u32[]{:S(2)}) copy-start(bf16[1024,128]{1,0:T(8,128)(2,1)} %wo_ref.3) | copy-start | bytes 786436
  108.3 23.0 %copy-start.6 = (bf16[128,512]{1,0:T(8,128)(2,1)S(1)}, bf16[128,512]{1,0:T(8,128)(2,1)}, u32[]{:S(2)}) copy-start(bf16[128,512]{1,0:T(8,128)(2,1)} %w_ref.4) | copy-start | bytes 393220
  151.2 15.9 %collective-permute-start.9 = (bf16[512,128]{1,0:T(8,128)(2,1)S(1)}, bf16[512,128]{1,0:T(8,128)(2,1)S(1)}, u32[]{:S(2)}, u32[]{:S(2)}) collective-permute-start(bf16[512,128]{1,0:T(8,128)(2,1)S(1)} %get-tuple-element.17.refs_0_), channel_id=1, source_target_pairs={{0,2},{1,3},{2,4},{3,5},{4,6},{5,7},{6,0},{7,1},{8,10},{9,11},{10,... | collective-permute-start | bytes 393224 | tf_op jit(solution)/shard_map/ppermute | solution.py:364
  154.9 13.7 %collective-permute-start.8 = (bf16[512,128]{1,0:T(8,128)(2,1)S(1)}, bf16[512,128]{1,0:T(8,128)(2,1)S(1)}, u32[]{:S(2)}, u32[]{:S(2)}) collective-permute-start(bf16[512,128]{1,0:T(8,128)(2,1)S(1)} %get-tuple-element.17.refs_0_), channel_id=1, source_target_pairs={{0,6},{1,7},{2,0},{3,1},{4,2},{5,3},{6,4},{7,5},{8,14},{9,15},{10,... | collective-permute-start | bytes 393224 | tf_op jit(solution)/shard_map/ppermute | solution.py:364
  168.5 49.4 %copy-start.9 = (bf16[128,128]{1,0:T(8,128)(2,1)S(1)}, bf16[128,128]{1,0:T(8,128)(2,1)}, u32[]{:S(2)}) copy-start(bf16[128,128]{1,0:T(8,128)(2,1)} %wg_ref.1) | copy-start | bytes 98308
  168.5 49.4 %copy-start.10 = (bf16[128,128]{1,0:T(8,128)(2,1)S(1)}, bf16[128,128]{1,0:T(8,128)(2,1)}, u32[]{:S(2)}) copy-start(bf16[128,128]{1,0:T(8,128)(2,1)} %w_ref.5) | copy-start | bytes 98308
  168.6 24.8 %collective-permute-start.11 = (bf16[3,512,128]{2,1,0:T(8,128)(2,1)S(1)}, bf16[3,512,128]{2,1,0:T(8,128)(2,1)S(1)}, u32[]{:S(2)}, u32[]{:S(2)}) collective-permute-start(bf16[3,512,128]{2,1,0:T(8,128)(2,1)S(1)} %pad_maximum_fusion.1), channel_id=1, source_target_pairs={{0,1},{1,0},{2,3},{3,2},{4,5},{5,4},{6,7},{7,6},{8,9},{9,8},{10,11... | collective-permute-start | bytes 1179656 | tf_op jit(solution)/shard_map/ppermute | solution.py:364
  170.5 19.6 %collective-permute-start.10 = (bf16[512,128]{1,0:T(8,128)(2,1)S(1)}, bf16[512,128]{1,0:T(8,128)(2,1)S(1)}, u32[]{:S(2)}, u32[]{:S(2)}) collective-permute-start(bf16[512,128]{1,0:T(8,128)(2,1)S(1)} %get-tuple-element.17.refs_0_), channel_id=1, source_target_pairs={{0,4},{1,5},{2,6},{3,7},{4,0},{5,1},{6,2},{7,3},{8,12},{9,13},{10,... | collective-permute-start | bytes 393224 | tf_op jit(solution)/shard_map/ppermute | solution.py:364
  190.1 3.2 %collective-permute-start.12 = (bf16[512,128]{1,0:T(8,128)(2,1)S(1)}, bf16[512,128]{1,0:T(8,128)(2,1)S(1)}, u32[]{:S(2)}, u32[]{:S(2)}) collective-permute-start(bf16[512,128]{1,0:T(8,128)(2,1)S(1)} %collective-permute-done.10.refs_3_), channel_id=1, source_target_pairs={{0,1},{1,0},{2,3},{3,2},{4,5},{5,4},{6,7},{7,6},{8,9},{9,8},{10,11... | collective-permute-start | bytes 393224 | tf_op jit(solution)/shard_map/ppermute | solution.py:364

commit v7 on v6

--- a/solution.py
+++ b/solution.py
@@ -298,19 +298,15 @@
 
 
 def triangle_kernel(place, left_ref, back_ref, *refs):
-    same, near, far, out_ref = refs[:4], refs[4], refs[5], refs[6]
+    same, other, out_ref = refs[:4], refs[4:6], refs[6]
     left = left_ref[...]
     lane = lax.broadcasted_iota(jnp.int32, (64, 128), 1) < 64
-    steps = (0, 1, 3, 2)
     for m in range(8):
-        step = steps[m // 2]
-        if m % 2 == 0:
-            right = same[m // 2][...]
-        else:
-            right = far[...] if step == 2 else near[m // 2]
+        step = m // 2
+        right = other[step % 2][step // 2] if m % 2 else same[step][...]
         product = mm(right, left, TN)
         block = jnp.where(lane, product[:64], product[64:]).astype(BF)
-        target = source_of(col_of(place), step * 2 + m % 2) * 2
+        target = source_of(col_of(place), m) * 2
         for b in range(4):
             for h in range(2):
                 out_ref[b * 16 + target + h, 0] = block[(b * 2 + h) * 8 : (b * 2 + h + 1) * 8]
@@ -371,6 +367,15 @@
     near = shifted(jnp.stack(same[:3]), 0, 1)
     far = shifted(same[3], 0, 1)
     return same + [near, far]
+
+
+def gather_far_first(x):
+    same, other = {0: x}, {}
+    for step in (2, 1, 3):
+        same[step] = shifted(x, step, 0)
+    for pair in ((0, 2), (1, 3)):
+        other[pair[0]] = shifted(jnp.stack([same[k] for k in pair]), 0, 1)
+    return [same[k] for k in range(4)] + [other[0], other[1]]
 
 
 def local(
@@ -460,7 +465,7 @@
     )
     message = exchange(message, both)
     tri_left = message[:, 0].reshape(512, 128)
-    rights = gather_col(message[:, 1].reshape(512, 128))
+    rights = gather_far_first(message[:, 1].reshape(512, 128))
     sums = in_vmem(triangle_kernel, [(64, 2, 8, 128)], [], place, tri_left, returning, *rights)
     sums = exchange(sums, both)
     parts, alignment_out = in_vmem(

time: 231 us -> 220 us (0.952)
  blocking collectives: 100 us -> 93.9 us
  waiting for transfers between devices: 39.7 us -> 34 us
    all_to_all x5, blocking collectives: 100 us -> 93.9 us  [local(): exchange = lambda x, axis: lax.all_to_all(x, axis, 0, 0, tiled=True)]
    ppermute x10, waiting for transfers between devices: 34 us -> 28.4 us  [shifted(): return lax.ppermute(x, 'col', perm)]
  transfers between devices with their start and end apart: 15 -> 15, of which waited for: 10 -> 9; matrix products, arithmetic and copies ran while one was open for 0% -> 0% of each run, Pallas kernels for 2% -> 2%
where the time goes in v7:
time: 220 us; the launch traced here: 219 us
  blocking collectives  93.9 us (43%)
  starting transfers between devices  73.2 us (33%)
  waiting for transfers between devices  34 us (15%)
  Pallas kernels  17 us (8%)
    all_to_all x5, blocking collectives, local(): exchange = lambda x, axis: lax.all_to_all(x, axis, 0, 0, tiled=True)  93.9 us
    ppermute x10, starting transfers between devices, shifted(): return lax.ppermute(x, 'col', perm)  48.6 us
    ppermute x10, waiting for transfers between devices, shifted(): return lax.ppermute(x, 'col', perm)  28.4 us
    pallas_call x7, Pallas kernels, in_vmem(): pl.pallas_call(kernel, out_shape=tuple(shapes), in_specs=[SM] + [HB] * lo...  16.1 us
    all_to_all x2, starting transfers between devices, local(): exchange = lambda x, axis: lax.all_to_all(x, axis, 0, 0, tiled=True)  14.7 us
    ppermute x3, starting transfers between devices, local(): lax.ppermute(left, 'branch', [(b, b ^ mask) for b in range(4)])  9.86 us
  transfers between devices with their start and end apart: 15, of which 9 were waited for; matrix products, arithmetic and copies ran while one was open for 0% of the time, Pallas kernels for 2%

profile of v7, /device:TPU:32, one launch (start us, length us, event | category | flops | bytes accessed | tf_op | source)
XLA Modules:
  0.0 219.3 jit_solution(13836530245775396684)
XLA Ops:
  0.6 9.2 %collective-permute-start.1 = (bf16[4,64,256]{2,1,0:T(8,128)(2,1)}, bf16[4,64,256]{2,1,0:T(8,128)(2,1)S(1)}, u32[]{:S(2)}, u32[]{:S(2)}) collective-permute-start(bf16[4,64,256]{2,1,0:T(8,128)(2,1)} %refs_0_.1), channel_id=1, source_target_pairs={{0,2},{1,3},{2,4},{3,5},{4,6},{5,7},{6,0},{7,1},{8,10},{9,11},{10,... | collective-permute-start | bytes 393224 | tf_op jit(solution)/shard_map/ppermute | solution.py:360
  9.9 4.7 %collective-permute-start = (bf16[4,64,256]{2,1,0:T(8,128)(2,1)}, bf16[4,64,256]{2,1,0:T(8,128)(2,1)S(1)}, u32[]{:S(2)}, u32[]{:S(2)}) collective-permute-start(bf16[4,64,256]{2,1,0:T(8,128)(2,1)} %refs_0_.1), channel_id=1, source_target_pairs={{0,6},{1,7},{2,0},{3,1},{4,2},{5,3},{6,4},{7,5},{8,14},{9,15},{10,... | collective-permute-start | bytes 393224 | tf_op jit(solution)/shard_map/ppermute | solution.py:360
  14.6 3.6 %shard_map.131 = bf16[16,32,512]{2,1,0:T(8,128)(2,1)} custom-call(s32[1]{0:T(128)} %bitcast.place, bf16[64,32,128]{2,1,0:T(8,128)(2,1)} %pair_ref.3, bf16[8,128]{1,0:T(8,128)(2,1)} %bitcast.26), custom_call_target="tpu_custom_call" | custom-call | tf_op jit(solution)/shard_map/pallas_call | solution.py:53
  18.1 7.0 %all-to-all-start = ((bf16[16,32,512]{2,1,0:T(8,128)(2,1)}), bf16[16,32,512]{2,1,0:T(8,128)(2,1)S(1)}, u32[]{:S(2)}, u32[]{:S(2)}) async-start(bf16[16,32,512]{2,1,0:T(8,128)(2,1)} %shard_map.131), calls=%async_computation | async-start | bytes 1048576 | tf_op jit(solution)/shard_map/all_to_all | solution.py:397
  25.2 0.0 collective-permute-done.1.refs_2_
  25.2 3.0 %collective-permute-done.refs_1_ = bf16[4,64,256]{2,1,0:T(8,128)(2,1)S(1)} collective-permute-done((bf16[4,64,256]{2,1,0:T(8,128)(2,1)}, bf16[4,64,256]{2,1,0:T(8,128)(2,1)S(1)}, u32[]{:S(2)}, u32[]{:S(2)}) %collective-permute-start) | collective-permute-done | bytes 131104 | tf_op jit(solution)/shard_map/ppermute | solution.py:360
  28.3 1.9 collective-permute-start.3
  30.2 9.2 %collective-permute-start.2 = (bf16[4,64,256]{2,1,0:T(8,128)(2,1)S(1)}, bf16[4,64,256]{2,1,0:T(8,128)(2,1)S(1)}, u32[]{:S(2)}, u32[]{:S(2)}) collective-permute-start(bf16[4,64,256]{2,1,0:T(8,128)(2,1)S(1)} %copy-done.3), channel_id=1, source_target_pairs={{0,4},{1,5},{2,6},{3,7},{4,0},{5,1},{6,2},{7,3},{8,12},{9,13},{10,... | collective-permute-start | bytes 393224 | tf_op jit(solution)/shard_map/ppermute | solution.py:360
  39.5 8.2 %collective-permute-done.2.refs_3_ = bf16[4,64,256]{2,1,0:T(8,128)(2,1)S(1)} collective-permute-done((bf16[4,64,256]{2,1,0:T(8,128)(2,1)S(1)}, bf16[4,64,256]{2,1,0:T(8,128)(2,1)S(1)}, u32[]{:S(2)}, u32[]{:S(2)}) %collective-permute-start.2) | collective-permute-done | bytes 131104 | tf_op jit(solution)/shard_map/ppermute | solution.py:360
  47.6 1.9 collective-permute-start.4
  49.6 1.3 collective-permute-done.4.refs_5_
  50.9 0.0 all-to-all-done
  50.9 0.0 copy-start.2
  50.9 0.0 copy-start.7
  50.9 0.0 copy-start.8
  50.9 4.4 %shard_map.132 = bf16[64,8,128]{2,1,0:T(8,128)(2,1)S(1)} custom-call(s32[1]{0:T(128)} %bitcast.place, bf16[4,64,256]{2,1,0:T(8,128)(2,1)S(1)} %copy-done.3, bf16[4,64,256]{2,1,0:T(8,128)(2,1)S(1)} %collective-permute-done.refs_1_, bf16[4,64,256]{2,1,0:T(8,128)(2,1)S(1)} %collective-permute-done.1.refs_2_, ...), custom_call_target="tpu_custom_call" | custom-call | tf_op jit(solution)/shard_map/pallas_call | solution.py:53
  55.3 27.0 %all_to_all.35.x_ref = bf16[64,8,128]{2,1,0:T(8,128)(2,1)S(1)} all-to-all(bf16[64,8,128]{2,1,0:T(8,128)(2,1)S(1)} %shard_map.132), channel_id=1, replica_groups=mesh['branch'=4,'row'=16,'col'=8] {'branch','row'}, dimensions={0} | all-to-all | bytes 262144 | tf_op jit(solution)/shard_map/all_to_all | solution.py:397
  82.3 2.7 %shard_map.133 = (bf16[64,8,128]{2,1,0:T(8,128)(2,1)S(1)}, bf16[32,256]{1,0:T(8,128)(2,1)S(1)}, bf16[8,32,256]{2,1,0:T(8,128)(2,1)}) custom-call(s32[1]{0:T(128)} %bitcast.place, bf16[64,8,128]{2,1,0:T(8,128)(2,1)S(1)} %all_to_all.35.x_ref, bf16[256,1024]{1,0:T(8,128)(2,1)S(1)} %copy-done.2, bf16[256,256]{1,0:T(8,128)(2,1)S(1)} %copy-done.7, ...), custom_call_target="tpu_custom_call" | custom-call | tf_op jit(solution)/shard_map/pallas_call | solution.py:53
  84.9 7.7 %all-to-all-start.2 = ((bf16[8,32,256]{2,1,0:T(8,128)(2,1)}), bf16[8,32,256]{2,1,0:T(8,128)(2,1)S(1)}, u32[]{:S(2)}, u32[]{:S(2)}) async-start(bf16[8,32,256]{2,1,0:T(8,128)(2,1)} %get-tuple-element.9), calls=%async_computation.2 | async-start | bytes 262144 | tf_op jit(solution)/shard_map/all_to_all | solution.py:397
  92.6 2.3 %collective-permute-start.7 = (bf16[32,256]{1,0:T(8,128)(2,1)S(1)}, bf16[32,256]{1,0:T(8,128)(2,1)S(1)}, u32[]{:S(2)}, u32[]{:S(2)}) collective-permute-start(bf16[32,256]{1,0:T(8,128)(2,1)S(1)} %get-tuple-element.10.refs_0_), channel_id=1, source_target_pairs={{0,384},{128,256},{256,128},{384,0},{1,385},{129,257},{257,129},{3... | collective-permute-start | bytes 49160 | tf_op jit(solution)/shard_map/ppermute | solution.py:447
  94.9 5.6 %collective-permute-start.6 = (bf16[32,256]{1,0:T(8,128)(2,1)S(1)}, bf16[32,256]{1,0:T(8,128)(2,1)S(1)}, u32[]{:S(2)}, u32[]{:S(2)}) collective-permute-start(bf16[32,256]{1,0:T(8,128)(2,1)S(1)} %get-tuple-element.10.refs_0_), channel_id=1, source_target_pairs={{0,256},{128,384},{256,0},{384,128},{1,257},{129,385},{257,1},{385... | collective-permute-start | bytes 49160 | tf_op jit(solution)/shard_map/ppermute | solution.py:447
  100.6 1.9 collective-permute-start.5
  102.5 0.0 collective-permute-done.7.refs_3_
  102.5 1.7 collective-permute-done.6.refs_2_
  104.2 2.0 collective-permute-done.5.refs_1_
  106.2 1.9 all-to-all-done.2.right_ref
  108.1 0.1 shard_map.134
  108.2 0.0 copy-start
  108.3 0.0 copy-start.4
  108.3 0.0 copy-start.6
  108.3 22.9 %all_to_all.36.factor_ref = bf16[16,160,256]{2,1,0:T(8,128)(2,1)S(1)} all-to-all(bf16[16,160,256]{2,1,0:T(8,128)(2,1)S(1)} %shard_map.134), channel_id=1, replica_groups=mesh['branch'=4,'row'=16,'col'=8] {'row'}, dimensions={0} | all-to-all | bytes 2621440 | tf_op jit(solution)/shard_map/all_to_all | solution.py:397
  131.2 3.1 %shard_map.135 = (bf16[512,128]{1,0:T(8,128)(2,1)S(1)}, bf16[64,2,8,128]{3,2,1,0:T(8,128)(2,1)S(1)}) custom-call(s32[1]{0:T(128)} %bitcast.place, bf16[16,160,256]{2,1,0:T(8,128)(2,1)S(1)} %all_to_all.36.factor_ref, bf16[64,32,128]{2,1,0:T(8,128)(2,1)S(1)} %copy-done, bf16[1024,128]{1,0:T(8,128)(2,1)S(1)} %copy-done.4, bf16[128,512]{1,0:T(8,128)(2,1)S(1)} %copy-done.6), custom_call_target="tpu_custom_call" | custom-call | tf_op jit(solution)/shard_map/pallas_call | solution.py:53
  134.3 16.8 %all_to_all.37 = bf16[64,2,8,128]{3,2,1,0:T(8,128)(2,1)S(1)} all-to-all(bf16[64,2,8,128]{3,2,1,0:T(8,128)(2,1)S(1)} %get-tuple-element.11), channel_id=1, replica_groups=mesh['branch'=4,'row'=16,'col'=8] {'branch','row'}, dimensions={0} | all-to-all | bytes 524288 | tf_op jit(solution)/shard_map/all_to_all | solution.py:397
  151.2 0.1 slice_bitcast_fusion.1
  151.2 3.6 %collective-permute-start.10 = (bf16[512,128]{1,0:T(8,128)(2,1)S(1)}, bf16[512,128]{1,0:T(8,128)(2,1)S(1)}, u32[]{:S(2)}, u32[]{:S(2)}) collective-permute-start(bf16[512,128]{1,0:T(8,128)(2,1)S(1)} %get-tuple-element.17.refs_0_), channel_id=1, source_target_pairs={{0,2},{1,3},{2,4},{3,5},{4,6},{5,7},{6,0},{7,1},{8,10},{9,11},{10,... | collective-permute-start | bytes 393224 | tf_op jit(solution)/shard_map/ppermute | solution.py:360
  154.9 6.1 %collective-permute-start.8 = (bf16[512,128]{1,0:T(8,128)(2,1)S(1)}, bf16[512,128]{1,0:T(8,128)(2,1)S(1)}, u32[]{:S(2)}, u32[]{:S(2)}) collective-permute-start(bf16[512,128]{1,0:T(8,128)(2,1)S(1)} %get-tuple-element.17.refs_0_), channel_id=1, source_target_pairs={{0,6},{1,7},{2,0},{3,1},{4,2},{5,3},{6,4},{7,5},{8,14},{9,15},{10,... | collective-permute-start | bytes 393224 | tf_op jit(solution)/shard_map/ppermute | solution.py:360
  161.0 8.1 %collective-permute-start.9 = (bf16[512,128]{1,0:T(8,128)(2,1)S(1)}, bf16[512,128]{1,0:T(8,128)(2,1)S(1)}, u32[]{:S(2)}, u32[]{:S(2)}) collective-permute-start(bf16[512,128]{1,0:T(8,128)(2,1)S(1)} %get-tuple-element.17.refs_0_), channel_id=1, source_target_pairs={{0,4},{1,5},{2,6},{3,7},{4,0},{5,1},{6,2},{7,3},{8,12},{9,13},{10,... | collective-permute-start | bytes 393224 | tf_op jit(solution)/shard_map/ppermute | solution.py:360
  169.1 0.0 collective-permute-done.10.refs_3_
  169.1 0.9 collective-permute-done.8.refs_1_
  170.1 1.9 collective-permute-start.12
  172.0 13.4 %collective-permute-done.9.refs_2_ = bf16[512,128]{1,0:T(8,128)(2,1)S(1)} collective-permute-done((bf16[512,128]{1,0:T(8,128)(2,1)S(1)}, bf16[512,128]{1,0:T(8,128)(2,1)S(1)}, u32[]{:S(2)}, u32[]{:S(2)}) %collective-permute-start.9) | collective-permute-done | bytes 131104 | tf_op jit(solution)/shard_map/ppermute | solution.py:360
  185.5 1.9 collective-permute-start.11
  187.4 1.5 collective-permute-done.11.refs_4_
  188.9 0.5 shard_map.136
  189.4 17.7 %all_to_all.38.sum_ref = bf16[64,2,8,128]{3,2,1,0:T(8,128)(2,1)S(1)} all-to-all(bf16[64,2,8,128]{3,2,1,0:T(8,128)(2,1)S(1)} %shard_map.136), channel_id=1, replica_groups=mesh['branch'=4,'row'=16,'col'=8] {'branch','row'}, dimensions={0} | all-to-all | bytes 524288 | tf_op jit(solution)/shard_map/all_to_all | solution.py:397
  207.1 1.8 shard_map.137
  209.0 9.4 %all_to_all.39.x_ref = bf16[4,4,32,128]{3,2,1,0:T(8,128)(2,1)S(1)} all-to-all(bf16[4,4,32,128]{3,2,1,0:T(8,128)(2,1)S(1)} %get-tuple-element.15), channel_id=1, replica_groups=mesh['branch'=4,'row'=16,'col'=8] {'branch'}, dimensions={0} | all-to-all | bytes 262144 | tf_op jit(solution)/shard_map/all_to_all | solution.py:397
  218.4 0.8 unpack.1
  (21 shorter events, 0.1 us)
Async XLA Ops:
  0.6 27.6 %copy-start.3 = (bf16[4,64,256]{2,1,0:T(8,128)(2,1)S(1)}, bf16[4,64,256]{2,1,0:T(8,128)(2,1)}, u32[]{:S(2)}) copy-start(bf16[4,64,256]{2,1,0:T(8,128)(2,1)} %refs_0_.1) | copy-start | bytes 393220
  0.6 24.6 %collective-permute-start.1 = (bf16[4,64,256]{2,1,0:T(8,128)(2,1)}, bf16[4,64,256]{2,1,0:T(8,128)(2,1)S(1)}, u32[]{:S(2)}, u32[]{:S(2)}) collective-permute-start(bf16[4,64,256]{2,1,0:T(8,128)(2,1)} %refs_0_.1), channel_id=1, source_target_pairs={{0,2},{1,3},{2,4},{3,5},{4,6},{5,7},{6,0},{7,1},{8,10},{9,11},{10,... | collective-permute-start | bytes 393224 | tf_op jit(solution)/shard_map/ppermute | solution.py:360
  9.9 18.4 %collective-permute-start = (bf16[4,64,256]{2,1,0:T(8,128)(2,1)}, bf16[4,64,256]{2,1,0:T(8,128)(2,1)S(1)}, u32[]{:S(2)}, u32[]{:S(2)}) collective-permute-start(bf16[4,64,256]{2,1,0:T(8,128)(2,1)} %refs_0_.1), channel_id=1, source_target_pairs={{0,6},{1,7},{2,0},{3,1},{4,2},{5,3},{6,4},{7,5},{8,14},{9,15},{10,... | collective-permute-start | bytes 393224 | tf_op jit(solution)/shard_map/ppermute | solution.py:360
  14.6 36.3 %copy-start.1 = (bf16[256,1024]{1,0:T(8,128)(2,1)S(1)}, bf16[256,1024]{1,0:T(8,128)(2,1)}, u32[]{:S(2)}) copy-start(bf16[256,1024]{1,0:T(8,128)(2,1)} %refs_6_.1) | copy-start | bytes 1572868
  14.6 36.3 %copy-start.5 = (bf16[256,256]{1,0:T(8,128)(2,1)S(1)}, bf16[256,256]{1,0:T(8,128)(2,1)}, u32[]{:S(2)}) copy-start(bf16[256,256]{1,0:T(8,128)(2,1)} %refs_8_.1) | copy-start | bytes 393220
  18.1 32.7 %all-to-all-start = ((bf16[16,32,512]{2,1,0:T(8,128)(2,1)}), bf16[16,32,512]{2,1,0:T(8,128)(2,1)S(1)}, u32[]{:S(2)}, u32[]{:S(2)}) async-start(bf16[16,32,512]{2,1,0:T(8,128)(2,1)} %shard_map.131), calls=%async_computation | async-start | bytes 1048576 | tf_op jit(solution)/shard_map/all_to_all | solution.py:397
  28.3 22.6 %collective-permute-start.3 = (bf16[3,4,64,256]{3,2,1,0:T(8,128)(2,1)S(1)}, bf16[3,4,64,256]{3,2,1,0:T(8,128)(2,1)S(1)}, u32[]{:S(2)}, u32[]{:S(2)}) collective-permute-start(bf16[3,4,64,256]{3,2,1,0:T(8,128)(2,1)S(1)} %pad_maximum_fusion), channel_id=1, source_target_pairs={{0,1},{1,0},{2,3},{3,2},{4,5},{5,4},{6,7},{7,6},{8,9},{9,8},{10,11... | collective-permute-start | bytes 1179656 | tf_op jit(solution)/shard_map/ppermute | solution.py:360
  30.2 17.4 %collective-permute-start.2 = (bf16[4,64,256]{2,1,0:T(8,128)(2,1)S(1)}, bf16[4,64,256]{2,1,0:T(8,128)(2,1)S(1)}, u32[]{:S(2)}, u32[]{:S(2)}) collective-permute-start(bf16[4,64,256]{2,1,0:T(8,128)(2,1)S(1)} %copy-done.3), channel_id=1, source_target_pairs={{0,4},{1,5},{2,6},{3,7},{4,0},{5,1},{6,2},{7,3},{8,12},{9,13},{10,... | collective-permute-start | bytes 393224 | tf_op jit(solution)/shard_map/ppermute | solution.py:360
  47.6 3.2 %collective-permute-start.4 = (bf16[4,64,256]{2,1,0:T(8,128)(2,1)S(1)}, bf16[4,64,256]{2,1,0:T(8,128)(2,1)S(1)}, u32[]{:S(2)}, u32[]{:S(2)}) collective-permute-start(bf16[4,64,256]{2,1,0:T(8,128)(2,1)S(1)} %collective-permute-done.2.refs_3_), channel_id=1, source_target_pairs={{0,1},{1,0},{2,3},{3,2},{4,5},{5,4},{6,7},{7,6},{8,9},{9,8},{10,11... | collective-permute-start | bytes 393224 | tf_op jit(solution)/shard_map/ppermute | solution.py:360
  50.9 31.4 %copy-start.2 = (bf16[256,1024]{1,0:T(8,128)(2,1)S(1)}, bf16[256,1024]{1,0:T(8,128)(2,1)}, u32[]{:S(2)}) copy-start(bf16[256,1024]{1,0:T(8,128)(2,1)} %w_ref.3) | copy-start | bytes 1572868
  50.9 31.3 %copy-start.7 = (bf16[256,256]{1,0:T(8,128)(2,1)S(1)}, bf16[256,256]{1,0:T(8,128)(2,1)}, u32[]{:S(2)}) copy-start(bf16[256,256]{1,0:T(8,128)(2,1)} %wo_ref.2) | copy-start | bytes 393220
  50.9 31.3 %copy-start.8 = (bf16[256,64]{0,1:T(8,128)(2,1)S(1)}, bf16[256,64]{0,1:T(8,128)(2,1)}, u32[]{:S(2)}) copy-start(bf16[256,64]{0,1:T(8,128)(2,1)} %param.19) | copy-start | bytes 98308
  84.9 23.2 %all-to-all-start.2 = ((bf16[8,32,256]{2,1,0:T(8,128)(2,1)}), bf16[8,32,256]{2,1,0:T(8,128)(2,1)S(1)}, u32[]{:S(2)}, u32[]{:S(2)}) async-start(bf16[8,32,256]{2,1,0:T(8,128)(2,1)} %get-tuple-element.9), calls=%async_computation.2 | async-start | bytes 262144 | tf_op jit(solution)/shard_map/all_to_all | solution.py:397
  92.6 9.9 %collective-permute-start.7 = (bf16[32,256]{1,0:T(8,128)(2,1)S(1)}, bf16[32,256]{1,0:T(8,128)(2,1)S(1)}, u32[]{:S(2)}, u32[]{:S(2)}) collective-permute-start(bf16[32,256]{1,0:T(8,128)(2,1)S(1)} %get-tuple-element.10.refs_0_), channel_id=1, source_target_pairs={{0,384},{128,256},{256,128},{384,0},{1,385},{129,257},{257,129},{3... | collective-permute-start | bytes 49160 | tf_op jit(solution)/shard_map/ppermute | solution.py:447
  94.9 9.2 %collective-permute-start.6 = (bf16[32,256]{1,0:T(8,128)(2,1)S(1)}, bf16[32,256]{1,0:T(8,128)(2,1)S(1)}, u32[]{:S(2)}, u32[]{:S(2)}) collective-permute-start(bf16[32,256]{1,0:T(8,128)(2,1)S(1)} %get-tuple-element.10.refs_0_), channel_id=1, source_target_pairs={{0,256},{128,384},{256,0},{384,128},{1,257},{129,385},{257,1},{385... | collective-permute-start | bytes 49160 | tf_op jit(solution)/shard_map/ppermute | solution.py:447
  100.6 5.6 %collective-permute-start.5 = (bf16[32,256]{1,0:T(8,128)(2,1)S(1)}, bf16[32,256]{1,0:T(8,128)(2,1)S(1)}, u32[]{:S(2)}, u32[]{:S(2)}) collective-permute-start(bf16[32,256]{1,0:T(8,128)(2,1)S(1)} %get-tuple-element.10.refs_0_), channel_id=1, source_target_pairs={{0,128},{128,0},{256,384},{384,256},{1,129},{129,1},{257,385},{385... | collective-permute-start | bytes 49160 | tf_op jit(solution)/shard_map/ppermute | solution.py:447
  108.2 23.0 %copy-start = (bf16[64,32,128]{2,1,0:T(8,128)(2,1)S(1)}, bf16[64,32,128]{2,1,0:T(8,128)(2,1)}, u32[]{:S(2)}) copy-start(bf16[64,32,128]{2,1,0:T(8,128)(2,1)} %pair_ref.3) | copy-start | bytes 1572868
  108.3 23.0 %copy-start.4 = (bf16[1024,128]{1,0:T(8,128)(2,1)S(1)}, bf16[1024,128]{1,0:T(8,128)(2,1)}, u32[]{:S(2)}) copy-start(bf16[1024,128]{1,0:T(8,128)(2,1)} %wo_ref.3) | copy-start | bytes 786436
  108.3 23.0 %copy-start.6 = (bf16[128,512]{1,0:T(8,128)(2,1)S(1)}, bf16[128,512]{1,0:T(8,128)(2,1)}, u32[]{:S(2)}) copy-start(bf16[128,512]{1,0:T(8,128)(2,1)} %w_ref.4) | copy-start | bytes 393220
  151.2 17.9 %collective-permute-start.10 = (bf16[512,128]{1,0:T(8,128)(2,1)S(1)}, bf16[512,128]{1,0:T(8,128)(2,1)S(1)}, u32[]{:S(2)}, u32[]{:S(2)}) collective-permute-start(bf16[512,128]{1,0:T(8,128)(2,1)S(1)} %get-tuple-element.17.refs_0_), channel_id=1, source_target_pairs={{0,2},{1,3},{2,4},{3,5},{4,6},{5,7},{6,0},{7,1},{8,10},{9,11},{10,... | collective-permute-start | bytes 393224 | tf_op jit(solution)/shard_map/ppermute | solution.py:360
  154.9 15.2 %collective-permute-start.8 = (bf16[512,128]{1,0:T(8,128)(2,1)S(1)}, bf16[512,128]{1,0:T(8,128)(2,1)S(1)}, u32[]{:S(2)}, u32[]{:S(2)}) collective-permute-start(bf16[512,128]{1,0:T(8,128)(2,1)S(1)} %get-tuple-element.17.refs_0_), channel_id=1, source_target_pairs={{0,6},{1,7},{2,0},{3,1},{4,2},{5,3},{6,4},{7,5},{8,14},{9,15},{10,... | collective-permute-start | bytes 393224 | tf_op jit(solution)/shard_map/ppermute | solution.py:360
  161.0 24.4 %collective-permute-start.9 = (bf16[512,128]{1,0:T(8,128)(2,1)S(1)}, bf16[512,128]{1,0:T(8,128)(2,1)S(1)}, u32[]{:S(2)}, u32[]{:S(2)}) collective-permute-start(bf16[512,128]{1,0:T(8,128)(2,1)S(1)} %get-tuple-element.17.refs_0_), channel_id=1, source_target_pairs={{0,4},{1,5},{2,6},{3,7},{4,0},{5,1},{6,2},{7,3},{8,12},{9,13},{10,... | collective-permute-start | bytes 393224 | tf_op jit(solution)/shard_map/ppermute | solution.py:360
  170.1 17.3 %collective-permute-start.12 = (bf16[2,512,128]{2,1,0:T(8,128)(2,1)S(1)}, bf16[2,512,128]{2,1,0:T(8,128)(2,1)S(1)}, u32[]{:S(2)}, u32[]{:S(2)}) collective-permute-start(bf16[2,512,128]{2,1,0:T(8,128)(2,1)S(1)} %pad_maximum_fusion.2), channel_id=1, source_target_pairs={{0,1},{1,0},{2,3},{3,2},{4,5},{5,4},{6,7},{7,6},{8,9},{9,8},{10,11... | collective-permute-start | bytes 786440 | tf_op jit(solution)/shard_map/ppermute | solution.py:360
  185.4 21.7 %copy-start.9 = (bf16[128,128]{1,0:T(8,128)(2,1)S(1)}, bf16[128,128]{1,0:T(8,128)(2,1)}, u32[]{:S(2)}) copy-start(bf16[128,128]{1,0:T(8,128)(2,1)} %wg_ref.1) | copy-start | bytes 98308
  185.4 21.7 %copy-start.10 = (bf16[128,128]{1,0:T(8,128)(2,1)S(1)}, bf16[128,128]{1,0:T(8,128)(2,1)}, u32[]{:S(2)}) copy-start(bf16[128,128]{1,0:T(8,128)(2,1)} %w_ref.5) | copy-start | bytes 98308
  185.5 3.4 %collective-permute-start.11 = (bf16[2,512,128]{2,1,0:T(8,128)(2,1)S(1)}, bf16[2,512,128]{2,1,0:T(8,128)(2,1)S(1)}, u32[]{:S(2)}, u32[]{:S(2)}) collective-permute-start(bf16[2,512,128]{2,1,0:T(8,128)(2,1)S(1)} %pad_maximum_fusion.1), channel_id=1, source_target_pairs={{0,1},{1,0},{2,3},{3,2},{4,5},{5,4},{6,7},{7,6},{8,9},{9,8},{10,11... | collective-permute-start | bytes 786440 | tf_op jit(solution)/shard_map/ppermute | solution.py:360

commit v8 on v7

--- a/solution.py
+++ b/solution.py
@@ -107,17 +107,17 @@
 
 
 def row_kernel(place, *refs):
-    own_ref, z1_ref, z3_ref, z2_ref, swap_ref, last_ref = refs[:6]
+    own_ref, z1_ref, z2_ref, z3_ref, even_ref, odd_ref = refs[:6]
     w_ref, bias_ref, wo_ref, out_ref, rows, keys, values, packed = refs[6:]
     for m, block in (
         (0, own_ref[...]),
+        (4, z2_ref[...]),
+        (1, even_ref[0]),
+        (5, even_ref[1]),
         (2, z1_ref[...]),
         (6, z3_ref[...]),
-        (1, swap_ref[0]),
-        (3, swap_ref[1]),
-        (7, swap_ref[2]),
-        (4, z2_ref[...]),
-        (5, last_ref[...]),
+        (3, odd_ref[0]),
+        (7, odd_ref[1]),
     ):
         start = pl.multiple_of(source_of(col_of(place), m) * 64, 64)
         normed = layer_norm(block.reshape(256, 256)).astype(BF)
@@ -361,15 +361,6 @@
 
 
 def gather_col(x):
-    same = [x]
-    for step in (1, 3, 2):
-        same.append(shifted(x, step, 0))
-    near = shifted(jnp.stack(same[:3]), 0, 1)
-    far = shifted(same[3], 0, 1)
-    return same + [near, far]
-
-
-def gather_far_first(x):
     same, other = {0: x}, {}
     for step in (2, 1, 3):
         same[step] = shifted(x, step, 0)
@@ -465,7 +456,7 @@
     )
     message = exchange(message, both)
     tri_left = message[:, 0].reshape(512, 128)
-    rights = gather_far_first(message[:, 1].reshape(512, 128))
+    rights = gather_col(message[:, 1].reshape(512, 128))
     sums = in_vmem(triangle_kernel, [(64, 2, 8, 128)], [], place, tri_left, returning, *rights)
     sums = exchange(sums, both)
     parts, alignment_out = in_vmem(

time: 220 us -> 206 us (0.936)
  blocking collectives: 93.9 us -> 82.8 us
  waiting for transfers between devices: 34 us -> 27.6 us
  starting transfers between devices: 73.2 us -> 76.3 us
    ppermute x10, waiting for transfers between devices: 28.4 us -> 16.9 us  [shifted(): return lax.ppermute(x, 'col', perm)]
    all_to_all x5, blocking collectives: 93.9 us -> 82.8 us  [local(): exchange = lambda x, axis: lax.all_to_all(x, axis, 0, 0, tiled=True)]
    all_to_all x2, waiting for transfers between devices: 1.93 us -> 6.98 us  [local(): exchange = lambda x, axis: lax.all_to_all(x, axis, 0, 0, tiled=True)]
    ppermute x10, starting transfers between devices: 48.6 us -> 50.8 us  [shifted(): return lax.ppermute(x, 'col', perm)]
  transfers between devices with their start and end apart: 15 -> 15, of which waited for: 9 -> 8; matrix products, arithmetic and copies ran while one was open for 0% -> 0% of each run, Pallas kernels for 2% -> 2%
where the time goes in v8:
time: 206 us; the launch traced here: 205 us
  blocking collectives  82.8 us (40%)
  starting transfers between devices  76.3 us (37%)
  waiting for transfers between devices  27.6 us (13%)
  Pallas kernels  16.9 us (8%)
    all_to_all x5, blocking collectives, local(): exchange = lambda x, axis: lax.all_to_all(x, axis, 0, 0, tiled=True)  82.8 us
    ppermute x10, starting transfers between devices, shifted(): return lax.ppermute(x, 'col', perm)  50.8 us
    ppermute x10, waiting for transfers between devices, shifted(): return lax.ppermute(x, 'col', perm)  16.9 us
    pallas_call x7, Pallas kernels, in_vmem(): pl.pallas_call(kernel, out_shape=tuple(shapes), in_specs=[SM] + [HB] * lo...  16.1 us
    all_to_all x2, starting transfers between devices, local(): exchange = lambda x, axis: lax.all_to_all(x, axis, 0, 0, tiled=True)  15.6 us
    ppermute x3, starting transfers between devices, local(): lax.ppermute(left, 'branch', [(b, b ^ mask) for b in range(4)])  9.86 us
    all_to_all x2, waiting for transfers between devices, local(): exchange = lambda x, axis: lax.all_to_all(x, axis, 0, 0, tiled=True)  6.98 us
  transfers between devices with their start and end apart: 15, of which 8 were waited for; matrix products, arithmetic and copies ran while one was open for 0% of the time, Pallas kernels for 2%

profile of v8, /device:TPU:32, one launch (start us, length us, event | category | flops | bytes accessed | tf_op | source)
XLA Modules:
  0.0 204.7 jit_solution(3321168772335009243)
XLA Ops:
  0.6 15.0 %collective-permute-start.1 = (bf16[4,64,256]{2,1,0:T(8,128)(2,1)}, bf16[4,64,256]{2,1,0:T(8,128)(2,1)S(1)}, u32[]{:S(2)}, u32[]{:S(2)}) collective-permute-start(bf16[4,64,256]{2,1,0:T(8,128)(2,1)} %refs_0_.1), channel_id=1, source_target_pairs={{0,4},{1,5},{2,6},{3,7},{4,0},{5,1},{6,2},{7,3},{8,12},{9,13},{10,... | collective-permute-start | bytes 393224 | tf_op jit(solution)/shard_map/ppermute | solution.py:360
  15.6 4.3 %collective-permute-start.2 = (bf16[4,64,256]{2,1,0:T(8,128)(2,1)}, bf16[4,64,256]{2,1,0:T(8,128)(2,1)S(1)}, u32[]{:S(2)}, u32[]{:S(2)}) collective-permute-start(bf16[4,64,256]{2,1,0:T(8,128)(2,1)} %refs_0_.1), channel_id=1, source_target_pairs={{0,2},{1,3},{2,4},{3,5},{4,6},{5,7},{6,0},{7,1},{8,10},{9,11},{10,... | collective-permute-start | bytes 393224 | tf_op jit(solution)/shard_map/ppermute | solution.py:360
  19.9 5.5 %collective-permute-start = (bf16[4,64,256]{2,1,0:T(8,128)(2,1)}, bf16[4,64,256]{2,1,0:T(8,128)(2,1)S(1)}, u32[]{:S(2)}, u32[]{:S(2)}) collective-permute-start(bf16[4,64,256]{2,1,0:T(8,128)(2,1)} %refs_0_.1), channel_id=1, source_target_pairs={{0,6},{1,7},{2,0},{3,1},{4,2},{5,3},{6,4},{7,5},{8,14},{9,15},{10,... | collective-permute-start | bytes 393224 | tf_op jit(solution)/shard_map/ppermute | solution.py:360
  25.4 3.5 %shard_map.131 = bf16[16,32,512]{2,1,0:T(8,128)(2,1)} custom-call(s32[1]{0:T(128)} %bitcast.place, bf16[64,32,128]{2,1,0:T(8,128)(2,1)} %pair_ref.3, bf16[8,128]{1,0:T(8,128)(2,1)} %bitcast.28), custom_call_target="tpu_custom_call" | custom-call | tf_op jit(solution)/shard_map/pallas_call | solution.py:53
  28.9 0.0 copy-start.1
  28.9 0.0 copy-start.5
  28.9 7.2 %all-to-all-start = ((bf16[16,32,512]{2,1,0:T(8,128)(2,1)}), bf16[16,32,512]{2,1,0:T(8,128)(2,1)S(1)}, u32[]{:S(2)}, u32[]{:S(2)}) async-start(bf16[16,32,512]{2,1,0:T(8,128)(2,1)} %shard_map.131), calls=%async_computation | async-start | bytes 1048576 | tf_op jit(solution)/shard_map/all_to_all | solution.py:388
  36.1 0.0 collective-permute-done.1.refs_2_
  36.1 1.9 collective-permute-start.3
  38.1 0.0 collective-permute-done.2.refs_3_
  38.1 2.4 %collective-permute-start.4 = (bf16[2,4,64,256]{3,2,1,0:T(8,128)(2,1)S(1)}, bf16[2,4,64,256]{3,2,1,0:T(8,128)(2,1)S(1)}, u32[]{:S(2)}, u32[]{:S(2)}) collective-permute-start(bf16[2,4,64,256]{3,2,1,0:T(8,128)(2,1)S(1)} %pad_maximum_fusion.1), channel_id=1, source_target_pairs={{0,1},{1,0},{2,3},{3,2},{4,5},{5,4},{6,7},{7,6},{8,9},{9,8},{10,11... | collective-permute-start | bytes 786440 | tf_op jit(solution)/shard_map/ppermute | solution.py:360
  40.6 1.1 collective-permute-done.4.refs_5_
  41.7 5.1 %all-to-all-done = bf16[16,32,512]{2,1,0:T(8,128)(2,1)S(1)} async-done(((bf16[16,32,512]{2,1,0:T(8,128)(2,1)}), bf16[16,32,512]{2,1,0:T(8,128)(2,1)S(1)}, u32[]{:S(2)}, u32[]{:S(2)}) %all-to-all-start) | async-done | bytes 524320 | tf_op jit(solution)/shard_map/all_to_all | solution.py:388
  46.8 0.0 copy-start.8
  46.8 4.4 %shard_map.132 = bf16[64,8,128]{2,1,0:T(8,128)(2,1)S(1)} custom-call(s32[1]{0:T(128)} %bitcast.place, bf16[4,64,256]{2,1,0:T(8,128)(2,1)S(1)} %copy-done.3, bf16[4,64,256]{2,1,0:T(8,128)(2,1)S(1)} %collective-permute-done.refs_1_, bf16[4,64,256]{2,1,0:T(8,128)(2,1)S(1)} %collective-permute-done.1.refs_2_, ...), custom_call_target="tpu_custom_call" | custom-call | tf_op jit(solution)/shard_map/pallas_call | solution.py:53
  51.1 15.6 %all_to_all.35.x_ref = bf16[64,8,128]{2,1,0:T(8,128)(2,1)S(1)} all-to-all(bf16[64,8,128]{2,1,0:T(8,128)(2,1)S(1)} %shard_map.132), channel_id=1, replica_groups=mesh['branch'=4,'row'=16,'col'=8] {'branch','row'}, dimensions={0} | all-to-all | bytes 262144 | tf_op jit(solution)/shard_map/all_to_all | solution.py:388
  66.7 2.7 %shard_map.133 = (bf16[64,8,128]{2,1,0:T(8,128)(2,1)S(1)}, bf16[32,256]{1,0:T(8,128)(2,1)S(1)}, bf16[8,32,256]{2,1,0:T(8,128)(2,1)}) custom-call(s32[1]{0:T(128)} %bitcast.place, bf16[64,8,128]{2,1,0:T(8,128)(2,1)S(1)} %all_to_all.35.x_ref, bf16[256,1024]{1,0:T(8,128)(2,1)S(1)} %copy-done.2, bf16[256,256]{1,0:T(8,128)(2,1)S(1)} %copy-done.7, ...), custom_call_target="tpu_custom_call" | custom-call | tf_op jit(solution)/shard_map/pallas_call | solution.py:53
  69.4 8.5 %all-to-all-start.2 = ((bf16[8,32,256]{2,1,0:T(8,128)(2,1)}), bf16[8,32,256]{2,1,0:T(8,128)(2,1)S(1)}, u32[]{:S(2)}, u32[]{:S(2)}) async-start(bf16[8,32,256]{2,1,0:T(8,128)(2,1)} %get-tuple-element.9), calls=%async_computation.2 | async-start | bytes 262144 | tf_op jit(solution)/shard_map/all_to_all | solution.py:388
  77.8 2.3 %collective-permute-start.7 = (bf16[32,256]{1,0:T(8,128)(2,1)S(1)}, bf16[32,256]{1,0:T(8,128)(2,1)S(1)}, u32[]{:S(2)}, u32[]{:S(2)}) collective-permute-start(bf16[32,256]{1,0:T(8,128)(2,1)S(1)} %get-tuple-element.10.refs_0_), channel_id=1, source_target_pairs={{0,384},{128,256},{256,128},{384,0},{1,385},{129,257},{257,129},{3... | collective-permute-start | bytes 49160 | tf_op jit(solution)/shard_map/ppermute | solution.py:438
  80.2 5.6 %collective-permute-start.6 = (bf16[32,256]{1,0:T(8,128)(2,1)S(1)}, bf16[32,256]{1,0:T(8,128)(2,1)S(1)}, u32[]{:S(2)}, u32[]{:S(2)}) collective-permute-start(bf16[32,256]{1,0:T(8,128)(2,1)S(1)} %get-tuple-element.10.refs_0_), channel_id=1, source_target_pairs={{0,256},{128,384},{256,0},{384,128},{1,257},{129,385},{257,1},{385... | collective-permute-start | bytes 49160 | tf_op jit(solution)/shard_map/ppermute | solution.py:438
  85.8 1.9 collective-permute-start.5
  87.7 0.0 collective-permute-done.7.refs_3_
  87.7 1.7 collective-permute-done.6.refs_2_
  89.4 2.0 collective-permute-done.5.refs_1_
  91.4 1.9 all-to-all-done.2.right_ref
  93.3 0.1 shard_map.134
  93.5 0.0 copy-start
  93.5 0.0 copy-start.4
  93.5 0.0 copy-start.6
  93.5 23.0 %all_to_all.36.factor_ref = bf16[16,160,256]{2,1,0:T(8,128)(2,1)S(1)} all-to-all(bf16[16,160,256]{2,1,0:T(8,128)(2,1)S(1)} %shard_map.134), channel_id=1, replica_groups=mesh['branch'=4,'row'=16,'col'=8] {'row'}, dimensions={0} | all-to-all | bytes 2621440 | tf_op jit(solution)/shard_map/all_to_all | solution.py:388
  116.5 3.1 %shard_map.135 = (bf16[512,128]{1,0:T(8,128)(2,1)S(1)}, bf16[64,2,8,128]{3,2,1,0:T(8,128)(2,1)S(1)}) custom-call(s32[1]{0:T(128)} %bitcast.place, bf16[16,160,256]{2,1,0:T(8,128)(2,1)S(1)} %all_to_all.36.factor_ref, bf16[64,32,128]{2,1,0:T(8,128)(2,1)S(1)} %copy-done, bf16[1024,128]{1,0:T(8,128)(2,1)S(1)} %copy-done.4, bf16[128,512]{1,0:T(8,128)(2,1)S(1)} %copy-done.6), custom_call_target="tpu_custom_call" | custom-call | tf_op jit(solution)/shard_map/pallas_call | solution.py:53
  119.6 16.7 %all_to_all.37 = bf16[64,2,8,128]{3,2,1,0:T(8,128)(2,1)S(1)} all-to-all(bf16[64,2,8,128]{3,2,1,0:T(8,128)(2,1)S(1)} %get-tuple-element.11), channel_id=1, replica_groups=mesh['branch'=4,'row'=16,'col'=8] {'branch','row'}, dimensions={0} | all-to-all | bytes 524288 | tf_op jit(solution)/shard_map/all_to_all | solution.py:388
  136.3 0.1 slice_bitcast_fusion.1
  136.3 3.7 %collective-permute-start.10 = (bf16[512,128]{1,0:T(8,128)(2,1)S(1)}, bf16[512,128]{1,0:T(8,128)(2,1)S(1)}, u32[]{:S(2)}, u32[]{:S(2)}) collective-permute-start(bf16[512,128]{1,0:T(8,128)(2,1)S(1)} %get-tuple-element.17.refs_0_), channel_id=1, source_target_pairs={{0,2},{1,3},{2,4},{3,5},{4,6},{5,7},{6,0},{7,1},{8,10},{9,11},{10,... | collective-permute-start | bytes 393224 | tf_op jit(solution)/shard_map/ppermute | solution.py:360
  140.1 6.0 %collective-permute-start.8 = (bf16[512,128]{1,0:T(8,128)(2,1)S(1)}, bf16[512,128]{1,0:T(8,128)(2,1)S(1)}, u32[]{:S(2)}, u32[]{:S(2)}) collective-permute-start(bf16[512,128]{1,0:T(8,128)(2,1)S(1)} %get-tuple-element.17.refs_0_), channel_id=1, source_target_pairs={{0,6},{1,7},{2,0},{3,1},{4,2},{5,3},{6,4},{7,5},{8,14},{9,15},{10,... | collective-permute-start | bytes 393224 | tf_op jit(solution)/shard_map/ppermute | solution.py:360
  146.1 8.2 %collective-permute-start.9 = (bf16[512,128]{1,0:T(8,128)(2,1)S(1)}, bf16[512,128]{1,0:T(8,128)(2,1)S(1)}, u32[]{:S(2)}, u32[]{:S(2)}) collective-permute-start(bf16[512,128]{1,0:T(8,128)(2,1)S(1)} %get-tuple-element.17.refs_0_), channel_id=1, source_target_pairs={{0,4},{1,5},{2,6},{3,7},{4,0},{5,1},{6,2},{7,3},{8,12},{9,13},{10,... | collective-permute-start | bytes 393224 | tf_op jit(solution)/shard_map/ppermute | solution.py:360
  154.3 0.0 collective-permute-done.10.refs_3_
  154.3 0.9 collective-permute-done.8.refs_1_
  155.3 1.9 collective-permute-start.12
  157.2 13.3 %collective-permute-done.9.refs_2_ = bf16[512,128]{1,0:T(8,128)(2,1)S(1)} collective-permute-done((bf16[512,128]{1,0:T(8,128)(2,1)S(1)}, bf16[512,128]{1,0:T(8,128)(2,1)S(1)}, u32[]{:S(2)}, u32[]{:S(2)}) %collective-permute-start.9) | collective-permute-done | bytes 131104 | tf_op jit(solution)/shard_map/ppermute | solution.py:360
  170.6 1.9 collective-permute-start.11
  172.5 0.0 collective-permute-done.12.refs_5_
  172.5 1.5 collective-permute-done.11.refs_4_
  174.0 0.5 shard_map.136
  174.5 18.1 %all_to_all.38.sum_ref = bf16[64,2,8,128]{3,2,1,0:T(8,128)(2,1)S(1)} all-to-all(bf16[64,2,8,128]{3,2,1,0:T(8,128)(2,1)S(1)} %shard_map.136), channel_id=1, replica_groups=mesh['branch'=4,'row'=16,'col'=8] {'branch','row'}, dimensions={0} | all-to-all | bytes 524288 | tf_op jit(solution)/shard_map/all_to_all | solution.py:388
  192.6 1.8 shard_map.137
  194.4 9.4 %all_to_all.39.x_ref = bf16[4,4,32,128]{3,2,1,0:T(8,128)(2,1)S(1)} all-to-all(bf16[4,4,32,128]{3,2,1,0:T(8,128)(2,1)S(1)} %get-tuple-element.15), channel_id=1, replica_groups=mesh['branch'=4,'row'=16,'col'=8] {'branch'}, dimensions={0} | all-to-all | bytes 262144 | tf_op jit(solution)/shard_map/all_to_all | solution.py:388
  203.9 0.8 unpack.1
  (22 shorter events, 0.1 us)
Async XLA Ops:
  0.6 35.5 %copy-start.3 = (bf16[4,64,256]{2,1,0:T(8,128)(2,1)S(1)}, bf16[4,64,256]{2,1,0:T(8,128)(2,1)}, u32[]{:S(2)}) copy-start(bf16[4,64,256]{2,1,0:T(8,128)(2,1)} %refs_0_.1) | copy-start | bytes 393220
  0.6 35.5 %collective-permute-start.1 = (bf16[4,64,256]{2,1,0:T(8,128)(2,1)}, bf16[4,64,256]{2,1,0:T(8,128)(2,1)S(1)}, u32[]{:S(2)}, u32[]{:S(2)}) collective-permute-start(bf16[4,64,256]{2,1,0:T(8,128)(2,1)} %refs_0_.1), channel_id=1, source_target_pairs={{0,4},{1,5},{2,6},{3,7},{4,0},{5,1},{6,2},{7,3},{8,12},{9,13},{10,... | collective-permute-start | bytes 393224 | tf_op jit(solution)/shard_map/ppermute | solution.py:360
  15.6 22.5 %collective-permute-start.2 = (bf16[4,64,256]{2,1,0:T(8,128)(2,1)}, bf16[4,64,256]{2,1,0:T(8,128)(2,1)S(1)}, u32[]{:S(2)}, u32[]{:S(2)}) collective-permute-start(bf16[4,64,256]{2,1,0:T(8,128)(2,1)} %refs_0_.1), channel_id=1, source_target_pairs={{0,2},{1,3},{2,4},{3,5},{4,6},{5,7},{6,0},{7,1},{8,10},{9,11},{10,... | collective-permute-start | bytes 393224 | tf_op jit(solution)/shard_map/ppermute | solution.py:360
  19.9 18.2 %collective-permute-start = (bf16[4,64,256]{2,1,0:T(8,128)(2,1)}, bf16[4,64,256]{2,1,0:T(8,128)(2,1)S(1)}, u32[]{:S(2)}, u32[]{:S(2)}) collective-permute-start(bf16[4,64,256]{2,1,0:T(8,128)(2,1)} %refs_0_.1), channel_id=1, source_target_pairs={{0,6},{1,7},{2,0},{3,1},{4,2},{5,3},{6,4},{7,5},{8,14},{9,15},{10,... | collective-permute-start | bytes 393224 | tf_op jit(solution)/shard_map/ppermute | solution.py:360
  28.9 17.9 %copy-start.1 = (bf16[256,1024]{1,0:T(8,128)(2,1)S(1)}, bf16[256,1024]{1,0:T(8,128)(2,1)}, u32[]{:S(2)}) copy-start(bf16[256,1024]{1,0:T(8,128)(2,1)} %refs_6_.1) | copy-start | bytes 1572868
  28.9 17.9 %copy-start.5 = (bf16[256,256]{1,0:T(8,128)(2,1)S(1)}, bf16[256,256]{1,0:T(8,128)(2,1)}, u32[]{:S(2)}) copy-start(bf16[256,256]{1,0:T(8,128)(2,1)} %refs_8_.1) | copy-start | bytes 393220
  28.9 17.8 %all-to-all-start = ((bf16[16,32,512]{2,1,0:T(8,128)(2,1)}), bf16[16,32,512]{2,1,0:T(8,128)(2,1)S(1)}, u32[]{:S(2)}, u32[]{:S(2)}) async-start(bf16[16,32,512]{2,1,0:T(8,128)(2,1)} %shard_map.131), calls=%async_computation | async-start | bytes 1048576 | tf_op jit(solution)/shard_map/all_to_all | solution.py:388
  36.1 4.4 %collective-permute-start.3 = (bf16[2,4,64,256]{3,2,1,0:T(8,128)(2,1)S(1)}, bf16[2,4,64,256]{3,2,1,0:T(8,128)(2,1)S(1)}, u32[]{:S(2)}, u32[]{:S(2)}) collective-permute-start(bf16[2,4,64,256]{3,2,1,0:T(8,128)(2,1)S(1)} %pad_maximum_fusion), channel_id=1, source_target_pairs={{0,1},{1,0},{2,3},{3,2},{4,5},{5,4},{6,7},{7,6},{8,9},{9,8},{10,11... | collective-permute-start | bytes 786440 | tf_op jit(solution)/shard_map/ppermute | solution.py:360
  38.1 3.6 %collective-permute-start.4 = (bf16[2,4,64,256]{3,2,1,0:T(8,128)(2,1)S(1)}, bf16[2,4,64,256]{3,2,1,0:T(8,128)(2,1)S(1)}, u32[]{:S(2)}, u32[]{:S(2)}) collective-permute-start(bf16[2,4,64,256]{3,2,1,0:T(8,128)(2,1)S(1)} %pad_maximum_fusion.1), channel_id=1, source_target_pairs={{0,1},{1,0},{2,3},{3,2},{4,5},{5,4},{6,7},{7,6},{8,9},{9,8},{10,11... | collective-permute-start | bytes 786440 | tf_op jit(solution)/shard_map/ppermute | solution.py:360
  46.7 20.0 %copy-start.2 = (bf16[256,1024]{1,0:T(8,128)(2,1)S(1)}, bf16[256,1024]{1,0:T(8,128)(2,1)}, u32[]{:S(2)}) copy-start(bf16[256,1024]{1,0:T(8,128)(2,1)} %w_ref.3) | copy-start | bytes 1572868
  46.7 20.0 %copy-start.7 = (bf16[256,256]{1,0:T(8,128)(2,1)S(1)}, bf16[256,256]{1,0:T(8,128)(2,1)}, u32[]{:S(2)}) copy-start(bf16[256,256]{1,0:T(8,128)(2,1)} %wo_ref.2) | copy-start | bytes 393220
  46.8 20.0 %copy-start.8 = (bf16[256,64]{0,1:T(8,128)(2,1)S(1)}, bf16[256,64]{0,1:T(8,128)(2,1)}, u32[]{:S(2)}) copy-start(bf16[256,64]{0,1:T(8,128)(2,1)} %param.19) | copy-start | bytes 98308
  69.4 24.0 %all-to-all-start.2 = ((bf16[8,32,256]{2,1,0:T(8,128)(2,1)}), bf16[8,32,256]{2,1,0:T(8,128)(2,1)S(1)}, u32[]{:S(2)}, u32[]{:S(2)}) async-start(bf16[8,32,256]{2,1,0:T(8,128)(2,1)} %get-tuple-element.9), calls=%async_computation.2 | async-start | bytes 262144 | tf_op jit(solution)/shard_map/all_to_all | solution.py:388
  77.8 9.9 %collective-permute-start.7 = (bf16[32,256]{1,0:T(8,128)(2,1)S(1)}, bf16[32,256]{1,0:T(8,128)(2,1)S(1)}, u32[]{:S(2)}, u32[]{:S(2)}) collective-permute-start(bf16[32,256]{1,0:T(8,128)(2,1)S(1)} %get-tuple-element.10.refs_0_), channel_id=1, source_target_pairs={{0,384},{128,256},{256,128},{384,0},{1,385},{129,257},{257,129},{3... | collective-permute-start | bytes 49160 | tf_op jit(solution)/shard_map/ppermute | solution.py:438
  80.2 9.2 %collective-permute-start.6 = (bf16[32,256]{1,0:T(8,128)(2,1)S(1)}, bf16[32,256]{1,0:T(8,128)(2,1)S(1)}, u32[]{:S(2)}, u32[]{:S(2)}) collective-permute-start(bf16[32,256]{1,0:T(8,128)(2,1)S(1)} %get-tuple-element.10.refs_0_), channel_id=1, source_target_pairs={{0,256},{128,384},{256,0},{384,128},{1,257},{129,385},{257,1},{385... | collective-permute-start | bytes 49160 | tf_op jit(solution)/shard_map/ppermute | solution.py:438
  85.8 5.6 %collective-permute-start.5 = (bf16[32,256]{1,0:T(8,128)(2,1)S(1)}, bf16[32,256]{1,0:T(8,128)(2,1)S(1)}, u32[]{:S(2)}, u32[]{:S(2)}) collective-permute-start(bf16[32,256]{1,0:T(8,128)(2,1)S(1)} %get-tuple-element.10.refs_0_), channel_id=1, source_target_pairs={{0,128},{128,0},{256,384},{384,256},{1,129},{129,1},{257,385},{385... | collective-permute-start | bytes 49160 | tf_op jit(solution)/shard_map/ppermute | solution.py:438
  93.5 23.0 %copy-start = (bf16[64,32,128]{2,1,0:T(8,128)(2,1)S(1)}, bf16[64,32,128]{2,1,0:T(8,128)(2,1)}, u32[]{:S(2)}) copy-start(bf16[64,32,128]{2,1,0:T(8,128)(2,1)} %pair_ref.3) | copy-start | bytes 1572868
  93.5 23.0 %copy-start.4 = (bf16[1024,128]{1,0:T(8,128)(2,1)S(1)}, bf16[1024,128]{1,0:T(8,128)(2,1)}, u32[]{:S(2)}) copy-start(bf16[1024,128]{1,0:T(8,128)(2,1)} %wo_ref.3) | copy-start | bytes 786436
  93.5 23.0 %copy-start.6 = (bf16[128,512]{1,0:T(8,128)(2,1)S(1)}, bf16[128,512]{1,0:T(8,128)(2,1)}, u32[]{:S(2)}) copy-start(bf16[128,512]{1,0:T(8,128)(2,1)} %w_ref.4) | copy-start | bytes 393220
  136.3 18.0 %collective-permute-start.10 = (bf16[512,128]{1,0:T(8,128)(2,1)S(1)}, bf16[512,128]{1,0:T(8,128)(2,1)S(1)}, u32[]{:S(2)}, u32[]{:S(2)}) collective-permute-start(bf16[512,128]{1,0:T(8,128)(2,1)S(1)} %get-tuple-element.17.refs_0_), channel_id=1, source_target_pairs={{0,2},{1,3},{2,4},{3,5},{4,6},{5,7},{6,0},{7,1},{8,10},{9,11},{10,... | collective-permute-start | bytes 393224 | tf_op jit(solution)/shard_map/ppermute | solution.py:360
  140.1 15.2 %collective-permute-start.8 = (bf16[512,128]{1,0:T(8,128)(2,1)S(1)}, bf16[512,128]{1,0:T(8,128)(2,1)S(1)}, u32[]{:S(2)}, u32[]{:S(2)}) collective-permute-start(bf16[512,128]{1,0:T(8,128)(2,1)S(1)} %get-tuple-element.17.refs_0_), channel_id=1, source_target_pairs={{0,6},{1,7},{2,0},{3,1},{4,2},{5,3},{6,4},{7,5},{8,14},{9,15},{10,... | collective-permute-start | bytes 393224 | tf_op jit(solution)/shard_map/ppermute | solution.py:360
  146.1 24.4 %collective-permute-start.9 = (bf16[512,128]{1,0:T(8,128)(2,1)S(1)}, bf16[512,128]{1,0:T(8,128)(2,1)S(1)}, u32[]{:S(2)}, u32[]{:S(2)}) collective-permute-start(bf16[512,128]{1,0:T(8,128)(2,1)S(1)} %get-tuple-element.17.refs_0_), channel_id=1, source_target_pairs={{0,4},{1,5},{2,6},{3,7},{4,0},{5,1},{6,2},{7,3},{8,12},{9,13},{10,... | collective-permute-start | bytes 393224 | tf_op jit(solution)/shard_map/ppermute | solution.py:360
  155.3 17.2 %collective-permute-start.12 = (bf16[2,512,128]{2,1,0:T(8,128)(2,1)S(1)}, bf16[2,512,128]{2,1,0:T(8,128)(2,1)S(1)}, u32[]{:S(2)}, u32[]{:S(2)}) collective-permute-start(bf16[2,512,128]{2,1,0:T(8,128)(2,1)S(1)} %pad_maximum_fusion.3), channel_id=1, source_target_pairs={{0,1},{1,0},{2,3},{3,2},{4,5},{5,4},{6,7},{7,6},{8,9},{9,8},{10,11... | collective-permute-start | bytes 786440 | tf_op jit(solution)/shard_map/ppermute | solution.py:360
  170.5 22.1 %copy-start.9 = (bf16[128,128]{1,0:T(8,128)(2,1)S(1)}, bf16[128,128]{1,0:T(8,128)(2,1)}, u32[]{:S(2)}) copy-start(bf16[128,128]{1,0:T(8,128)(2,1)} %wg_ref.1) | copy-start | bytes 98308
  170.5 22.1 %copy-start.10 = (bf16[128,128]{1,0:T(8,128)(2,1)S(1)}, bf16[128,128]{1,0:T(8,128)(2,1)}, u32[]{:S(2)}) copy-start(bf16[128,128]{1,0:T(8,128)(2,1)} %w_ref.5) | copy-start | bytes 98308
  170.6 3.4 %collective-permute-start.11 = (bf16[2,512,128]{2,1,0:T(8,128)(2,1)S(1)}, bf16[2,512,128]{2,1,0:T(8,128)(2,1)S(1)}, u32[]{:S(2)}, u32[]{:S(2)}) collective-permute-start(bf16[2,512,128]{2,1,0:T(8,128)(2,1)S(1)} %pad_maximum_fusion.2), channel_id=1, source_target_pairs={{0,1},{1,0},{2,3},{3,2},{4,5},{5,4},{6,7},{7,6},{8,9},{9,8},{10,11... | collective-permute-start | bytes 786440 | tf_op jit(solution)/shard_map/ppermute | solution.py:360

commit v9 on v8

--- a/solution.py
+++ b/solution.py
@@ -162,9 +162,8 @@
         for h in range(2):
             for b in range(4):
                 source = (h * 4 + b) * 8
-                target = (b * 2 + h) * 8
                 for half in range(2):
-                    packed[target : target + 8, half * 4 + s, :] = result[
+                    packed[pl.ds(h * 32 + b, 8, stride=4), half * 4 + s, :] = result[
                         source : source + 8, half * 128 : (half + 1) * 128
                     ]
     out_ref[...] = packed[...].astype(BF)
@@ -309,7 +308,7 @@
         target = source_of(col_of(place), m) * 2
         for b in range(4):
             for h in range(2):
-                out_ref[b * 16 + target + h, 0] = block[(b * 2 + h) * 8 : (b * 2 + h + 1) * 8]
+                out_ref[(target + h) * 4 + b, 0] = block[(b * 2 + h) * 8 : (b * 2 + h + 1) * 8]
     out_ref[:, 1] = back_ref[...]
 
 
@@ -339,11 +338,12 @@
         for b in range(4):
             out_ref[b, j] = part[b * 32 : (b + 1) * 32]
     rows[...] = sum_ref[:, 1].astype(F32)
-    order = [(b * 2 + h) * 8 for h in range(2) for b in range(4)]
+    starts = [h * 32 + b for h in range(2) for b in range(4)]
     for s in range(4):
         for half in range(2):
-            block = rows[:, half * 4 + s, :]
-            block = jnp.concatenate([block[k : k + 8] for k in order], axis=0)
+            block = jnp.concatenate(
+                [rows[pl.ds(k, 8, stride=4), half * 4 + s, :] for k in starts], axis=0
+            )
             back_ref[s, :, half * 128 : (half + 1) * 128] = block.astype(BF)
 
 
@@ -383,7 +383,7 @@
     w_triangle_gate,
     w_triangle_out,
 ):
-    both = ("branch", "row")
+    both = ("row", "branch")
     place = lax.axis_index(("branch", "row", "col")).astype(jnp.int32).reshape(1)
     exchange = lambda x, axis: lax.all_to_all(x, axis, 0, 0, tiled=True)
 

time: 206 us -> 205 us (level)
  no operation moved by 1% of the time
where the time goes in v9:
time: 205 us; the launch traced here: 204 us
  blocking collectives  81.5 us (40%)
  starting transfers between devices  75.7 us (37%)
  waiting for transfers between devices  29 us (14%)
  Pallas kernels  16.9 us (8%)
    all_to_all x5, blocking collectives, local(): exchange = lambda x, axis: lax.all_to_all(x, axis, 0, 0, tiled=True)  81.5 us
    ppermute x10, starting transfers between devices, shifted(): return lax.ppermute(x, 'col', perm)  50.5 us
    ppermute x10, waiting for transfers between devices, shifted(): return lax.ppermute(x, 'col', perm)  17.7 us
    pallas_call x7, Pallas kernels, in_vmem(): pl.pallas_call(kernel, out_shape=tuple(shapes), in_specs=[SM] + [HB] * lo...  16.1 us
    all_to_all x2, starting transfers between devices, local(): exchange = lambda x, axis: lax.all_to_all(x, axis, 0, 0, tiled=True)  15.6 us
    ppermute x3, starting transfers between devices, local(): lax.ppermute(left, 'branch', [(b, b ^ mask) for b in range(4)])  9.51 us
    all_to_all x2, waiting for transfers between devices, local(): exchange = lambda x, axis: lax.all_to_all(x, axis, 0, 0, tiled=True)  7.61 us
  transfers between devices with their start and end apart: 15, of which 8 were waited for; matrix products, arithmetic and copies ran while one was open for 0% of the time, Pallas kernels for 2%

profile of v9, /device:TPU:32, one launch (start us, length us, event | category | flops | bytes accessed | tf_op | source)
XLA Modules:
  0.0 204.3 jit_solution(7216471847475796004)
XLA Ops:
  0.6 15.0 %collective-permute-start.1 = (bf16[4,64,256]{2,1,0:T(8,128)(2,1)}, bf16[4,64,256]{2,1,0:T(8,128)(2,1)S(1)}, u32[]{:S(2)}, u32[]{:S(2)}) collective-permute-start(bf16[4,64,256]{2,1,0:T(8,128)(2,1)} %refs_0_.1), channel_id=1, source_target_pairs={{0,4},{1,5},{2,6},{3,7},{4,0},{5,1},{6,2},{7,3},{8,12},{9,13},{10,... | collective-permute-start | bytes 393224 | tf_op jit(solution)/shard_map/ppermute | solution.py:360
  15.6 4.3 %collective-permute-start.2 = (bf16[4,64,256]{2,1,0:T(8,128)(2,1)}, bf16[4,64,256]{2,1,0:T(8,128)(2,1)S(1)}, u32[]{:S(2)}, u32[]{:S(2)}) collective-permute-start(bf16[4,64,256]{2,1,0:T(8,128)(2,1)} %refs_0_.1), channel_id=1, source_target_pairs={{0,2},{1,3},{2,4},{3,5},{4,6},{5,7},{6,0},{7,1},{8,10},{9,11},{10,... | collective-permute-start | bytes 393224 | tf_op jit(solution)/shard_map/ppermute | solution.py:360
  19.9 5.5 %collective-permute-start = (bf16[4,64,256]{2,1,0:T(8,128)(2,1)}, bf16[4,64,256]{2,1,0:T(8,128)(2,1)S(1)}, u32[]{:S(2)}, u32[]{:S(2)}) collective-permute-start(bf16[4,64,256]{2,1,0:T(8,128)(2,1)} %refs_0_.1), channel_id=1, source_target_pairs={{0,6},{1,7},{2,0},{3,1},{4,2},{5,3},{6,4},{7,5},{8,14},{9,15},{10,... | collective-permute-start | bytes 393224 | tf_op jit(solution)/shard_map/ppermute | solution.py:360
  25.4 3.5 %shard_map.131 = bf16[16,32,512]{2,1,0:T(8,128)(2,1)} custom-call(s32[1]{0:T(128)} %bitcast.place, bf16[64,32,128]{2,1,0:T(8,128)(2,1)} %pair_ref.3, bf16[8,128]{1,0:T(8,128)(2,1)} %bitcast.28), custom_call_target="tpu_custom_call" | custom-call | tf_op jit(solution)/shard_map/pallas_call | solution.py:53
  28.9 0.0 copy-start.1
  28.9 0.0 copy-start.5
  28.9 7.2 %all-to-all-start = ((bf16[16,32,512]{2,1,0:T(8,128)(2,1)}), bf16[16,32,512]{2,1,0:T(8,128)(2,1)S(1)}, u32[]{:S(2)}, u32[]{:S(2)}) async-start(bf16[16,32,512]{2,1,0:T(8,128)(2,1)} %shard_map.131), calls=%async_computation | async-start | bytes 1048576 | tf_op jit(solution)/shard_map/all_to_all | solution.py:388
  36.1 0.0 collective-permute-done.1.refs_2_
  36.1 1.9 collective-permute-start.3
  38.1 0.0 collective-permute-done.2.refs_3_
  38.1 0.0 collective-permute-done.refs_1_
  38.1 2.4 %collective-permute-start.4 = (bf16[2,4,64,256]{3,2,1,0:T(8,128)(2,1)S(1)}, bf16[2,4,64,256]{3,2,1,0:T(8,128)(2,1)S(1)}, u32[]{:S(2)}, u32[]{:S(2)}) collective-permute-start(bf16[2,4,64,256]{3,2,1,0:T(8,128)(2,1)S(1)} %pad_maximum_fusion.1), channel_id=1, source_target_pairs={{0,1},{1,0},{2,3},{3,2},{4,5},{5,4},{6,7},{7,6},{8,9},{9,8},{10,11... | collective-permute-start | bytes 786440 | tf_op jit(solution)/shard_map/ppermute | solution.py:360
  40.5 0.0 collective-permute-done.3.refs_4_
  40.6 1.1 collective-permute-done.4.refs_5_
  41.7 5.1 %all-to-all-done = bf16[16,32,512]{2,1,0:T(8,128)(2,1)S(1)} async-done(((bf16[16,32,512]{2,1,0:T(8,128)(2,1)}), bf16[16,32,512]{2,1,0:T(8,128)(2,1)S(1)}, u32[]{:S(2)}, u32[]{:S(2)}) %all-to-all-start) | async-done | bytes 524320 | tf_op jit(solution)/shard_map/all_to_all | solution.py:388
  46.8 0.0 copy-start.8
  46.8 4.4 %shard_map.132 = bf16[64,8,128]{2,1,0:T(8,128)(2,1)S(1)} custom-call(s32[1]{0:T(128)} %bitcast.place, bf16[4,64,256]{2,1,0:T(8,128)(2,1)S(1)} %copy-done.3, bf16[4,64,256]{2,1,0:T(8,128)(2,1)S(1)} %collective-permute-done.refs_1_, bf16[4,64,256]{2,1,0:T(8,128)(2,1)S(1)} %collective-permute-done.1.refs_2_, ...), custom_call_target="tpu_custom_call" | custom-call | tf_op jit(solution)/shard_map/pallas_call | solution.py:53
  51.1 15.6 %all_to_all.35.x_ref = bf16[64,8,128]{2,1,0:T(8,128)(2,1)S(1)} all-to-all(bf16[64,8,128]{2,1,0:T(8,128)(2,1)S(1)} %shard_map.132), channel_id=1, replica_groups=mesh['branch'=4,'row'=16,'col'=8] {'row','branch'}, dimensions={0} | all-to-all | bytes 262144 | tf_op jit(solution)/shard_map/all_to_all | solution.py:388
  66.8 2.7 %shard_map.133 = (bf16[64,8,128]{2,1,0:T(8,128)(2,1)S(1)}, bf16[32,256]{1,0:T(8,128)(2,1)S(1)}, bf16[8,32,256]{2,1,0:T(8,128)(2,1)}) custom-call(s32[1]{0:T(128)} %bitcast.place, bf16[64,8,128]{2,1,0:T(8,128)(2,1)S(1)} %all_to_all.35.x_ref, bf16[256,1024]{1,0:T(8,128)(2,1)S(1)} %copy-done.2, bf16[256,256]{1,0:T(8,128)(2,1)S(1)} %copy-done.7, ...), custom_call_target="tpu_custom_call" | custom-call | tf_op jit(solution)/shard_map/pallas_call | solution.py:53
  69.4 8.5 %all-to-all-start.2 = ((bf16[8,32,256]{2,1,0:T(8,128)(2,1)}), bf16[8,32,256]{2,1,0:T(8,128)(2,1)S(1)}, u32[]{:S(2)}, u32[]{:S(2)}) async-start(bf16[8,32,256]{2,1,0:T(8,128)(2,1)} %get-tuple-element.9), calls=%async_computation.2 | async-start | bytes 262144 | tf_op jit(solution)/shard_map/all_to_all | solution.py:388
  77.9 2.4 %collective-permute-start.7 = (bf16[32,256]{1,0:T(8,128)(2,1)S(1)}, bf16[32,256]{1,0:T(8,128)(2,1)S(1)}, u32[]{:S(2)}, u32[]{:S(2)}) collective-permute-start(bf16[32,256]{1,0:T(8,128)(2,1)S(1)} %get-tuple-element.10.refs_0_), channel_id=1, source_target_pairs={{0,384},{128,256},{256,128},{384,0},{1,385},{129,257},{257,129},{3... | collective-permute-start | bytes 49160 | tf_op jit(solution)/shard_map/ppermute | solution.py:438
  80.3 5.2 %collective-permute-start.6 = (bf16[32,256]{1,0:T(8,128)(2,1)S(1)}, bf16[32,256]{1,0:T(8,128)(2,1)S(1)}, u32[]{:S(2)}, u32[]{:S(2)}) collective-permute-start(bf16[32,256]{1,0:T(8,128)(2,1)S(1)} %get-tuple-element.10.refs_0_), channel_id=1, source_target_pairs={{0,256},{128,384},{256,0},{384,128},{1,257},{129,385},{257,1},{385... | collective-permute-start | bytes 49160 | tf_op jit(solution)/shard_map/ppermute | solution.py:438
  85.5 1.9 collective-permute-start.5
  87.4 1.9 collective-permute-done.6.refs_2_
  89.3 1.8 collective-permute-done.5.refs_1_
  91.1 2.6 %all-to-all-done.2.right_ref = bf16[8,32,256]{2,1,0:T(8,128)(2,1)S(1)} async-done(((bf16[8,32,256]{2,1,0:T(8,128)(2,1)}), bf16[8,32,256]{2,1,0:T(8,128)(2,1)S(1)}, u32[]{:S(2)}, u32[]{:S(2)}) %all-to-all-start.2) | async-done | bytes 131104 | tf_op jit(solution)/shard_map/all_to_all | solution.py:388
  93.7 0.1 shard_map.134
  93.8 0.0 copy-start
  93.8 0.0 copy-start.4
  93.8 0.0 copy-start.6
  93.9 23.1 %all_to_all.36.factor_ref = bf16[16,160,256]{2,1,0:T(8,128)(2,1)S(1)} all-to-all(bf16[16,160,256]{2,1,0:T(8,128)(2,1)S(1)} %shard_map.134), channel_id=1, replica_groups=mesh['branch'=4,'row'=16,'col'=8] {'row'}, dimensions={0} | all-to-all | bytes 2621440 | tf_op jit(solution)/shard_map/all_to_all | solution.py:388
  117.0 3.1 %shard_map.135 = (bf16[512,128]{1,0:T(8,128)(2,1)S(1)}, bf16[64,2,8,128]{3,2,1,0:T(8,128)(2,1)S(1)}) custom-call(s32[1]{0:T(128)} %bitcast.place, bf16[16,160,256]{2,1,0:T(8,128)(2,1)S(1)} %all_to_all.36.factor_ref, bf16[64,32,128]{2,1,0:T(8,128)(2,1)S(1)} %copy-done, bf16[1024,128]{1,0:T(8,128)(2,1)S(1)} %copy-done.4, bf16[128,512]{1,0:T(8,128)(2,1)S(1)} %copy-done.6), custom_call_target="tpu_custom_call" | custom-call | tf_op jit(solution)/shard_map/pallas_call | solution.py:53
  120.1 16.6 %all_to_all.37 = bf16[64,2,8,128]{3,2,1,0:T(8,128)(2,1)S(1)} all-to-all(bf16[64,2,8,128]{3,2,1,0:T(8,128)(2,1)S(1)} %get-tuple-element.11), channel_id=1, replica_groups=mesh['branch'=4,'row'=16,'col'=8] {'row','branch'}, dimensions={0} | all-to-all | bytes 524288 | tf_op jit(solution)/shard_map/all_to_all | solution.py:388
  136.6 0.1 slice_bitcast_fusion.1
  136.7 3.7 %collective-permute-start.10 = (bf16[512,128]{1,0:T(8,128)(2,1)S(1)}, bf16[512,128]{1,0:T(8,128)(2,1)S(1)}, u32[]{:S(2)}, u32[]{:S(2)}) collective-permute-start(bf16[512,128]{1,0:T(8,128)(2,1)S(1)} %get-tuple-element.17.refs_0_), channel_id=1, source_target_pairs={{0,2},{1,3},{2,4},{3,5},{4,6},{5,7},{6,0},{7,1},{8,10},{9,11},{10,... | collective-permute-start | bytes 393224 | tf_op jit(solution)/shard_map/ppermute | solution.py:360
  140.4 6.1 %collective-permute-start.8 = (bf16[512,128]{1,0:T(8,128)(2,1)S(1)}, bf16[512,128]{1,0:T(8,128)(2,1)S(1)}, u32[]{:S(2)}, u32[]{:S(2)}) collective-permute-start(bf16[512,128]{1,0:T(8,128)(2,1)S(1)} %get-tuple-element.17.refs_0_), channel_id=1, source_target_pairs={{0,6},{1,7},{2,0},{3,1},{4,2},{5,3},{6,4},{7,5},{8,14},{9,15},{10,... | collective-permute-start | bytes 393224 | tf_op jit(solution)/shard_map/ppermute | solution.py:360
  146.5 7.9 %collective-permute-start.9 = (bf16[512,128]{1,0:T(8,128)(2,1)S(1)}, bf16[512,128]{1,0:T(8,128)(2,1)S(1)}, u32[]{:S(2)}, u32[]{:S(2)}) collective-permute-start(bf16[512,128]{1,0:T(8,128)(2,1)S(1)} %get-tuple-element.17.refs_0_), channel_id=1, source_target_pairs={{0,4},{1,5},{2,6},{3,7},{4,0},{5,1},{6,2},{7,3},{8,12},{9,13},{10,... | collective-permute-start | bytes 393224 | tf_op jit(solution)/shard_map/ppermute | solution.py:360
  154.4 2.3 %collective-permute-done.8.refs_1_ = bf16[512,128]{1,0:T(8,128)(2,1)S(1)} collective-permute-done((bf16[512,128]{1,0:T(8,128)(2,1)S(1)}, bf16[512,128]{1,0:T(8,128)(2,1)S(1)}, u32[]{:S(2)}, u32[]{:S(2)}) %collective-permute-start.8) | collective-permute-done | bytes 131104 | tf_op jit(solution)/shard_map/ppermute | solution.py:360
  156.7 1.9 collective-permute-start.12
  158.6 12.8 %collective-permute-done.9.refs_2_ = bf16[512,128]{1,0:T(8,128)(2,1)S(1)} collective-permute-done((bf16[512,128]{1,0:T(8,128)(2,1)S(1)}, bf16[512,128]{1,0:T(8,128)(2,1)S(1)}, u32[]{:S(2)}, u32[]{:S(2)}) %collective-permute-start.9) | collective-permute-done | bytes 131104 | tf_op jit(solution)/shard_map/ppermute | solution.py:360
  171.5 1.9 collective-permute-start.11
  173.4 0.0 collective-permute-done.12.refs_5_
  173.4 1.5 collective-permute-done.11.refs_4_
  174.9 0.5 shard_map.136
  175.4 17.2 %all_to_all.38.sum_ref = bf16[64,2,8,128]{3,2,1,0:T(8,128)(2,1)S(1)} all-to-all(bf16[64,2,8,128]{3,2,1,0:T(8,128)(2,1)S(1)} %shard_map.136), channel_id=1, replica_groups=mesh['branch'=4,'row'=16,'col'=8] {'row','branch'}, dimensions={0} | all-to-all | bytes 524288 | tf_op jit(solution)/shard_map/all_to_all | solution.py:388
  192.6 1.8 shard_map.137
  194.4 9.1 %all_to_all.39.x_ref = bf16[4,4,32,128]{3,2,1,0:T(8,128)(2,1)S(1)} all-to-all(bf16[4,4,32,128]{3,2,1,0:T(8,128)(2,1)S(1)} %get-tuple-element.15), channel_id=1, replica_groups=mesh['branch'=4,'row'=16,'col'=8] {'branch'}, dimensions={0} | all-to-all | bytes 262144 | tf_op jit(solution)/shard_map/all_to_all | solution.py:388
  203.5 0.8 unpack.1
  (22 shorter events, 0.1 us)
Async XLA Ops:
  0.6 35.5 %copy-start.3 = (bf16[4,64,256]{2,1,0:T(8,128)(2,1)S(1)}, bf16[4,64,256]{2,1,0:T(8,128)(2,1)}, u32[]{:S(2)}) copy-start(bf16[4,64,256]{2,1,0:T(8,128)(2,1)} %refs_0_.1) | copy-start | bytes 393220
  0.6 35.5 %collective-permute-start.1 = (bf16[4,64,256]{2,1,0:T(8,128)(2,1)}, bf16[4,64,256]{2,1,0:T(8,128)(2,1)S(1)}, u32[]{:S(2)}, u32[]{:S(2)}) collective-permute-start(bf16[4,64,256]{2,1,0:T(8,128)(2,1)} %refs_0_.1), channel_id=1, source_target_pairs={{0,4},{1,5},{2,6},{3,7},{4,0},{5,1},{6,2},{7,3},{8,12},{9,13},{10,... | collective-permute-start | bytes 393224 | tf_op jit(solution)/shard_map/ppermute | solution.py:360
  15.6 22.5 %collective-permute-start.2 = (bf16[4,64,256]{2,1,0:T(8,128)(2,1)}, bf16[4,64,256]{2,1,0:T(8,128)(2,1)S(1)}, u32[]{:S(2)}, u32[]{:S(2)}) collective-permute-start(bf16[4,64,256]{2,1,0:T(8,128)(2,1)} %refs_0_.1), channel_id=1, source_target_pairs={{0,2},{1,3},{2,4},{3,5},{4,6},{5,7},{6,0},{7,1},{8,10},{9,11},{10,... | collective-permute-start | bytes 393224 | tf_op jit(solution)/shard_map/ppermute | solution.py:360
  19.9 18.2 %collective-permute-start = (bf16[4,64,256]{2,1,0:T(8,128)(2,1)}, bf16[4,64,256]{2,1,0:T(8,128)(2,1)S(1)}, u32[]{:S(2)}, u32[]{:S(2)}) collective-permute-start(bf16[4,64,256]{2,1,0:T(8,128)(2,1)} %refs_0_.1), channel_id=1, source_target_pairs={{0,6},{1,7},{2,0},{3,1},{4,2},{5,3},{6,4},{7,5},{8,14},{9,15},{10,... | collective-permute-start | bytes 393224 | tf_op jit(solution)/shard_map/ppermute | solution.py:360
  28.9 17.9 %copy-start.1 = (bf16[256,1024]{1,0:T(8,128)(2,1)S(1)}, bf16[256,1024]{1,0:T(8,128)(2,1)}, u32[]{:S(2)}) copy-start(bf16[256,1024]{1,0:T(8,128)(2,1)} %refs_6_.1) | copy-start | bytes 1572868
  28.9 17.9 %copy-start.5 = (bf16[256,256]{1,0:T(8,128)(2,1)S(1)}, bf16[256,256]{1,0:T(8,128)(2,1)}, u32[]{:S(2)}) copy-start(bf16[256,256]{1,0:T(8,128)(2,1)} %refs_8_.1) | copy-start | bytes 393220
  28.9 17.8 %all-to-all-start = ((bf16[16,32,512]{2,1,0:T(8,128)(2,1)}), bf16[16,32,512]{2,1,0:T(8,128)(2,1)S(1)}, u32[]{:S(2)}, u32[]{:S(2)}) async-start(bf16[16,32,512]{2,1,0:T(8,128)(2,1)} %shard_map.131), calls=%async_computation | async-start | bytes 1048576 | tf_op jit(solution)/shard_map/all_to_all | solution.py:388
  36.1 4.4 %collective-permute-start.3 = (bf16[2,4,64,256]{3,2,1,0:T(8,128)(2,1)S(1)}, bf16[2,4,64,256]{3,2,1,0:T(8,128)(2,1)S(1)}, u32[]{:S(2)}, u32[]{:S(2)}) collective-permute-start(bf16[2,4,64,256]{3,2,1,0:T(8,128)(2,1)S(1)} %pad_maximum_fusion), channel_id=1, source_target_pairs={{0,1},{1,0},{2,3},{3,2},{4,5},{5,4},{6,7},{7,6},{8,9},{9,8},{10,11... | collective-permute-start | bytes 786440 | tf_op jit(solution)/shard_map/ppermute | solution.py:360
  38.1 3.6 %collective-permute-start.4 = (bf16[2,4,64,256]{3,2,1,0:T(8,128)(2,1)S(1)}, bf16[2,4,64,256]{3,2,1,0:T(8,128)(2,1)S(1)}, u32[]{:S(2)}, u32[]{:S(2)}) collective-permute-start(bf16[2,4,64,256]{3,2,1,0:T(8,128)(2,1)S(1)} %pad_maximum_fusion.1), channel_id=1, source_target_pairs={{0,1},{1,0},{2,3},{3,2},{4,5},{5,4},{6,7},{7,6},{8,9},{9,8},{10,11... | collective-permute-start | bytes 786440 | tf_op jit(solution)/shard_map/ppermute | solution.py:360
  46.7 20.0 %copy-start.2 = (bf16[256,1024]{1,0:T(8,128)(2,1)S(1)}, bf16[256,1024]{1,0:T(8,128)(2,1)}, u32[]{:S(2)}) copy-start(bf16[256,1024]{1,0:T(8,128)(2,1)} %w_ref.3) | copy-start | bytes 1572868
  46.7 20.0 %copy-start.7 = (bf16[256,256]{1,0:T(8,128)(2,1)S(1)}, bf16[256,256]{1,0:T(8,128)(2,1)}, u32[]{:S(2)}) copy-start(bf16[256,256]{1,0:T(8,128)(2,1)} %wo_ref.2) | copy-start | bytes 393220
  46.8 20.0 %copy-start.8 = (bf16[256,64]{0,1:T(8,128)(2,1)S(1)}, bf16[256,64]{0,1:T(8,128)(2,1)}, u32[]{:S(2)}) copy-start(bf16[256,64]{0,1:T(8,128)(2,1)} %param.19) | copy-start | bytes 98308
  69.4 24.3 %all-to-all-start.2 = ((bf16[8,32,256]{2,1,0:T(8,128)(2,1)}), bf16[8,32,256]{2,1,0:T(8,128)(2,1)S(1)}, u32[]{:S(2)}, u32[]{:S(2)}) async-start(bf16[8,32,256]{2,1,0:T(8,128)(2,1)} %get-tuple-element.9), calls=%async_computation.2 | async-start | bytes 262144 | tf_op jit(solution)/shard_map/all_to_all | solution.py:388
  77.9 9.5 %collective-permute-start.7 = (bf16[32,256]{1,0:T(8,128)(2,1)S(1)}, bf16[32,256]{1,0:T(8,128)(2,1)S(1)}, u32[]{:S(2)}, u32[]{:S(2)}) collective-permute-start(bf16[32,256]{1,0:T(8,128)(2,1)S(1)} %get-tuple-element.10.refs_0_), channel_id=1, source_target_pairs={{0,384},{128,256},{256,128},{384,0},{1,385},{129,257},{257,129},{3... | collective-permute-start | bytes 49160 | tf_op jit(solution)/shard_map/ppermute | solution.py:438
  80.3 9.0 %collective-permute-start.6 = (bf16[32,256]{1,0:T(8,128)(2,1)S(1)}, bf16[32,256]{1,0:T(8,128)(2,1)S(1)}, u32[]{:S(2)}, u32[]{:S(2)}) collective-permute-start(bf16[32,256]{1,0:T(8,128)(2,1)S(1)} %get-tuple-element.10.refs_0_), channel_id=1, source_target_pairs={{0,256},{128,384},{256,0},{384,128},{1,257},{129,385},{257,1},{385... | collective-permute-start | bytes 49160 | tf_op jit(solution)/shard_map/ppermute | solution.py:438
  85.5 5.6 %collective-permute-start.5 = (bf16[32,256]{1,0:T(8,128)(2,1)S(1)}, bf16[32,256]{1,0:T(8,128)(2,1)S(1)}, u32[]{:S(2)}, u32[]{:S(2)}) collective-permute-start(bf16[32,256]{1,0:T(8,128)(2,1)S(1)} %get-tuple-element.10.refs_0_), channel_id=1, source_target_pairs={{0,128},{128,0},{256,384},{384,256},{1,129},{129,1},{257,385},{385... | collective-permute-start | bytes 49160 | tf_op jit(solution)/shard_map/ppermute | solution.py:438
  93.8 23.2 %copy-start = (bf16[64,32,128]{2,1,0:T(8,128)(2,1)S(1)}, bf16[64,32,128]{2,1,0:T(8,128)(2,1)}, u32[]{:S(2)}) copy-start(bf16[64,32,128]{2,1,0:T(8,128)(2,1)} %pair_ref.3) | copy-start | bytes 1572868
  93.8 23.2 %copy-start.4 = (bf16[1024,128]{1,0:T(8,128)(2,1)S(1)}, bf16[1024,128]{1,0:T(8,128)(2,1)}, u32[]{:S(2)}) copy-start(bf16[1024,128]{1,0:T(8,128)(2,1)} %wo_ref.3) | copy-start | bytes 786436
  93.8 23.1 %copy-start.6 = (bf16[128,512]{1,0:T(8,128)(2,1)S(1)}, bf16[128,512]{1,0:T(8,128)(2,1)}, u32[]{:S(2)}) copy-start(bf16[128,512]{1,0:T(8,128)(2,1)} %w_ref.4) | copy-start | bytes 393220
  136.7 17.7 %collective-permute-start.10 = (bf16[512,128]{1,0:T(8,128)(2,1)S(1)}, bf16[512,128]{1,0:T(8,128)(2,1)S(1)}, u32[]{:S(2)}, u32[]{:S(2)}) collective-permute-start(bf16[512,128]{1,0:T(8,128)(2,1)S(1)} %get-tuple-element.17.refs_0_), channel_id=1, source_target_pairs={{0,2},{1,3},{2,4},{3,5},{4,6},{5,7},{6,0},{7,1},{8,10},{9,11},{10,... | collective-permute-start | bytes 393224 | tf_op jit(solution)/shard_map/ppermute | solution.py:360
  140.4 16.3 %collective-permute-start.8 = (bf16[512,128]{1,0:T(8,128)(2,1)S(1)}, bf16[512,128]{1,0:T(8,128)(2,1)S(1)}, u32[]{:S(2)}, u32[]{:S(2)}) collective-permute-start(bf16[512,128]{1,0:T(8,128)(2,1)S(1)} %get-tuple-element.17.refs_0_), channel_id=1, source_target_pairs={{0,6},{1,7},{2,0},{3,1},{4,2},{5,3},{6,4},{7,5},{8,14},{9,15},{10,... | collective-permute-start | bytes 393224 | tf_op jit(solution)/shard_map/ppermute | solution.py:360
  146.5 25.0 %collective-permute-start.9 = (bf16[512,128]{1,0:T(8,128)(2,1)S(1)}, bf16[512,128]{1,0:T(8,128)(2,1)S(1)}, u32[]{:S(2)}, u32[]{:S(2)}) collective-permute-start(bf16[512,128]{1,0:T(8,128)(2,1)S(1)} %get-tuple-element.17.refs_0_), channel_id=1, source_target_pairs={{0,4},{1,5},{2,6},{3,7},{4,0},{5,1},{6,2},{7,3},{8,12},{9,13},{10,... | collective-permute-start | bytes 393224 | tf_op jit(solution)/shard_map/ppermute | solution.py:360
  156.7 16.7 %collective-permute-start.12 = (bf16[2,512,128]{2,1,0:T(8,128)(2,1)S(1)}, bf16[2,512,128]{2,1,0:T(8,128)(2,1)S(1)}, u32[]{:S(2)}, u32[]{:S(2)}) collective-permute-start(bf16[2,512,128]{2,1,0:T(8,128)(2,1)S(1)} %pad_maximum_fusion.3), channel_id=1, source_target_pairs={{0,1},{1,0},{2,3},{3,2},{4,5},{5,4},{6,7},{7,6},{8,9},{9,8},{10,11... | collective-permute-start | bytes 786440 | tf_op jit(solution)/shard_map/ppermute | solution.py:360
  171.4 21.1 %copy-start.9 = (bf16[128,128]{1,0:T(8,128)(2,1)S(1)}, bf16[128,128]{1,0:T(8,128)(2,1)}, u32[]{:S(2)}) copy-start(bf16[128,128]{1,0:T(8,128)(2,1)} %wg_ref.1) | copy-start | bytes 98308
  171.4 21.1 %copy-start.10 = (bf16[128,128]{1,0:T(8,128)(2,1)S(1)}, bf16[128,128]{1,0:T(8,128)(2,1)}, u32[]{:S(2)}) copy-start(bf16[128,128]{1,0:T(8,128)(2,1)} %w_ref.5) | copy-start | bytes 98308
  171.5 3.4 %collective-permute-start.11 = (bf16[2,512,128]{2,1,0:T(8,128)(2,1)S(1)}, bf16[2,512,128]{2,1,0:T(8,128)(2,1)S(1)}, u32[]{:S(2)}, u32[]{:S(2)}) collective-permute-start(bf16[2,512,128]{2,1,0:T(8,128)(2,1)S(1)} %pad_maximum_fusion.2), channel_id=1, source_target_pairs={{0,1},{1,0},{2,3},{3,2},{4,5},{5,4},{6,7},{7,6},{8,9},{9,8},{10,11... | collective-permute-start | bytes 786440 | tf_op jit(solution)/shard_map/ppermute | solution.py:360
